TPU v7x, 32 devices: a whole 2x2x4 slice. The times are simulated.
32 devices in a mesh: rt: 8 (over y, x, core), ct: 4 (over z).
Axes of the slice: x: 2, y: 2, z: 4, core: 2. Of those that a mesh axis runs over, the one named last changes fastest.
Arguments:
- factor_rows: float32 [48, 2, 1024, 1024], P('rt', None, 'ct'), as said below
- slot_row: int32 [48], replicated, may hold values from -1 to 31, as said below
- known: float32 [48, 1024, 256], P('rt', 'ct'), may hold values from -6 to 6
- rhs: float32 [2, 1024, 256], P(None, 'ct', 'rt'), may hold values from -6 to 6
Outputs:
- solved: float32 [2, 1024, 256], P(None, 'ct', 'rt')
Inputs may be any that keep to these rules, and one draw needn't show every extreme that they name: `slot_row`: each row tile 0 to 31 stands in exactly one slot; the other slots hold -1. The slots of one index of rt are the 6 consecutive ones; at most 6 are live, and some index of rt has all 6 live. `factor_rows`: diagonal tiles L[0, 0] and L[1, 1] are lower triangular with diagonal entries from 1 to 2; the entry block (0, 1) is zero; entries of empty slots are arbitrary.
All inputs are finite; a program needn't handle non-finite values.
Results may differ from a plain program's by a relative error of at most 0.0003.
Values sent between devices are 32-bit elements; how exact they have to be, the bound alone decides.
No kernel may reach another device: no remote copies, remote signals or barrier semaphores. Data moves between devices by JAX's collectives and lax.ppermute only.
A program may use at most 64 MiB of HBM per device.

v0:
```python
import jax
import jax.numpy as jnp
from jax import lax
from jax.sharding import PartitionSpec as P


def spread(value, axis, root):
    mine = lax.axis_index(axis) == root
    return lax.psum(jnp.where(mine, value, jnp.zeros_like(value)), axis)


def shards(factor_rows, slot_row, known, rhs):
    high = lax.Precision.HIGHEST
    band = known.shape[1]
    columns = rhs.shape[2]
    slot_count = factor_rows.shape[0]
    offset = lax.axis_index("ct") * band
    col_offset = lax.axis_index("rt") * columns
    local_rows = lax.dynamic_slice_in_dim(
        slot_row, lax.axis_index("rt") * slot_count, slot_count, 0
    )
    live = (local_rows >= 2).astype(jnp.float32)
    masked = known * live[:, None, None]
    partial_value = jnp.einsum("scka,skr->car", factor_rows, masked, precision=high)
    pick_zero = local_rows == 0
    pick_one = local_rows == 1
    diag_zero = jnp.sum(jnp.where(pick_zero[:, None, None], factor_rows[:, 0], 0.0), 0)
    diag_one = jnp.sum(jnp.where(pick_one[:, None, None], factor_rows[:, 1], 0.0), 0)
    lower_one = jnp.sum(jnp.where(pick_one[:, None, None], factor_rows[:, 0], 0.0), 0)
    owner_zero = jnp.argmax(slot_row == 0) // slot_count
    owner_one = jnp.argmax(slot_row == 1) // slot_count
    tile_zero = spread(diag_zero, "rt", owner_zero)
    tile_one, tile_lower = (spread(diag_one, "rt", owner_one), spread(lower_one, "rt", owner_one))
    total = lax.psum(partial_value, ("rt", "ct"))
    rows_mine = lax.dynamic_slice_in_dim(total, offset, band, 1)
    mine = lax.dynamic_slice_in_dim(rows_mine, col_offset, columns, 2)
    residual = lax.all_gather(rhs - mine, "ct", axis=1, tiled=True)
    whole_zero, whole_one = (
        lax.all_gather(tile_zero, "ct", axis=0, tiled=True),
        lax.all_gather(tile_one, "ct", axis=0, tiled=True),
    )
    solved_one = lax.linalg.triangular_solve(
        whole_one, residual[1], left_side=True, lower=True, transpose_a=True
    )
    one_band = lax.dynamic_slice_in_dim(solved_one, offset, band, 0)
    coupling = jnp.einsum("ka,kr->ar", tile_lower, one_band, precision=high)
    coupled = lax.psum(coupling, "ct")
    solved_zero = lax.linalg.triangular_solve(
        whole_zero, residual[0] - coupled, left_side=True, lower=True, transpose_a=True
    )
    zero_band = lax.dynamic_slice_in_dim(solved_zero, offset, band, 0)
    return jnp.stack([zero_band, one_band])


def solution(mesh):
    in_specs = (P("rt", None, "ct", None), P(), P("rt", "ct", None), P(None, "ct", "rt"))
    out_specs = P(None, "ct", "rt")
    return jax.shard_map(shards, mesh=mesh, in_specs=in_specs, out_specs=out_specs, check_vma=False)
```

profile of v0, /device:TPU:0, one launch (start us, length us, event | category | flops | bytes accessed | tf_op | source)
XLA Modules:
  0.0 562.1 jit_solution(5160775739267857526)
XLA Ops:
  6.5 1.4 compare_reduce_fusion
  10.0 1.4 compare_reduce_fusion.1
  13.5 0.7 compare_convert_fusion
  14.2 6.1 %fusion.2 = (f32[256,1024]{1,0:T(8,128)S(1)}, f32[256,1024]{1,0:T(8,128)S(1)}, f32[256,1024]{1,0:T(8,128)S(1)}) fusion(f32[6,2,256,1024]{3,2,1,0:T(8,128)} %param.6, pred[6]{0:T(512)(128)(4,1)S(1)} %get-tuple-element.53, pred[6]{0:T(512)(128)(4,1)S(1)} %get-tuple-element.54), kind=kLoop, calls=%fused_computation.9 | loop fusion | flops 8650752 | bytes 15728652 | tf_op jit(solution)/shard_map/reduce_sum | solution.py:29
  20.3 1.1 broadcast_select_fusion.2
  21.4 1.6 broadcast_select_fusion
  23.3 14.9 %convolution_bitcast_fusion = f32[2,1024,256]{1,2,0:T(8,128)} fusion(f32[6,2,256,1024]{3,2,1,0:T(8,128)} %param.6, f32[6,256,256]{2,1,0:T(8,128)S(1)} %copy-done, f32[6]{0:T(128)S(1)} %get-tuple-element.52), kind=kOutput, calls=%fused_computation.13 | convolution fusion | flops 9664069632 | bytes 16252952 | tf_op jit(solution)/shard_map/scka,skr->car/dot_general | solution.py:24
  38.3 57.5 %all-reduce.9.cloned.1.call-done = (f32[256,1024]{1,0:T(8,128)}, f32[256,1024]{1,0:T(8,128)}, f32[256,1024]{1,0:T(8,128)}) async-done(((f32[256,1024]{1,0:T(8,128)}, f32[256,1024]{1,0:T(8,128)}, f32[256,1024]{1,0:T(8,128)}), (f32[256,1024]{1,0:T(8,128)}, f32[256,1024]{1,0:T(8,128)}, f32[256,1024]{1,0:T(8,128)})) %all-reduce.9.cloned.1.call-update) | async-done | bytes 3145744 | tf_op jit(solution)/shard_map/psum | solution.py:9
  95.9 140.0 %all-reduce.5.cloned.1.call-done = f32[2,1024,256]{1,2,0:T(8,128)} async-done(((f32[2,1024,256]{1,2,0:T(8,128)}), f32[2,1024,256]{1,2,0:T(8,128)}) %all-reduce.5.cloned.1.call-update) | async-done | bytes 2097168 | tf_op jit(solution)/shard_map/psum | solution.py:34
  235.9 1.0 dynamic-slice_subtract_fusion
  236.9 14.7 %all_gather.10 = f32[2,1024,32]{1,2,0:T(8,128)S(1)} all-gather(f32[2,256,32]{1,2,0:T(8,128)S(1)} %dynamic-slice_subtract_fusion), channel_id=1, replica_groups=mesh['rt'=8,'ct'=4] {'ct'}, dimensions={1}, use_global_device_ids=true | all-gather | bytes 327680 | tf_op jit(solution)/shard_map/all_gather | solution.py:37
  251.8 66.0 %all-gather.5.cloned.1.call-done = f32[1024,1024]{1,0:T(8,128)} async-done(((f32[256,1024]{1,0:T(8,128)}), f32[1024,1024]{1,0:T(8,128)}) %all-gather.5.cloned.1.call-update) | async-done | bytes 4194320 | tf_op jit(solution)/shard_map/all_gather | solution.py:40
  317.8 4.7 fusion.3
  322.6 22.5 %while.4 = (s32[]{:T(128)}, f32[1024,1024]{1,0:T(8,128)}, s32[8,2]{0,1:T(2,128)S(1)}, f32[8,128,128]{2,1,0:T(8,128)S(1)}, s32[]{:T(128)}) while((s32[]{:T(128)}, f32[1024,1024]{1,0:T(8,128)}, s32[8,2]{0,1:T(2,128)S(1)}, f32[8,128,128]{2,1,0:T(8,128)S(1)}, s32[]{:T(128)}) %tuple.49), condition=%wide.while_cond, body=%wide.while_body.sunk | while | flops 2 | bytes 131181 | solution.py:42
  322.7 0.5 fusion.106
  323.2 2.2 bitcast_dynamic-update-slice_fusion.4
  326.1 2.2 bitcast_dynamic-update-slice_fusion.4
  328.9 2.2 bitcast_dynamic-update-slice_fusion.4
  331.2 0.5 fusion.106
  331.7 2.2 bitcast_dynamic-update-slice_fusion.4
  334.0 0.5 fusion.106
  334.5 2.2 bitcast_dynamic-update-slice_fusion.4
  336.8 0.5 fusion.106
  337.3 2.2 bitcast_dynamic-update-slice_fusion.4
  339.6 0.5 fusion.106
  340.2 2.2 bitcast_dynamic-update-slice_fusion.4
  343.0 2.1 bitcast_dynamic-update-slice_fusion.4
  345.1 78.6 %custom-call.4 = f32[8,128,128]{1,2,0:T(8,128)S(1)} custom-call(f32[8,128,128]{2,1,0:T(8,128)S(1)} %get-tuple-element.24), custom_call_target="InvertDiagBlocksLowerTriangular" | custom-call | tf_op jit(solution)/shard_map/triangular_solve/custom-call.1 | solution.py:42
  423.9 1.0 convolution_subtract_fusion.7
  425.2 1.1 convolution_subtract_fusion.6
  426.5 1.2 convolution_subtract_fusion.5
  427.9 1.2 convolution_subtract_fusion.4
  429.4 1.3 convolution_subtract_fusion.13
  431.0 1.3 convolution_subtract_fusion.12
  432.6 1.4 convolution_subtract_fusion.11
  434.3 1.4 fusion.67
  435.8 4.7 fusion.4
  440.5 24.2 %while.5 = (s32[]{:T(128)}, f32[1024,1024]{1,0:T(8,128)}, s32[8,2]{0,1:T(2,128)S(1)}, f32[8,128,128]{2,1,0:T(8,128)S(1)}, s32[]{:T(128)}) while((s32[]{:T(128)}, f32[1024,1024]{1,0:T(8,128)}, s32[8,2]{0,1:T(2,128)S(1)}, f32[8,128,128]{2,1,0:T(8,128)S(1)}, s32[]{:T(128)}) %tuple.66), condition=%wide.while_cond.clone, body=%wide.while_body.clone.sunk | while | flops 2 | bytes 131181 | solution.py:48
  440.6 0.6 fusion.107
  441.2 2.3 bitcast_dynamic-update-slice_fusion.5
  443.6 0.6 fusion.107
  444.2 2.3 bitcast_dynamic-update-slice_fusion.5
  446.7 0.6 fusion.107
  447.3 2.3 bitcast_dynamic-update-slice_fusion.5
  449.7 0.6 fusion.107
  450.3 2.3 bitcast_dynamic-update-slice_fusion.5
  452.7 0.6 fusion.107
  453.3 2.3 bitcast_dynamic-update-slice_fusion.5
  455.8 0.6 fusion.107
  456.4 2.3 bitcast_dynamic-update-slice_fusion.5
  458.8 0.6 fusion.107
  459.4 2.3 bitcast_dynamic-update-slice_fusion.5
  461.8 0.6 fusion.107
  462.4 2.3 bitcast_dynamic-update-slice_fusion.5
  464.7 78.6 %custom-call.5 = f32[8,128,128]{1,2,0:T(8,128)S(1)} custom-call(f32[8,128,128]{2,1,0:T(8,128)S(1)} %get-tuple-element.25), custom_call_target="InvertDiagBlocksLowerTriangular" | custom-call | tf_op jit(solution)/shard_map/triangular_solve/custom-call.1 | solution.py:48
  543.3 0.9 fusion.20
  544.5 1.0 convolution_subtract_fusion.3
  545.7 1.1 convolution_subtract_fusion.2
  547.0 1.2 convolution_subtract_fusion.1
  548.4 1.2 convolution_subtract_fusion
  550.0 1.3 convolution_subtract_fusion.10
  551.5 1.3 convolution_subtract_fusion.9
  553.2 1.4 convolution_subtract_fusion.8
  554.9 0.6 pad_maximum_fusion
  (104 shorter events, 6.9 us)
Async XLA Ops:
  6.5 89.3 %all-reduce.9.cloned.1.call-start = ((), (), s32[]{:S(2)}) async-start(), calls=%async_computation.4 | async-start | bytes 6291456 | tf_op jit(solution)/shard_map/psum | solution.py:9
  21.4 1.9 copy-start
  23.1 212.8 %all-reduce.5.cloned.1.call-start = ((), (), s32[]{:S(2)}) async-start(), calls=%async_computation.1 | async-start | bytes 4194304 | tf_op jit(solution)/shard_map/psum | solution.py:34
  23.3 212.6 %copy-start.2 = (f32[2,256,32]{1,2,0:T(8,128)S(1)}, f32[2,256,32]{1,2,0:T(8,128)}, u32[]{:S(2)}) copy-start(f32[2,256,32]{1,2,0:T(8,128)} %param.9) | copy-start | bytes 196612
  38.2 279.6 %all-gather.5.cloned.1.call-start = ((), (), s32[]{:S(2)}) async-start(), calls=%async_computation.2 | async-start | bytes 5242880 | tf_op jit(solution)/shard_map/all_gather | solution.py:40
  95.8 339.9 %all-gather.3.cloned.1.call-start = ((), (), s32[]{:S(2)}) async-start(), calls=%async_computation | async-start | bytes 5242880 | tf_op jit(solution)/shard_map/all_gather | solution.py:39
  251.6 291.7 %all-reduce.7.cloned.1.call-start = ((), (), s32[]{:S(2)}) async-start(), calls=%async_computation.3 | async-start | bytes 262144 | tf_op jit(solution)/shard_map/psum | solution.py:47
  322.6 111.8 %copy-start.1 = (f32[256,1024]{1,0:T(8,128)S(1)}, f32[256,1024]{1,0:T(8,128)}, u32[]{:S(2)}) copy-start(f32[256,1024]{1,0:T(8,128)} %get-tuple-element.47) | copy-start | bytes 3145732
Sparse Core Ops, SparseCore 0:
  23.2 72.5 all-reduce.8
  102.0 133.8 all-reduce.4
  237.5 80.3 all-gather.4
  319.2 79.3 all-gather.2
  435.9 33.0 all-reduce.6
where the time goes:
time: 564 us; the launch traced here: 562 us
  waiting for transfers between devices  264 us (47%)
  other arithmetic  182 us (32%)
  local copies, waits for them, and re-layouts  47 us (8%)
  matrix products  36.6 us (6%)
  between operations  18 us (3%)
  blocking collectives  14.7 us (3%)
    psum x1, waiting for transfers between devices, shards(): total = lax.psum(partial_value, ('rt', 'ct'))  140 us
    another operation x3, other arithmetic, shards(): lax.linalg.triangular_solve(whole_zero, residual[0] - coupled, left_side=...  83.3 us
    another operation x2, other arithmetic, shards(): lax.linalg.triangular_solve(whole_one, residual[1], left_side=True, lower...  83.3 us
    all_gather x1, waiting for transfers between devices, shards(): lax.all_gather(tile_one, 'ct', axis=0, tiled=True)  66 us
    psum x1, waiting for transfers between devices, spread(): return lax.psum(jnp.where(mine, value, jnp.zeros_like(value)), axis)  57.5 us
    another operation x31, local copies, waits for them, and re-layouts, shards(): lax.linalg.triangular_solve(whole_zero, residual[0] - coupled, left_side=...  24.1 us
    another operation x28, local copies, waits for them, and re-layouts, shards(): lax.linalg.triangular_solve(whole_one, residual[1], left_side=True, lower...  22.4 us
    dot_general x1, matrix products, shards(): jnp.einsum('scka,skr->car', factor_rows, masked, precision=high)  14.9 us
  transfers between devices with their start and end apart: 5, of which 3 were waited for; matrix products, arithmetic and copies ran while one was open for 43% of the time, Pallas kernels for 0%

commit v1 on v0

v1 whole, which is shorter than its diff:
```python
import functools

import jax
import jax.numpy as jnp
from jax import lax
from jax.experimental import pallas as pl
from jax.experimental.pallas import tpu as pltpu
from jax.sharding import PartitionSpec as P

F32 = jnp.float32
BF16 = jnp.bfloat16
VMEM = pltpu.MemorySpace.VMEM
SMEM = pltpu.MemorySpace.SMEM


def split(value):
    high = value.astype(BF16)
    return high, (value - high.astype(F32)).astype(BF16)


def dot_split(a, b, dims):
    (ah, al), (bh, bl) = a, b

    def one(u, v):
        return lax.dot_general(u, v, (dims, ((), ())), preferred_element_type=F32)

    return one(al, bh) + one(ah, bl) + one(ah, bh)


def dot3(a, b):
    return dot_split(split(a), split(b), ((1,), (0,)))


def partial_kernel(rows_ref, order_ref, factor_ref, known_ref, out_ref, acc_ref, *, columns, groups):
    step = pl.program_id(0)

    @pl.when(step == 0)
    def _():
        acc_ref[...] = jnp.zeros_like(acc_ref)

    @pl.when(rows_ref[step] >= 2)
    def _():
        acc_ref[...] += dot_split(split(known_ref[0]), split(factor_ref[0, 0]), ((0,), (0,)))

    @pl.when(step == pl.num_programs(0) - 1)
    def _():
        for place in range(groups):
            start = pl.multiple_of(order_ref[place] * columns, columns)
            out_ref[place] = acc_ref[pl.ds(start, columns), :]


def partial_product(local_rows, order, factor_rows, known, column, columns):
    slots, _, band, width = factor_rows.shape
    total = known.shape[2]
    groups = total // columns
    return pl.pallas_call(
        functools.partial(partial_kernel, columns=columns, groups=groups),
        out_shape=jax.ShapeDtypeStruct((groups, columns, width), F32),
        grid_spec=pltpu.PrefetchScalarGridSpec(
            num_scalar_prefetch=2,
            grid=(slots,),
            in_specs=[
                pl.BlockSpec((1, 1, band, width), lambda s, r, o: (s, column, 0, 0)),
                pl.BlockSpec((1, band, total), lambda s, r, o: (s, 0, 0)),
            ],
            out_specs=pl.BlockSpec((groups, columns, width), lambda s, r, o: (0, 0, 0)),
            scratch_shapes=[pltpu.VMEM((total, width), F32)],
        ),
        compiler_params=pltpu.CompilerParams(vmem_limit_bytes=32 << 20),
        name="partial",
    )(local_rows, order, factor_rows, known)


def invert_kernel(block_ref, out_ref):
    size = block_ref.shape[0]
    block = block_ref[...]
    row = lax.broadcasted_iota(jnp.int32, (size, size), 0)
    col = lax.broadcasted_iota(jnp.int32, (size, size), 1)
    diag = jnp.where(row == col, block, 0.0)
    recip_row = 1.0 / jnp.sum(diag, axis=0, keepdims=True)
    recip_col = 1.0 / jnp.sum(diag, axis=1, keepdims=True)
    pair = (row - col == 1) & (lax.rem(row, 2) == 1)
    inverse = jnp.where(row == col, recip_row, jnp.where(pair, -(block * recip_row) * recip_col, 0.0))
    step = 2
    while step < size:
        half = lax.div(row, step)
        below = (half - lax.div(col, step) == 1) & (lax.rem(half, 2) == 1)
        lower = jnp.where(below, block, 0.0)
        parts = split(inverse)
        middle = dot_split(split(lower), parts, ((1,), (0,)))
        inverse = inverse - dot_split(parts, split(middle), ((1,), (0,)))
        step *= 2
    out_ref[...] = inverse


def invert(block):
    return pl.pallas_call(
        invert_kernel,
        out_shape=jax.ShapeDtypeStruct(block.shape, F32),
        in_specs=[pl.BlockSpec(memory_space=VMEM)],
        out_specs=pl.BlockSpec(memory_space=VMEM),
        compiler_params=pltpu.CompilerParams(vmem_limit_bytes=32 << 20),
        name="invert",
    )(block)


def stage_kernel(place_ref, base_ref, inverse_ref, tile_ref, add_ref, message_ref, held_ref, solved_ref, update_ref, *, stage):
    band = base_ref.shape[1]

    @pl.when(place_ref[0] == stage)
    def _():
        message = message_ref[...]
        right = base_ref[...] - message[:, stage * band :]
        solved = dot3(right, inverse_ref[...])
        solved_ref[...] = solved
        if stage > 0:
            update = message[:, : stage * band] + dot3(solved, tile_ref[:, : stage * band])
            update_ref[...] = update + add_ref[:, : stage * band]

    @pl.when(place_ref[0] != stage)
    def _():
        solved_ref[...] = held_ref[...]


def run_stage(place, base, inverse, tile, add, message, held, stage):
    columns, band = base.shape
    width = max(stage, 1) * band
    vmem = pl.BlockSpec(memory_space=VMEM)
    return pl.pallas_call(
        functools.partial(stage_kernel, stage=stage),
        out_shape=(jax.ShapeDtypeStruct((columns, band), F32), jax.ShapeDtypeStruct((columns, width), F32)),
        in_specs=[pl.BlockSpec(memory_space=SMEM)] + [vmem] * 6,
        out_specs=(vmem, vmem),
        compiler_params=pltpu.CompilerParams(vmem_limit_bytes=32 << 20),
        name="stage",
    )(place, base, inverse, tile, add, message, held)


def run_stage_plain(place, base, inverse, tile, add, message, held, stage):
    high = lax.Precision.HIGHEST
    band = base.shape[1]
    right = base - message[:, stage * band :]
    solved = jnp.dot(right, inverse, precision=high)
    active = place[0] == stage
    width = max(stage, 1) * band
    update = jnp.dot(solved, tile[:, :width], precision=high) + add[:, :width]
    if stage > 0:
        update = update + message[:, :width]
    return jnp.where(active, solved, held), update


def sweep(place, base, inverse, tile, add, bands):
    columns, band = base.shape
    run = run_stage if band % 128 == 0 else run_stage_plain
    message = jnp.zeros((columns, bands * band), F32)
    held = jnp.zeros((columns, band), F32)
    for stage in range(bands - 1, -1, -1):
        held, update = run(place, base, inverse, tile, add, message, held, stage)
        if stage > 0:
            message = lax.ppermute(update, "ct", [(stage, stage - 1)])
    return held


def stage_orders(members):
    bits = members.bit_length() - 1
    first = list(range(1, bits))
    return first, first[::-1]


def core_pairs(members):
    return [(i, i ^ 1) for i in range(members)]


def stage_pairs(members, stage):
    orders = stage_orders(members)
    return [(i, i ^ (1 << orders[i & 1][stage])) for i in range(members)]


def send_order(members, me):
    orders = stage_orders(members)
    count = len(orders[0])
    tables = []
    for core in range(2):
        table = []
        for place in range(members):
            other = place >> count
            rest = place & ((1 << count) - 1)
            relative = other
            for stage in range(count):
                if (rest >> (count - 1 - stage)) & 1:
                    relative |= 1 << orders[core ^ other][stage]
            table.append(relative)
        tables.append(jnp.array(table, jnp.int32))
    return me ^ jnp.where((me & 1) == 0, tables[0], tables[1])


def reduce_rows(value, members):
    half = members // 2
    value = value[:half] + lax.ppermute(value[half:], "rt", core_pairs(members))
    stage = 0
    while half > 1:
        half //= 2
        value = value[:half] + lax.ppermute(value[half:], "rt", stage_pairs(members, stage))
        stage += 1
    return value[0]


def share_band(factor_rows, local_rows, row, column, members, core):
    slots, _, band, width = factor_rows.shape
    half = band // 2
    match = local_rows == row
    slot = jnp.argmax(match).astype(jnp.int32)
    mine = jnp.any(match)

    def part(which):
        piece = lax.dynamic_slice(factor_rows, (slot, column, which * half, 0), (1, 1, half, width))
        return jnp.where(mine, piece.reshape(half, width), 0.0)

    value = part(core) + lax.ppermute(part(1 - core), "rt", core_pairs(members))
    for stage in range(len(stage_orders(members)[0])):
        value = value + lax.ppermute(value, "rt", stage_pairs(members, stage))
    other = lax.ppermute(value, "rt", core_pairs(members))
    first = core == 0
    return jnp.concatenate([jnp.where(first, value, other), jnp.where(first, other, value)], 0)


def shards(factor_rows, slot_row, known, rhs, *, members, bands):
    slots, _, band, width = factor_rows.shape
    columns = rhs.shape[2]
    me = lax.axis_index("rt")
    place = lax.axis_index("ct")
    core = me & 1
    place_ref = place.astype(jnp.int32).reshape(1)
    local_rows = lax.dynamic_slice_in_dim(slot_row, me * slots, slots, 0)
    order = send_order(members, me).astype(jnp.int32)

    def own(value, where):
        return lax.dynamic_slice(value, (0, where * band), (value.shape[0], band))

    tile_one = share_band(factor_rows, local_rows, 1, 1, members, core)
    sum_one = reduce_rows(partial_product(local_rows, order, factor_rows, known, 1, columns), members)
    sum_zero = reduce_rows(partial_product(local_rows, order, factor_rows, known, 0, columns), members)
    tile_lower = share_band(factor_rows, local_rows, 1, 0, members, core)
    tile_zero = share_band(factor_rows, local_rows, 0, 0, members, core)
    inverse_one = invert(own(tile_one, place))
    inverse_zero = invert(own(tile_zero, place))

    base = rhs[1].T - own(sum_one, place)
    for shift in range(1, bands):
        piece = own(sum_one, jnp.minimum(place + shift, bands - 1))
        base = base - lax.ppermute(piece, "ct", [(i, i + shift) for i in range(bands - shift)])
    solved_one = sweep(place_ref, base, inverse_one, tile_one, sum_one, bands)

    coupling = sum_zero + jnp.dot(solved_one, tile_lower, precision=lax.Precision.HIGH)
    base = rhs[0].T - own(coupling, place)
    for mask in range(bands - 1, 0, -1):
        piece = own(coupling, place ^ mask)
        base = base - lax.ppermute(piece, "ct", [(i, i ^ mask) for i in range(bands)])
    nothing = jnp.zeros((columns, width), F32)
    solved_zero = sweep(place_ref, base, inverse_zero, tile_zero, nothing, bands)
    return jnp.stack([solved_zero.T, solved_one.T])


def solution(mesh):
    members, bands = mesh.shape["rt"], mesh.shape["ct"]
    in_specs = (P("rt", None, "ct", None), P(), P("rt", "ct", None), P(None, "ct", "rt"))
    out_specs = P(None, "ct", "rt")
    body = functools.partial(shards, members=members, bands=bands)
    return jax.shard_map(body, mesh=mesh, in_specs=in_specs, out_specs=out_specs, check_vma=False)
```

time: 564 us -> 132 us (0.23)
  waiting for transfers between devices: 264 us -> 40.8 us
  other arithmetic: 182 us -> 20.1 us
  matrix products: 36.6 us -> 0.39 us
  local copies, waits for them, and re-layouts: 47 us -> 13.1 us
  starting transfers between devices: 0.35 us -> 33 us
  Pallas kernels: 0 us -> 18.9 us
  blocking collectives: 14.7 us -> 0 us
  between operations: 18 us -> 4.26 us
    psum x3 -> x0, waiting for transfers between devices: 198 us -> none  [the longest x1 140 us: shards(): total = lax.psum(partial_value, ('rt', 'ct'))]
    another operation x8 -> x3, other arithmetic: 170 us -> 2.07 us  [the longest x2 1.44 us: share_band(): slot = jnp.argmax(match).astype(jnp.int32)]
    all_gather x2 -> x0, waiting for transfers between devices: 66 us -> none  [the longest x1 66 us: shards(): lax.all_gather(tile_one, 'ct', axis=0, tiled=True)]
    another operation x61 -> x2, local copies, waits for them, and re-layouts: 46.5 us -> 0.01 us  [the longest x31 24.1 us: shards(): lax.linalg.triangular_solve(whole_zero, residual[0] - coupled, left_side=...]
    ppermute x0 -> x30, waiting for transfers between devices: none -> 40.8 us  [the longest x6 24 us: sweep(): message = lax.ppermute(update, 'ct', [(stage, stage - 1)])]
    ppermute x0 -> x30, starting transfers between devices: none -> 33 us  [the longest x3 10.5 us: shards(): lax.ppermute(piece, 'ct', [(i, i + shift) for i in range(bands - shift)])]
    another operation x30 -> x0, matrix products: 20.3 us -> none  [the longest x15 10.2 us: shards(): lax.linalg.triangular_solve(whole_one, residual[1], left_side=True, lower...]
    pallas_call x0 -> x12, Pallas kernels: none -> 18.9 us  [the longest x2 9.38 us: invert(): pl.pallas_call(invert_kernel, out_shape=jax.ShapeDtypeStruct(block.shape,...]
  transfers between devices with their start and end apart: 5 -> 30, of which waited for: 3 -> 5; matrix products, arithmetic and copies ran while one was open for 43% -> 11% of each run, Pallas kernels for 0% -> 14%
where the time goes in v1:
time: 132 us; the launch traced here: 131 us
  waiting for transfers between devices  40.8 us (31%)
  starting transfers between devices  33 us (25%)
  other arithmetic  20.1 us (15%)
  Pallas kernels  18.9 us (14%)
  local copies, waits for them, and re-layouts  13.1 us (10%)
  between operations  4.26 us (3%)
    ppermute x6, waiting for transfers between devices, sweep(): message = lax.ppermute(update, 'ct', [(stage, stage - 1)])  24 us
    ppermute x4, waiting for transfers between devices, reduce_rows(): lax.ppermute(value[half:], 'rt', stage_pairs(members, stage))  16.6 us
    unnamed x12, local copies, waits for them, and re-layouts  11.3 us
    ppermute x3, starting transfers between devices, shards(): lax.ppermute(piece, 'ct', [(i, i + shift) for i in range(bands - shift)])  10.5 us
    pallas_call x2, Pallas kernels, invert(): pl.pallas_call(invert_kernel, out_shape=jax.ShapeDtypeStruct(block.shape,...  9.38 us
    pallas_call x2, Pallas kernels, partial_product(): pl.pallas_call(functools.partial(partial_kernel, columns=columns, groups=...  7.76 us
    ppermute x4, starting transfers between devices, reduce_rows(): lax.ppermute(value[half:], 'rt', stage_pairs(members, stage))  5.39 us
    ppermute x6, starting transfers between devices, sweep(): message = lax.ppermute(update, 'ct', [(stage, stage - 1)])  5.24 us
  transfers between devices with their start and end apart: 30, of which 5 were waited for; matrix products, arithmetic and copies ran while one was open for 11% of the time, Pallas kernels for 14%

profile of v1, /device:TPU:0, one launch (start us, length us, event | category | flops | bytes accessed | tf_op | source)
XLA Modules:
  0.0 130.5 jit_solution(13090670219265134457)
XLA Ops:
  0.0 1.4 %compare_reduce_fusion.1 = (pred[]{:T(512)}, pred[]{:T(512)}, s32[6]{0:T(128)S(1)}) fusion(s32[48]{0:T(128)} %param.7, s32[]{:T(128)S(6)} %select_n.137), kind=kLoop, calls=%fused_computation.48 | loop fusion | flops 22 | bytes 54 | tf_op jit(solution)/shard_map/reduce_or | solution.py:213
  1.4 0.7 compare_reduce_fusion
  3.4 0.7 compare_reduce_fusion.2
  6.6 4.0 %select_bitcast_fusion = (f32[128,1024]{1,0:T(8,128)}, f32[128,1024]{1,0:T(8,128)}, f32[128,1024]{1,0:T(8,128)}) fusion(f32[6,2,256,1024]{3,2,1,0:T(8,128)} %factor_ref.3, s32[]{:T(128)S(6)} %select_n.165, s32[]{:T(128)S(6)} %select_n.150, pred[]{:T(512)} %get-tuple-element.37, s32[]{:T(128)S(6)} %select_n.146, pred[]{:T(512)} %get-tuple-element.38), kind=kLoop, calls=%fused_computation.15 | loop fusion | flops 393216 | bytes 3145742 | tf_op jit(solution)/shard_map/jit(_where)/select_n | solution.py:217
  10.7 0.4 collective-permute-start.23
  11.1 0.1 collective-permute-start.16
  11.2 0.4 collective-permute-start.9
  11.6 0.7 fusion.14.order_ref
  12.3 4.6 %copy-done = f32[6,2,256,1024]{3,2,1,0:T(8,128)S(1)} copy-done((f32[6,2,256,1024]{3,2,1,0:T(8,128)S(1)}, f32[6,2,256,1024]{3,2,1,0:T(8,128)}, u32[]{:S(2)}) %copy-start) | copy-done | bytes 12582936
  16.8 1.4 %copy-done.2 = f32[6,256,256]{2,1,0:T(8,128)S(1)} copy-done((f32[6,256,256]{2,1,0:T(8,128)S(1)}, f32[6,256,256]{2,1,0:T(8,128)}, u32[]{:S(2)}) %copy-start.2) | copy-done | bytes 1572888
  18.2 3.9 %partial.3 = f32[8,32,1024]{2,1,0:T(8,128)S(1)} custom-call(s32[6]{0:T(128)S(1)} %get-tuple-element.39.rows_ref, s32[8]{0:T(128)S(1)} %fusion.14.order_ref, f32[6,2,256,1024]{3,2,1,0:T(8,128)S(1)} %copy-done, f32[6,256,256]{2,1,0:T(8,128)S(1)} %copy-done.2), custom_call_target="tpu_custom_call" | custom-call | tf_op jit(solution)/shard_map/partial/pallas_call | solution.py:56
  22.1 0.8 slice.63
  23.0 0.7 collective-permute-start.3
  23.7 0.8 copy-done.4
  24.5 3.5 %bitcast_add_fusion = (f32[128,1024]{1,0:T(8,128)S(1)}, f32[128,1024]{1,0:T(8,128)S(1)}, f32[128,1024]{1,0:T(8,128)S(1)}) fusion(f32[128,1024]{1,0:T(8,128)} %copy-done.4, f32[6,2,256,1024]{3,2,1,0:T(8,128)} %factor_ref.3, s32[]{:T(128)S(6)} %select_n.165, s32[]{:T(128)S(6)} %select_n.147, pred[]{:T(512)} %get-tuple-element.37, ...), kind=kLoop, calls=%fused_computation.12 | loop fusion | flops 786432 | bytes 4718606 | tf_op jit(solution)/shard_map/add | solution.py:219
  28.0 1.3 collective-permute-start.24
  29.2 0.8 collective-permute-start.10
  30.1 1.1 slice_add_fusion
  31.2 1.3 collective-permute-start.4
  32.5 4.6 %copy-done.1 = f32[6,2,256,1024]{3,2,1,0:T(8,128)S(1)} copy-done((f32[6,2,256,1024]{3,2,1,0:T(8,128)S(1)}, f32[6,2,256,1024]{3,2,1,0:T(8,128)}, u32[]{:S(2)}) %copy-start.1) | copy-done | bytes 12582936
  37.1 3.9 %partial.2 = f32[8,32,1024]{2,1,0:T(8,128)S(1)} custom-call(s32[6]{0:T(128)S(1)} %get-tuple-element.39.rows_ref, s32[8]{0:T(128)S(1)} %fusion.14.order_ref, f32[6,2,256,1024]{3,2,1,0:T(8,128)S(1)} %copy-done.1, f32[6,256,256]{2,1,0:T(8,128)S(1)} %copy-done.3), custom_call_target="tpu_custom_call" | custom-call | tf_op jit(solution)/shard_map/partial/pallas_call | solution.py:56
  41.0 0.8 slice.57
  41.8 0.3 collective-permute-start
  42.2 0.5 collective-permute-start.25
  42.7 0.1 collective-permute-done.10
  42.9 1.8 %collective-permute-start.11 = (f32[128,1024]{1,0:T(8,128)S(1)}, f32[128,1024]{1,0:T(8,128)}, u32[]{:S(2)}, u32[]{:S(2)}) collective-permute-start(f32[128,1024]{1,0:T(8,128)S(1)} %add.122), channel_id=1, source_target_pairs={{0,16},{4,12},{8,24},{12,4},{16,0},{20,28},{24,8},{28,20},{1,17},{... | collective-permute-start | bytes 1572872 | tf_op jit(solution)/shard_map/ppermute | solution.py:221
  44.7 1.5 %collective-permute-done.4 = f32[2,32,1024]{2,1,0:T(8,128)S(1)} collective-permute-done((f32[2,32,1024]{2,1,0:T(8,128)S(1)}, f32[2,32,1024]{2,1,0:T(8,128)S(1)}, u32[]{:S(2)}, u32[]{:S(2)}) %collective-permute-start.4) | collective-permute-done | bytes 262176 | tf_op jit(solution)/shard_map/ppermute | solution.py:203
  46.2 1.8 %collective-permute-start.5 = (f32[1,32,1024]{2,1,0:T(8,128)S(1)}, f32[1,32,1024]{2,1,0:T(8,128)S(1)}, u32[]{:S(2)}, u32[]{:S(2)}) collective-permute-start(f32[1,32,1024]{2,1,0:T(8,128)S(1)} %slice.67), channel_id=1, source_target_pairs={{0,16},{4,12},{8,24},{12,4},{16,0},{20,28},{24,8},{28,20},{1,17},{... | collective-permute-start | bytes 393224 | tf_op jit(solution)/shard_map/ppermute | solution.py:203
  48.1 15.1 %collective-permute-done.5 = f32[1,32,1024]{2,1,0:T(8,128)S(1)} collective-permute-done((f32[1,32,1024]{2,1,0:T(8,128)S(1)}, f32[1,32,1024]{2,1,0:T(8,128)S(1)}, u32[]{:S(2)}, u32[]{:S(2)}) %collective-permute-start.5) | collective-permute-done | bytes 131104 | tf_op jit(solution)/shard_map/ppermute | solution.py:203
  63.2 6.7 %collective-permute-start.8 = (f32[32,256]{1,0:T(8,128)S(1)}, f32[32,256]{1,0:T(8,128)S(1)}, u32[]{:S(2)}, u32[]{:S(2)}) collective-permute-start(f32[32,256]{1,0:T(8,128)S(1)} %get-tuple-element.56), channel_id=1, source_target_pairs={{0,3},{4,7},{8,11},{12,15},{16,19},{20,23},{24,27},{28,31}} | collective-permute-start | bytes 98312 | tf_op jit(solution)/shard_map/ppermute | solution.py:251
  69.9 1.1 add.125
  71.0 0.4 collective-permute-start.18
  71.4 1.1 add.134
  72.5 0.3 collective-permute-start.26
  72.8 1.1 add.123
  73.9 0.3 collective-permute-start.12
  74.3 1.3 collective-permute-start.7
  75.6 2.5 %collective-permute-start.6 = (f32[32,256]{1,0:T(8,128)S(1)}, f32[32,256]{1,0:T(8,128)S(1)}, u32[]{:S(2)}, u32[]{:S(2)}) collective-permute-start(f32[32,256]{1,0:T(8,128)S(1)} %get-tuple-element.55), channel_id=1, source_target_pairs={{0,1},{1,2},{2,3},{4,5},{5,6},{6,7},{8,9},{9,10},{10,11},{12,13},{... | collective-permute-start | bytes 98312 | tf_op jit(solution)/shard_map/ppermute | solution.py:251
  78.1 1.1 slice_add_fusion.1
  79.2 1.8 %collective-permute-start.1 = (f32[2,32,1024]{2,1,0:T(8,128)S(1)}, f32[2,32,1024]{2,1,0:T(8,128)S(1)}, u32[]{:S(2)}, u32[]{:S(2)}) collective-permute-start(f32[2,32,1024]{2,1,0:T(8,128)S(1)} %slice.59), channel_id=1, source_target_pairs={{0,8},{4,20},{8,0},{12,28},{16,24},{20,4},{24,16},{28,12},{1,9},{5... | collective-permute-start | bytes 786440 | tf_op jit(solution)/shard_map/ppermute | solution.py:203
  81.1 1.1 add.126
  82.2 0.1 collective-permute-start.19
  82.3 1.2 broadcast_select_fusion
  83.5 4.7 %invert.2.inverse_ref = f32[256,256]{1,0:T(8,128)S(1)} custom-call(f32[256,256]{1,0:T(8,128)S(1)} %fusion.5.block_ref), custom_call_target="tpu_custom_call" | custom-call | tf_op jit(solution)/shard_map/invert/pallas_call | solution.py:97
  88.2 0.1 pad_maximum_fusion.tile_ref
  88.4 0.7 collective-permute-start.13
  89.1 0.5 collective-permute-start.2
  89.6 0.7 collective-permute-start.14
  90.3 0.1 broadcast_select_fusion.3
  90.4 1.3 collective-permute-start.15
  91.7 0.1 pad_maximum_fusion.1.tile_ref
  91.8 12.7 %collective-permute-done.15.message_ref = f32[32,256]{1,0:T(8,128)S(1)} collective-permute-done((f32[32,256]{1,0:T(8,128)S(1)}, f32[32,256]{1,0:T(8,128)S(1)}, u32[]{:S(2)}, u32[]{:S(2)}) %collective-permute-start.15) | collective-permute-done | bytes 32800 | tf_op jit(solution)/shard_map/ppermute | solution.py:160
  104.5 0.8 stage.11
  105.4 0.4 fusion.7
  105.8 0.1 collective-permute-start.22
  105.9 0.1 collective-permute-start.21
  105.9 4.3 %collective-permute-start.20 = (f32[32,256]{1,0:T(8,128)S(1)}, f32[32,256]{1,0:T(8,128)S(1)}, u32[]{:S(2)}, u32[]{:S(2)}) collective-permute-start(f32[32,256]{1,0:T(8,128)S(1)} %get-tuple-element.52), channel_id=1, source_target_pairs={{0,3},{1,2},{2,1},{3,0},{4,7},{5,6},{6,5},{7,4},{8,11},{9,10},{10,... | collective-permute-start | bytes 98312 | tf_op jit(solution)/shard_map/ppermute | solution.py:258
  110.3 4.7 %invert.3.inverse_ref = f32[256,256]{1,0:T(8,128)S(1)} custom-call(f32[256,256]{1,0:T(8,128)S(1)} %fusion.4.block_ref), custom_call_target="tpu_custom_call" | custom-call | tf_op jit(solution)/shard_map/invert/pallas_call | solution.py:97
  115.0 0.7 collective-permute-start.27
  115.7 0.7 collective-permute-start.28
  116.5 1.3 collective-permute-start.29
  117.8 11.3 %collective-permute-done.29.message_ref = f32[32,256]{1,0:T(8,128)S(1)} collective-permute-done((f32[32,256]{1,0:T(8,128)S(1)}, f32[32,256]{1,0:T(8,128)S(1)}, u32[]{:S(2)}, u32[]{:S(2)}) %collective-permute-start.29) | collective-permute-done | bytes 32800 | tf_op jit(solution)/shard_map/ppermute | solution.py:160
  129.1 0.8 stage.15
  129.9 0.6 pad_maximum_fusion.2
  (57 shorter events, 0.6 us)
Async XLA Ops:
  6.6 25.9 %copy-start.3 = (f32[6,256,256]{2,1,0:T(8,128)S(1)}, f32[6,256,256]{2,1,0:T(8,128)}, u32[]{:S(2)}) copy-start(f32[6,256,256]{2,1,0:T(8,128)} %known_ref.3) | copy-start | bytes 4718596
  10.7 13.0 %collective-permute-start.23 = (f32[128,1024]{1,0:T(8,128)}, f32[128,1024]{1,0:T(8,128)S(1)}, u32[]{:S(2)}, u32[]{:S(2)}) collective-permute-start(f32[128,1024]{1,0:T(8,128)} %get-tuple-element.43), channel_id=1, source_target_pairs={{0,4},{4,0},{8,12},{12,8},{16,20},{20,16},{24,28},{28,24},{1,5},{5... | collective-permute-start | bytes 1572872 | tf_op jit(solution)/shard_map/ppermute | solution.py:219
  11.1 12.6 %collective-permute-start.16 = (f32[128,1024]{1,0:T(8,128)}, f32[128,1024]{1,0:T(8,128)}, u32[]{:S(2)}, u32[]{:S(2)}) collective-permute-start(f32[128,1024]{1,0:T(8,128)} %get-tuple-element.44), channel_id=1, source_target_pairs={{0,4},{4,0},{8,12},{12,8},{16,20},{20,16},{24,28},{28,24},{1,5},{5... | collective-permute-start | bytes 1572872 | tf_op jit(solution)/shard_map/ppermute | solution.py:219
  11.2 13.3 %collective-permute-start.9 = (f32[128,1024]{1,0:T(8,128)}, f32[128,1024]{1,0:T(8,128)}, u32[]{:S(2)}, u32[]{:S(2)}) collective-permute-start(f32[128,1024]{1,0:T(8,128)} %get-tuple-element.45), channel_id=1, source_target_pairs={{0,4},{4,0},{8,12},{12,8},{16,20},{20,16},{24,28},{28,24},{1,5},{5... | collective-permute-start | bytes 1572872 | tf_op jit(solution)/shard_map/ppermute | solution.py:219
  12.3 4.6 %copy-start = (f32[6,2,256,1024]{3,2,1,0:T(8,128)S(1)}, f32[6,2,256,1024]{3,2,1,0:T(8,128)}, u32[]{:S(2)}) copy-start(f32[6,2,256,1024]{3,2,1,0:T(8,128)} %factor_ref.3) | copy-start | bytes 37748740
  16.8 1.4 %copy-start.2 = (f32[6,256,256]{2,1,0:T(8,128)S(1)}, f32[6,256,256]{2,1,0:T(8,128)}, u32[]{:S(2)}) copy-start(f32[6,256,256]{2,1,0:T(8,128)} %known_ref.3) | copy-start | bytes 4718596
  23.0 7.1 %collective-permute-start.3 = (f32[4,32,1024]{2,1,0:T(8,128)}, f32[4,32,1024]{2,1,0:T(8,128)}, u32[]{:S(2)}, u32[]{:S(2)}) collective-permute-start(f32[4,32,1024]{2,1,0:T(8,128)} %slice.63), channel_id=1, source_target_pairs={{0,4},{4,0},{8,12},{12,8},{16,20},{20,16},{24,28},{28,24},{1,5},{5... | collective-permute-start | bytes 1572872 | tf_op jit(solution)/shard_map/ppermute | solution.py:199
  23.7 0.8 copy-start.4
  28.0 14.1 %collective-permute-start.24 = (f32[128,1024]{1,0:T(8,128)S(1)}, f32[128,1024]{1,0:T(8,128)S(1)}, u32[]{:S(2)}, u32[]{:S(2)}) collective-permute-start(f32[128,1024]{1,0:T(8,128)S(1)} %get-tuple-element.40), channel_id=1, source_target_pairs={{0,8},{4,20},{8,0},{12,28},{16,24},{20,4},{24,16},{28,12},{1,9},{5... | collective-permute-start | bytes 1572872 | tf_op jit(solution)/shard_map/ppermute | solution.py:221
  29.2 13.6 %collective-permute-start.10 = (f32[128,1024]{1,0:T(8,128)S(1)}, f32[128,1024]{1,0:T(8,128)S(1)}, u32[]{:S(2)}, u32[]{:S(2)}) collective-permute-start(f32[128,1024]{1,0:T(8,128)S(1)} %get-tuple-element.42), channel_id=1, source_target_pairs={{0,8},{4,20},{8,0},{12,28},{16,24},{20,4},{24,16},{28,12},{1,9},{5... | collective-permute-start | bytes 1572872 | tf_op jit(solution)/shard_map/ppermute | solution.py:221
  31.2 15.0 %collective-permute-start.4 = (f32[2,32,1024]{2,1,0:T(8,128)S(1)}, f32[2,32,1024]{2,1,0:T(8,128)S(1)}, u32[]{:S(2)}, u32[]{:S(2)}) collective-permute-start(f32[2,32,1024]{2,1,0:T(8,128)S(1)} %slice.65), channel_id=1, source_target_pairs={{0,8},{4,20},{8,0},{12,28},{16,24},{20,4},{24,16},{28,12},{1,9},{5... | collective-permute-start | bytes 786440 | tf_op jit(solution)/shard_map/ppermute | solution.py:203
  32.5 4.6 %copy-start.1 = (f32[6,2,256,1024]{3,2,1,0:T(8,128)S(1)}, f32[6,2,256,1024]{3,2,1,0:T(8,128)}, u32[]{:S(2)}) copy-start(f32[6,2,256,1024]{3,2,1,0:T(8,128)} %factor_ref.3) | copy-start | bytes 37748740
  37.1 44.0 %copy-start.5 = (f32[2,256,32]{1,2,0:T(8,128)S(1)}, f32[2,256,32]{1,2,0:T(8,128)}, u32[]{:S(2)}) copy-start(f32[2,256,32]{1,2,0:T(8,128)} %param.9) | copy-start | bytes 196612
  41.8 32.5 %collective-permute-start = (f32[4,32,1024]{2,1,0:T(8,128)}, f32[4,32,1024]{2,1,0:T(8,128)}, u32[]{:S(2)}, u32[]{:S(2)}) collective-permute-start(f32[4,32,1024]{2,1,0:T(8,128)} %slice.57), channel_id=1, source_target_pairs={{0,4},{4,0},{8,12},{12,8},{16,20},{20,16},{24,28},{28,24},{1,5},{5... | collective-permute-start | bytes 1572872 | tf_op jit(solution)/shard_map/ppermute | solution.py:199
  42.1 27.8 %collective-permute-start.17 = (f32[128,1024]{1,0:T(8,128)S(1)}, f32[128,1024]{1,0:T(8,128)}, u32[]{:S(2)}, u32[]{:S(2)}) collective-permute-start(f32[128,1024]{1,0:T(8,128)S(1)} %get-tuple-element.41), channel_id=1, source_target_pairs={{0,8},{4,20},{8,0},{12,28},{16,24},{20,4},{24,16},{28,12},{1,9},{5... | collective-permute-start | bytes 1572872 | tf_op jit(solution)/shard_map/ppermute | solution.py:221
  42.2 29.3 %collective-permute-start.25 = (f32[128,1024]{1,0:T(8,128)S(1)}, f32[128,1024]{1,0:T(8,128)}, u32[]{:S(2)}, u32[]{:S(2)}) collective-permute-start(f32[128,1024]{1,0:T(8,128)S(1)} %add.133), channel_id=1, source_target_pairs={{0,16},{4,12},{8,24},{12,4},{16,0},{20,28},{24,8},{28,20},{1,17},{... | collective-permute-start | bytes 1572872 | tf_op jit(solution)/shard_map/ppermute | solution.py:221
  42.9 29.9 %collective-permute-start.11 = (f32[128,1024]{1,0:T(8,128)S(1)}, f32[128,1024]{1,0:T(8,128)}, u32[]{:S(2)}, u32[]{:S(2)}) collective-permute-start(f32[128,1024]{1,0:T(8,128)S(1)} %add.122), channel_id=1, source_target_pairs={{0,16},{4,12},{8,24},{12,4},{16,0},{20,28},{24,8},{28,20},{1,17},{... | collective-permute-start | bytes 1572872 | tf_op jit(solution)/shard_map/ppermute | solution.py:221
  46.2 16.9 %collective-permute-start.5 = (f32[1,32,1024]{2,1,0:T(8,128)S(1)}, f32[1,32,1024]{2,1,0:T(8,128)S(1)}, u32[]{:S(2)}, u32[]{:S(2)}) collective-permute-start(f32[1,32,1024]{2,1,0:T(8,128)S(1)} %slice.67), channel_id=1, source_target_pairs={{0,16},{4,12},{8,24},{12,4},{16,0},{20,28},{24,8},{28,20},{1,17},{... | collective-permute-start | bytes 393224 | tf_op jit(solution)/shard_map/ppermute | solution.py:203
  63.2 12.4 %collective-permute-start.8 = (f32[32,256]{1,0:T(8,128)S(1)}, f32[32,256]{1,0:T(8,128)S(1)}, u32[]{:S(2)}, u32[]{:S(2)}) collective-permute-start(f32[32,256]{1,0:T(8,128)S(1)} %get-tuple-element.56), channel_id=1, source_target_pairs={{0,3},{4,7},{8,11},{12,15},{16,19},{20,23},{24,27},{28,31}} | collective-permute-start | bytes 98312 | tf_op jit(solution)/shard_map/ppermute | solution.py:251
  71.0 10.0 %collective-permute-start.18 = (f32[128,1024]{1,0:T(8,128)S(1)}, f32[128,1024]{1,0:T(8,128)}, u32[]{:S(2)}, u32[]{:S(2)}) collective-permute-start(f32[128,1024]{1,0:T(8,128)S(1)} %add.125), channel_id=1, source_target_pairs={{0,16},{4,12},{8,24},{12,4},{16,0},{20,28},{24,8},{28,20},{1,17},{... | collective-permute-start | bytes 1572872 | tf_op jit(solution)/shard_map/ppermute | solution.py:221
  72.5 9.7 %collective-permute-start.26 = (f32[128,1024]{1,0:T(8,128)S(1)}, f32[128,1024]{1,0:T(8,128)}, u32[]{:S(2)}, u32[]{:S(2)}) collective-permute-start(f32[128,1024]{1,0:T(8,128)S(1)} %add.134), channel_id=1, source_target_pairs={{0,4},{4,0},{8,12},{12,8},{16,20},{20,16},{24,28},{28,24},{1,5},{5... | collective-permute-start | bytes 1572872 | tf_op jit(solution)/shard_map/ppermute | solution.py:222
  73.9 8.3 %collective-permute-start.12 = (f32[128,1024]{1,0:T(8,128)S(1)}, f32[128,1024]{1,0:T(8,128)S(1)}, u32[]{:S(2)}, u32[]{:S(2)}) collective-permute-start(f32[128,1024]{1,0:T(8,128)S(1)} %add.123), channel_id=1, source_target_pairs={{0,4},{4,0},{8,12},{12,8},{16,20},{20,16},{24,28},{28,24},{1,5},{5... | collective-permute-start | bytes 1572872 | tf_op jit(solution)/shard_map/ppermute | solution.py:222
  74.3 5.0 %collective-permute-start.7 = (f32[32,256]{1,0:T(8,128)S(1)}, f32[32,256]{1,0:T(8,128)S(1)}, u32[]{:S(2)}, u32[]{:S(2)}) collective-permute-start(f32[32,256]{1,0:T(8,128)S(1)} %get-tuple-element.57), channel_id=1, source_target_pairs={{0,2},{1,3},{4,6},{5,7},{8,10},{9,11},{12,14},{13,15},{16,18},{17,... | collective-permute-start | bytes 98312 | tf_op jit(solution)/shard_map/ppermute | solution.py:251
  75.6 5.5 %collective-permute-start.6 = (f32[32,256]{1,0:T(8,128)S(1)}, f32[32,256]{1,0:T(8,128)S(1)}, u32[]{:S(2)}, u32[]{:S(2)}) collective-permute-start(f32[32,256]{1,0:T(8,128)S(1)} %get-tuple-element.55), channel_id=1, source_target_pairs={{0,1},{1,2},{2,3},{4,5},{5,6},{6,7},{8,9},{9,10},{10,11},{12,13},{... | collective-permute-start | bytes 98312 | tf_op jit(solution)/shard_map/ppermute | solution.py:251
  79.2 9.8 %collective-permute-start.1 = (f32[2,32,1024]{2,1,0:T(8,128)S(1)}, f32[2,32,1024]{2,1,0:T(8,128)S(1)}, u32[]{:S(2)}, u32[]{:S(2)}) collective-permute-start(f32[2,32,1024]{2,1,0:T(8,128)S(1)} %slice.59), channel_id=1, source_target_pairs={{0,8},{4,20},{8,0},{12,28},{16,24},{20,4},{24,16},{28,12},{1,9},{5... | collective-permute-start | bytes 786440 | tf_op jit(solution)/shard_map/ppermute | solution.py:203
  82.2 8.1 %collective-permute-start.19 = (f32[128,1024]{1,0:T(8,128)S(1)}, f32[128,1024]{1,0:T(8,128)S(1)}, u32[]{:S(2)}, u32[]{:S(2)}) collective-permute-start(f32[128,1024]{1,0:T(8,128)S(1)} %add.126), channel_id=1, source_target_pairs={{0,4},{4,0},{8,12},{12,8},{16,20},{20,16},{24,28},{28,24},{1,5},{5... | collective-permute-start | bytes 1572872 | tf_op jit(solution)/shard_map/ppermute | solution.py:222
  88.4 1.2 collective-permute-start.13
  89.1 16.2 %collective-permute-start.2 = (f32[1,32,1024]{2,1,0:T(8,128)S(1)}, f32[1,32,1024]{2,1,0:T(8,128)S(1)}, u32[]{:S(2)}, u32[]{:S(2)}) collective-permute-start(f32[1,32,1024]{2,1,0:T(8,128)S(1)} %slice.61), channel_id=1, source_target_pairs={{0,16},{4,12},{8,24},{12,4},{16,0},{20,28},{24,8},{28,20},{1,17},{... | collective-permute-start | bytes 393224 | tf_op jit(solution)/shard_map/ppermute | solution.py:203
  89.6 0.8 collective-permute-start.14
  90.4 14.1 %collective-permute-start.15 = (f32[32,256]{1,0:T(8,128)S(1)}, f32[32,256]{1,0:T(8,128)S(1)}, u32[]{:S(2)}, u32[]{:S(2)}) collective-permute-start(f32[32,256]{1,0:T(8,128)S(1)} %get-tuple-element.26), channel_id=1, source_target_pairs={{1,0},{5,4},{9,8},{13,12},{17,16},{21,20},{25,24},{29,28}} | collective-permute-start | bytes 98312 | tf_op jit(solution)/shard_map/ppermute | solution.py:160
  105.8 9.2 %collective-permute-start.22 = (f32[32,256]{1,0:T(8,128)S(1)}, f32[32,256]{1,0:T(8,128)S(1)}, u32[]{:S(2)}, u32[]{:S(2)}) collective-permute-start(f32[32,256]{1,0:T(8,128)S(1)} %get-tuple-element.53), channel_id=1, source_target_pairs={{0,1},{1,0},{2,3},{3,2},{4,5},{5,4},{6,7},{7,6},{8,9},{9,8},{10,11... | collective-permute-start | bytes 98312 | tf_op jit(solution)/shard_map/ppermute | solution.py:258
  105.9 9.1 %collective-permute-start.21 = (f32[32,256]{1,0:T(8,128)S(1)}, f32[32,256]{1,0:T(8,128)S(1)}, u32[]{:S(2)}, u32[]{:S(2)}) collective-permute-start(f32[32,256]{1,0:T(8,128)S(1)} %get-tuple-element.54), channel_id=1, source_target_pairs={{0,2},{1,3},{2,0},{3,1},{4,6},{5,7},{6,4},{7,5},{8,10},{9,11},{10,... | collective-permute-start | bytes 98312 | tf_op jit(solution)/shard_map/ppermute | solution.py:258
  105.9 9.0 %collective-permute-start.20 = (f32[32,256]{1,0:T(8,128)S(1)}, f32[32,256]{1,0:T(8,128)S(1)}, u32[]{:S(2)}, u32[]{:S(2)}) collective-permute-start(f32[32,256]{1,0:T(8,128)S(1)} %get-tuple-element.52), channel_id=1, source_target_pairs={{0,3},{1,2},{2,1},{3,0},{4,7},{5,6},{6,5},{7,4},{8,11},{9,10},{10,... | collective-permute-start | bytes 98312 | tf_op jit(solution)/shard_map/ppermute | solution.py:258
  115.0 0.7 collective-permute-start.27
  115.7 0.7 collective-permute-start.28
  116.5 12.6 %collective-permute-start.29 = (f32[32,256]{1,0:T(8,128)S(1)}, f32[32,256]{1,0:T(8,128)S(1)}, u32[]{:S(2)}, u32[]{:S(2)}) collective-permute-start(f32[32,256]{1,0:T(8,128)S(1)} %get-tuple-element.34), channel_id=1, source_target_pairs={{1,0},{5,4},{9,8},{13,12},{17,16},{21,20},{25,24},{29,28}} | collective-permute-start | bytes 98312 | tf_op jit(solution)/shard_map/ppermute | solution.py:160

commit v2 on v1

--- a/solution.py
+++ b/solution.py
@@ -31,49 +31,75 @@
     return dot_split(split(a), split(b), ((1,), (0,)))
 
 
-def partial_kernel(rows_ref, order_ref, factor_ref, known_ref, out_ref, acc_ref, *, columns, groups):
+def send_tables(members):
+    orders = stage_orders(members)
+    count = len(orders[0])
+    tables = []
+    for core in range(2):
+        table = []
+        for place in range(members):
+            other = place >> count
+            rest = place & ((1 << count) - 1)
+            relative = other
+            for stage in range(count):
+                if (rest >> (count - 1 - stage)) & 1:
+                    relative |= 1 << orders[core ^ other][stage]
+            table.append(relative)
+        tables.append(table)
+    return tables
+
+
+def partial_kernel(where_ref, rows_ref, factor_ref, known_ref, keep_ref, send_ref, acc_ref, *, columns, tables):
     step = pl.program_id(0)
+    slots = pl.num_programs(0)
+    me = where_ref[0]
 
     @pl.when(step == 0)
     def _():
         acc_ref[...] = jnp.zeros_like(acc_ref)
 
-    @pl.when(rows_ref[step] >= 2)
+    @pl.when(rows_ref[me * slots + step] >= 2)
     def _():
         acc_ref[...] += dot_split(split(known_ref[0]), split(factor_ref[0, 0]), ((0,), (0,)))
 
-    @pl.when(step == pl.num_programs(0) - 1)
-    def _():
-        for place in range(groups):
-            start = pl.multiple_of(order_ref[place] * columns, columns)
-            out_ref[place] = acc_ref[pl.ds(start, columns), :]
-
-
-def partial_product(local_rows, order, factor_rows, known, column, columns):
+    @pl.when(step == slots - 1)
+    def _():
+        half = len(tables[0]) // 2
+        for spot, (even, odd) in enumerate(zip(*tables)):
+            group = me ^ jnp.where((me & 1) == 0, even, odd)
+            rows = acc_ref[pl.ds(pl.multiple_of(group * columns, columns), columns), :]
+            if spot < half:
+                keep_ref[spot] = rows
+            else:
+                send_ref[spot - half] = rows
+
+
+def partial_product(where, slot_row, factor_rows, known, column, columns):
     slots, _, band, width = factor_rows.shape
     total = known.shape[2]
     groups = total // columns
+    shape = jax.ShapeDtypeStruct((groups // 2, columns, width), F32)
+    whole = pl.BlockSpec(shape.shape, lambda s, w, r: (0, 0, 0))
     return pl.pallas_call(
-        functools.partial(partial_kernel, columns=columns, groups=groups),
-        out_shape=jax.ShapeDtypeStruct((groups, columns, width), F32),
+        functools.partial(partial_kernel, columns=columns, tables=send_tables(groups)),
+        out_shape=(shape, shape),
         grid_spec=pltpu.PrefetchScalarGridSpec(
             num_scalar_prefetch=2,
             grid=(slots,),
             in_specs=[
-                pl.BlockSpec((1, 1, band, width), lambda s, r, o: (s, column, 0, 0)),
-                pl.BlockSpec((1, band, total), lambda s, r, o: (s, 0, 0)),
+                pl.BlockSpec((1, 1, band, width), lambda s, w, r: (s, column, 0, 0)),
+                pl.BlockSpec((1, band, total), lambda s, w, r: (s, 0, 0)),
             ],
-            out_specs=pl.BlockSpec((groups, columns, width), lambda s, r, o: (0, 0, 0)),
+            out_specs=(whole, whole),
             scratch_shapes=[pltpu.VMEM((total, width), F32)],
         ),
         compiler_params=pltpu.CompilerParams(vmem_limit_bytes=32 << 20),
         name="partial",
-    )(local_rows, order, factor_rows, known)
-
-
-def invert_kernel(block_ref, out_ref):
-    size = block_ref.shape[0]
-    block = block_ref[...]
+    )(where, slot_row, factor_rows, known)
+
+
+def inverse_of(block):
+    size = block.shape[0]
     row = lax.broadcasted_iota(jnp.int32, (size, size), 0)
     col = lax.broadcasted_iota(jnp.int32, (size, size), 1)
     diag = jnp.where(row == col, block, 0.0)
@@ -90,7 +116,11 @@
         middle = dot_split(split(lower), parts, ((1,), (0,)))
         inverse = inverse - dot_split(parts, split(middle), ((1,), (0,)))
         step *= 2
-    out_ref[...] = inverse
+    return inverse
+
+
+def invert_kernel(block_ref, out_ref):
+    out_ref[...] = inverse_of(block_ref[...])
 
 
 def invert(block):
@@ -102,6 +132,84 @@
         compiler_params=pltpu.CompilerParams(vmem_limit_bytes=32 << 20),
         name="invert",
     )(block)
+
+
+def band_kernel(where_ref, rows_ref, factor_ref, keep_ref, send_ref, sems, *, row, column, slots):
+    half = keep_ref.shape[0]
+    me = where_ref[0]
+    core = me & 1
+    slot = jnp.int32(-1)
+    for s in range(slots):
+        slot = jnp.where(rows_ref[me * slots + s] == row, s, slot)
+
+    @pl.when(slot >= 0)
+    def _():
+        copies = []
+        for index, (target, which) in enumerate(((send_ref, 1 - core), (keep_ref, core))):
+            start = pl.multiple_of(which * half, half)
+            source = factor_ref.at[slot, column, pl.ds(start, half), :]
+            copies.append(pltpu.make_async_copy(source, target, sems.at[index]))
+        for copy in copies:
+            copy.start()
+        for copy in copies:
+            copy.wait()
+
+    @pl.when(slot < 0)
+    def _():
+        keep_ref[...] = jnp.zeros_like(keep_ref)
+        send_ref[...] = jnp.zeros_like(send_ref)
+
+
+def inverted_band_kernel(where_ref, rows_ref, factor_ref, keep_ref, send_ref, tile_ref, sem, *, row, column, slots):
+    half = keep_ref.shape[0]
+    band = 2 * half
+    me, place = where_ref[0], where_ref[1]
+    core = me & 1
+    slot = jnp.int32(-1)
+    for s in range(slots):
+        slot = jnp.where(rows_ref[me * slots + s] == row, s, slot)
+
+    @pl.when(slot >= 0)
+    def _():
+        copy = pltpu.make_async_copy(factor_ref.at[slot, column], tile_ref, sem)
+        copy.start()
+        copy.wait()
+        for spot in range(tile_ref.shape[1] // band):
+
+            @pl.when(place == spot)
+            def _():
+                here = slice(spot * band, (spot + 1) * band)
+                tile_ref[:, here] = inverse_of(tile_ref[:, here])
+
+        keep_ref[...] = tile_ref[pl.ds(pl.multiple_of(core * half, half), half), :]
+        send_ref[...] = tile_ref[pl.ds(pl.multiple_of((1 - core) * half, half), half), :]
+
+    @pl.when(slot < 0)
+    def _():
+        keep_ref[...] = jnp.zeros_like(keep_ref)
+        send_ref[...] = jnp.zeros_like(send_ref)
+
+
+def owned_band(where, slot_row, factor_rows, row, column, inverted):
+    slots, _, band, width = factor_rows.shape
+    shape = jax.ShapeDtypeStruct((band // 2, width), F32)
+    vmem = pl.BlockSpec(memory_space=VMEM)
+    smem = pl.BlockSpec(memory_space=SMEM)
+    if inverted:
+        body = inverted_band_kernel
+        scratch = [pltpu.VMEM((band, width), F32), pltpu.SemaphoreType.DMA(())]
+    else:
+        body = band_kernel
+        scratch = [pltpu.SemaphoreType.DMA((2,))]
+    return pl.pallas_call(
+        functools.partial(body, row=row, column=column, slots=slots),
+        out_shape=(shape, shape),
+        in_specs=[smem, smem, pl.BlockSpec(memory_space=pl.ANY)],
+        out_specs=(vmem, vmem),
+        scratch_shapes=scratch,
+        compiler_params=pltpu.CompilerParams(vmem_limit_bytes=32 << 20),
+        name="band",
+    )(where, slot_row, factor_rows)
 
 
 def stage_kernel(place_ref, base_ref, inverse_ref, tile_ref, add_ref, message_ref, held_ref, solved_ref, update_ref, *, stage):
@@ -167,59 +275,21 @@
     return first, first[::-1]
 
 
-def core_pairs(members):
-    return [(i, i ^ 1) for i in range(members)]
-
-
-def stage_pairs(members, stage):
+def swap_core(value, members):
+    return lax.ppermute(value, "rt", [(i, i ^ 1) for i in range(members)])
+
+
+def swap_chip(value, members, stage):
     orders = stage_orders(members)
-    return [(i, i ^ (1 << orders[i & 1][stage])) for i in range(members)]
-
-
-def send_order(members, me):
-    orders = stage_orders(members)
-    count = len(orders[0])
-    tables = []
-    for core in range(2):
-        table = []
-        for place in range(members):
-            other = place >> count
-            rest = place & ((1 << count) - 1)
-            relative = other
-            for stage in range(count):
-                if (rest >> (count - 1 - stage)) & 1:
-                    relative |= 1 << orders[core ^ other][stage]
-            table.append(relative)
-        tables.append(jnp.array(table, jnp.int32))
-    return me ^ jnp.where((me & 1) == 0, tables[0], tables[1])
-
-
-def reduce_rows(value, members):
-    half = members // 2
-    value = value[:half] + lax.ppermute(value[half:], "rt", core_pairs(members))
-    stage = 0
-    while half > 1:
-        half //= 2
-        value = value[:half] + lax.ppermute(value[half:], "rt", stage_pairs(members, stage))
-        stage += 1
-    return value[0]
-
-
-def share_band(factor_rows, local_rows, row, column, members, core):
-    slots, _, band, width = factor_rows.shape
-    half = band // 2
-    match = local_rows == row
-    slot = jnp.argmax(match).astype(jnp.int32)
-    mine = jnp.any(match)
-
-    def part(which):
-        piece = lax.dynamic_slice(factor_rows, (slot, column, which * half, 0), (1, 1, half, width))
-        return jnp.where(mine, piece.reshape(half, width), 0.0)
-
-    value = part(core) + lax.ppermute(part(1 - core), "rt", core_pairs(members))
-    for stage in range(len(stage_orders(members)[0])):
-        value = value + lax.ppermute(value, "rt", stage_pairs(members, stage))
-    other = lax.ppermute(value, "rt", core_pairs(members))
+    return lax.ppermute(value, "rt", [(i, i ^ (1 << orders[i & 1][stage])) for i in range(members)])
+
+
+def after(value, *others):
+    return lax.optimization_barrier((value,) + others)[0]
+
+
+def join_halves(value, members, core):
+    other = swap_core(value, members)
     first = core == 0
     return jnp.concatenate([jnp.where(first, value, other), jnp.where(first, other, value)], 0)
 
@@ -227,28 +297,62 @@
 def shards(factor_rows, slot_row, known, rhs, *, members, bands):
     slots, _, band, width = factor_rows.shape
     columns = rhs.shape[2]
+    stages = len(stage_orders(members)[0])
     me = lax.axis_index("rt")
     place = lax.axis_index("ct")
     core = me & 1
-    place_ref = place.astype(jnp.int32).reshape(1)
-    local_rows = lax.dynamic_slice_in_dim(slot_row, me * slots, slots, 0)
-    order = send_order(members, me).astype(jnp.int32)
-
-    def own(value, where):
-        return lax.dynamic_slice(value, (0, where * band), (value.shape[0], band))
-
-    tile_one = share_band(factor_rows, local_rows, 1, 1, members, core)
-    sum_one = reduce_rows(partial_product(local_rows, order, factor_rows, known, 1, columns), members)
-    sum_zero = reduce_rows(partial_product(local_rows, order, factor_rows, known, 0, columns), members)
-    tile_lower = share_band(factor_rows, local_rows, 1, 0, members, core)
-    tile_zero = share_band(factor_rows, local_rows, 0, 0, members, core)
-    inverse_one = invert(own(tile_one, place))
-    inverse_zero = invert(own(tile_zero, place))
+    where = jnp.stack([me, place]).astype(jnp.int32)
+    place_ref = where[1:]
+    factor_rows = pltpu.with_memory_space_constraint(factor_rows, pltpu.HBM)
+    known = pltpu.with_memory_space_constraint(known, pltpu.HBM)
+
+    def own(value, spot):
+        return lax.dynamic_slice(value, (0, spot * band), (value.shape[0], band))
+
+    keep, send = owned_band(where, slot_row, factor_rows, 1, 1, False)
+    tile_one = keep + swap_core(send, members)
+
+    keep_one, send_one = partial_product(after(where, tile_one), slot_row, factor_rows, known, 1, columns)
+    sum_one = keep_one + swap_core(send_one, members)
+    later = after(where, sum_one)
+    keep_zero, send_zero = partial_product(later, slot_row, factor_rows, known, 0, columns)
+    keep_low, send_low = owned_band(later, slot_row, factor_rows, 1, 0, False)
+    keep_top, send_top = owned_band(later, slot_row, factor_rows, 0, 0, True)
+
+    def reduce_step(value, stage):
+        half = value.shape[0] // 2
+        return value[:half] + swap_chip(value[half:], members, stage)
+
+    for stage in range(stages):
+        sum_one = reduce_step(sum_one, stage)
+        tile_one = tile_one + swap_chip(tile_one, members, stage)
+    sum_one = sum_one[0]
+
+    sum_zero = keep_zero + swap_core(send_zero, members)
+    tile_lower = keep_low + swap_core(send_low, members)
+    tile_zero = keep_top + swap_core(send_top, members)
 
     base = rhs[1].T - own(sum_one, place)
     for shift in range(1, bands):
         piece = own(sum_one, jnp.minimum(place + shift, bands - 1))
         base = base - lax.ppermute(piece, "ct", [(i, i + shift) for i in range(bands - shift)])
+
+    tile_one = join_halves(tile_one, members, core)
+    inverse_one = invert(own(tile_one, place))
+
+    tile_lower = after(tile_lower, sum_one, tile_one)
+    sum_zero = after(sum_zero, sum_one, tile_one)
+    for stage in range(stages):
+        sum_zero = reduce_step(sum_zero, stage)
+        tile_lower = tile_lower + swap_chip(tile_lower, members, stage)
+        tile_zero = after(tile_zero, tile_lower)
+    sum_zero = sum_zero[0]
+    for stage in range(stages):
+        tile_zero = tile_zero + swap_chip(tile_zero, members, stage)
+    tile_lower = join_halves(tile_lower, members, core)
+    tile_zero = join_halves(tile_zero, members, core)
+    inverse_zero = own(tile_zero, place)
+
     solved_one = sweep(place_ref, base, inverse_one, tile_one, sum_one, bands)
 
     coupling = sum_zero + jnp.dot(solved_one, tile_lower, precision=lax.Precision.HIGH)

time: 132 us -> 121 us (0.917)
  local copies, waits for them, and re-layouts: 13.1 us -> 2.16 us
  other arithmetic: 20.1 us -> 10.1 us
  waiting for transfers between devices: 40.8 us -> 49.5 us
  Pallas kernels: 18.9 us -> 23.8 us
  between operations: 4.26 us -> 0.55 us
    unnamed x12 -> x8, local copies, waits for them, and re-layouts: 11.3 us -> 1.35 us
    pallas_call x2 -> x5, Pallas kernels: 7.76 us -> 17.3 us  [the longest x2 14.4 us: partial_product(): pl.pallas_call(functools.partial(partial_kernel, columns=columns, tables=...]
    ppermute x18, waiting for transfers between devices: 16.7 us -> 22.2 us  [the longest x10 19.6 us: swap_chip(): lax.ppermute(value, 'rt', [(i, i ^ 1 << orders[i & 1][stage]) for i in ra...]
    pallas_call x2 -> x1, Pallas kernels: 9.38 us -> 4.69 us  [invert(): pl.pallas_call(invert_kernel, out_shape=jax.ShapeDtypeStruct(block.shape,...]
    select_n x3, other arithmetic: 5.36 us -> 1.29 us  [the longest x1 1.14 us: join_halves(): jnp.where(first, value, other)]
    ppermute x3, waiting for transfers between devices: 0.01 us -> 3.43 us  [shards(): lax.ppermute(piece, 'ct', [(i, i ^ mask) for i in range(bands)])]
    add x12 -> x14, other arithmetic: 10.3 us -> 6.95 us  [the longest x2 2.16 us: shards(): tile_lower = tile_lower + swap_chip(tile_lower, members, stage)]
    ppermute x18, starting transfers between devices: 12.8 us -> 14.5 us  [the longest x10 13.6 us: swap_chip(): lax.ppermute(value, 'rt', [(i, i ^ 1 << orders[i & 1][stage]) for i in ra...]
  transfers between devices with their start and end apart: 30 -> 30, of which waited for: 5 -> 9; matrix products, arithmetic and copies ran while one was open for 11% -> 8% of each run, Pallas kernels for 14% -> 19%
where the time goes in v2:
time: 121 us; the launch traced here: 120 us
  waiting for transfers between devices  49.5 us (41%)
  starting transfers between devices  33.5 us (28%)
  Pallas kernels  23.8 us (20%)
  other arithmetic  10.1 us (8%)
  local copies, waits for them, and re-layouts  2.16 us (2%)
    ppermute x6, waiting for transfers between devices, sweep(): message = lax.ppermute(update, 'ct', [(stage, stage - 1)])  23.9 us
    ppermute x10, waiting for transfers between devices, swap_chip(): lax.ppermute(value, 'rt', [(i, i ^ 1 << orders[i & 1][stage]) for i in ra...  19.6 us
    pallas_call x2, Pallas kernels, partial_product(): pl.pallas_call(functools.partial(partial_kernel, columns=columns, tables=...  14.4 us
    ppermute x10, starting transfers between devices, swap_chip(): lax.ppermute(value, 'rt', [(i, i ^ 1 << orders[i & 1][stage]) for i in ra...  13.6 us
    ppermute x3, starting transfers between devices, shards(): lax.ppermute(piece, 'ct', [(i, i + shift) for i in range(bands - shift)])  9.26 us
    ppermute x6, starting transfers between devices, sweep(): message = lax.ppermute(update, 'ct', [(stage, stage - 1)])  5.25 us
    pallas_call x1, Pallas kernels, invert(): pl.pallas_call(invert_kernel, out_shape=jax.ShapeDtypeStruct(block.shape,...  4.69 us
    ppermute x3, starting transfers between devices, shards(): lax.ppermute(piece, 'ct', [(i, i ^ mask) for i in range(bands)])  4.51 us
  transfers between devices with their start and end apart: 30, of which 9 were waited for; matrix products, arithmetic and copies ran while one was open for 8% of the time, Pallas kernels for 19%

profile of v2, /device:TPU:0, one launch (start us, length us, event | category | flops | bytes accessed | tf_op | source)
XLA Modules:
  0.0 120.1 jit_solution(4718823307527902556)
XLA Ops:
  0.0 0.1 pad_add_fusion.where_ref
  0.1 0.7 copy-done
  0.7 0.6 band.3
  1.4 0.5 collective-permute-start
  1.9 1.5 %collective-permute-done = f32[128,1024]{1,0:T(8,128)S(1)} collective-permute-done((f32[128,1024]{1,0:T(8,128)S(1)}, f32[128,1024]{1,0:T(8,128)S(1)}, u32[]{:S(2)}, u32[]{:S(2)}) %collective-permute-start) | collective-permute-done | bytes 524320 | tf_op jit(solution)/shard_map/ppermute | solution.py:279
  3.4 0.1 add.81
  3.5 4.1 %collective-permute-start.5 = (f32[128,1024]{1,0:T(8,128)S(1)}, f32[128,1024]{1,0:T(8,128)S(1)}, u32[]{:S(2)}, u32[]{:S(2)}) collective-permute-start(f32[128,1024]{1,0:T(8,128)S(1)} %add.81), channel_id=1, source_target_pairs={{0,8},{4,20},{8,0},{12,28},{16,24},{20,4},{24,16},{28,12},{1,9},{5... | collective-permute-start | bytes 1572872 | tf_op jit(solution)/shard_map/ppermute | solution.py:284
  7.6 7.2 %partial.2 = (f32[4,32,1024]{2,1,0:T(8,128)S(1)}, f32[4,32,1024]{2,1,0:T(8,128)S(1)}) custom-call(s32[2]{0:T(128)S(1)} %pad_add_fusion.where_ref, s32[48]{0:T(128)S(1)} %copy-done, f32[6,2,256,1024]{3,2,1,0:T(8,128)} %factor_ref.9, f32[6,256,256]{2,1,0:T(8,128)} %known_ref.3), custom_call_target="tpu_custom_call" | custom-call | tf_op jit(solution)/shard_map/partial/pallas_call | solution.py:83
  14.8 0.1 collective-permute-start.1
  14.9 0.8 collective-permute-start.6
  15.8 1.0 collective-permute-done.1
  16.8 0.1 add.82
  16.9 0.6 collective-permute-start.3
  17.4 0.6 band.4
  18.2 8.8 %collective-permute-done.6 = f32[128,1024]{1,0:T(8,128)S(1)} collective-permute-done((f32[128,1024]{1,0:T(8,128)S(1)}, f32[128,1024]{1,0:T(8,128)S(1)}, u32[]{:S(2)}, u32[]{:S(2)}) %collective-permute-start.6) | collective-permute-done | bytes 524320 | tf_op jit(solution)/shard_map/ppermute | solution.py:284
  27.1 0.1 collective-permute-start.7
  27.2 0.8 collective-permute-start.4
  28.0 4.2 %collective-permute-done.4 = f32[1,32,1024]{2,1,0:T(8,128)S(1)} collective-permute-done((f32[1,32,1024]{2,1,0:T(8,128)S(1)}, f32[1,32,1024]{2,1,0:T(8,128)S(1)}, u32[]{:S(2)}, u32[]{:S(2)}) %collective-permute-start.4) | collective-permute-done | bytes 131104 | tf_op jit(solution)/shard_map/ppermute | solution.py:284
  32.3 0.1 add.97
  32.4 0.1 broadcast_select_fusion.4
  32.5 0.1 pad_maximum_fusion.tile_ref
  32.6 0.7 copy-done.2
  33.2 1.4 %collective-permute-start.17 = (f32[128,1024]{1,0:T(8,128)S(1)}, f32[128,1024]{1,0:T(8,128)S(1)}, u32[]{:S(2)}, u32[]{:S(2)}) collective-permute-start(f32[128,1024]{1,0:T(8,128)S(1)} %add.97), channel_id=1, source_target_pairs={{0,8},{4,20},{8,0},{12,28},{16,24},{20,4},{24,16},{28,12},{1,9},{5... | collective-permute-start | bytes 1572872 | tf_op jit(solution)/shard_map/ppermute | solution.py:284
  34.7 1.7 %band.5 = (f32[128,1024]{1,0:T(8,128)S(1)}, f32[128,1024]{1,0:T(8,128)}) custom-call(s32[2]{0:T(128)S(1)} %pad_add_fusion.where_ref, s32[48]{0:T(128)S(1)} %copy-done.1, f32[6,2,256,1024]{3,2,1,0:T(8,128)} %factor_ref.9), custom_call_target="tpu_custom_call" | custom-call | tf_op jit(solution)/shard_map/band/pallas_call | solution.py:204
  36.4 0.1 collective-permute-start.23
  36.4 6.0 %collective-permute-done.17 = f32[128,1024]{1,0:T(8,128)S(1)} collective-permute-done((f32[128,1024]{1,0:T(8,128)S(1)}, f32[128,1024]{1,0:T(8,128)S(1)}, u32[]{:S(2)}, u32[]{:S(2)}) %collective-permute-start.17) | collective-permute-done | bytes 524320 | tf_op jit(solution)/shard_map/ppermute | solution.py:284
  42.4 0.9 add.98
  43.3 0.8 collective-permute-start.18
  44.1 7.2 %partial.3 = (f32[4,32,1024]{2,1,0:T(8,128)S(1)}, f32[4,32,1024]{2,1,0:T(8,128)S(1)}) custom-call(s32[2]{0:T(128)S(1)} %pad_add_fusion.where_ref, s32[48]{0:T(128)S(1)} %copy-done.1, f32[6,2,256,1024]{3,2,1,0:T(8,128)} %factor_ref.9, f32[6,256,256]{2,1,0:T(8,128)} %known_ref.3), custom_call_target="tpu_custom_call" | custom-call | tf_op jit(solution)/shard_map/partial/pallas_call | solution.py:83
  51.3 0.1 collective-permute-start.2
  51.4 5.5 %collective-permute-start.12 = (f32[32,256]{1,0:T(8,128)S(1)}, f32[32,256]{1,0:T(8,128)S(1)}, u32[]{:S(2)}, u32[]{:S(2)}) collective-permute-start(f32[32,256]{1,0:T(8,128)S(1)} %get-tuple-element.75), channel_id=1, source_target_pairs={{0,3},{4,7},{8,11},{12,15},{16,19},{20,23},{24,27},{28,31}} | collective-permute-start | bytes 98312 | tf_op jit(solution)/shard_map/ppermute | solution.py:338
  56.9 1.3 %collective-permute-start.11 = (f32[32,256]{1,0:T(8,128)S(1)}, f32[32,256]{1,0:T(8,128)S(1)}, u32[]{:S(2)}, u32[]{:S(2)}) collective-permute-start(f32[32,256]{1,0:T(8,128)S(1)} %get-tuple-element.76), channel_id=1, source_target_pairs={{0,2},{1,3},{4,6},{5,7},{8,10},{9,11},{12,14},{13,15},{16,18},{17,... | collective-permute-start | bytes 98312 | tf_op jit(solution)/shard_map/ppermute | solution.py:338
  58.2 2.5 %collective-permute-start.10 = (f32[32,256]{1,0:T(8,128)S(1)}, f32[32,256]{1,0:T(8,128)S(1)}, u32[]{:S(2)}, u32[]{:S(2)}) collective-permute-start(f32[32,256]{1,0:T(8,128)S(1)} %get-tuple-element.74), channel_id=1, source_target_pairs={{0,1},{1,2},{2,3},{4,5},{5,6},{6,7},{8,9},{9,10},{10,11},{12,13},{... | collective-permute-start | bytes 98312 | tf_op jit(solution)/shard_map/ppermute | solution.py:338
  60.7 1.1 add.104
  61.9 1.3 %add.99 = f32[128,1024]{1,0:T(8,128)S(1)} add(f32[128,1024]{1,0:T(8,128)} %add.98, f32[128,1024]{1,0:T(8,128)} %collective-permute-done.18) | non-fusion elementwise | flops 131072 | bytes 1572864 | tf_op jit(solution)/shard_map/add | solution.py:347
  63.1 0.3 collective-permute-start.24
  63.5 1.1 add.83
  64.6 0.7 slice.36
  65.3 1.8 %collective-permute-start.8 = (f32[2,32,1024]{2,1,0:T(8,128)}, f32[2,32,1024]{2,1,0:T(8,128)}, u32[]{:S(2)}, u32[]{:S(2)}) collective-permute-start(f32[2,32,1024]{2,1,0:T(8,128)} %slice.36), channel_id=1, source_target_pairs={{0,8},{4,20},{8,0},{12,28},{16,24},{20,4},{24,16},{28,12},{1,9},{5... | collective-permute-start | bytes 786440 | tf_op jit(solution)/shard_map/ppermute | solution.py:284
  67.1 0.9 fusion.5.block_ref
  68.0 4.7 %invert.1.inverse_ref = f32[256,256]{1,0:T(8,128)S(1)} custom-call(f32[256,256]{1,0:T(8,128)S(1)} %fusion.5.block_ref), custom_call_target="tpu_custom_call" | custom-call | tf_op jit(solution)/shard_map/invert/pallas_call | solution.py:127
  72.8 0.7 collective-permute-start.13
  73.5 0.7 collective-permute-start.14
  74.2 1.3 %collective-permute-start.15 = (f32[32,256]{1,0:T(8,128)S(1)}, f32[32,256]{1,0:T(8,128)S(1)}, u32[]{:S(2)}, u32[]{:S(2)}) collective-permute-start(f32[32,256]{1,0:T(8,128)S(1)} %get-tuple-element.48), channel_id=1, source_target_pairs={{1,0},{5,4},{9,8},{13,12},{17,16},{21,20},{25,24},{29,28}} | collective-permute-start | bytes 98312 | tf_op jit(solution)/shard_map/ppermute | solution.py:268
  75.6 0.8 collective-permute-start.25
  76.4 11.1 %collective-permute-done.15.message_ref = f32[32,256]{1,0:T(8,128)S(1)} collective-permute-done((f32[32,256]{1,0:T(8,128)S(1)}, f32[32,256]{1,0:T(8,128)S(1)}, u32[]{:S(2)}, u32[]{:S(2)}) %collective-permute-start.15) | collective-permute-done | bytes 32800 | tf_op jit(solution)/shard_map/ppermute | solution.py:268
  87.4 0.8 stage.11
  88.2 1.0 slice_add_fusion.1
  89.2 2.2 %collective-permute-start.9 = (f32[1,32,1024]{2,1,0:T(8,128)S(1)}, f32[1,32,1024]{2,1,0:T(8,128)S(1)}, u32[]{:S(2)}, u32[]{:S(2)}) collective-permute-start(f32[1,32,1024]{2,1,0:T(8,128)S(1)} %slice.45), channel_id=1, source_target_pairs={{0,16},{4,12},{8,24},{12,4},{16,0},{20,28},{24,8},{28,20},{1,17},{... | collective-permute-start | bytes 393224 | tf_op jit(solution)/shard_map/ppermute | solution.py:284
  91.4 1.1 broadcast_select_fusion.3
  92.6 1.1 add.106
  93.7 0.1 collective-permute-start.26
  93.8 0.6 collective-permute-done.9
  94.4 0.4 fusion.7
  94.8 2.1 %collective-permute-start.22 = (f32[32,256]{1,0:T(8,128)S(1)}, f32[32,256]{1,0:T(8,128)S(1)}, u32[]{:S(2)}, u32[]{:S(2)}) collective-permute-start(f32[32,256]{1,0:T(8,128)S(1)} %get-tuple-element.72), channel_id=1, source_target_pairs={{0,1},{1,0},{2,3},{3,2},{4,5},{5,4},{6,7},{7,6},{8,9},{9,8},{10,11... | collective-permute-start | bytes 98312 | tf_op jit(solution)/shard_map/ppermute | solution.py:362
  96.9 2.4 %collective-permute-start.20 = (f32[32,256]{1,0:T(8,128)S(1)}, f32[32,256]{1,0:T(8,128)S(1)}, u32[]{:S(2)}, u32[]{:S(2)}) collective-permute-start(f32[32,256]{1,0:T(8,128)S(1)} %get-tuple-element.71), channel_id=1, source_target_pairs={{0,3},{1,2},{2,1},{3,0},{4,7},{5,6},{6,5},{7,4},{8,11},{9,10},{10,... | collective-permute-start | bytes 98312 | tf_op jit(solution)/shard_map/ppermute | solution.py:362
  99.3 3.4 %collective-permute-done.21 = f32[32,256]{1,0:T(8,128)S(1)} collective-permute-done((f32[32,256]{1,0:T(8,128)S(1)}, f32[32,256]{1,0:T(8,128)S(1)}, u32[]{:S(2)}, u32[]{:S(2)}) %collective-permute-start.21) | collective-permute-done | bytes 32800 | tf_op jit(solution)/shard_map/ppermute | solution.py:362
  102.8 0.1 broadcast_select_fusion
  103.0 0.7 collective-permute-start.27
  103.7 0.7 collective-permute-start.28
  104.4 1.3 %collective-permute-start.29 = (f32[32,256]{1,0:T(8,128)S(1)}, f32[32,256]{1,0:T(8,128)S(1)}, u32[]{:S(2)}, u32[]{:S(2)}) collective-permute-start(f32[32,256]{1,0:T(8,128)S(1)} %get-tuple-element.62), channel_id=1, source_target_pairs={{1,0},{5,4},{9,8},{13,12},{17,16},{21,20},{25,24},{29,28}} | collective-permute-start | bytes 98312 | tf_op jit(solution)/shard_map/ppermute | solution.py:268
  105.7 12.9 %collective-permute-done.29.message_ref = f32[32,256]{1,0:T(8,128)S(1)} collective-permute-done((f32[32,256]{1,0:T(8,128)S(1)}, f32[32,256]{1,0:T(8,128)S(1)}, u32[]{:S(2)}, u32[]{:S(2)}) %collective-permute-start.29) | collective-permute-done | bytes 32800 | tf_op jit(solution)/shard_map/ppermute | solution.py:268
  118.6 0.8 stage.15
  119.4 0.6 pad_maximum_fusion.2
  (52 shorter events, 0.7 us)
Async XLA Ops:
  0.1 0.7 copy-start
  1.4 2.1 %collective-permute-start = (f32[128,1024]{1,0:T(8,128)S(1)}, f32[128,1024]{1,0:T(8,128)S(1)}, u32[]{:S(2)}, u32[]{:S(2)}) collective-permute-start(f32[128,1024]{1,0:T(8,128)S(1)} %get-tuple-element.36), channel_id=1, source_target_pairs={{0,4},{4,0},{8,12},{12,8},{16,20},{20,16},{24,28},{28,24},{1,5},{5... | collective-permute-start | bytes 1572872 | tf_op jit(solution)/shard_map/ppermute | solution.py:279
  3.5 11.4 %collective-permute-start.5 = (f32[128,1024]{1,0:T(8,128)S(1)}, f32[128,1024]{1,0:T(8,128)S(1)}, u32[]{:S(2)}, u32[]{:S(2)}) collective-permute-start(f32[128,1024]{1,0:T(8,128)S(1)} %add.81), channel_id=1, source_target_pairs={{0,8},{4,20},{8,0},{12,28},{16,24},{20,4},{24,16},{28,12},{1,9},{5... | collective-permute-start | bytes 1572872 | tf_op jit(solution)/shard_map/ppermute | solution.py:284
  14.8 19.9 %copy-start.1 = (s32[48]{0:T(128)S(1)}, s32[48]{0:T(128)}, u32[]{:S(2)}) copy-start(s32[48]{0:T(128)} %rows_ref.9) | copy-start | bytes 580
  14.8 2.0 %collective-permute-start.1 = (f32[4,32,1024]{2,1,0:T(8,128)S(1)}, f32[4,32,1024]{2,1,0:T(8,128)S(1)}, u32[]{:S(2)}, u32[]{:S(2)}) collective-permute-start(f32[4,32,1024]{2,1,0:T(8,128)S(1)} %get-tuple-element.39), channel_id=1, source_target_pairs={{0,4},{4,0},{8,12},{12,8},{16,20},{20,16},{24,28},{28,24},{1,5},{5... | collective-permute-start | bytes 1572872 | tf_op jit(solution)/shard_map/ppermute | solution.py:279
  14.9 12.1 %collective-permute-start.6 = (f32[128,1024]{1,0:T(8,128)S(1)}, f32[128,1024]{1,0:T(8,128)S(1)}, u32[]{:S(2)}, u32[]{:S(2)}) collective-permute-start(f32[128,1024]{1,0:T(8,128)S(1)} %add.86), channel_id=1, source_target_pairs={{0,16},{4,12},{8,24},{12,4},{16,0},{20,28},{24,8},{28,20},{1,17},{... | collective-permute-start | bytes 1572872 | tf_op jit(solution)/shard_map/ppermute | solution.py:284
  16.9 10.3 %collective-permute-start.3 = (f32[2,32,1024]{2,1,0:T(8,128)S(1)}, f32[2,32,1024]{2,1,0:T(8,128)S(1)}, u32[]{:S(2)}, u32[]{:S(2)}) collective-permute-start(f32[2,32,1024]{2,1,0:T(8,128)S(1)} %slice.41), channel_id=1, source_target_pairs={{0,8},{4,20},{8,0},{12,28},{16,24},{20,4},{24,16},{28,12},{1,9},{5... | collective-permute-start | bytes 786440 | tf_op jit(solution)/shard_map/ppermute | solution.py:284
  18.1 14.2 %collective-permute-start.16 = (f32[128,1024]{1,0:T(8,128)S(1)}, f32[128,1024]{1,0:T(8,128)S(1)}, u32[]{:S(2)}, u32[]{:S(2)}) collective-permute-start(f32[128,1024]{1,0:T(8,128)S(1)} %get-tuple-element.52), channel_id=1, source_target_pairs={{0,4},{4,0},{8,12},{12,8},{16,20},{20,16},{24,28},{28,24},{1,5},{5... | collective-permute-start | bytes 1572872 | tf_op jit(solution)/shard_map/ppermute | solution.py:279
  27.1 5.3 %collective-permute-start.7 = (f32[128,1024]{1,0:T(8,128)S(1)}, f32[128,1024]{1,0:T(8,128)S(1)}, u32[]{:S(2)}, u32[]{:S(2)}) collective-permute-start(f32[128,1024]{1,0:T(8,128)S(1)} %add.87), channel_id=1, source_target_pairs={{0,4},{4,0},{8,12},{12,8},{16,20},{20,16},{24,28},{28,24},{1,5},{5... | collective-permute-start | bytes 1572872 | tf_op jit(solution)/shard_map/ppermute | solution.py:279
  27.2 5.0 %collective-permute-start.4 = (f32[1,32,1024]{2,1,0:T(8,128)S(1)}, f32[1,32,1024]{2,1,0:T(8,128)S(1)}, u32[]{:S(2)}, u32[]{:S(2)}) collective-permute-start(f32[1,32,1024]{2,1,0:T(8,128)S(1)} %slice.43), channel_id=1, source_target_pairs={{0,16},{4,12},{8,24},{12,4},{16,0},{20,28},{24,8},{28,20},{1,17},{... | collective-permute-start | bytes 393224 | tf_op jit(solution)/shard_map/ppermute | solution.py:284
  32.4 0.8 copy-start.2
  33.2 9.2 %collective-permute-start.17 = (f32[128,1024]{1,0:T(8,128)S(1)}, f32[128,1024]{1,0:T(8,128)S(1)}, u32[]{:S(2)}, u32[]{:S(2)}) collective-permute-start(f32[128,1024]{1,0:T(8,128)S(1)} %add.97), channel_id=1, source_target_pairs={{0,8},{4,20},{8,0},{12,28},{16,24},{20,4},{24,16},{28,12},{1,9},{5... | collective-permute-start | bytes 1572872 | tf_op jit(solution)/shard_map/ppermute | solution.py:284
  36.3 27.1 %copy-start.3 = (f32[2,256,32]{1,2,0:T(8,128)S(1)}, f32[2,256,32]{1,2,0:T(8,128)}, u32[]{:S(2)}) copy-start(f32[2,256,32]{1,2,0:T(8,128)} %param.7) | copy-start | bytes 196612
  36.4 21.9 %collective-permute-start.23 = (f32[128,1024]{1,0:T(8,128)}, f32[128,1024]{1,0:T(8,128)}, u32[]{:S(2)}, u32[]{:S(2)}) collective-permute-start(f32[128,1024]{1,0:T(8,128)} %get-tuple-element.55), channel_id=1, source_target_pairs={{0,4},{4,0},{8,12},{12,8},{16,20},{20,16},{24,28},{28,24},{1,5},{5... | collective-permute-start | bytes 1572872 | tf_op jit(solution)/shard_map/ppermute | solution.py:279
  43.3 18.5 %collective-permute-start.18 = (f32[128,1024]{1,0:T(8,128)}, f32[128,1024]{1,0:T(8,128)}, u32[]{:S(2)}, u32[]{:S(2)}) collective-permute-start(f32[128,1024]{1,0:T(8,128)} %add.98), channel_id=1, source_target_pairs={{0,16},{4,12},{8,24},{12,4},{16,0},{20,28},{24,8},{28,20},{1,17},{... | collective-permute-start | bytes 1572872 | tf_op jit(solution)/shard_map/ppermute | solution.py:284
  51.3 12.2 %collective-permute-start.2 = (f32[4,32,1024]{2,1,0:T(8,128)S(1)}, f32[4,32,1024]{2,1,0:T(8,128)}, u32[]{:S(2)}, u32[]{:S(2)}) collective-permute-start(f32[4,32,1024]{2,1,0:T(8,128)S(1)} %get-tuple-element.42), channel_id=1, source_target_pairs={{0,4},{4,0},{8,12},{12,8},{16,20},{20,16},{24,28},{28,24},{1,5},{5... | collective-permute-start | bytes 1572872 | tf_op jit(solution)/shard_map/ppermute | solution.py:279
  51.4 12.0 %collective-permute-start.12 = (f32[32,256]{1,0:T(8,128)S(1)}, f32[32,256]{1,0:T(8,128)S(1)}, u32[]{:S(2)}, u32[]{:S(2)}) collective-permute-start(f32[32,256]{1,0:T(8,128)S(1)} %get-tuple-element.75), channel_id=1, source_target_pairs={{0,3},{4,7},{8,11},{12,15},{16,19},{20,23},{24,27},{28,31}} | collective-permute-start | bytes 98312 | tf_op jit(solution)/shard_map/ppermute | solution.py:338
  56.9 6.5 %collective-permute-start.11 = (f32[32,256]{1,0:T(8,128)S(1)}, f32[32,256]{1,0:T(8,128)S(1)}, u32[]{:S(2)}, u32[]{:S(2)}) collective-permute-start(f32[32,256]{1,0:T(8,128)S(1)} %get-tuple-element.76), channel_id=1, source_target_pairs={{0,2},{1,3},{4,6},{5,7},{8,10},{9,11},{12,14},{13,15},{16,18},{17,... | collective-permute-start | bytes 98312 | tf_op jit(solution)/shard_map/ppermute | solution.py:338
  58.2 5.2 %collective-permute-start.10 = (f32[32,256]{1,0:T(8,128)S(1)}, f32[32,256]{1,0:T(8,128)S(1)}, u32[]{:S(2)}, u32[]{:S(2)}) collective-permute-start(f32[32,256]{1,0:T(8,128)S(1)} %get-tuple-element.74), channel_id=1, source_target_pairs={{0,1},{1,2},{2,3},{4,5},{5,6},{6,7},{8,9},{9,10},{10,11},{12,13},{... | collective-permute-start | bytes 98312 | tf_op jit(solution)/shard_map/ppermute | solution.py:338
  63.1 12.4 %collective-permute-start.24 = (f32[128,1024]{1,0:T(8,128)S(1)}, f32[128,1024]{1,0:T(8,128)S(1)}, u32[]{:S(2)}, u32[]{:S(2)}) collective-permute-start(f32[128,1024]{1,0:T(8,128)S(1)} %add.104), channel_id=1, source_target_pairs={{0,8},{4,20},{8,0},{12,28},{16,24},{20,4},{24,16},{28,12},{1,9},{5... | collective-permute-start | bytes 1572872 | tf_op jit(solution)/shard_map/ppermute | solution.py:284
  65.3 22.9 %collective-permute-start.8 = (f32[2,32,1024]{2,1,0:T(8,128)}, f32[2,32,1024]{2,1,0:T(8,128)}, u32[]{:S(2)}, u32[]{:S(2)}) collective-permute-start(f32[2,32,1024]{2,1,0:T(8,128)} %slice.36), channel_id=1, source_target_pairs={{0,8},{4,20},{8,0},{12,28},{16,24},{20,4},{24,16},{28,12},{1,9},{5... | collective-permute-start | bytes 786440 | tf_op jit(solution)/shard_map/ppermute | solution.py:284
  67.1 24.3 %collective-permute-start.19 = (f32[128,1024]{1,0:T(8,128)S(1)}, f32[128,1024]{1,0:T(8,128)}, u32[]{:S(2)}, u32[]{:S(2)}) collective-permute-start(f32[128,1024]{1,0:T(8,128)S(1)} %add.99), channel_id=1, source_target_pairs={{0,4},{4,0},{8,12},{12,8},{16,20},{20,16},{24,28},{28,24},{1,5},{5... | collective-permute-start | bytes 1572872 | tf_op jit(solution)/shard_map/ppermute | solution.py:279
  72.8 0.7 collective-permute-start.13
  73.5 0.7 collective-permute-start.14
  74.2 13.2 %collective-permute-start.15 = (f32[32,256]{1,0:T(8,128)S(1)}, f32[32,256]{1,0:T(8,128)S(1)}, u32[]{:S(2)}, u32[]{:S(2)}) collective-permute-start(f32[32,256]{1,0:T(8,128)S(1)} %get-tuple-element.48), channel_id=1, source_target_pairs={{1,0},{5,4},{9,8},{13,12},{17,16},{21,20},{25,24},{29,28}} | collective-permute-start | bytes 98312 | tf_op jit(solution)/shard_map/ppermute | solution.py:268
  75.6 17.0 %collective-permute-start.25 = (f32[128,1024]{1,0:T(8,128)S(1)}, f32[128,1024]{1,0:T(8,128)}, u32[]{:S(2)}, u32[]{:S(2)}) collective-permute-start(f32[128,1024]{1,0:T(8,128)S(1)} %add.105), channel_id=1, source_target_pairs={{0,16},{4,12},{8,24},{12,4},{16,0},{20,28},{24,8},{28,20},{1,17},{... | collective-permute-start | bytes 1572872 | tf_op jit(solution)/shard_map/ppermute | solution.py:284
  89.2 5.2 %collective-permute-start.9 = (f32[1,32,1024]{2,1,0:T(8,128)S(1)}, f32[1,32,1024]{2,1,0:T(8,128)S(1)}, u32[]{:S(2)}, u32[]{:S(2)}) collective-permute-start(f32[1,32,1024]{2,1,0:T(8,128)S(1)} %slice.45), channel_id=1, source_target_pairs={{0,16},{4,12},{8,24},{12,4},{16,0},{20,28},{24,8},{28,20},{1,17},{... | collective-permute-start | bytes 393224 | tf_op jit(solution)/shard_map/ppermute | solution.py:284
  93.7 9.1 %collective-permute-start.26 = (f32[128,1024]{1,0:T(8,128)S(1)}, f32[128,1024]{1,0:T(8,128)S(1)}, u32[]{:S(2)}, u32[]{:S(2)}) collective-permute-start(f32[128,1024]{1,0:T(8,128)S(1)} %add.106), channel_id=1, source_target_pairs={{0,4},{4,0},{8,12},{12,8},{16,20},{20,16},{24,28},{28,24},{1,5},{5... | collective-permute-start | bytes 1572872 | tf_op jit(solution)/shard_map/ppermute | solution.py:279
  94.8 4.5 %collective-permute-start.22 = (f32[32,256]{1,0:T(8,128)S(1)}, f32[32,256]{1,0:T(8,128)S(1)}, u32[]{:S(2)}, u32[]{:S(2)}) collective-permute-start(f32[32,256]{1,0:T(8,128)S(1)} %get-tuple-element.72), channel_id=1, source_target_pairs={{0,1},{1,0},{2,3},{3,2},{4,5},{5,4},{6,7},{7,6},{8,9},{9,8},{10,11... | collective-permute-start | bytes 98312 | tf_op jit(solution)/shard_map/ppermute | solution.py:362
  96.9 5.9 %collective-permute-start.21 = (f32[32,256]{1,0:T(8,128)S(1)}, f32[32,256]{1,0:T(8,128)S(1)}, u32[]{:S(2)}, u32[]{:S(2)}) collective-permute-start(f32[32,256]{1,0:T(8,128)S(1)} %get-tuple-element.73), channel_id=1, source_target_pairs={{0,2},{1,3},{2,0},{3,1},{4,6},{5,7},{6,4},{7,5},{8,10},{9,11},{10,... | collective-permute-start | bytes 98312 | tf_op jit(solution)/shard_map/ppermute | solution.py:362
  96.9 5.9 %collective-permute-start.20 = (f32[32,256]{1,0:T(8,128)S(1)}, f32[32,256]{1,0:T(8,128)S(1)}, u32[]{:S(2)}, u32[]{:S(2)}) collective-permute-start(f32[32,256]{1,0:T(8,128)S(1)} %get-tuple-element.71), channel_id=1, source_target_pairs={{0,3},{1,2},{2,1},{3,0},{4,7},{5,6},{6,5},{7,4},{8,11},{9,10},{10,... | collective-permute-start | bytes 98312 | tf_op jit(solution)/shard_map/ppermute | solution.py:362
  103.0 0.7 collective-permute-start.27
  103.7 0.7 collective-permute-start.28
  104.4 14.2 %collective-permute-start.29 = (f32[32,256]{1,0:T(8,128)S(1)}, f32[32,256]{1,0:T(8,128)S(1)}, u32[]{:S(2)}, u32[]{:S(2)}) collective-permute-start(f32[32,256]{1,0:T(8,128)S(1)} %get-tuple-element.62), channel_id=1, source_target_pairs={{1,0},{5,4},{9,8},{13,12},{17,16},{21,20},{25,24},{29,28}} | collective-permute-start | bytes 98312 | tf_op jit(solution)/shard_map/ppermute | solution.py:268

commit v3 on v2

v3 whole, which is shorter than its diff:
```python
import functools

import jax
import jax.numpy as jnp
from jax import lax
from jax.experimental import pallas as pl
from jax.experimental.pallas import tpu as pltpu
from jax.sharding import PartitionSpec as P

F32 = jnp.float32
BF16 = jnp.bfloat16
VMEM = pltpu.MemorySpace.VMEM
SMEM = pltpu.MemorySpace.SMEM


def split(value):
    high = value.astype(BF16)
    return high, (value - high.astype(F32)).astype(BF16)


def dot_split(a, b, dims):
    (ah, al), (bh, bl) = a, b

    def one(u, v):
        return lax.dot_general(u, v, (dims, ((), ())), preferred_element_type=F32)

    return one(al, bh) + one(ah, bl) + one(ah, bh)


def dot3(a, b):
    return dot_split(split(a), split(b), ((1,), (0,)))


def send_tables(members):
    orders = stage_orders(members)
    count = len(orders[0])
    tables = []
    for core in range(2):
        table = []
        for place in range(members):
            other = place >> count
            rest = place & ((1 << count) - 1)
            relative = other
            for stage in range(count):
                if (rest >> (count - 1 - stage)) & 1:
                    relative |= 1 << orders[core ^ other][stage]
            table.append(relative)
        tables.append(table)
    return tables


def partial_kernel(
    where_ref, rows_ref, factor_ref, known_ref, keep_ref, send_ref, factor_buf, known_buf, acc_ref, sems, *, column, tables
):
    slots = factor_buf.shape[0]
    columns = keep_ref.shape[1]
    me = where_ref[0]

    def copies(slot):
        return (
            pltpu.make_async_copy(known_ref.at[slot], known_buf.at[slot], sems.at[0, slot]),
            pltpu.make_async_copy(factor_ref.at[slot, column], factor_buf.at[slot], sems.at[1, slot]),
        )

    for slot in range(slots):

        @pl.when(rows_ref[me * slots + slot] >= 2)
        def _():
            for copy in copies(slot):
                copy.start()

    acc_ref[...] = jnp.zeros_like(acc_ref)
    for slot in range(slots):

        @pl.when(rows_ref[me * slots + slot] >= 2)
        def _():
            for copy in copies(slot):
                copy.wait()
            acc_ref[...] += dot_split(split(known_buf[slot]), split(factor_buf[slot]), ((0,), (0,)))

    half = len(tables[0]) // 2
    for spot, (even, odd) in enumerate(zip(*tables)):
        group = me ^ jnp.where((me & 1) == 0, even, odd)
        rows = acc_ref[pl.ds(pl.multiple_of(group * columns, columns), columns), :]
        if spot < half:
            keep_ref[spot] = rows
        else:
            send_ref[spot - half] = rows


def partial_product(where, slot_row, factor_rows, known, column, columns):
    slots, _, band, width = factor_rows.shape
    total = known.shape[2]
    groups = total // columns
    shape = jax.ShapeDtypeStruct((groups // 2, columns, width), F32)
    vmem = pl.BlockSpec(memory_space=VMEM)
    smem = pl.BlockSpec(memory_space=SMEM)
    hbm = pl.BlockSpec(memory_space=pl.ANY)
    return pl.pallas_call(
        functools.partial(partial_kernel, column=column, tables=send_tables(groups)),
        out_shape=(shape, shape),
        in_specs=[smem, smem, hbm, hbm],
        out_specs=(vmem, vmem),
        scratch_shapes=[
            pltpu.VMEM((slots, band, width), F32),
            pltpu.VMEM((slots, band, total), F32),
            pltpu.VMEM((total, width), F32),
            pltpu.SemaphoreType.DMA((2, slots)),
        ],
        compiler_params=pltpu.CompilerParams(vmem_limit_bytes=40 << 20),
        name="partial",
    )(where, slot_row, factor_rows, known)


def inverse_of(block):
    size = block.shape[0]
    row = lax.broadcasted_iota(jnp.int32, (size, size), 0)
    col = lax.broadcasted_iota(jnp.int32, (size, size), 1)
    diag = jnp.where(row == col, block, 0.0)
    recip_row = 1.0 / jnp.sum(diag, axis=0, keepdims=True)
    recip_col = 1.0 / jnp.sum(diag, axis=1, keepdims=True)
    pair = (row - col == 1) & (lax.rem(row, 2) == 1)
    inverse = jnp.where(row == col, recip_row, jnp.where(pair, -(block * recip_row) * recip_col, 0.0))
    step = 2
    while step < size:
        half = lax.div(row, step)
        below = (half - lax.div(col, step) == 1) & (lax.rem(half, 2) == 1)
        lower = jnp.where(below, block, 0.0)
        parts = split(inverse)
        middle = dot_split(split(lower), parts, ((1,), (0,)))
        inverse = inverse - dot_split(parts, split(middle), ((1,), (0,)))
        step *= 2
    return inverse


def invert_diagonal(tile_ref, place, band):
    for spot in range(tile_ref.shape[1] // band):

        @pl.when(place == spot)
        def _():
            here = slice(spot * band, (spot + 1) * band)
            tile_ref[:, here] = inverse_of(tile_ref[:, here])


def join_kernel(where_ref, mine_ref, other_ref, tile_ref, *, inverted):
    half = mine_ref.shape[0]
    core = where_ref[0] & 1
    tile_ref[pl.ds(pl.multiple_of(core * half, half), half), :] = mine_ref[...]
    tile_ref[pl.ds(pl.multiple_of((1 - core) * half, half), half), :] = other_ref[...]
    if inverted:
        invert_diagonal(tile_ref, where_ref[1], 2 * half)


def join_halves(where, mine, other, inverted):
    half, width = mine.shape
    vmem = pl.BlockSpec(memory_space=VMEM)
    return pl.pallas_call(
        functools.partial(join_kernel, inverted=inverted),
        out_shape=jax.ShapeDtypeStruct((2 * half, width), F32),
        in_specs=[pl.BlockSpec(memory_space=SMEM), vmem, vmem],
        out_specs=vmem,
        compiler_params=pltpu.CompilerParams(vmem_limit_bytes=32 << 20),
        name="join",
    )(where, mine, other)


def band_kernel(where_ref, rows_ref, factor_ref, keep_ref, send_ref, sems, *, row, column, slots):
    half = keep_ref.shape[0]
    me = where_ref[0]
    core = me & 1
    slot = jnp.int32(-1)
    for s in range(slots):
        slot = jnp.where(rows_ref[me * slots + s] == row, s, slot)

    @pl.when(slot >= 0)
    def _():
        copies = []
        for index, (target, which) in enumerate(((send_ref, 1 - core), (keep_ref, core))):
            start = pl.multiple_of(which * half, half)
            source = factor_ref.at[slot, column, pl.ds(start, half), :]
            copies.append(pltpu.make_async_copy(source, target, sems.at[index]))
        for copy in copies:
            copy.start()
        for copy in copies:
            copy.wait()

    @pl.when(slot < 0)
    def _():
        keep_ref[...] = jnp.zeros_like(keep_ref)
        send_ref[...] = jnp.zeros_like(send_ref)


def inverted_band_kernel(where_ref, rows_ref, factor_ref, keep_ref, send_ref, tile_ref, sem, *, row, column, slots):
    half = keep_ref.shape[0]
    band = 2 * half
    me, place = where_ref[0], where_ref[1]
    core = me & 1
    slot = jnp.int32(-1)
    for s in range(slots):
        slot = jnp.where(rows_ref[me * slots + s] == row, s, slot)

    @pl.when(slot >= 0)
    def _():
        copy = pltpu.make_async_copy(factor_ref.at[slot, column], tile_ref, sem)
        copy.start()
        copy.wait()
        invert_diagonal(tile_ref, place, band)
        keep_ref[...] = tile_ref[pl.ds(pl.multiple_of(core * half, half), half), :]
        send_ref[...] = tile_ref[pl.ds(pl.multiple_of((1 - core) * half, half), half), :]

    @pl.when(slot < 0)
    def _():
        keep_ref[...] = jnp.zeros_like(keep_ref)
        send_ref[...] = jnp.zeros_like(send_ref)


def owned_band(where, slot_row, factor_rows, row, column, inverted):
    slots, _, band, width = factor_rows.shape
    shape = jax.ShapeDtypeStruct((band // 2, width), F32)
    vmem = pl.BlockSpec(memory_space=VMEM)
    smem = pl.BlockSpec(memory_space=SMEM)
    if inverted:
        body = inverted_band_kernel
        scratch = [pltpu.VMEM((band, width), F32), pltpu.SemaphoreType.DMA(())]
    else:
        body = band_kernel
        scratch = [pltpu.SemaphoreType.DMA((2,))]
    return pl.pallas_call(
        functools.partial(body, row=row, column=column, slots=slots),
        out_shape=(shape, shape),
        in_specs=[smem, smem, pl.BlockSpec(memory_space=pl.ANY)],
        out_specs=(vmem, vmem),
        scratch_shapes=scratch,
        compiler_params=pltpu.CompilerParams(vmem_limit_bytes=32 << 20),
        name="band",
    )(where, slot_row, factor_rows)


def stage_kernel(where_ref, base_ref, tile_ref, add_ref, message_ref, held_ref, solved_ref, update_ref, *, stage):
    band = base_ref.shape[1]
    left = stage * band

    @pl.when(where_ref[1] == stage)
    def _():
        message = message_ref[...]
        right = base_ref[...] - message[:, left:]
        solved = dot3(right, tile_ref[:, left : left + band])
        solved_ref[...] = solved
        if stage > 0:
            update_ref[...] = message[:, :left] + dot3(solved, tile_ref[:, :left]) + add_ref[:, :left]

    @pl.when(where_ref[1] != stage)
    def _():
        solved_ref[...] = held_ref[...]


def run_stage(where, base, tile, add, message, held, stage):
    columns, band = base.shape
    width = max(stage, 1) * band
    vmem = pl.BlockSpec(memory_space=VMEM)
    return pl.pallas_call(
        functools.partial(stage_kernel, stage=stage),
        out_shape=(jax.ShapeDtypeStruct((columns, band), F32), jax.ShapeDtypeStruct((columns, width), F32)),
        in_specs=[pl.BlockSpec(memory_space=SMEM)] + [vmem] * 5,
        out_specs=(vmem, vmem),
        compiler_params=pltpu.CompilerParams(vmem_limit_bytes=32 << 20),
        name="stage",
    )(where, base, tile, add, message, held)


def run_stage_plain(where, base, tile, add, message, held, stage):
    high = lax.Precision.HIGHEST
    band = base.shape[1]
    left = stage * band
    right = base - message[:, left:]
    solved = jnp.dot(right, tile[:, left : left + band], precision=high)
    width = max(left, band)
    update = jnp.dot(solved, tile[:, :width], precision=high) + add[:, :width]
    if stage > 0:
        update = update + message[:, :width]
    return jnp.where(where[1] == stage, solved, held), update


def first_message(columns, width, band):
    return jnp.zeros((columns, width), F32), jnp.zeros((columns, band), F32)


def hop(update, stage):
    return lax.ppermute(update, "ct", [(stage, stage - 1)])


def stage_orders(members):
    bits = members.bit_length() - 1
    first = list(range(1, bits))
    return first, first[::-1]


def swap_core(value, members):
    return lax.ppermute(value, "rt", [(i, i ^ 1) for i in range(members)])


def swap_chip(value, members, stage):
    orders = stage_orders(members)
    return lax.ppermute(value, "rt", [(i, i ^ (1 << orders[i & 1][stage])) for i in range(members)])


def after(value, *others):
    return lax.optimization_barrier((value,) + others)[0]


def shards(factor_rows, slot_row, known, rhs, *, members, bands):
    slots, _, band, width = factor_rows.shape
    columns = rhs.shape[2]
    stages = len(stage_orders(members)[0])
    run = run_stage if band % 128 == 0 else run_stage_plain
    me = lax.axis_index("rt")
    place = lax.axis_index("ct")
    where = jnp.stack([me, place]).astype(jnp.int32)
    factor_rows = pltpu.with_memory_space_constraint(factor_rows, pltpu.HBM)
    known = pltpu.with_memory_space_constraint(known, pltpu.HBM)

    def own(value, spot):
        return lax.dynamic_slice(value, (0, spot * band), (value.shape[0], band))

    def partial(ready, column):
        return partial_product(ready, slot_row, factor_rows, known, column, columns)

    def owned(ready, row, column, inverted):
        return owned_band(ready, slot_row, factor_rows, row, column, inverted)

    def chip_half(value, stage):
        return swap_chip(value[value.shape[0] // 2 :], members, stage)

    keep, send = owned(where, 1, 1, False)
    tile_one = keep + swap_core(send, members)
    got_tile = swap_chip(tile_one, members, 0)
    keep, send = partial(after(where, tile_one), 1)
    sum_one = keep + swap_core(send, members)
    keep_zero = send_zero = keep_low = send_low = keep_top = send_top = None
    for stage in range(stages):
        got_sum = chip_half(sum_one, stage)
        if stage == 0:
            later = after(where, sum_one)
            keep_zero, send_zero = partial(later, 0)
            keep_low, send_low = owned(after(where, keep_zero), 1, 0, False)
            got_tile, got_sum = after(got_tile, keep_zero, keep_low), after(got_sum, keep_zero, keep_low)
        tile_one = tile_one + got_tile
        if stage < stages - 1:
            got_tile = swap_chip(tile_one, members, stage + 1)
        half = sum_one.shape[0] // 2
        sum_one = sum_one[:half] + after(got_sum, tile_one)
        if stage == 0:
            keep_top, send_top = owned(after(where, sum_one), 0, 0, True)
    sum_one = after(sum_one, keep_top)[0]

    got_up = []
    for shift in range(1, bands):
        piece = own(sum_one, jnp.minimum(place + shift, bands - 1))
        got_up.append(lax.ppermute(piece, "ct", [(i, i + shift) for i in range(bands - shift)]))

    other = swap_core(tile_one, members)
    sum_zero = after(keep_zero, sum_one) + swap_core(after(send_zero, sum_one), members)
    tile_low = after(keep_low, sum_one) + swap_core(after(send_low, sum_one), members)
    tile_top = after(keep_top, sum_one) + swap_core(after(send_top, sum_one), members)
    got_low = swap_chip(after(tile_low, other), members, 0)
    got_zero = chip_half(after(sum_zero, other), 0)
    tile_one = join_halves(where, tile_one, other, True)
    got_top = swap_chip(after(tile_top, tile_low), members, 0)

    base = rhs[1].T - own(sum_one, place)
    for piece in got_up:
        base = base - after(piece, tile_one)

    message, held = first_message(columns, width, band)
    for stage in range(bands - 1, -1, -1):
        held, update = run(where, base, tile_one, sum_one, message, held, stage)
        if stage > 0:
            message = hop(update, stage)
        index = bands - 1 - stage
        if index < stages:
            gate = held
            tile_low = tile_low + after(got_low, gate)
            half = sum_zero.shape[0] // 2
            sum_zero = sum_zero[:half] + after(got_zero, gate)
            tile_top = tile_top + after(got_top, gate, tile_low)
            if index < stages - 1:
                got_low = swap_chip(tile_low, members, index + 1)
                got_zero = chip_half(sum_zero, index + 1)
                got_top = swap_chip(tile_top, members, index + 1)
        if index == stages - 1:
            tile_low = join_halves(where, tile_low, swap_core(tile_low, members), False)
            tile_top_other = swap_core(tile_top, members)
            message = after(message, tile_low, sum_zero)
    solved_one = held
    sum_zero = sum_zero[0]

    coupling = sum_zero + jnp.dot(solved_one, tile_low, precision=lax.Precision.HIGH)
    base = rhs[0].T - own(coupling, place)
    tile_top = join_halves(where, tile_top, tile_top_other, False)
    for mask in range(bands - 1, 0, -1):
        piece = own(coupling, place ^ mask)
        got = lax.ppermute(piece, "ct", [(i, i ^ mask) for i in range(bands)])
        base = base - after(got, tile_top)

    nothing = jnp.zeros((columns, width), F32)
    message, held = first_message(columns, width, band)
    for stage in range(bands - 1, -1, -1):
        held, update = run(where, base, tile_top, nothing, message, held, stage)
        if stage > 0:
            message = hop(update, stage)
    return jnp.stack([held.T, solved_one.T])


def solution(mesh):
    members, bands = mesh.shape["rt"], mesh.shape["ct"]
    in_specs = (P("rt", None, "ct", None), P(), P("rt", "ct", None), P(None, "ct", "rt"))
    out_specs = P(None, "ct", "rt")
    body = functools.partial(shards, members=members, bands=bands)
    return jax.shard_map(body, mesh=mesh, in_specs=in_specs, out_specs=out_specs, check_vma=False)
```

time: 121 us -> 114 us (0.942)
  waiting for transfers between devices: 49.5 us -> 39.3 us
  starting transfers between devices: 33.5 us -> 39.5 us
  other arithmetic: 10.1 us -> 7.08 us
  Pallas kernels: 23.8 us -> 25.3 us
  local copies, waits for them, and re-layouts: 2.16 us -> 0.76 us
    ppermute x9, waiting for transfers between devices: 27.4 us -> 18.7 us  [the longest x6 17.5 us: hop(): return lax.ppermute(update, 'ct', [(stage, stage - 1)])]
    pallas_call x8, Pallas kernels: 1.74 us -> 6.94 us  [run_stage(): pl.pallas_call(functools.partial(stage_kernel, stage=stage), out_shape=(j...]
    pallas_call x3 -> x5, Pallas kernels: 19.1 us -> 13.9 us  [the longest x2 7.38 us: partial_product(): pl.pallas_call(functools.partial(partial_kernel, column=column, tables=se...]
    ppermute x10, starting transfers between devices: 13.6 us -> 17 us  [swap_chip(): lax.ppermute(value, 'rt', [(i, i ^ 1 << orders[i & 1][stage]) for i in ra...]
    ppermute x10, waiting for transfers between devices: 19.6 us -> 16.7 us  [swap_chip(): lax.ppermute(value, 'rt', [(i, i ^ 1 << orders[i & 1][stage]) for i in ra...]
    ppermute x8, starting transfers between devices: 0.95 us -> 3.63 us  [swap_core(): return lax.ppermute(value, 'rt', [(i, i ^ 1) for i in range(members)])]
    pallas_call x3, Pallas kernels: 2.94 us -> 4.4 us  [owned_band(): pl.pallas_call(functools.partial(body, row=row, column=column, slots=slot...]
    add x13 -> x14, other arithmetic: 6.87 us -> 5.52 us  [the longest x2 1.32 us: shards(): tile_low = tile_low + after(got_low, gate)]
  transfers between devices with their start and end apart: 30 -> 30, of which waited for: 9 -> 12; matrix products, arithmetic and copies ran while one was open for 8% -> 6% of each run, Pallas kernels for 19% -> 15%
where the time goes in v3:
time: 114 us
  starting transfers between devices  39.5 us (35%)
  waiting for transfers between devices  39.3 us (34%)
  Pallas kernels  25.3 us (22%)
  other arithmetic  7.08 us (6%)
  matrix products  1.33 us (1%)
    ppermute x6, waiting for transfers between devices, hop(): return lax.ppermute(update, 'ct', [(stage, stage - 1)])  17.5 us
    ppermute x10, starting transfers between devices, swap_chip(): lax.ppermute(value, 'rt', [(i, i ^ 1 << orders[i & 1][stage]) for i in ra...  17 us
    ppermute x10, waiting for transfers between devices, swap_chip(): lax.ppermute(value, 'rt', [(i, i ^ 1 << orders[i & 1][stage]) for i in ra...  16.7 us
    ppermute x3, starting transfers between devices, shards(): lax.ppermute(piece, 'ct', [(i, i + shift) for i in range(bands - shift)])  9.26 us
    pallas_call x2, Pallas kernels, partial_product(): pl.pallas_call(functools.partial(partial_kernel, column=column, tables=se...  7.38 us
    pallas_call x8, Pallas kernels, run_stage(): pl.pallas_call(functools.partial(stage_kernel, stage=stage), out_shape=(j...  6.94 us
    pallas_call x3, Pallas kernels, join_halves(): pl.pallas_call(functools.partial(join_kernel, inverted=inverted), out_sha...  6.55 us
    ppermute x6, starting transfers between devices, hop(): return lax.ppermute(update, 'ct', [(stage, stage - 1)])  5.21 us
  transfers between devices with their start and end apart: 30, of which 12 were waited for; matrix products, arithmetic and copies ran while one was open for 6% of the time, Pallas kernels for 15%

profile of v3, /device:TPU:0, one launch (start us, length us, event | category | flops | bytes accessed | tf_op | source)
XLA Modules:
  0.0 113.7 jit_solution(15790964828484764594)
XLA Ops:
  0.1 0.7 copy-done
  0.7 1.8 %band.3 = (f32[128,1024]{1,0:T(8,128)S(1)}, f32[128,1024]{1,0:T(8,128)S(1)}) custom-call(s32[2]{0:T(128)S(1)} %pad_add_fusion.where_ref, s32[48]{0:T(128)S(1)} %copy-done, f32[6,2,256,1024]{3,2,1,0:T(8,128)} %factor_ref.9), custom_call_target="tpu_custom_call" | custom-call | tf_op jit(solution)/shard_map/band/pallas_call | solution.py:228
  2.6 1.9 %collective-permute-done = f32[128,1024]{1,0:T(8,128)S(1)} collective-permute-done((f32[128,1024]{1,0:T(8,128)S(1)}, f32[128,1024]{1,0:T(8,128)S(1)}, u32[]{:S(2)}, u32[]{:S(2)}) %collective-permute-start) | collective-permute-done | bytes 524320 | tf_op jit(solution)/shard_map/ppermute | solution.py:299
  4.6 3.3 %partial.2 = (f32[4,32,1024]{2,1,0:T(8,128)S(1)}, f32[4,32,1024]{2,1,0:T(8,128)S(1)}) custom-call(s32[2]{0:T(128)S(1)} %pad_add_fusion.where_ref, s32[48]{0:T(128)S(1)} %copy-done.1, f32[6,2,256,1024]{3,2,1,0:T(8,128)} %factor_ref.9, f32[6,256,256]{2,1,0:T(8,128)} %known_ref.3), custom_call_target="tpu_custom_call" | custom-call | tf_op jit(solution)/shard_map/partial/pallas_call | solution.py:99
  7.9 1.4 %collective-permute-start.1 = (f32[4,32,1024]{2,1,0:T(8,128)S(1)}, f32[4,32,1024]{2,1,0:T(8,128)S(1)}, u32[]{:S(2)}, u32[]{:S(2)}) collective-permute-start(f32[4,32,1024]{2,1,0:T(8,128)S(1)} %get-tuple-element.64), channel_id=1, source_target_pairs={{0,4},{4,0},{8,12},{12,8},{16,20},{20,16},{24,28},{28,24},{1,5},{5... | collective-permute-start | bytes 1572872 | tf_op jit(solution)/shard_map/ppermute | solution.py:299
  9.3 2.4 %collective-permute-start.3 = (f32[128,1024]{1,0:T(8,128)S(1)}, f32[128,1024]{1,0:T(8,128)S(1)}, u32[]{:S(2)}, u32[]{:S(2)}) collective-permute-start(f32[128,1024]{1,0:T(8,128)S(1)} %add.79), channel_id=1, source_target_pairs={{0,8},{4,20},{8,0},{12,28},{16,24},{20,4},{24,16},{28,12},{1,9},{5... | collective-permute-start | bytes 1572872 | tf_op jit(solution)/shard_map/ppermute | solution.py:304
  11.7 0.1 add.80
  11.8 1.6 %collective-permute-start.2 = (f32[2,32,1024]{2,1,0:T(8,128)S(1)}, f32[2,32,1024]{2,1,0:T(8,128)S(1)}, u32[]{:S(2)}, u32[]{:S(2)}) collective-permute-start(f32[2,32,1024]{2,1,0:T(8,128)S(1)} %slice.41), channel_id=1, source_target_pairs={{0,8},{4,20},{8,0},{12,28},{16,24},{20,4},{24,16},{28,12},{1,9},{5... | collective-permute-start | bytes 786440 | tf_op jit(solution)/shard_map/ppermute | solution.py:304
  13.4 4.1 %partial.3 = (f32[4,32,1024]{2,1,0:T(8,128)S(1)}, f32[4,32,1024]{2,1,0:T(8,128)}) custom-call(s32[2]{0:T(128)S(1)} %pad_add_fusion.where_ref, s32[48]{0:T(128)S(1)} %copy-done.1, f32[6,2,256,1024]{3,2,1,0:T(8,128)} %factor_ref.9, f32[6,256,256]{2,1,0:T(8,128)} %known_ref.3), custom_call_target="tpu_custom_call" | custom-call | tf_op jit(solution)/shard_map/partial/pallas_call | solution.py:99
  17.5 1.8 %band.4 = (f32[128,1024]{1,0:T(8,128)S(1)}, f32[128,1024]{1,0:T(8,128)S(1)}) custom-call(s32[2]{0:T(128)S(1)} %pad_add_fusion.where_ref, s32[48]{0:T(128)S(1)} %copy-done.1, f32[6,2,256,1024]{3,2,1,0:T(8,128)} %factor_ref.9), custom_call_target="tpu_custom_call" | custom-call | tf_op jit(solution)/shard_map/band/pallas_call | solution.py:228
  19.4 2.5 %collective-permute-start.5 = (f32[128,1024]{1,0:T(8,128)S(1)}, f32[128,1024]{1,0:T(8,128)S(1)}, u32[]{:S(2)}, u32[]{:S(2)}) collective-permute-start(f32[128,1024]{1,0:T(8,128)S(1)} %add.81), channel_id=1, source_target_pairs={{0,16},{4,12},{8,24},{12,4},{16,0},{20,28},{24,8},{28,20},{1,17},{... | collective-permute-start | bytes 1572872 | tf_op jit(solution)/shard_map/ppermute | solution.py:304
  22.0 2.5 %collective-permute-start.4 = (f32[1,32,1024]{2,1,0:T(8,128)S(1)}, f32[1,32,1024]{2,1,0:T(8,128)S(1)}, u32[]{:S(2)}, u32[]{:S(2)}) collective-permute-start(f32[1,32,1024]{2,1,0:T(8,128)S(1)} %slice.43), channel_id=1, source_target_pairs={{0,16},{4,12},{8,24},{12,4},{16,0},{20,28},{24,8},{28,20},{1,17},{... | collective-permute-start | bytes 393224 | tf_op jit(solution)/shard_map/ppermute | solution.py:304
  24.5 0.9 band.5
  25.3 3.8 %collective-permute-done.5 = f32[128,1024]{1,0:T(8,128)S(1)} collective-permute-done((f32[128,1024]{1,0:T(8,128)S(1)}, f32[128,1024]{1,0:T(8,128)S(1)}, u32[]{:S(2)}, u32[]{:S(2)}) %collective-permute-start.5) | collective-permute-done | bytes 524320 | tf_op jit(solution)/shard_map/ppermute | solution.py:304
  29.2 1.3 %collective-permute-done.4 = f32[1,32,1024]{2,1,0:T(8,128)S(1)} collective-permute-done((f32[1,32,1024]{2,1,0:T(8,128)S(1)}, f32[1,32,1024]{2,1,0:T(8,128)S(1)}, u32[]{:S(2)}, u32[]{:S(2)}) %collective-permute-start.4) | collective-permute-done | bytes 131104 | tf_op jit(solution)/shard_map/ppermute | solution.py:304
  30.6 0.5 collective-permute-start.7
  31.1 0.1 collective-permute-start.21
  31.2 1.3 %collective-permute-done.15 = f32[128,1024]{1,0:T(8,128)S(1)} collective-permute-done((f32[128,1024]{1,0:T(8,128)S(1)}, f32[128,1024]{1,0:T(8,128)S(1)}, u32[]{:S(2)}, u32[]{:S(2)}) %collective-permute-start.15) | collective-permute-done | bytes 524320 | tf_op jit(solution)/shard_map/ppermute | solution.py:299
  32.5 0.9 add.95
  33.4 0.6 collective-permute-done.7.other_ref
  34.0 1.1 collective-permute-start.16
  35.1 0.8 collective-permute-start.6
  35.9 3.5 %collective-permute-start.9 = (f32[32,256]{1,0:T(8,128)S(1)}, f32[32,256]{1,0:T(8,128)S(1)}, u32[]{:S(2)}, u32[]{:S(2)}) collective-permute-start(f32[32,256]{1,0:T(8,128)S(1)} %get-tuple-element.118), channel_id=1, source_target_pairs={{0,1},{1,2},{2,3},{4,5},{5,6},{6,7},{8,9},{9,10},{10,11},{12,13},{... | collective-permute-start | bytes 98312 | tf_op jit(solution)/shard_map/ppermute | solution.py:359
  39.4 4.5 %collective-permute-start.10 = (f32[32,256]{1,0:T(8,128)S(1)}, f32[32,256]{1,0:T(8,128)S(1)}, u32[]{:S(2)}, u32[]{:S(2)}) collective-permute-start(f32[32,256]{1,0:T(8,128)S(1)} %get-tuple-element.120), channel_id=1, source_target_pairs={{0,2},{1,3},{4,6},{5,7},{8,10},{9,11},{12,14},{13,15},{16,18},{17,... | collective-permute-start | bytes 98312 | tf_op jit(solution)/shard_map/ppermute | solution.py:359
  43.9 1.3 %collective-permute-start.11 = (f32[32,256]{1,0:T(8,128)S(1)}, f32[32,256]{1,0:T(8,128)S(1)}, u32[]{:S(2)}, u32[]{:S(2)}) collective-permute-start(f32[32,256]{1,0:T(8,128)S(1)} %get-tuple-element.119), channel_id=1, source_target_pairs={{0,3},{4,7},{8,11},{12,15},{16,19},{20,23},{24,27},{28,31}} | collective-permute-start | bytes 98312 | tf_op jit(solution)/shard_map/ppermute | solution.py:359
  45.2 1.1 add.100
  46.3 5.3 %join.3.tile_ref = f32[256,1024]{1,0:T(8,128)S(1)} custom-call(s32[2]{0:T(128)S(1)} %pad_add_fusion.where_ref, f32[128,1024]{1,0:T(8,128)S(1)} %add.83.mine_ref, f32[128,1024]{1,0:T(8,128)S(1)} %collective-permute-done.7.other_ref), custom_call_target="tpu_custom_call" | custom-call | tf_op jit(solution)/shard_map/join/pallas_call | solution.py:157
  51.7 1.0 collective-permute-start.22
  52.7 0.6 stage.8
  53.3 1.3 %add.96 = f32[128,1024]{1,0:T(8,128)S(1)} add(f32[128,1024]{1,0:T(8,128)} %add.95, f32[128,1024]{1,0:T(8,128)} %collective-permute-done.16) | non-fusion elementwise | flops 131072 | bytes 1572864 | tf_op jit(solution)/shard_map/add | solution.py:382
  54.5 1.3 %collective-permute-start.17 = (f32[128,1024]{1,0:T(8,128)S(1)}, f32[128,1024]{1,0:T(8,128)S(1)}, u32[]{:S(2)}, u32[]{:S(2)}) collective-permute-start(f32[128,1024]{1,0:T(8,128)S(1)} %add.96), channel_id=1, source_target_pairs={{0,16},{4,12},{8,24},{12,4},{16,0},{20,28},{24,8},{28,20},{1,17},{... | collective-permute-start | bytes 1572872 | tf_op jit(solution)/shard_map/ppermute | solution.py:304
  55.9 1.1 add.85
  57.0 1.0 collective-permute-start.8
  58.0 6.7 %collective-permute-done.22 = f32[128,1024]{1,0:T(8,128)S(1)} collective-permute-done((f32[128,1024]{1,0:T(8,128)S(1)}, f32[128,1024]{1,0:T(8,128)S(1)}, u32[]{:S(2)}, u32[]{:S(2)}) %collective-permute-start.22) | collective-permute-done | bytes 524320 | tf_op jit(solution)/shard_map/ppermute | solution.py:304
  64.8 1.8 %collective-permute-start.23 = (f32[128,1024]{1,0:T(8,128)S(1)}, f32[128,1024]{1,0:T(8,128)S(1)}, u32[]{:S(2)}, u32[]{:S(2)}) collective-permute-start(f32[128,1024]{1,0:T(8,128)S(1)} %add.101), channel_id=1, source_target_pairs={{0,16},{4,12},{8,24},{12,4},{16,0},{20,28},{24,8},{28,20},{1,17},{... | collective-permute-start | bytes 1572872 | tf_op jit(solution)/shard_map/ppermute | solution.py:304
  66.6 0.7 collective-permute-start.13
  67.2 0.8 stage.9
  68.1 2.3 %collective-permute-done.8 = f32[2,32,1024]{2,1,0:T(8,128)S(1)} collective-permute-done((f32[2,32,1024]{2,1,0:T(8,128)S(1)}, f32[2,32,1024]{2,1,0:T(8,128)S(1)}, u32[]{:S(2)}, u32[]{:S(2)}) %collective-permute-start.8) | collective-permute-done | bytes 262176 | tf_op jit(solution)/shard_map/ppermute | solution.py:304
  70.5 1.8 %collective-permute-start.12 = (f32[1,32,1024]{2,1,0:T(8,128)S(1)}, f32[1,32,1024]{2,1,0:T(8,128)S(1)}, u32[]{:S(2)}, u32[]{:S(2)}) collective-permute-start(f32[1,32,1024]{2,1,0:T(8,128)S(1)} %slice.46), channel_id=1, source_target_pairs={{0,16},{4,12},{8,24},{12,4},{16,0},{20,28},{24,8},{28,20},{1,17},{... | collective-permute-start | bytes 393224 | tf_op jit(solution)/shard_map/ppermute | solution.py:304
  72.3 0.7 collective-permute-start.14
  73.0 2.6 %collective-permute-done.12 = f32[1,32,1024]{2,1,0:T(8,128)S(1)} collective-permute-done((f32[1,32,1024]{2,1,0:T(8,128)S(1)}, f32[1,32,1024]{2,1,0:T(8,128)S(1)}, u32[]{:S(2)}, u32[]{:S(2)}) %collective-permute-start.12) | collective-permute-done | bytes 131104 | tf_op jit(solution)/shard_map/ppermute | solution.py:304
  75.6 0.7 collective-permute-start.24
  76.3 0.7 slice_add_fusion.2
  77.0 0.6 join.4
  77.6 1.2 %stage.10 = (f32[32,256]{1,0:T(8,128)S(1)}, f32[32,256]{1,0:T(8,128)}) custom-call(s32[2]{0:T(128)S(1)} %pad_add_fusion.where_ref, f32[32,256]{1,0:T(8,128)S(1)} %fusion.2.base_ref, f32[256,1024]{1,0:T(8,128)S(1)} %join.3.tile_ref, f32[32,1024]{1,0:T(8,128)S(1)} %bitcast.43, f32[32,512]{1,0:T(8,128)S(1)} %collective-permute-done.14.message_ref, ...), custom_call_target="tpu_custom_call" | custom-call | tf_op jit(solution)/shard_map/stage/pallas_call | solution.py:261
  78.8 1.3 %collective-permute-start.19 = (f32[32,256]{1,0:T(8,128)}, f32[32,256]{1,0:T(8,128)S(1)}, u32[]{:S(2)}, u32[]{:S(2)}) collective-permute-start(f32[32,256]{1,0:T(8,128)} %get-tuple-element.96), channel_id=1, source_target_pairs={{1,0},{5,4},{9,8},{13,12},{17,16},{21,20},{25,24},{29,28}} | collective-permute-start | bytes 98312 | tf_op jit(solution)/shard_map/ppermute | solution.py:289
  80.1 4.7 %collective-permute-done.19.message_ref = f32[32,256]{1,0:T(8,128)S(1)} collective-permute-done((f32[32,256]{1,0:T(8,128)}, f32[32,256]{1,0:T(8,128)S(1)}, u32[]{:S(2)}, u32[]{:S(2)}) %collective-permute-start.19) | collective-permute-done | bytes 32800 | tf_op jit(solution)/shard_map/ppermute | solution.py:289
  84.8 1.4 %stage.11 = (f32[32,256]{1,0:T(8,128)S(1)}, f32[32,256]{1,0:T(8,128)}) custom-call(s32[2]{0:T(128)S(1)} %pad_add_fusion.where_ref, f32[32,256]{1,0:T(8,128)S(1)} %fusion.2.base_ref, f32[256,1024]{1,0:T(8,128)S(1)} %join.3.tile_ref, f32[32,1024]{1,0:T(8,128)S(1)} %bitcast.44, f32[32,256]{1,0:T(8,128)S(1)} %collective-permute-done.19.message_ref, ...), custom_call_target="tpu_custom_call" | custom-call | tf_op jit(solution)/shard_map/stage/pallas_call | solution.py:261
  86.1 1.3 %bitcast_add_fusion = f32[32,1024]{1,0:T(8,128)S(1)} fusion(f32[1,32,1024]{2,1,0:T(8,128)} %slice_add_fusion.2, f32[32,256]{1,0:T(8,128)S(1)} %get-tuple-element.98, f32[256,1024]{1,0:T(8,128)S(1)} %join.4), kind=kOutput, calls=%fused_computation.4 | convolution fusion | flops 50364416 | bytes 1343488 | tf_op jit(solution)/shard_map/dot_general | solution.py:397
  87.6 1.1 collective-permute-start.25
  88.7 3.3 %collective-permute-start.26 = (f32[32,256]{1,0:T(8,128)S(1)}, f32[32,256]{1,0:T(8,128)S(1)}, u32[]{:S(2)}, u32[]{:S(2)}) collective-permute-start(f32[32,256]{1,0:T(8,128)S(1)} %get-tuple-element.116), channel_id=1, source_target_pairs={{0,1},{1,0},{2,3},{3,2},{4,5},{5,4},{6,7},{7,6},{8,9},{9,8},{10,11... | collective-permute-start | bytes 98312 | tf_op jit(solution)/shard_map/ppermute | solution.py:402
  92.0 0.6 join.5.tile_ref
  92.6 0.7 collective-permute-done.20
  93.3 0.6 collective-permute-done.26
  93.8 0.8 fusion.5.base_ref
  94.6 0.6 stage.12
  95.2 0.7 collective-permute-start.27
  95.9 0.6 stage.13
  96.4 0.7 collective-permute-start.28
  97.1 0.6 stage.14
  97.7 1.3 %collective-permute-start.29 = (f32[32,256]{1,0:T(8,128)S(1)}, f32[32,256]{1,0:T(8,128)S(1)}, u32[]{:S(2)}, u32[]{:S(2)}) collective-permute-start(f32[32,256]{1,0:T(8,128)S(1)} %get-tuple-element.112), channel_id=1, source_target_pairs={{1,0},{5,4},{9,8},{13,12},{17,16},{21,20},{25,24},{29,28}} | collective-permute-start | bytes 98312 | tf_op jit(solution)/shard_map/ppermute | solution.py:289
  99.0 12.7 %collective-permute-done.29.message_ref = f32[32,256]{1,0:T(8,128)S(1)} collective-permute-done((f32[32,256]{1,0:T(8,128)S(1)}, f32[32,256]{1,0:T(8,128)S(1)}, u32[]{:S(2)}, u32[]{:S(2)}) %collective-permute-start.29) | collective-permute-done | bytes 32800 | tf_op jit(solution)/shard_map/ppermute | solution.py:289
  111.7 1.4 %stage.15 = (f32[32,256]{1,0:T(8,128)S(1)}, f32[32,256]{1,0:T(8,128)}) custom-call(s32[2]{0:T(128)S(1)} %pad_add_fusion.where_ref, f32[32,256]{1,0:T(8,128)S(1)} %fusion.5.base_ref, f32[256,1024]{1,0:T(8,128)S(1)} %join.5.tile_ref, f32[32,1024]{1,0:T(8,128)S(1)} %broadcast_3_message_ref_add_ref.2.message_ref.add_ref, ...), custom_call_target="tpu_custom_call" | custom-call | tf_op jit(solution)/shard_map/stage/pallas_call | solution.py:261
  113.1 0.6 pad_maximum_fusion
  (46 shorter events, 1.0 us)
Async XLA Ops:
  0.0 4.6 %copy-start.1 = (s32[48]{0:T(128)S(1)}, s32[48]{0:T(128)}, u32[]{:S(2)}) copy-start(s32[48]{0:T(128)} %rows_ref.9) | copy-start | bytes 580
  0.1 0.7 copy-start
  2.5 2.0 %collective-permute-start = (f32[128,1024]{1,0:T(8,128)S(1)}, f32[128,1024]{1,0:T(8,128)S(1)}, u32[]{:S(2)}, u32[]{:S(2)}) collective-permute-start(f32[128,1024]{1,0:T(8,128)S(1)} %get-tuple-element.61), channel_id=1, source_target_pairs={{0,4},{4,0},{8,12},{12,8},{16,20},{20,16},{24,28},{28,24},{1,5},{5... | collective-permute-start | bytes 1572872 | tf_op jit(solution)/shard_map/ppermute | solution.py:299
  7.9 3.9 %collective-permute-start.1 = (f32[4,32,1024]{2,1,0:T(8,128)S(1)}, f32[4,32,1024]{2,1,0:T(8,128)S(1)}, u32[]{:S(2)}, u32[]{:S(2)}) collective-permute-start(f32[4,32,1024]{2,1,0:T(8,128)S(1)} %get-tuple-element.64), channel_id=1, source_target_pairs={{0,4},{4,0},{8,12},{12,8},{16,20},{20,16},{24,28},{28,24},{1,5},{5... | collective-permute-start | bytes 1572872 | tf_op jit(solution)/shard_map/ppermute | solution.py:299
  9.3 10.0 %collective-permute-start.3 = (f32[128,1024]{1,0:T(8,128)S(1)}, f32[128,1024]{1,0:T(8,128)S(1)}, u32[]{:S(2)}, u32[]{:S(2)}) collective-permute-start(f32[128,1024]{1,0:T(8,128)S(1)} %add.79), channel_id=1, source_target_pairs={{0,8},{4,20},{8,0},{12,28},{16,24},{20,4},{24,16},{28,12},{1,9},{5... | collective-permute-start | bytes 1572872 | tf_op jit(solution)/shard_map/ppermute | solution.py:304
  11.8 10.1 %collective-permute-start.2 = (f32[2,32,1024]{2,1,0:T(8,128)S(1)}, f32[2,32,1024]{2,1,0:T(8,128)S(1)}, u32[]{:S(2)}, u32[]{:S(2)}) collective-permute-start(f32[2,32,1024]{2,1,0:T(8,128)S(1)} %slice.41), channel_id=1, source_target_pairs={{0,8},{4,20},{8,0},{12,28},{16,24},{20,4},{24,16},{28,12},{1,9},{5... | collective-permute-start | bytes 786440 | tf_op jit(solution)/shard_map/ppermute | solution.py:304
  19.3 33.3 %copy-start.2 = (f32[2,256,32]{1,2,0:T(8,128)S(1)}, f32[2,256,32]{1,2,0:T(8,128)}, u32[]{:S(2)}) copy-start(f32[2,256,32]{1,2,0:T(8,128)} %param.7) | copy-start | bytes 196612
  19.4 9.7 %collective-permute-start.5 = (f32[128,1024]{1,0:T(8,128)S(1)}, f32[128,1024]{1,0:T(8,128)S(1)}, u32[]{:S(2)}, u32[]{:S(2)}) collective-permute-start(f32[128,1024]{1,0:T(8,128)S(1)} %add.81), channel_id=1, source_target_pairs={{0,16},{4,12},{8,24},{12,4},{16,0},{20,28},{24,8},{28,20},{1,17},{... | collective-permute-start | bytes 1572872 | tf_op jit(solution)/shard_map/ppermute | solution.py:304
  22.0 8.5 %collective-permute-start.4 = (f32[1,32,1024]{2,1,0:T(8,128)S(1)}, f32[1,32,1024]{2,1,0:T(8,128)S(1)}, u32[]{:S(2)}, u32[]{:S(2)}) collective-permute-start(f32[1,32,1024]{2,1,0:T(8,128)S(1)} %slice.43), channel_id=1, source_target_pairs={{0,16},{4,12},{8,24},{12,4},{16,0},{20,28},{24,8},{28,20},{1,17},{... | collective-permute-start | bytes 393224 | tf_op jit(solution)/shard_map/ppermute | solution.py:304
  30.5 2.0 %collective-permute-start.15 = (f32[128,1024]{1,0:T(8,128)S(1)}, f32[128,1024]{1,0:T(8,128)S(1)}, u32[]{:S(2)}, u32[]{:S(2)}) collective-permute-start(f32[128,1024]{1,0:T(8,128)S(1)} %get-tuple-element.91), channel_id=1, source_target_pairs={{0,4},{4,0},{8,12},{12,8},{16,20},{20,16},{24,28},{28,24},{1,5},{5... | collective-permute-start | bytes 1572872 | tf_op jit(solution)/shard_map/ppermute | solution.py:299
  30.6 3.4 %collective-permute-start.7 = (f32[128,1024]{1,0:T(8,128)S(1)}, f32[128,1024]{1,0:T(8,128)S(1)}, u32[]{:S(2)}, u32[]{:S(2)}) collective-permute-start(f32[128,1024]{1,0:T(8,128)S(1)} %add.83.mine_ref), channel_id=1, source_target_pairs={{0,4},{4,0},{8,12},{12,8},{16,20},{20,16},{24,28},{28,24},{1,5},{5... | collective-permute-start | bytes 1572872 | tf_op jit(solution)/shard_map/ppermute | solution.py:299
  31.1 12.8 %collective-permute-start.21 = (f32[128,1024]{1,0:T(8,128)S(1)}, f32[128,1024]{1,0:T(8,128)}, u32[]{:S(2)}, u32[]{:S(2)}) collective-permute-start(f32[128,1024]{1,0:T(8,128)S(1)} %get-tuple-element.101), channel_id=1, source_target_pairs={{0,4},{4,0},{8,12},{12,8},{16,20},{20,16},{24,28},{28,24},{1,5},{5... | collective-permute-start | bytes 1572872 | tf_op jit(solution)/shard_map/ppermute | solution.py:299
  34.0 19.3 %collective-permute-start.16 = (f32[128,1024]{1,0:T(8,128)}, f32[128,1024]{1,0:T(8,128)}, u32[]{:S(2)}, u32[]{:S(2)}) collective-permute-start(f32[128,1024]{1,0:T(8,128)} %add.95), channel_id=1, source_target_pairs={{0,8},{4,20},{8,0},{12,28},{16,24},{20,4},{24,16},{28,12},{1,9},{5... | collective-permute-start | bytes 1572872 | tf_op jit(solution)/shard_map/ppermute | solution.py:304
  35.1 20.8 %collective-permute-start.6 = (f32[4,32,1024]{2,1,0:T(8,128)}, f32[4,32,1024]{2,1,0:T(8,128)}, u32[]{:S(2)}, u32[]{:S(2)}) collective-permute-start(f32[4,32,1024]{2,1,0:T(8,128)} %get-tuple-element.78), channel_id=1, source_target_pairs={{0,4},{4,0},{8,12},{12,8},{16,20},{20,16},{24,28},{28,24},{1,5},{5... | collective-permute-start | bytes 1572872 | tf_op jit(solution)/shard_map/ppermute | solution.py:299
  35.9 15.8 %collective-permute-start.9 = (f32[32,256]{1,0:T(8,128)S(1)}, f32[32,256]{1,0:T(8,128)S(1)}, u32[]{:S(2)}, u32[]{:S(2)}) collective-permute-start(f32[32,256]{1,0:T(8,128)S(1)} %get-tuple-element.118), channel_id=1, source_target_pairs={{0,1},{1,2},{2,3},{4,5},{5,6},{6,7},{8,9},{9,10},{10,11},{12,13},{... | collective-permute-start | bytes 98312 | tf_op jit(solution)/shard_map/ppermute | solution.py:359
  39.4 13.3 %collective-permute-start.10 = (f32[32,256]{1,0:T(8,128)S(1)}, f32[32,256]{1,0:T(8,128)S(1)}, u32[]{:S(2)}, u32[]{:S(2)}) collective-permute-start(f32[32,256]{1,0:T(8,128)S(1)} %get-tuple-element.120), channel_id=1, source_target_pairs={{0,2},{1,3},{4,6},{5,7},{8,10},{9,11},{12,14},{13,15},{16,18},{17,... | collective-permute-start | bytes 98312 | tf_op jit(solution)/shard_map/ppermute | solution.py:359
  43.9 8.8 %collective-permute-start.11 = (f32[32,256]{1,0:T(8,128)S(1)}, f32[32,256]{1,0:T(8,128)S(1)}, u32[]{:S(2)}, u32[]{:S(2)}) collective-permute-start(f32[32,256]{1,0:T(8,128)S(1)} %get-tuple-element.119), channel_id=1, source_target_pairs={{0,3},{4,7},{8,11},{12,15},{16,19},{20,23},{24,27},{28,31}} | collective-permute-start | bytes 98312 | tf_op jit(solution)/shard_map/ppermute | solution.py:359
  51.7 13.1 %collective-permute-start.22 = (f32[128,1024]{1,0:T(8,128)S(1)}, f32[128,1024]{1,0:T(8,128)S(1)}, u32[]{:S(2)}, u32[]{:S(2)}) collective-permute-start(f32[128,1024]{1,0:T(8,128)S(1)} %add.100), channel_id=1, source_target_pairs={{0,8},{4,20},{8,0},{12,28},{16,24},{20,4},{24,16},{28,12},{1,9},{5... | collective-permute-start | bytes 1572872 | tf_op jit(solution)/shard_map/ppermute | solution.py:304
  54.5 15.8 %collective-permute-start.17 = (f32[128,1024]{1,0:T(8,128)S(1)}, f32[128,1024]{1,0:T(8,128)S(1)}, u32[]{:S(2)}, u32[]{:S(2)}) collective-permute-start(f32[128,1024]{1,0:T(8,128)S(1)} %add.96), channel_id=1, source_target_pairs={{0,16},{4,12},{8,24},{12,4},{16,0},{20,28},{24,8},{28,20},{1,17},{... | collective-permute-start | bytes 1572872 | tf_op jit(solution)/shard_map/ppermute | solution.py:304
  57.0 13.3 %collective-permute-start.8 = (f32[2,32,1024]{2,1,0:T(8,128)S(1)}, f32[2,32,1024]{2,1,0:T(8,128)S(1)}, u32[]{:S(2)}, u32[]{:S(2)}) collective-permute-start(f32[2,32,1024]{2,1,0:T(8,128)S(1)} %slice.36), channel_id=1, source_target_pairs={{0,8},{4,20},{8,0},{12,28},{16,24},{20,4},{24,16},{28,12},{1,9},{5... | collective-permute-start | bytes 786440 | tf_op jit(solution)/shard_map/ppermute | solution.py:304
  64.8 10.8 %collective-permute-start.23 = (f32[128,1024]{1,0:T(8,128)S(1)}, f32[128,1024]{1,0:T(8,128)S(1)}, u32[]{:S(2)}, u32[]{:S(2)}) collective-permute-start(f32[128,1024]{1,0:T(8,128)S(1)} %add.101), channel_id=1, source_target_pairs={{0,16},{4,12},{8,24},{12,4},{16,0},{20,28},{24,8},{28,20},{1,17},{... | collective-permute-start | bytes 1572872 | tf_op jit(solution)/shard_map/ppermute | solution.py:304
  66.6 0.7 collective-permute-start.13
  70.4 6.6 %collective-permute-start.18 = (f32[128,1024]{1,0:T(8,128)S(1)}, f32[128,1024]{1,0:T(8,128)S(1)}, u32[]{:S(2)}, u32[]{:S(2)}) collective-permute-start(f32[128,1024]{1,0:T(8,128)S(1)} %add.97.mine_ref), channel_id=1, source_target_pairs={{0,4},{4,0},{8,12},{12,8},{16,20},{20,16},{24,28},{28,24},{1,5},{5... | collective-permute-start | bytes 1572872 | tf_op jit(solution)/shard_map/ppermute | solution.py:299
  70.5 5.0 %collective-permute-start.12 = (f32[1,32,1024]{2,1,0:T(8,128)S(1)}, f32[1,32,1024]{2,1,0:T(8,128)S(1)}, u32[]{:S(2)}, u32[]{:S(2)}) collective-permute-start(f32[1,32,1024]{2,1,0:T(8,128)S(1)} %slice.46), channel_id=1, source_target_pairs={{0,16},{4,12},{8,24},{12,4},{16,0},{20,28},{24,8},{28,20},{1,17},{... | collective-permute-start | bytes 393224 | tf_op jit(solution)/shard_map/ppermute | solution.py:304
  72.3 5.3 %collective-permute-start.14 = (f32[32,512]{1,0:T(8,128)S(1)}, f32[32,512]{1,0:T(8,128)S(1)}, u32[]{:S(2)}, u32[]{:S(2)}) collective-permute-start(f32[32,512]{1,0:T(8,128)S(1)} %get-tuple-element.88), channel_id=1, source_target_pairs={{2,1},{6,5},{10,9},{14,13},{18,17},{22,21},{26,25},{30,29}} | collective-permute-start | bytes 196616 | tf_op jit(solution)/shard_map/ppermute | solution.py:289
  75.6 16.3 %collective-permute-start.24 = (f32[128,1024]{1,0:T(8,128)S(1)}, f32[128,1024]{1,0:T(8,128)S(1)}, u32[]{:S(2)}, u32[]{:S(2)}) collective-permute-start(f32[128,1024]{1,0:T(8,128)S(1)} %add.102.mine_ref), channel_id=1, source_target_pairs={{0,4},{4,0},{8,12},{12,8},{16,20},{20,16},{24,28},{28,24},{1,5},{5... | collective-permute-start | bytes 1572872 | tf_op jit(solution)/shard_map/ppermute | solution.py:299
  78.8 6.0 %collective-permute-start.19 = (f32[32,256]{1,0:T(8,128)}, f32[32,256]{1,0:T(8,128)S(1)}, u32[]{:S(2)}, u32[]{:S(2)}) collective-permute-start(f32[32,256]{1,0:T(8,128)} %get-tuple-element.96), channel_id=1, source_target_pairs={{1,0},{5,4},{9,8},{13,12},{17,16},{21,20},{25,24},{29,28}} | collective-permute-start | bytes 98312 | tf_op jit(solution)/shard_map/ppermute | solution.py:289
  87.5 5.8 %collective-permute-start.20 = (f32[32,256]{1,0:T(8,128)S(1)}, f32[32,256]{1,0:T(8,128)S(1)}, u32[]{:S(2)}, u32[]{:S(2)}) collective-permute-start(f32[32,256]{1,0:T(8,128)S(1)} %get-tuple-element.115), channel_id=1, source_target_pairs={{0,3},{1,2},{2,1},{3,0},{4,7},{5,6},{6,5},{7,4},{8,11},{9,10},{10,... | collective-permute-start | bytes 98312 | tf_op jit(solution)/shard_map/ppermute | solution.py:402
  87.6 5.7 %collective-permute-start.25 = (f32[32,256]{1,0:T(8,128)S(1)}, f32[32,256]{1,0:T(8,128)S(1)}, u32[]{:S(2)}, u32[]{:S(2)}) collective-permute-start(f32[32,256]{1,0:T(8,128)S(1)} %get-tuple-element.117), channel_id=1, source_target_pairs={{0,2},{1,3},{2,0},{3,1},{4,6},{5,7},{6,4},{7,5},{8,10},{9,11},{10,... | collective-permute-start | bytes 98312 | tf_op jit(solution)/shard_map/ppermute | solution.py:402
  88.7 5.2 %collective-permute-start.26 = (f32[32,256]{1,0:T(8,128)S(1)}, f32[32,256]{1,0:T(8,128)S(1)}, u32[]{:S(2)}, u32[]{:S(2)}) collective-permute-start(f32[32,256]{1,0:T(8,128)S(1)} %get-tuple-element.116), channel_id=1, source_target_pairs={{0,1},{1,0},{2,3},{3,2},{4,5},{5,4},{6,7},{7,6},{8,9},{9,8},{10,11... | collective-permute-start | bytes 98312 | tf_op jit(solution)/shard_map/ppermute | solution.py:402
  95.2 0.7 collective-permute-start.27
  96.4 0.7 collective-permute-start.28
  97.7 14.0 %collective-permute-start.29 = (f32[32,256]{1,0:T(8,128)S(1)}, f32[32,256]{1,0:T(8,128)S(1)}, u32[]{:S(2)}, u32[]{:S(2)}) collective-permute-start(f32[32,256]{1,0:T(8,128)S(1)} %get-tuple-element.112), channel_id=1, source_target_pairs={{1,0},{5,4},{9,8},{13,12},{17,16},{21,20},{25,24},{29,28}} | collective-permute-start | bytes 98312 | tf_op jit(solution)/shard_map/ppermute | solution.py:289

commit v4 on v0

v4 whole, which is shorter than its diff:
```python
import functools

import jax
import jax.numpy as jnp
from jax import lax
from jax.experimental import pallas as pl
from jax.experimental.pallas import tpu as pltpu
from jax.sharding import PartitionSpec as P

F32 = jnp.float32
BF16 = jnp.bfloat16
VMEM = pl.BlockSpec(memory_space=pltpu.MemorySpace.VMEM)
SMEM = pl.BlockSpec(memory_space=pltpu.MemorySpace.SMEM)
HBM = pl.BlockSpec(memory_space=pl.ANY)


def shape(*dims):
    return jax.ShapeDtypeStruct(dims, F32)


def call(body, out, specs, args, name, scratch=(), aliases=None, micros=1.0):
    multiple = isinstance(out, tuple)
    return pl.pallas_call(
        body,
        out_shape=out,
        in_specs=list(specs),
        out_specs=tuple(VMEM for _ in out) if multiple else VMEM,
        scratch_shapes=list(scratch),
        input_output_aliases=aliases or {},
        compiler_params=pltpu.CompilerParams(vmem_limit_bytes=40 << 20),
        cost_estimate=pl.CostEstimate(flops=0, transcendentals=0, bytes_accessed=int(micros * 3.0e6)),
        name=name,
    )(*args)


def split(value):
    high = value.astype(BF16)
    return high, (value - high.astype(F32)).astype(BF16)


def dot_split(a, b, dims):
    (ah, al), (bh, bl) = a, b

    def one(u, v):
        return lax.dot_general(u, v, (dims, ((), ())), preferred_element_type=F32)

    return one(al, bh) + one(ah, bl) + one(ah, bh)


def dot3(a, b):
    return dot_split(split(a), split(b), ((1,), (0,)))


def stage_orders(members):
    bits = members.bit_length() - 1
    first = list(range(1, bits))
    return first, first[::-1]


def swap_core(value, members):
    return lax.ppermute(value, "rt", [(i, i ^ 1) for i in range(members)])


def swap_chip(value, members, stage):
    orders = stage_orders(members)
    return lax.ppermute(value, "rt", [(i, i ^ (1 << orders[i & 1][stage])) for i in range(members)])


def send_tables(members):
    orders = stage_orders(members)
    count = len(orders[0])
    tables = []
    for core in range(2):
        table = []
        for place in range(members):
            other = place >> count
            rest = place & ((1 << count) - 1)
            relative = other
            for stage in range(count):
                if (rest >> (count - 1 - stage)) & 1:
                    relative |= 1 << orders[core ^ other][stage]
            table.append(relative)
        tables.append(table)
    return tables


def accumulate(where_ref, rows_ref, factor_ref, known_ref, factor_buf, known_buf, acc_ref, sems, column):
    slots = factor_buf.shape[0]
    depth = 2
    me = where_ref[0]

    def live(slot):
        return rows_ref[me * slots + slot] >= 2

    def copies(slot):
        return (
            pltpu.make_async_copy(known_ref.at[slot], known_buf.at[slot], sems.at[0, slot]),
            pltpu.make_async_copy(factor_ref.at[slot, column], factor_buf.at[slot], sems.at[1, slot]),
        )

    def start(slot):
        @pl.when(live(slot))
        def _():
            for copy in copies(slot):
                copy.start()

    for slot in range(min(depth, slots)):
        start(slot)
    acc_ref[...] = jnp.zeros_like(acc_ref)
    for slot in range(slots):

        @pl.when(live(slot))
        def _():
            for copy in copies(slot):
                copy.wait()

        if slot + depth < slots:
            start(slot + depth)

        @pl.when(live(slot))
        def _():
            acc_ref[...] += dot_split(split(known_buf[slot]), split(factor_buf[slot]), ((0,), (0,)))


def in_send_order(where_ref, acc_ref, keep_ref, send_ref, first, tables):
    count = len(tables[0])
    columns = acc_ref.shape[0] // count
    me = where_ref[0]
    for spot, (even, odd) in enumerate(zip(*tables)):
        group = me ^ jnp.where((me & 1) == 0, even, odd)
        rows = acc_ref[pl.ds(pl.multiple_of(group * columns, columns), columns), :]
        target, start = (keep_ref, spot) if spot < count // 2 else (send_ref, spot - count // 2)
        target[first + start * columns : first + (start + 1) * columns, :] = rows


def owned_slot(where_ref, rows_ref, row, slots):
    slot = jnp.int32(-1)
    for s in range(slots):
        slot = jnp.where(rows_ref[where_ref[0] * slots + s] == row, s, slot)
    return slot


def band_copies(where_ref, factor_ref, slot, column, keep_ref, send_ref, first, half, sems):
    core = where_ref[0] & 1
    copies = []
    for index, (target, which) in enumerate(((send_ref, 1 - core), (keep_ref, core))):
        start = pl.multiple_of(which * half, half)
        source = factor_ref.at[slot, column, pl.ds(start, half), :]
        copies.append(pltpu.make_async_copy(source, target.at[pl.ds(first, half), :], sems.at[index]))
    return copies


def put_band(where_ref, rows_ref, factor_ref, row, column, keep_ref, send_ref, first, half, sems):
    slot = owned_slot(where_ref, rows_ref, row, factor_ref.shape[0])

    @pl.when(slot >= 0)
    def _():
        for copy in band_copies(where_ref, factor_ref, slot, column, keep_ref, send_ref, first, half, sems):
            copy.start()

    @pl.when(slot < 0)
    def _():
        keep_ref[first : first + half, :] = jnp.zeros((half, keep_ref.shape[1]), F32)
        send_ref[first : first + half, :] = jnp.zeros((half, keep_ref.shape[1]), F32)

    def finish():
        @pl.when(slot >= 0)
        def _():
            for copy in band_copies(where_ref, factor_ref, slot, column, keep_ref, send_ref, first, half, sems):
                copy.wait()

    return finish


def partial_scratch(slots, band, width, total):
    return [
        pltpu.VMEM((slots, band, width), F32),
        pltpu.VMEM((slots, band, total), F32),
        pltpu.VMEM((total, width), F32),
        pltpu.SemaphoreType.DMA((2, slots)),
    ]


def first_band(where, slot_row, factor_rows):
    _, _, band, width = factor_rows.shape
    half = band // 2

    def body(where_ref, rows_ref, factor_ref, keep_ref, send_ref, sems):
        put_band(where_ref, rows_ref, factor_ref, 1, 1, keep_ref, send_ref, 0, half, sems)()

    out = (shape(half, width), shape(half, width))
    scratch = [pltpu.SemaphoreType.DMA((2,))]
    return call(body, out, (SMEM, SMEM, HBM), (where, slot_row, factor_rows), "first_band", scratch)


def partial_one(where, slot_row, factor_rows, known, members):
    slots, _, band, width = factor_rows.shape
    total = known.shape[2]
    tables = send_tables(members)

    def body(where_ref, rows_ref, factor_ref, known_ref, keep_ref, send_ref, factor_buf, known_buf, acc_ref, sems):
        accumulate(where_ref, rows_ref, factor_ref, known_ref, factor_buf, known_buf, acc_ref, sems, 1)
        in_send_order(where_ref, acc_ref, keep_ref, send_ref, 0, tables)

    out = (shape(total // 2, width), shape(total // 2, width))
    scratch = partial_scratch(slots, band, width, total)
    args = (where, slot_row, factor_rows, known)
    return call(body, out, (SMEM, SMEM, HBM, HBM), args, "partial_one", scratch, micros=5.0)


def pack_rest(where, slot_row, factor_rows, known, members):
    slots, _, band, width = factor_rows.shape
    half, total = band // 2, known.shape[2]
    tables = send_tables(members)

    def body(where_ref, rows_ref, factor_ref, known_ref, keep_ref, send_ref, factor_buf, known_buf, acc_ref, sems, low, top):
        finish_low = put_band(where_ref, rows_ref, factor_ref, 1, 0, keep_ref, send_ref, 0, half, low)
        finish_top = put_band(where_ref, rows_ref, factor_ref, 0, 0, keep_ref, send_ref, half, half, top)
        accumulate(where_ref, rows_ref, factor_ref, known_ref, factor_buf, known_buf, acc_ref, sems, 0)
        in_send_order(where_ref, acc_ref, keep_ref, send_ref, band, tables)
        finish_low()
        finish_top()

    rows = band + total // 2
    out = (shape(rows, width), shape(rows, width))
    scratch = partial_scratch(slots, band, width, total) + [pltpu.SemaphoreType.DMA((2,))] * 2
    args = (where, slot_row, factor_rows, known)
    return call(body, out, (SMEM, SMEM, HBM, HBM), args, "pack_rest", scratch, micros=6.0)


def after(value, *others):
    return lax.optimization_barrier((value,) + others)[0]


def pack_parts(sums, skip, got, tile_rows, final):
    width = got.shape[1]
    count = got.shape[0] - tile_rows
    go = count if final else count // 2

    def add(tiles_ref, sums_ref, got_ref, out_ref, keep_ref):
        out_ref[:tile_rows, :] = tiles_ref[:tile_rows, :] + got_ref[:tile_rows, :]
        keep_ref[...] = sums_ref[skip : skip + go, :] + got_ref[tile_rows : tile_rows + go, :]
        if not final:
            out_ref[tile_rows:, :] = sums_ref[skip + go : skip + count, :] + got_ref[tile_rows + go :, :]

    return add, (shape(tile_rows + count - go, width), shape(go, width))


def pack_step(tiles, sums, skip, got, tile_rows, final):
    add, out = pack_parts(sums, skip, got, tile_rows, final)
    return call(add, out, (VMEM,) * 3, (tiles, sums, got), "pack_step")


def inverse_of(block):
    size = block.shape[0]
    row = lax.broadcasted_iota(jnp.int32, (size, size), 0)
    col = lax.broadcasted_iota(jnp.int32, (size, size), 1)
    diag = jnp.where(row == col, block, 0.0)
    recip_row = 1.0 / jnp.sum(diag, axis=0, keepdims=True)
    recip_col = 1.0 / jnp.sum(diag, axis=1, keepdims=True)
    pair = (row - col == 1) & (lax.rem(row, 2) == 1)
    inverse = jnp.where(row == col, recip_row, jnp.where(pair, -(block * recip_row) * recip_col, 0.0))
    step = 2
    while step < size:
        half = lax.div(row, step)
        below = (half - lax.div(col, step) == 1) & (lax.rem(half, 2) == 1)
        lower = jnp.where(below, block, 0.0)
        parts = split(inverse)
        middle = dot_split(split(lower), parts, ((1,), (0,)))
        inverse = inverse - dot_split(parts, split(middle), ((1,), (0,)))
        step *= 2
    return inverse


def invert_diagonal(tile_ref, place, chosen, band):
    for spot in chosen:

        @pl.when(place == spot)
        def _():
            here = slice(spot * band, (spot + 1) * band)
            tile_ref[:, here] = inverse_of(tile_ref[:, here])


def join_halves(where, mine, other, first, half, chosen):
    width = mine.shape[1]

    def body(where_ref, mine_ref, other_ref, tile_ref):
        core = where_ref[0] & 1
        tile_ref[pl.ds(pl.multiple_of(core * half, half), half), :] = mine_ref[first : first + half, :]
        tile_ref[pl.ds(pl.multiple_of((1 - core) * half, half), half), :] = other_ref[first : first + half, :]
        invert_diagonal(tile_ref, where_ref[1], chosen, 2 * half)

    return call(body, shape(2 * half, width), (SMEM, VMEM, VMEM), (where, mine, other), "join", micros=5.0)


def invert_late(where, tile, chosen):
    band = tile.shape[0]

    def body(where_ref, old_ref, tile_ref):
        invert_diagonal(tile_ref, where_ref[1], chosen, band)

    return call(body, shape(*tile.shape), (SMEM, VMEM), (where, tile), "invert_late", aliases={1: 0}, micros=4.0)


def run_stage(where, base, tile, add, near, far, held, stage, pack=None):
    columns, band = base.shape
    left = stage * band
    last = max(left - band, 0)
    more = () if pack is None else pack[:2] + (pack[3],)
    add_pack, out_pack = (None, ()) if pack is None else pack_parts(*pack[1:])

    def body(where_ref, base_ref, tile_ref, add_ref, near_ref, far_ref, held_ref, *refs):
        solved_ref, update_ref = refs[len(more) : len(more) + 2]

        @pl.when(where_ref[1] == stage)
        def _():
            right = base_ref[...] - near_ref[...] - far_ref[:, left : left + band]
            solved = dot3(right, tile_ref[:, left : left + band])
            solved_ref[...] = solved
            if stage > 0:
                here = slice(last, left)
                update_ref[...] = far_ref[:, here] + add_ref[:, here] + dot3(solved, tile_ref[:, here])

        @pl.when(where_ref[1] != stage)
        def _():
            solved_ref[...] = held_ref[...]

        if more:
            add_pack(*refs[: len(more)], *refs[len(more) + 2 :])

    out = (shape(columns, band), shape(columns, band)) + out_pack
    specs = (SMEM,) + (VMEM,) * (6 + len(more))
    return call(body, out, specs, (where, base, tile, add, near, far, held) + more, "stage")


def run_rest(where, tile, add, far, solved, stage):
    columns, band = solved.shape
    last = (stage - 1) * band

    def body(where_ref, tile_ref, add_ref, far_ref, solved_ref, rest_ref):
        @pl.when(where_ref[1] == stage)
        def _():
            rest_ref[...] = far_ref[:, :last] + add_ref[:, :last] + dot3(solved_ref[...], tile_ref[:, :last])

    return call(body, shape(columns, last), (SMEM,) + (VMEM,) * 4, (where, tile, add, far, solved), "rest", micros=3.0)


def run_stage_plain(where, base, tile, add, near, far, held, stage, pack=None):
    high = lax.Precision.HIGHEST
    band = base.shape[1]
    left = stage * band
    here = slice(max(left - band, 0), max(left, band))
    solved = jnp.dot(base - near - far[:, left : left + band], tile[:, left : left + band], precision=high)
    update = jnp.dot(solved, tile[:, here], precision=high) + add[:, here] + far[:, here]
    more = () if pack is None else tuple(pack_step(*pack))
    return (jnp.where(where[1] == stage, solved, held), update) + more


def run_rest_plain(where, tile, add, far, solved, stage):
    last = (stage - 1) * solved.shape[1]
    return far[:, :last] + add[:, :last] + jnp.dot(solved, tile[:, :last], precision=lax.Precision.HIGHEST)


def sweep(where, base, tile, add, bands, packs=None):
    columns, band = base.shape
    aligned = band % 128 == 0
    stage_of, rest_of = (run_stage, run_rest) if aligned else (run_stage_plain, run_rest_plain)
    near = jnp.zeros((columns, band), F32)
    held = jnp.zeros((columns, band), F32)
    fars = [jnp.zeros((columns, bands * band), F32)] * 2
    for stage in range(bands - 1, -1, -1):
        far = fars.pop(0)
        pack = packs.take(stage) if packs else None
        held, update, *more = stage_of(where, base, tile, add, near, far, held, stage, pack)
        if stage > 0:
            near = lax.ppermute(update, "ct", [(stage, stage - 1)])
        if stage > 1:
            rest = rest_of(where, tile, add, far, held, stage)
            fars.append(lax.ppermute(rest, "ct", [(stage, stage - 2)]))
        if more:
            packs.put(*more)
    return held


class Packs:
    def __init__(self, tiles, sums, got, band, steps, at, members):
        self.tiles, self.sums, self.got, self.band = tiles, sums, got, band
        self.step, self.steps, self.at, self.members = 0, steps, at, members

    def take(self, stage):
        if self.step == self.steps or stage != self.at[self.step]:
            return None
        return (self.tiles, self.sums, 0, self.got, self.band, self.step == self.steps - 1)

    def put(self, tiles, sums):
        self.tiles, self.sums, self.step = tiles, sums, self.step + 1
        if self.step < self.steps:
            self.got = swap_chip(tiles, self.members, self.step)
        else:
            self.got = swap_core(tiles, self.members)


def couple(where, sums, solved, tile, bands):
    columns, band = solved.shape

    def body(where_ref, sums_ref, solved_ref, tile_ref, out_ref, whole_ref):
        whole_ref[...] = sums_ref[...] + dot3(solved_ref[...], tile_ref[...])
        for mask in range(bands):
            start = pl.multiple_of((where_ref[1] ^ mask) * band, band)
            out_ref[mask] = whole_ref[:, pl.ds(start, band)]

    scratch = [pltpu.VMEM((columns, bands * band), F32)]
    return call(body, shape(bands, columns, band), (SMEM,) + (VMEM,) * 3, (where, sums, solved, tile), "couple", scratch)


def couple_plain(where, sums, solved, tile, bands):
    band = solved.shape[1]
    whole = sums + jnp.dot(solved, tile, precision=lax.Precision.HIGHEST)
    return jnp.stack([own_band(whole, where[1] ^ mask, band) for mask in range(bands)])


def own_band(value, spot, band):
    return lax.dynamic_slice(value, (0, spot * band), (value.shape[0], band))


def shards(factor_rows, slot_row, known, rhs, *, members, bands):
    slots, _, band, width = factor_rows.shape
    half = band // 2
    columns = rhs.shape[2]
    stages = len(stage_orders(members)[0])
    aligned = band % 128 == 0
    place = lax.axis_index("ct")
    where = jnp.stack([lax.axis_index("rt"), place]).astype(jnp.int32)
    factor_rows = pltpu.with_memory_space_constraint(factor_rows, pltpu.HBM)
    known = pltpu.with_memory_space_constraint(known, pltpu.HBM)

    keep, send = first_band(where, slot_row, factor_rows)
    tile_one = keep + swap_core(send, members)
    got_tile = swap_chip(tile_one, members, 0)
    keep, send = partial_one(after(where, tile_one), slot_row, factor_rows, known, members)
    got_sum = swap_core(send, members)
    tile_one = tile_one + after(got_tile, keep)
    got_tile = swap_chip(tile_one, members, 1) if stages > 1 else None
    sum_one = keep + after(got_sum, tile_one)
    keep = send = None
    for stage in range(stages):
        rows = sum_one.shape[0] // 2
        got_sum = swap_chip(sum_one[rows:], members, stage)
        if stage == 0:
            keep, send = pack_rest(after(where, sum_one), slot_row, factor_rows, known, members)
        if stage < stages - 1:
            tile_one = tile_one + after(got_tile, keep)
            got_tile = swap_chip(tile_one, members, stage + 2) if stage < stages - 2 else None
        sum_one = sum_one[:rows] + after(got_sum, tile_one)
        if stage == 0:
            second = sum_one

    got_up = []
    for shift in range(1, bands):
        piece = own_band(sum_one, jnp.minimum(place + shift, bands - 1), band)
        got_up.append(lax.ppermute(piece, "ct", [(i, i + shift) for i in range(bands - shift)]))

    got = swap_core(after(send, second), members)
    tiles, sums = pack_step(keep, keep, band, after(got, sum_one), band, False)
    got_pack = swap_chip(tiles, members, 0)

    other = swap_core(tile_one, members)
    tile_one = join_halves(after(where, sum_one), tile_one, other, 0, half, range(bands))
    base = rhs[1].T - own_band(sum_one, place, band)
    for piece in got_up:
        base = base - after(piece, tile_one)

    at = [2 * (stages - 1 - step) for step in range(stages)]
    packs = Packs(tiles, sums, got_pack, band, stages, at, members)
    solved_one = sweep(where, base, tile_one, sum_one, bands, packs)
    tile_low = join_halves(where, packs.tiles, packs.got, 0, half, ())
    tile_zero = join_halves(where, packs.tiles, packs.got, half, half, range(1, bands))

    pieces = (couple if aligned else couple_plain)(where, packs.sums, solved_one, tile_low, bands)
    base = rhs[0].T - pieces[0]
    got = [lax.ppermute(pieces[mask], "ct", [(i, i ^ mask) for i in range(bands)]) for mask in range(bands - 1, 0, -1)]
    tile_zero = invert_late(after(where, pieces), tile_zero, (0,))
    for piece in got:
        base = base - after(piece, tile_zero)

    nothing = jnp.zeros((columns, width), F32)
    solved_zero = sweep(where, base, tile_zero, nothing, bands)
    return jnp.stack([solved_zero.T, solved_one.T])


def solution(mesh):
    members, bands = mesh.shape["rt"], mesh.shape["ct"]
    in_specs = (P("rt", None, "ct", None), P(), P("rt", "ct", None), P(None, "ct", "rt"))
    out_specs = P(None, "ct", "rt")
    body = functools.partial(shards, members=members, bands=bands)
    return jax.shard_map(body, mesh=mesh, in_specs=in_specs, out_specs=out_specs, check_vma=False)
```

time: 564 us -> 106 us (0.19)
  waiting for transfers between devices: 264 us -> 29.8 us
  other arithmetic: 182 us -> 1.85 us
  local copies, waits for them, and re-layouts: 47 us -> 1.35 us
  starting transfers between devices: 0.35 us -> 37.2 us
  matrix products: 36.6 us -> 0 us
  Pallas kernels: 0 us -> 35.4 us
  between operations: 18 us -> 0.46 us
  blocking collectives: 14.7 us -> 0 us
    psum x3 -> x0, waiting for transfers between devices: 198 us -> none  [the longest x1 140 us: shards(): total = lax.psum(partial_value, ('rt', 'ct'))]
    another operation x8 -> x2, other arithmetic: 170 us -> 0.71 us  [the longest x1 0.63 us: shards(): return jnp.stack([solved_zero.T, solved_one.T])]
    all_gather x2 -> x0, waiting for transfers between devices: 66 us -> none  [the longest x1 66 us: shards(): lax.all_gather(tile_one, 'ct', axis=0, tiled=True)]
    another operation x61 -> x2, local copies, waits for them, and re-layouts: 46.5 us -> 0.01 us  [the longest x31 24.1 us: shards(): lax.linalg.triangular_solve(whole_zero, residual[0] - coupled, left_side=...]
    ppermute x0 -> x27, starting transfers between devices: none -> 37.2 us  [the longest x6 12.5 us: swap_chip(): lax.ppermute(value, 'rt', [(i, i ^ 1 << orders[i & 1][stage]) for i in ra...]
    pallas_call x0 -> x21, Pallas kernels: none -> 35.4 us  [call(): pl.pallas_call(body, out_shape=out, in_specs=list(specs), out_specs=tuple...]
    ppermute x0 -> x27, waiting for transfers between devices: none -> 29.8 us  [the longest x4 12.3 us: sweep(): fars.append(lax.ppermute(rest, 'ct', [(stage, stage - 2)]))]
    another operation x30 -> x0, matrix products: 20.3 us -> none  [the longest x15 10.2 us: shards(): lax.linalg.triangular_solve(whole_one, residual[1], left_side=True, lower...]
  transfers between devices with their start and end apart: 5 -> 27, of which waited for: 3 -> 10; matrix products, arithmetic and copies ran while one was open for 43% -> 2% of each run, Pallas kernels for 0% -> 27%
where the time goes in v4:
time: 106 us
  starting transfers between devices  37.2 us (35%)
  Pallas kernels  35.4 us (33%)
  waiting for transfers between devices  29.8 us (28%)
  other arithmetic  1.85 us (2%)
  local copies, waits for them, and re-layouts  1.35 us (1%)
    pallas_call x21, Pallas kernels, call(): pl.pallas_call(body, out_shape=out, in_specs=list(specs), out_specs=tuple...  35.4 us
    ppermute x6, starting transfers between devices, swap_chip(): lax.ppermute(value, 'rt', [(i, i ^ 1 << orders[i & 1][stage]) for i in ra...  12.5 us
    ppermute x4, waiting for transfers between devices, sweep(): fars.append(lax.ppermute(rest, 'ct', [(stage, stage - 2)]))  12.3 us
    ppermute x3, starting transfers between devices, shards(): lax.ppermute(piece, 'ct', [(i, i + shift) for i in range(bands - shift)])  10.5 us
    ppermute x6, waiting for transfers between devices, swap_chip(): lax.ppermute(value, 'rt', [(i, i ^ 1 << orders[i & 1][stage]) for i in ra...  8.12 us
    ppermute x6, starting transfers between devices, sweep(): near = lax.ppermute(update, 'ct', [(stage, stage - 1)])  5.24 us
    ppermute x6, waiting for transfers between devices, sweep(): near = lax.ppermute(update, 'ct', [(stage, stage - 1)])  5.16 us
    ppermute x3, starting transfers between devices, shards(): lax.ppermute(pieces[mask], 'ct', [(i, i ^ mask) for i in range(bands)])  4.45 us
  transfers between devices with their start and end apart: 27, of which 10 were waited for; matrix products, arithmetic and copies ran while one was open for 2% of the time, Pallas kernels for 27%

profile of v4, /device:TPU:0, one launch (start us, length us, event | category | flops | bytes accessed | tf_op | source)
XLA Modules:
  0.0 106.0 jit_solution(17788539734109391617)
XLA Ops:
  0.0 0.1 pad_add_fusion.where_ref
  0.1 0.7 copy-done
  0.7 0.6 first_band.1
  1.4 0.5 collective-permute-start
  1.9 1.5 %collective-permute-done = f32[128,1024]{1,0:T(8,128)S(1)} collective-permute-done((f32[128,1024]{1,0:T(8,128)S(1)}, f32[128,1024]{1,0:T(8,128)S(1)}, u32[]{:S(2)}, u32[]{:S(2)}) %collective-permute-start) | collective-permute-done | bytes 524320 | tf_op jit(solution)/shard_map/ppermute | solution.py:61
  3.5 2.9 %collective-permute-start.2 = (f32[128,1024]{1,0:T(8,128)S(1)}, f32[128,1024]{1,0:T(8,128)S(1)}, u32[]{:S(2)}, u32[]{:S(2)}) collective-permute-start(f32[128,1024]{1,0:T(8,128)S(1)} %add.39), channel_id=1, source_target_pairs={{0,8},{4,20},{8,0},{12,28},{16,24},{20,4},{24,16},{28,12},{1,9},{5... | collective-permute-start | bytes 1572872 | tf_op jit(solution)/shard_map/ppermute | solution.py:66
  6.4 6.1 %partial_one.1 = (f32[128,1024]{1,0:T(8,128)S(1)}, f32[128,1024]{1,0:T(8,128)S(1)}) custom-call(s32[2]{0:T(128)S(1)} %pad_add_fusion.where_ref, s32[48]{0:T(128)S(1)} %copy-done, f32[6,2,256,1024]{3,2,1,0:T(8,128)} %factor_ref.5, f32[6,256,256]{2,1,0:T(8,128)} %known_ref.3), custom_call_target="tpu_custom_call" | custom-call | bytes 15000000 | tf_op jit(solution)/shard_map/partial_one/pallas_call | solution.py:23
  12.5 0.1 collective-permute-start.1
  12.6 1.0 collective-permute-done.2
  13.6 0.1 add.40
  13.7 2.7 %collective-permute-start.4 = (f32[128,1024]{1,0:T(8,128)S(1)}, f32[128,1024]{1,0:T(8,128)S(1)}, u32[]{:S(2)}, u32[]{:S(2)}) collective-permute-start(f32[128,1024]{1,0:T(8,128)S(1)} %add.40), channel_id=1, source_target_pairs={{0,16},{4,12},{8,24},{12,4},{16,0},{20,28},{24,8},{28,20},{1,17},{... | collective-permute-start | bytes 1572872 | tf_op jit(solution)/shard_map/ppermute | solution.py:66
  16.4 0.1 add.41
  16.5 2.1 %collective-permute-start.3 = (f32[64,1024]{1,0:T(8,128)S(1)}, f32[64,1024]{1,0:T(8,128)S(1)}, u32[]{:S(2)}, u32[]{:S(2)}) collective-permute-start(f32[64,1024]{1,0:T(8,128)S(1)} %slice.41), channel_id=1, source_target_pairs={{0,8},{4,20},{8,0},{12,28},{16,24},{20,4},{24,16},{28,12},{1,9},{5... | collective-permute-start | bytes 786440 | tf_op jit(solution)/shard_map/ppermute | solution.py:66
  18.6 6.3 %pack_rest.1 = (f32[384,1024]{1,0:T(8,128)S(1)}, f32[384,1024]{1,0:T(8,128)S(1)}) custom-call(s32[2]{0:T(128)S(1)} %pad_add_fusion.where_ref, s32[48]{0:T(128)S(1)} %copy-done, f32[6,2,256,1024]{3,2,1,0:T(8,128)} %factor_ref.5, f32[6,256,256]{2,1,0:T(8,128)} %known_ref.3), custom_call_target="tpu_custom_call" | custom-call | bytes 18000000 | tf_op jit(solution)/shard_map/pack_rest/pallas_call | solution.py:23
  24.8 1.5 %collective-permute-done.4 = f32[128,1024]{1,0:T(8,128)S(1)} collective-permute-done((f32[128,1024]{1,0:T(8,128)S(1)}, f32[128,1024]{1,0:T(8,128)S(1)}, u32[]{:S(2)}, u32[]{:S(2)}) %collective-permute-start.4) | collective-permute-done | bytes 524320 | tf_op jit(solution)/shard_map/ppermute | solution.py:66
  26.3 0.1 add.42.mine_ref
  26.5 0.1 collective-permute-start.11
  26.6 2.1 %collective-permute-start.5 = (f32[32,1024]{1,0:T(8,128)S(1)}, f32[32,1024]{1,0:T(8,128)S(1)}, u32[]{:S(2)}, u32[]{:S(2)}) collective-permute-start(f32[32,1024]{1,0:T(8,128)S(1)} %slice.43), channel_id=1, source_target_pairs={{0,16},{4,12},{8,24},{12,4},{16,0},{20,28},{24,8},{28,20},{1,17},{... | collective-permute-start | bytes 393224 | tf_op jit(solution)/shard_map/ppermute | solution.py:66
  28.7 2.9 %collective-permute-done.5 = f32[32,1024]{1,0:T(8,128)S(1)} collective-permute-done((f32[32,1024]{1,0:T(8,128)S(1)}, f32[32,1024]{1,0:T(8,128)S(1)}, u32[]{:S(2)}, u32[]{:S(2)}) %collective-permute-start.5) | collective-permute-done | bytes 131104 | tf_op jit(solution)/shard_map/ppermute | solution.py:66
  31.6 0.2 pack_step.1
  31.8 1.9 %collective-permute-start.12 = (f32[320,1024]{1,0:T(8,128)S(1)}, f32[320,1024]{1,0:T(8,128)S(1)}, u32[]{:S(2)}, u32[]{:S(2)}) collective-permute-start(f32[320,1024]{1,0:T(8,128)S(1)} %get-tuple-element.69.refs_0_), channel_id=1, source_target_pairs={{0,8},{4,20},{8,0},{12,28},{16,24},{20,4},{24,16},{28,12},{1,9},{5... | collective-permute-start | bytes 3932168 | tf_op jit(solution)/shard_map/ppermute | solution.py:66
  33.7 0.6 constant_dynamic-slice_fusion.2
  34.3 4.1 %collective-permute-start.6 = (f32[32,256]{1,0:T(8,128)}, f32[32,256]{1,0:T(8,128)}, u32[]{:S(2)}, u32[]{:S(2)}) collective-permute-start(f32[32,256]{1,0:T(8,128)} %get-tuple-element.94), channel_id=1, source_target_pairs={{0,1},{1,2},{2,3},{4,5},{5,6},{6,7},{8,9},{9,10},{10,11},{12,13},{... | collective-permute-start | bytes 98312 | tf_op jit(solution)/shard_map/ppermute | solution.py:461
  38.4 4.5 %collective-permute-start.8 = (f32[32,256]{1,0:T(8,128)}, f32[32,256]{1,0:T(8,128)}, u32[]{:S(2)}, u32[]{:S(2)}) collective-permute-start(f32[32,256]{1,0:T(8,128)} %get-tuple-element.96), channel_id=1, source_target_pairs={{0,2},{1,3},{4,6},{5,7},{8,10},{9,11},{12,14},{13,15},{16,18},{17,... | collective-permute-start | bytes 98312 | tf_op jit(solution)/shard_map/ppermute | solution.py:461
  42.9 1.9 %collective-permute-start.9 = (f32[32,256]{1,0:T(8,128)}, f32[32,256]{1,0:T(8,128)}, u32[]{:S(2)}, u32[]{:S(2)}) collective-permute-start(f32[32,256]{1,0:T(8,128)} %get-tuple-element.95), channel_id=1, source_target_pairs={{0,3},{4,7},{8,11},{12,15},{16,19},{20,23},{24,27},{28,31}} | collective-permute-start | bytes 98312 | tf_op jit(solution)/shard_map/ppermute | solution.py:461
  44.8 6.0 %join.3.tile_ref = f32[256,1024]{1,0:T(8,128)S(1)} custom-call(s32[2]{0:T(128)S(1)} %pad_add_fusion.where_ref, f32[128,1024]{1,0:T(8,128)S(1)} %add.42.mine_ref, f32[128,1024]{1,0:T(8,128)} %collective-permute-done.7.other_ref), custom_call_target="tpu_custom_call" | custom-call | bytes 15000000 | tf_op jit(solution)/shard_map/join/pallas_call | solution.py:23
  50.9 0.8 fusion.6.base_ref
  51.7 0.6 stage.8
  52.3 0.7 collective-permute-start.10
  53.0 0.7 stage.9
  53.7 0.8 collective-permute-start.17
  54.5 0.5 rest.4
  55.0 0.7 collective-permute-start.14
  55.7 0.7 collective-permute-start.13
  56.4 0.6 rest.5
  56.9 1.3 %collective-permute-start.16 = (f32[32,256]{1,0:T(8,128)S(1)}, f32[32,256]{1,0:T(8,128)S(1)}, u32[]{:S(2)}, u32[]{:S(2)}) collective-permute-start(f32[32,256]{1,0:T(8,128)S(1)} %rest.5), channel_id=1, source_target_pairs={{2,0},{6,4},{10,8},{14,12},{18,16},{22,20},{26,24},{30,28}} | collective-permute-start | bytes 98312 | tf_op jit(solution)/shard_map/ppermute | solution.py:379
  58.2 0.6 stage.10
  58.8 1.3 %collective-permute-start.15 = (f32[32,256]{1,0:T(8,128)S(1)}, f32[32,256]{1,0:T(8,128)S(1)}, u32[]{:S(2)}, u32[]{:S(2)}) collective-permute-start(f32[32,256]{1,0:T(8,128)S(1)} %get-tuple-element.73), channel_id=1, source_target_pairs={{1,0},{5,4},{9,8},{13,12},{17,16},{21,20},{25,24},{29,28}} | collective-permute-start | bytes 98312 | tf_op jit(solution)/shard_map/ppermute | solution.py:376
  60.1 4.6 %collective-permute-done.16.far_ref = f32[32,256]{1,0:T(8,128)S(1)} collective-permute-done((f32[32,256]{1,0:T(8,128)S(1)}, f32[32,256]{1,0:T(8,128)S(1)}, u32[]{:S(2)}, u32[]{:S(2)}) %collective-permute-start.16) | collective-permute-done | bytes 32800 | tf_op jit(solution)/shard_map/ppermute | solution.py:379
  64.7 2.6 %collective-permute-done.15.near_ref = f32[32,256]{1,0:T(8,128)S(1)} collective-permute-done((f32[32,256]{1,0:T(8,128)S(1)}, f32[32,256]{1,0:T(8,128)S(1)}, u32[]{:S(2)}, u32[]{:S(2)}) %collective-permute-start.15) | collective-permute-done | bytes 32800 | tf_op jit(solution)/shard_map/ppermute | solution.py:376
  67.3 2.7 %collective-permute-done.17.refs_2_ = f32[288,1024]{1,0:T(8,128)S(1)} collective-permute-done((f32[288,1024]{1,0:T(8,128)S(1)}, f32[288,1024]{1,0:T(8,128)S(1)}, u32[]{:S(2)}, u32[]{:S(2)}) %collective-permute-start.17) | collective-permute-done | bytes 1179680 | tf_op jit(solution)/shard_map/ppermute | solution.py:66
  70.0 1.5 %stage.11 = (f32[32,256]{1,0:T(8,128)S(1)}, f32[32,256]{1,0:T(8,128)}, f32[256,1024]{1,0:T(8,128)S(1)}, f32[32,1024]{1,0:T(8,128)S(1)}) custom-call(s32[2]{0:T(128)S(1)} %pad_add_fusion.where_ref, f32[32,256]{1,0:T(8,128)S(1)} %fusion.6.base_ref, f32[256,1024]{1,0:T(8,128)S(1)} %join.3.tile_ref, f32[32,1024]{1,0:T(8,128)S(1)} %slice_add_fusion.1.add_ref, ...), custom_call_target="tpu_custom_call" | custom-call | bytes 3000000 | tf_op jit(solution)/shard_map/stage/pallas_call | solution.py:23
  71.4 2.7 %collective-permute-done.18.other_ref = f32[256,1024]{1,0:T(8,128)S(1)} collective-permute-done((f32[256,1024]{1,0:T(8,128)S(1)}, f32[256,1024]{1,0:T(8,128)S(1)}, u32[]{:S(2)}, u32[]{:S(2)}) %collective-permute-start.18) | collective-permute-done | bytes 1048608 | tf_op jit(solution)/shard_map/ppermute | solution.py:61
  74.1 0.6 join.4.tile_ref
  74.7 0.9 couple.1
  75.7 2.3 %collective-permute-start.19 = (f32[32,256]{1,0:T(8,128)S(1)}, f32[32,256]{1,0:T(8,128)S(1)}, u32[]{:S(2)}, u32[]{:S(2)}) collective-permute-start(f32[32,256]{1,0:T(8,128)S(1)} %get-tuple-element.91), channel_id=1, source_target_pairs={{0,3},{1,2},{2,1},{3,0},{4,7},{5,6},{6,5},{7,4},{8,11},{9,10},{10,... | collective-permute-start | bytes 98312 | tf_op jit(solution)/shard_map/ppermute | solution.py:481
  78.0 1.3 %collective-permute-start.20 = (f32[32,256]{1,0:T(8,128)S(1)}, f32[32,256]{1,0:T(8,128)S(1)}, u32[]{:S(2)}, u32[]{:S(2)}) collective-permute-start(f32[32,256]{1,0:T(8,128)S(1)} %get-tuple-element.93), channel_id=1, source_target_pairs={{0,2},{1,3},{2,0},{3,1},{4,6},{5,7},{6,4},{7,5},{8,10},{9,11},{10,... | collective-permute-start | bytes 98312 | tf_op jit(solution)/shard_map/ppermute | solution.py:481
  79.3 0.8 collective-permute-start.21
  80.1 0.8 join.5.old_ref
  81.0 5.2 %invert_late.1.tile_ref = f32[256,1024]{1,0:T(8,128)S(1)} custom-call(s32[2]{0:T(128)S(1)} %pad_add_fusion.where_ref, f32[256,1024]{1,0:T(8,128)S(1)} %join.5.old_ref), custom_call_target="tpu_custom_call", output_to_operand_aliasing={{}: (1, {})} | custom-call | bytes 12000000 | tf_op jit(solution)/shard_map/invert_late/pallas_call | solution.py:23
  86.3 0.6 stage.12
  86.9 0.7 collective-permute-start.22
  87.5 0.6 rest.6
  88.1 0.7 collective-permute-start.24
  88.8 0.6 stage.13
  89.3 0.7 collective-permute-start.23
  90.0 0.6 rest.7
  90.6 1.3 %collective-permute-start.26 = (f32[32,256]{1,0:T(8,128)S(1)}, f32[32,256]{1,0:T(8,128)S(1)}, u32[]{:S(2)}, u32[]{:S(2)}) collective-permute-start(f32[32,256]{1,0:T(8,128)S(1)} %rest.7), channel_id=1, source_target_pairs={{2,0},{6,4},{10,8},{14,12},{18,16},{22,20},{26,24},{30,28}} | collective-permute-start | bytes 98312 | tf_op jit(solution)/shard_map/ppermute | solution.py:379
  91.9 0.6 stage.14
  92.5 1.3 %collective-permute-start.25 = (f32[32,256]{1,0:T(8,128)S(1)}, f32[32,256]{1,0:T(8,128)S(1)}, u32[]{:S(2)}, u32[]{:S(2)}) collective-permute-start(f32[32,256]{1,0:T(8,128)S(1)} %get-tuple-element.88), channel_id=1, source_target_pairs={{1,0},{5,4},{9,8},{13,12},{17,16},{21,20},{25,24},{29,28}} | collective-permute-start | bytes 98312 | tf_op jit(solution)/shard_map/ppermute | solution.py:376
  93.8 7.8 %collective-permute-done.26.far_ref = f32[32,256]{1,0:T(8,128)S(1)} collective-permute-done((f32[32,256]{1,0:T(8,128)S(1)}, f32[32,256]{1,0:T(8,128)S(1)}, u32[]{:S(2)}, u32[]{:S(2)}) %collective-permute-start.26) | collective-permute-done | bytes 32800 | tf_op jit(solution)/shard_map/ppermute | solution.py:379
  101.5 2.5 %collective-permute-done.25.near_ref = f32[32,256]{1,0:T(8,128)S(1)} collective-permute-done((f32[32,256]{1,0:T(8,128)S(1)}, f32[32,256]{1,0:T(8,128)S(1)}, u32[]{:S(2)}, u32[]{:S(2)}) %collective-permute-start.25) | collective-permute-done | bytes 32800 | tf_op jit(solution)/shard_map/ppermute | solution.py:376
  104.1 1.4 %stage.15 = (f32[32,256]{1,0:T(8,128)S(1)}, f32[32,256]{1,0:T(8,128)}) custom-call(s32[2]{0:T(128)S(1)} %pad_add_fusion.where_ref, f32[32,256]{1,0:T(8,128)S(1)} %fusion.3.base_ref, f32[256,1024]{1,0:T(8,128)S(1)} %invert_late.1.tile_ref, f32[32,1024]{1,0:T(8,128)S(1)} %broadcast_2_far_ref_add_ref.2.far_ref.add_ref, ...), custom_call_target="tpu_custom_call" | custom-call | bytes 3000000 | tf_op jit(solution)/shard_map/stage/pallas_call | solution.py:23
  105.4 0.6 pad_maximum_fusion
  (31 shorter events, 0.2 us)
Async XLA Ops:
  0.1 0.7 copy-start
  1.4 2.1 %collective-permute-start = (f32[128,1024]{1,0:T(8,128)S(1)}, f32[128,1024]{1,0:T(8,128)S(1)}, u32[]{:S(2)}, u32[]{:S(2)}) collective-permute-start(f32[128,1024]{1,0:T(8,128)S(1)} %get-tuple-element.49), channel_id=1, source_target_pairs={{0,4},{4,0},{8,12},{12,8},{16,20},{20,16},{24,28},{28,24},{1,5},{5... | collective-permute-start | bytes 1572872 | tf_op jit(solution)/shard_map/ppermute | solution.py:61
  3.5 10.1 %collective-permute-start.2 = (f32[128,1024]{1,0:T(8,128)S(1)}, f32[128,1024]{1,0:T(8,128)S(1)}, u32[]{:S(2)}, u32[]{:S(2)}) collective-permute-start(f32[128,1024]{1,0:T(8,128)S(1)} %add.39), channel_id=1, source_target_pairs={{0,8},{4,20},{8,0},{12,28},{16,24},{20,4},{24,16},{28,12},{1,9},{5... | collective-permute-start | bytes 1572872 | tf_op jit(solution)/shard_map/ppermute | solution.py:66
  12.5 3.9 %collective-permute-start.1 = (f32[128,1024]{1,0:T(8,128)S(1)}, f32[128,1024]{1,0:T(8,128)S(1)}, u32[]{:S(2)}, u32[]{:S(2)}) collective-permute-start(f32[128,1024]{1,0:T(8,128)S(1)} %get-tuple-element.52), channel_id=1, source_target_pairs={{0,4},{4,0},{8,12},{12,8},{16,20},{20,16},{24,28},{28,24},{1,5},{5... | collective-permute-start | bytes 1572872 | tf_op jit(solution)/shard_map/ppermute | solution.py:61
  13.7 12.7 %collective-permute-start.4 = (f32[128,1024]{1,0:T(8,128)S(1)}, f32[128,1024]{1,0:T(8,128)S(1)}, u32[]{:S(2)}, u32[]{:S(2)}) collective-permute-start(f32[128,1024]{1,0:T(8,128)S(1)} %add.40), channel_id=1, source_target_pairs={{0,16},{4,12},{8,24},{12,4},{16,0},{20,28},{24,8},{28,20},{1,17},{... | collective-permute-start | bytes 1572872 | tf_op jit(solution)/shard_map/ppermute | solution.py:66
  16.5 10.0 %collective-permute-start.3 = (f32[64,1024]{1,0:T(8,128)S(1)}, f32[64,1024]{1,0:T(8,128)S(1)}, u32[]{:S(2)}, u32[]{:S(2)}) collective-permute-start(f32[64,1024]{1,0:T(8,128)S(1)} %slice.41), channel_id=1, source_target_pairs={{0,8},{4,20},{8,0},{12,28},{16,24},{20,4},{24,16},{28,12},{1,9},{5... | collective-permute-start | bytes 786440 | tf_op jit(solution)/shard_map/ppermute | solution.py:66
  26.5 5.2 %collective-permute-start.11 = (f32[384,1024]{1,0:T(8,128)S(1)}, f32[384,1024]{1,0:T(8,128)S(1)}, u32[]{:S(2)}, u32[]{:S(2)}) collective-permute-start(f32[384,1024]{1,0:T(8,128)S(1)} %get-tuple-element.67), channel_id=1, source_target_pairs={{0,4},{4,0},{8,12},{12,8},{16,20},{20,16},{24,28},{28,24},{1,5},{5... | collective-permute-start | bytes 4718600 | tf_op jit(solution)/shard_map/ppermute | solution.py:61
  26.6 5.0 %collective-permute-start.5 = (f32[32,1024]{1,0:T(8,128)S(1)}, f32[32,1024]{1,0:T(8,128)S(1)}, u32[]{:S(2)}, u32[]{:S(2)}) collective-permute-start(f32[32,1024]{1,0:T(8,128)S(1)} %slice.43), channel_id=1, source_target_pairs={{0,16},{4,12},{8,24},{12,4},{16,0},{20,28},{24,8},{28,20},{1,17},{... | collective-permute-start | bytes 393224 | tf_op jit(solution)/shard_map/ppermute | solution.py:66
  31.8 21.2 %collective-permute-start.12 = (f32[320,1024]{1,0:T(8,128)S(1)}, f32[320,1024]{1,0:T(8,128)S(1)}, u32[]{:S(2)}, u32[]{:S(2)}) collective-permute-start(f32[320,1024]{1,0:T(8,128)S(1)} %get-tuple-element.69.refs_0_), channel_id=1, source_target_pairs={{0,8},{4,20},{8,0},{12,28},{16,24},{20,4},{24,16},{28,12},{1,9},{5... | collective-permute-start | bytes 3932168 | tf_op jit(solution)/shard_map/ppermute | solution.py:66
  33.7 11.1 %collective-permute-start.7 = (f32[128,1024]{1,0:T(8,128)S(1)}, f32[128,1024]{1,0:T(8,128)}, u32[]{:S(2)}, u32[]{:S(2)}) collective-permute-start(f32[128,1024]{1,0:T(8,128)S(1)} %add.42.mine_ref), channel_id=1, source_target_pairs={{0,4},{4,0},{8,12},{12,8},{16,20},{20,16},{24,28},{28,24},{1,5},{5... | collective-permute-start | bytes 1572872 | tf_op jit(solution)/shard_map/ppermute | solution.py:61
  34.3 16.5 %collective-permute-start.6 = (f32[32,256]{1,0:T(8,128)}, f32[32,256]{1,0:T(8,128)}, u32[]{:S(2)}, u32[]{:S(2)}) collective-permute-start(f32[32,256]{1,0:T(8,128)} %get-tuple-element.94), channel_id=1, source_target_pairs={{0,1},{1,2},{2,3},{4,5},{5,6},{6,7},{8,9},{9,10},{10,11},{12,13},{... | collective-permute-start | bytes 98312 | tf_op jit(solution)/shard_map/ppermute | solution.py:461
  38.4 12.4 %collective-permute-start.8 = (f32[32,256]{1,0:T(8,128)}, f32[32,256]{1,0:T(8,128)}, u32[]{:S(2)}, u32[]{:S(2)}) collective-permute-start(f32[32,256]{1,0:T(8,128)} %get-tuple-element.96), channel_id=1, source_target_pairs={{0,2},{1,3},{4,6},{5,7},{8,10},{9,11},{12,14},{13,15},{16,18},{17,... | collective-permute-start | bytes 98312 | tf_op jit(solution)/shard_map/ppermute | solution.py:461
  42.9 8.0 %collective-permute-start.9 = (f32[32,256]{1,0:T(8,128)}, f32[32,256]{1,0:T(8,128)}, u32[]{:S(2)}, u32[]{:S(2)}) collective-permute-start(f32[32,256]{1,0:T(8,128)} %get-tuple-element.95), channel_id=1, source_target_pairs={{0,3},{4,7},{8,11},{12,15},{16,19},{20,23},{24,27},{28,31}} | collective-permute-start | bytes 98312 | tf_op jit(solution)/shard_map/ppermute | solution.py:461
  44.8 6.1 %copy-start.1 = (f32[2,256,32]{1,2,0:T(8,128)S(1)}, f32[2,256,32]{1,2,0:T(8,128)}, u32[]{:S(2)}) copy-start(f32[2,256,32]{1,2,0:T(8,128)} %param.7) | copy-start | bytes 196612
  52.3 0.7 collective-permute-start.10
  53.7 16.3 %collective-permute-start.17 = (f32[288,1024]{1,0:T(8,128)S(1)}, f32[288,1024]{1,0:T(8,128)S(1)}, u32[]{:S(2)}, u32[]{:S(2)}) collective-permute-start(f32[288,1024]{1,0:T(8,128)S(1)} %get-tuple-element.75.refs_0_), channel_id=1, source_target_pairs={{0,16},{4,12},{8,24},{12,4},{16,0},{20,28},{24,8},{28,20},{1,17},{... | collective-permute-start | bytes 3538952 | tf_op jit(solution)/shard_map/ppermute | solution.py:66
  55.0 3.2 %collective-permute-start.14 = (f32[32,512]{1,0:T(8,128)S(1)}, f32[32,512]{1,0:T(8,128)S(1)}, u32[]{:S(2)}, u32[]{:S(2)}) collective-permute-start(f32[32,512]{1,0:T(8,128)S(1)} %rest.4), channel_id=1, source_target_pairs={{3,1},{7,5},{11,9},{15,13},{19,17},{23,21},{27,25},{31,29}} | collective-permute-start | bytes 196616 | tf_op jit(solution)/shard_map/ppermute | solution.py:379
  55.7 2.5 %collective-permute-start.13 = (f32[32,256]{1,0:T(8,128)S(1)}, f32[32,256]{1,0:T(8,128)S(1)}, u32[]{:S(2)}, u32[]{:S(2)}) collective-permute-start(f32[32,256]{1,0:T(8,128)S(1)} %get-tuple-element.71), channel_id=1, source_target_pairs={{2,1},{6,5},{10,9},{14,13},{18,17},{22,21},{26,25},{30,29}} | collective-permute-start | bytes 98312 | tf_op jit(solution)/shard_map/ppermute | solution.py:376
  56.9 7.8 %collective-permute-start.16 = (f32[32,256]{1,0:T(8,128)S(1)}, f32[32,256]{1,0:T(8,128)S(1)}, u32[]{:S(2)}, u32[]{:S(2)}) collective-permute-start(f32[32,256]{1,0:T(8,128)S(1)} %rest.5), channel_id=1, source_target_pairs={{2,0},{6,4},{10,8},{14,12},{18,16},{22,20},{26,24},{30,28}} | collective-permute-start | bytes 98312 | tf_op jit(solution)/shard_map/ppermute | solution.py:379
  58.8 8.5 %collective-permute-start.15 = (f32[32,256]{1,0:T(8,128)S(1)}, f32[32,256]{1,0:T(8,128)S(1)}, u32[]{:S(2)}, u32[]{:S(2)}) collective-permute-start(f32[32,256]{1,0:T(8,128)S(1)} %get-tuple-element.73), channel_id=1, source_target_pairs={{1,0},{5,4},{9,8},{13,12},{17,16},{21,20},{25,24},{29,28}} | collective-permute-start | bytes 98312 | tf_op jit(solution)/shard_map/ppermute | solution.py:376
  71.4 2.7 %collective-permute-start.18 = (f32[256,1024]{1,0:T(8,128)S(1)}, f32[256,1024]{1,0:T(8,128)S(1)}, u32[]{:S(2)}, u32[]{:S(2)}) collective-permute-start(f32[256,1024]{1,0:T(8,128)S(1)} %get-tuple-element.79.mine_ref), channel_id=1, source_target_pairs={{0,4},{4,0},{8,12},{12,8},{16,20},{20,16},{24,28},{28,24},{1,5},{5... | collective-permute-start | bytes 3145736 | tf_op jit(solution)/shard_map/ppermute | solution.py:61
  75.7 10.6 %collective-permute-start.19 = (f32[32,256]{1,0:T(8,128)S(1)}, f32[32,256]{1,0:T(8,128)S(1)}, u32[]{:S(2)}, u32[]{:S(2)}) collective-permute-start(f32[32,256]{1,0:T(8,128)S(1)} %get-tuple-element.91), channel_id=1, source_target_pairs={{0,3},{1,2},{2,1},{3,0},{4,7},{5,6},{6,5},{7,4},{8,11},{9,10},{10,... | collective-permute-start | bytes 98312 | tf_op jit(solution)/shard_map/ppermute | solution.py:481
  78.0 8.3 %collective-permute-start.20 = (f32[32,256]{1,0:T(8,128)S(1)}, f32[32,256]{1,0:T(8,128)S(1)}, u32[]{:S(2)}, u32[]{:S(2)}) collective-permute-start(f32[32,256]{1,0:T(8,128)S(1)} %get-tuple-element.93), channel_id=1, source_target_pairs={{0,2},{1,3},{2,0},{3,1},{4,6},{5,7},{6,4},{7,5},{8,10},{9,11},{10,... | collective-permute-start | bytes 98312 | tf_op jit(solution)/shard_map/ppermute | solution.py:481
  79.3 6.9 %collective-permute-start.21 = (f32[32,256]{1,0:T(8,128)S(1)}, f32[32,256]{1,0:T(8,128)S(1)}, u32[]{:S(2)}, u32[]{:S(2)}) collective-permute-start(f32[32,256]{1,0:T(8,128)S(1)} %get-tuple-element.92), channel_id=1, source_target_pairs={{0,1},{1,0},{2,3},{3,2},{4,5},{5,4},{6,7},{7,6},{8,9},{9,8},{10,11... | collective-permute-start | bytes 98312 | tf_op jit(solution)/shard_map/ppermute | solution.py:481
  86.9 1.9 %collective-permute-start.22 = (f32[32,256]{1,0:T(8,128)S(1)}, f32[32,256]{1,0:T(8,128)S(1)}, u32[]{:S(2)}, u32[]{:S(2)}) collective-permute-start(f32[32,256]{1,0:T(8,128)S(1)} %get-tuple-element.84), channel_id=1, source_target_pairs={{3,2},{7,6},{11,10},{15,14},{19,18},{23,22},{27,26},{31,30}} | collective-permute-start | bytes 98312 | tf_op jit(solution)/shard_map/ppermute | solution.py:376
  88.1 3.8 %collective-permute-start.24 = (f32[32,512]{1,0:T(8,128)S(1)}, f32[32,512]{1,0:T(8,128)S(1)}, u32[]{:S(2)}, u32[]{:S(2)}) collective-permute-start(f32[32,512]{1,0:T(8,128)S(1)} %rest.6), channel_id=1, source_target_pairs={{3,1},{7,5},{11,9},{15,13},{19,17},{23,21},{27,25},{31,29}} | collective-permute-start | bytes 196616 | tf_op jit(solution)/shard_map/ppermute | solution.py:379
  89.3 2.5 %collective-permute-start.23 = (f32[32,256]{1,0:T(8,128)S(1)}, f32[32,256]{1,0:T(8,128)S(1)}, u32[]{:S(2)}, u32[]{:S(2)}) collective-permute-start(f32[32,256]{1,0:T(8,128)S(1)} %get-tuple-element.86), channel_id=1, source_target_pairs={{2,1},{6,5},{10,9},{14,13},{18,17},{22,21},{26,25},{30,29}} | collective-permute-start | bytes 98312 | tf_op jit(solution)/shard_map/ppermute | solution.py:376
  90.6 10.9 %collective-permute-start.26 = (f32[32,256]{1,0:T(8,128)S(1)}, f32[32,256]{1,0:T(8,128)S(1)}, u32[]{:S(2)}, u32[]{:S(2)}) collective-permute-start(f32[32,256]{1,0:T(8,128)S(1)} %rest.7), channel_id=1, source_target_pairs={{2,0},{6,4},{10,8},{14,12},{18,16},{22,20},{26,24},{30,28}} | collective-permute-start | bytes 98312 | tf_op jit(solution)/shard_map/ppermute | solution.py:379
  92.5 11.6 %collective-permute-start.25 = (f32[32,256]{1,0:T(8,128)S(1)}, f32[32,256]{1,0:T(8,128)S(1)}, u32[]{:S(2)}, u32[]{:S(2)}) collective-permute-start(f32[32,256]{1,0:T(8,128)S(1)} %get-tuple-element.88), channel_id=1, source_target_pairs={{1,0},{5,4},{9,8},{13,12},{17,16},{21,20},{25,24},{29,28}} | collective-permute-start | bytes 98312 | tf_op jit(solution)/shard_map/ppermute | solution.py:376

commit v5 on v4

v5 whole, which is shorter than its diff:
```python
import functools

import jax
import jax.numpy as jnp
from jax import lax
from jax.experimental import pallas as pl
from jax.experimental.pallas import tpu as pltpu
from jax.sharding import PartitionSpec as P

F32 = jnp.float32
BF16 = jnp.bfloat16
VMEM = pl.BlockSpec(memory_space=pltpu.MemorySpace.VMEM)
SMEM = pl.BlockSpec(memory_space=pltpu.MemorySpace.SMEM)
HBM = pl.BlockSpec(memory_space=pl.ANY)


def shape(*dims):
    return jax.ShapeDtypeStruct(dims, F32)


def call(body, out, specs, args, name, scratch=(), aliases=None):
    multiple = isinstance(out, tuple)
    return pl.pallas_call(
        body,
        out_shape=out,
        in_specs=list(specs),
        out_specs=tuple(VMEM for _ in out) if multiple else VMEM,
        scratch_shapes=list(scratch),
        input_output_aliases=aliases or {},
        compiler_params=pltpu.CompilerParams(vmem_limit_bytes=40 << 20),
        name=name,
    )(*args)


def split(value):
    high = value.astype(BF16)
    return high, (value - high.astype(F32)).astype(BF16)


def dot_split(a, b, dims):
    (ah, al), (bh, bl) = a, b

    def one(u, v):
        return lax.dot_general(u, v, (dims, ((), ())), preferred_element_type=F32)

    return one(al, bh) + one(ah, bl) + one(ah, bh)


def dot3(a, b):
    return dot_split(split(a), split(b), ((1,), (0,)))


def stage_orders(members):
    bits = members.bit_length() - 1
    first = list(range(1, bits))
    return first, first[::-1]


def swap_core(value, members):
    return lax.ppermute(value, "rt", [(i, i ^ 1) for i in range(members)])


def swap_chip(value, members, stage):
    orders = stage_orders(members)
    return lax.ppermute(value, "rt", [(i, i ^ (1 << orders[i & 1][stage])) for i in range(members)])


def send_tables(members):
    orders = stage_orders(members)
    count = len(orders[0])
    tables = []
    for core in range(2):
        table = []
        for place in range(members):
            other = place >> count
            rest = place & ((1 << count) - 1)
            relative = other
            for stage in range(count):
                if (rest >> (count - 1 - stage)) & 1:
                    relative |= 1 << orders[core ^ other][stage]
            table.append(relative)
        tables.append(table)
    return tables


def front_kernel(
    where_ref, rows_ref, factor_ref, known_ref, keep_one, send_one, keep_ref, send_ref, factor_buf, known_buf, acc_ref, sems, low,
    *, tables
):
    slots, _, band, _ = factor_buf.shape
    me = where_ref[0]

    def live(slot):
        return rows_ref[me * slots + slot] >= 2

    def copies(slot, column):
        copy = pltpu.make_async_copy(factor_ref.at[slot, column], factor_buf.at[slot, column], sems.at[column, slot])
        if column == 0:
            return [copy]
        return [pltpu.make_async_copy(known_ref.at[slot], known_buf.at[slot], sems.at[2, slot]), copy]

    for column in (1, 0):
        for slot in range(slots):

            @pl.when(live(slot))
            def _():
                for copy in copies(slot, column):
                    copy.start()

    finish = put_band(where_ref, rows_ref, factor_ref, 1, 0, keep_ref, send_ref, 0, band // 2, low)
    for column, keep, send, first in ((1, keep_one, send_one, 0), (0, keep_ref, send_ref, band // 2)):
        acc_ref[...] = jnp.zeros_like(acc_ref)
        for slot in range(slots):

            @pl.when(live(slot))
            def _():
                for copy in copies(slot, column):
                    copy.wait()
                acc_ref[...] += dot_split(split(known_buf[slot]), split(factor_buf[slot, column]), ((0,), (0,)))

        in_send_order(where_ref, acc_ref, keep, send, first, tables)
    finish()


def in_send_order(where_ref, acc_ref, keep_ref, send_ref, first, tables):
    count = len(tables[0])
    columns = acc_ref.shape[0] // count
    me = where_ref[0]
    for spot, (even, odd) in enumerate(zip(*tables)):
        group = me ^ jnp.where((me & 1) == 0, even, odd)
        rows = acc_ref[pl.ds(pl.multiple_of(group * columns, columns), columns), :]
        target, start = (keep_ref, spot) if spot < count // 2 else (send_ref, spot - count // 2)
        target[first + start * columns : first + (start + 1) * columns, :] = rows


def owned_slot(where_ref, rows_ref, row, slots):
    slot = jnp.int32(-1)
    for s in range(slots):
        slot = jnp.where(rows_ref[where_ref[0] * slots + s] == row, s, slot)
    return slot


def band_copies(where_ref, factor_ref, slot, column, keep_ref, send_ref, first, half, sems):
    core = where_ref[0] & 1
    copies = []
    for index, (target, which) in enumerate(((send_ref, 1 - core), (keep_ref, core))):
        start = pl.multiple_of(which * half, half)
        source = factor_ref.at[slot, column, pl.ds(start, half), :]
        copies.append(pltpu.make_async_copy(source, target.at[pl.ds(first, half), :], sems.at[index]))
    return copies


def put_band(where_ref, rows_ref, factor_ref, row, column, keep_ref, send_ref, first, half, sems):
    slot = owned_slot(where_ref, rows_ref, row, factor_ref.shape[0])

    @pl.when(slot >= 0)
    def _():
        for copy in band_copies(where_ref, factor_ref, slot, column, keep_ref, send_ref, first, half, sems):
            copy.start()

    @pl.when(slot < 0)
    def _():
        keep_ref[first : first + half, :] = jnp.zeros((half, keep_ref.shape[1]), F32)
        send_ref[first : first + half, :] = jnp.zeros((half, keep_ref.shape[1]), F32)

    def finish():
        @pl.when(slot >= 0)
        def _():
            for copy in band_copies(where_ref, factor_ref, slot, column, keep_ref, send_ref, first, half, sems):
                copy.wait()

    return finish


def first_band(where, slot_row, factor_rows):
    _, _, band, width = factor_rows.shape
    half = band // 2

    def body(where_ref, rows_ref, factor_ref, keep_ref, send_ref, sems):
        put_band(where_ref, rows_ref, factor_ref, 1, 1, keep_ref, send_ref, 0, half, sems)()

    out = (shape(half, width), shape(half, width))
    scratch = [pltpu.SemaphoreType.DMA((2,))]
    return call(body, out, (SMEM, SMEM, HBM), (where, slot_row, factor_rows), "first_band", scratch)


def front(where, slot_row, factor_rows, known, members):
    slots, _, band, width = factor_rows.shape
    total = known.shape[2]
    one, rest = shape(total // 2, width), shape(band // 2 + total // 2, width)
    scratch = [
        pltpu.VMEM(factor_rows.shape, F32),
        pltpu.VMEM(known.shape, F32),
        pltpu.VMEM((total, width), F32),
        pltpu.SemaphoreType.DMA((3, slots)),
        pltpu.SemaphoreType.DMA((2,)),
    ]
    body = functools.partial(front_kernel, tables=send_tables(members))
    args = (where, slot_row, factor_rows, known)
    return call(body, (one, one, rest, rest), (SMEM, SMEM, HBM, HBM), args, "front", scratch)


def top_band(where, slot_row, factor_rows):
    slots, _, band, width = factor_rows.shape
    half = band // 2

    def body(where_ref, rows_ref, factor_ref, keep_ref, send_ref, tile_ref, sem):
        slot = owned_slot(where_ref, rows_ref, 0, slots)
        core = where_ref[0] & 1

        @pl.when(slot >= 0)
        def _():
            copy = pltpu.make_async_copy(factor_ref.at[slot, 0], tile_ref, sem)
            copy.start()
            copy.wait()
            invert_diagonal(tile_ref, where_ref[1], range(width // band), band)
            keep_ref[...] = tile_ref[pl.ds(pl.multiple_of(core * half, half), half), :]
            send_ref[...] = tile_ref[pl.ds(pl.multiple_of((1 - core) * half, half), half), :]

        @pl.when(slot < 0)
        def _():
            keep_ref[...] = jnp.zeros_like(keep_ref)
            send_ref[...] = jnp.zeros_like(send_ref)

    out = (shape(half, width), shape(half, width))
    scratch = [pltpu.VMEM((band, width), F32), pltpu.SemaphoreType.DMA(())]
    return call(body, out, (SMEM, SMEM, HBM), (where, slot_row, factor_rows), "top_band", scratch)


def after(value, *others):
    return lax.optimization_barrier((value,) + others)[0]


def pack_parts(sums, skip, got, tile_rows, final):
    width = got.shape[1]
    count = got.shape[0] - tile_rows
    go = count if final else count // 2

    def add(tiles_ref, sums_ref, got_ref, out_ref, keep_ref):
        out_ref[:tile_rows, :] = tiles_ref[:tile_rows, :] + got_ref[:tile_rows, :]
        keep_ref[...] = sums_ref[skip : skip + go, :] + got_ref[tile_rows : tile_rows + go, :]
        if not final:
            out_ref[tile_rows:, :] = sums_ref[skip + go : skip + count, :] + got_ref[tile_rows + go :, :]

    def add_tile(tiles_ref, got_ref, out_ref):
        out_ref[...] = tiles_ref[...] + got_ref[...]

    if sums is None:
        return add_tile, (shape(tile_rows, width),)
    return add, (shape(tile_rows + count - go, width), shape(go, width))


def pack_inputs(tiles, sums, skip, got, tile_rows, final):
    return (tiles, got) if sums is None else (tiles, sums, got)


def pack_step(*pack):
    add, out = pack_parts(*pack[1:])
    args = pack_inputs(*pack)
    return call(add, out, (VMEM,) * len(args), args, "pack_step")


def inverse_of(block):
    size = block.shape[0]
    base = min(size, 64)
    row = lax.broadcasted_iota(jnp.int32, (base, base), 0)
    col = lax.broadcasted_iota(jnp.int32, (base, base), 1)
    pair = (row - col == 1) & (row & 1 == 1)
    starts = range(0, size, base)
    blocks = [block[at : at + base, at : at + base] for at in starts]
    inverses = []
    for part in blocks:
        diag = jnp.where(row == col, part, 0.0)
        recip_row = 1.0 / jnp.sum(diag, axis=0, keepdims=True)
        recip_col = 1.0 / jnp.sum(diag, axis=1, keepdims=True)
        off = -(part * recip_row) * recip_col
        inverses.append(jnp.where(row == col, recip_row, jnp.where(pair, off, 0.0)))
    step = 2
    while step < base:
        half = lax.div(row, step)
        below = (half - lax.div(col, step) == 1) & (half & 1 == 1)
        parts = [split(inverse) for inverse in inverses]
        middle = [dot_split(split(jnp.where(below, b, 0.0)), p, ((1,), (0,))) for b, p in zip(blocks, parts)]
        inverses = [i - dot_split(p, split(m), ((1,), (0,))) for i, p, m in zip(inverses, parts, middle)]
        step *= 2
    width = base
    while len(inverses) > 1:
        merged = []
        for index in range(0, len(inverses), 2):
            first, second = inverses[index : index + 2]
            lower = block[(index + 1) * width : (index + 2) * width, index * width : (index + 1) * width]
            corner = -dot3(second, dot3(lower, first))
            top = jnp.concatenate([first, jnp.zeros_like(first)], 1)
            merged.append(jnp.concatenate([top, jnp.concatenate([corner, second], 1)], 0))
        inverses = merged
        width *= 2
    return inverses[0]


def invert_diagonal(tile_ref, place, chosen, band):
    for spot in chosen:

        @pl.when(place == spot)
        def _():
            here = slice(spot * band, (spot + 1) * band)
            tile_ref[:, here] = inverse_of(tile_ref[:, here])


def join_halves(where, mine, other, first, half, chosen):
    width = mine.shape[1]

    def body(where_ref, mine_ref, other_ref, tile_ref):
        core = where_ref[0] & 1
        tile_ref[pl.ds(pl.multiple_of(core * half, half), half), :] = mine_ref[first : first + half, :]
        tile_ref[pl.ds(pl.multiple_of((1 - core) * half, half), half), :] = other_ref[first : first + half, :]
        invert_diagonal(tile_ref, where_ref[1], chosen, 2 * half)

    return call(body, shape(2 * half, width), (SMEM, VMEM, VMEM), (where, mine, other), "join")


def run_stage(where, base, tile, add, near, far, held, stage, packs=()):
    columns, band = base.shape
    left = stage * band
    last = max(left - band, 0)
    inputs = [pack_inputs(*pack) for pack in packs]
    more = [pack_parts(*pack[1:]) for pack in packs]
    count = sum(len(args) for args in inputs)

    def body(where_ref, base_ref, tile_ref, add_ref, near_ref, far_ref, held_ref, *refs):
        ins, (solved_ref, update_ref), outs = refs[:count], refs[count : count + 2], refs[count + 2 :]

        @pl.when(where_ref[1] == stage)
        def _():
            right = base_ref[...] - near_ref[...] - far_ref[:, left : left + band]
            solved = dot3(right, tile_ref[:, left : left + band])
            solved_ref[...] = solved
            if stage > 0:
                here = slice(last, left)
                update_ref[...] = far_ref[:, here] + add_ref[:, here] + dot3(solved, tile_ref[:, here])

        @pl.when(where_ref[1] != stage)
        def _():
            solved_ref[...] = held_ref[...]

        for args, (add_pack, out) in zip(inputs, more):
            add_pack(*ins[: len(args)], *outs[: len(out)])
            ins, outs = ins[len(args) :], outs[len(out) :]

    out = (shape(columns, band), shape(columns, band)) + sum((out for _, out in more), ())
    args = (where, base, tile, add, near, far, held) + sum(inputs, ())
    return call(body, out, (SMEM,) + (VMEM,) * (len(args) - 1), args, "stage")


def run_rest(where, tile, add, far, solved, stage):
    columns, band = solved.shape
    last = (stage - 1) * band

    def body(where_ref, tile_ref, add_ref, far_ref, solved_ref, rest_ref):
        @pl.when(where_ref[1] == stage)
        def _():
            rest_ref[...] = far_ref[:, :last] + add_ref[:, :last] + dot3(solved_ref[...], tile_ref[:, :last])

    return call(body, shape(columns, last), (SMEM,) + (VMEM,) * 4, (where, tile, add, far, solved), "rest")


def run_stage_plain(where, base, tile, add, near, far, held, stage, packs=()):
    high = lax.Precision.HIGHEST
    band = base.shape[1]
    left = stage * band
    here = slice(max(left - band, 0), max(left, band))
    solved = jnp.dot(base - near - far[:, left : left + band], tile[:, left : left + band], precision=high)
    update = jnp.dot(solved, tile[:, here], precision=high) + add[:, here] + far[:, here]
    more = sum((tuple(pack_step(*pack)) for pack in packs), ())
    return (jnp.where(where[1] == stage, solved, held), update) + more


def run_rest_plain(where, tile, add, far, solved, stage):
    last = (stage - 1) * solved.shape[1]
    return far[:, :last] + add[:, :last] + jnp.dot(solved, tile[:, :last], precision=lax.Precision.HIGHEST)


def sweep(where, base, tile, add, bands, packs=None):
    columns, band = base.shape
    aligned = band % 128 == 0
    stage_of, rest_of = (run_stage, run_rest) if aligned else (run_stage_plain, run_rest_plain)
    near = jnp.zeros((columns, band), F32)
    held = jnp.zeros((columns, band), F32)
    fars = [jnp.zeros((columns, bands * band), F32)] * 2
    for stage in range(bands - 1, -1, -1):
        far = fars.pop(0)
        taken = packs.take(bands - 1 - stage) if packs else ()
        held, update, *more = stage_of(where, base, tile, add, near, far, held, stage, taken)
        if stage > 0:
            near = lax.ppermute(update, "ct", [(stage, stage - 1)])
        if stage > 1:
            rest = rest_of(where, tile, add, far, held, stage)
            fars.append(lax.ppermute(rest, "ct", [(stage, stage - 2)]))
        if more:
            packs.put(*more)
    return held


class Packs:
    def __init__(self, pack, got, top, steps, bands, members):
        self.pack, self.got, self.top, self.got_top = pack, got, top, None
        self.steps, self.members = steps, members
        self.low_at = [bands - 2 - 2 * (steps - 1 - step) for step in range(steps)]
        self.top_at = [bands - steps + step for step in range(steps)]

    def take(self, index):
        taken = ()
        if index in self.low_at:
            tiles, sums, rows = self.pack
            taken += ((tiles, sums, 0, self.got, rows, index == self.low_at[-1]),)
        if index in self.top_at:
            taken += ((self.top, None, 0, self.got_top, self.top.shape[0], True),)
        self.index = index
        return taken

    def put(self, *outs):
        if self.index in self.low_at:
            tiles, sums, *outs = outs
            self.pack = (tiles, sums, self.pack[2])
            step = self.low_at.index(self.index) + 1
            if step < self.steps:
                self.got = swap_chip(tiles, self.members, step)
            else:
                self.got = swap_core(tiles, self.members)
            if step == 1:
                self.got_top = swap_chip(after(self.top, tiles), self.members, 0)
        if self.index in self.top_at:
            (self.top,) = outs
            step = self.top_at.index(self.index) + 1
            if step < self.steps:
                self.got_top = swap_chip(self.top, self.members, step)
            else:
                self.got_top = swap_core(self.top, self.members)


def couple(where, sums, solved, mine, other, bands):
    columns, band = solved.shape
    half, width = mine.shape

    def body(where_ref, sums_ref, solved_ref, mine_ref, other_ref, out_ref, tile_ref, whole_ref):
        core = where_ref[0] & 1
        tile_ref[pl.ds(pl.multiple_of(core * half, half), half), :] = mine_ref[...]
        tile_ref[pl.ds(pl.multiple_of((1 - core) * half, half), half), :] = other_ref[...]
        whole_ref[...] = sums_ref[...] + dot3(solved_ref[...], tile_ref[...])
        for mask in range(bands):
            start = pl.multiple_of((where_ref[1] ^ mask) * band, band)
            out_ref[mask] = whole_ref[:, pl.ds(start, band)]

    scratch = [pltpu.VMEM((band, width), F32), pltpu.VMEM((columns, width), F32)]
    args = (where, sums, solved, mine, other)
    return call(body, shape(bands, columns, band), (SMEM,) + (VMEM,) * 4, args, "couple", scratch)


def couple_plain(where, sums, solved, mine, other, bands):
    band = solved.shape[1]
    tile = join_halves(where, mine, other, 0, band // 2, ())
    whole = sums + jnp.dot(solved, tile, precision=lax.Precision.HIGHEST)
    return jnp.stack([own_band(whole, where[1] ^ mask, band) for mask in range(bands)])


def own_band(value, spot, band):
    return lax.dynamic_slice(value, (0, spot * band), (value.shape[0], band))


def shards(factor_rows, slot_row, known, rhs, *, members, bands):
    slots, _, band, width = factor_rows.shape
    half = band // 2
    columns = rhs.shape[2]
    stages = len(stage_orders(members)[0])
    aligned = band % 128 == 0
    place = lax.axis_index("ct")
    where = jnp.stack([lax.axis_index("rt"), place]).astype(jnp.int32)
    factor_rows = pltpu.with_memory_space_constraint(factor_rows, pltpu.HBM)
    known = pltpu.with_memory_space_constraint(known, pltpu.HBM)

    keep, send = first_band(where, slot_row, factor_rows)
    tile_one = keep + swap_core(send, members)
    got_tile = swap_chip(tile_one, members, 0)
    keep_one, send_one, keep, send = front(after(where, tile_one), slot_row, factor_rows, known, members)
    got_sum = swap_core(send_one, members)
    tile_one = tile_one + after(got_tile, keep_one)
    got_tile = swap_chip(tile_one, members, 1)
    sum_one = keep_one + after(got_sum, tile_one)
    got_pack = got_top = top = None
    for stage in range(stages):
        rows = sum_one.shape[0] // 2
        got_sum = swap_chip(sum_one[rows:], members, stage)
        if stage == 0:
            got_pack = swap_core(after(send, sum_one), members)
            top, send_top = top_band(after(where, sum_one), slot_row, factor_rows)
            got_sum = after(got_sum, top)
        sum_one = sum_one[:rows] + got_sum
        if stage == 0:
            got_top = swap_core(after(send_top, sum_one), members)
        if stage < stages - 1:
            tile_one = tile_one + after(got_tile, sum_one)
            got_tile = swap_chip(tile_one, members, stage + 2) if stage < stages - 2 else None

    got_up = []
    for shift in range(1, bands):
        piece = own_band(sum_one, jnp.minimum(place + shift, bands - 1), band)
        got_up.append(lax.ppermute(piece, "ct", [(i, i + shift) for i in range(bands - shift)]))

    other = swap_core(tile_one, members)

    tiles, sums = pack_step(keep, keep, half, after(got_pack, sum_one), half, False)
    got_pack = swap_chip(tiles, members, 0)
    top = top + after(got_top, sum_one)

    tile_one = join_halves(after(where, sum_one, top), tile_one, other, 0, half, range(bands))
    base = rhs[1].T - own_band(sum_one, place, band)
    for piece in got_up:
        base = base - after(piece, tile_one)

    packs = Packs((tiles, sums, half), got_pack, top, stages, bands, members)
    solved_one = sweep(where, base, tile_one, sum_one, bands, packs)

    low, sums, _ = packs.pack
    pieces = (couple if aligned else couple_plain)(where, sums, solved_one, low, packs.got, bands)
    base = rhs[0].T - pieces[0]
    tile_zero = join_halves(where, packs.top, packs.got_top, 0, half, ())
    for mask in range(bands - 1, 0, -1):
        got = lax.ppermute(pieces[mask], "ct", [(i, i ^ mask) for i in range(bands)])
        base = base - after(got, tile_zero)

    nothing = jnp.zeros((columns, width), F32)
    solved_zero = sweep(where, base, tile_zero, nothing, bands)
    return jnp.stack([solved_zero.T, solved_one.T])


def solution(mesh):
    members, bands = mesh.shape["rt"], mesh.shape["ct"]
    in_specs = (P("rt", None, "ct", None), P(), P("rt", "ct", None), P(None, "ct", "rt"))
    out_specs = P(None, "ct", "rt")
    body = functools.partial(shards, members=members, bands=bands)
    return jax.shard_map(body, mesh=mesh, in_specs=in_specs, out_specs=out_specs, check_vma=False)
```

time: 106 us -> 104 us (0.981)
  Pallas kernels: 35.4 us -> 22.9 us
  waiting for transfers between devices: 29.8 us -> 38.4 us
  other arithmetic: 1.85 us -> 3.03 us
    pallas_call x21 -> x19, Pallas kernels: 35.4 us -> 22.9 us  [call(): pl.pallas_call(body, out_shape=out, in_specs=list(specs), out_specs=tuple...]
    ppermute x6 -> x8, waiting for transfers between devices: 8.12 us -> 20.3 us  [swap_chip(): lax.ppermute(value, 'rt', [(i, i ^ 1 << orders[i & 1][stage]) for i in ra...]
    ppermute x4, waiting for transfers between devices: 12.3 us -> 10.2 us  [sweep(): fars.append(lax.ppermute(rest, 'ct', [(stage, stage - 2)]))]
    ppermute x6, waiting for transfers between devices: 5.16 us -> 3.19 us  [sweep(): near = lax.ppermute(update, 'ct', [(stage, stage - 1)])]
    ppermute x5 -> x7, starting transfers between devices: 0.66 us -> 2.32 us  [swap_core(): return lax.ppermute(value, 'rt', [(i, i ^ 1) for i in range(members)])]
    ppermute x3, waiting for transfers between devices: 0.01 us -> 1.64 us  [shards(): lax.ppermute(pieces[mask], 'ct', [(i, i ^ mask) for i in range(bands)])]
    ppermute x5 -> x7, waiting for transfers between devices: 4.2 us -> 3.02 us  [swap_core(): return lax.ppermute(value, 'rt', [(i, i ^ 1) for i in range(members)])]
    add x5 -> x6, other arithmetic: 0.26 us -> 1.41 us  [the longest x1 1.17 us: shards(): top = top + after(got_top, sum_one)]
  transfers between devices with their start and end apart: 27 -> 31, of which waited for: 10 -> 13; matrix products, arithmetic and copies ran while one was open for 2% -> 3% of each run, Pallas kernels for 27% -> 18%
where the time goes in v5:
time: 104 us
  waiting for transfers between devices  38.4 us (37%)
  starting transfers between devices  37.8 us (36%)
  Pallas kernels  22.9 us (22%)
  other arithmetic  3.03 us (3%)
  local copies, waits for them, and re-layouts  1.35 us (1%)
    pallas_call x19, Pallas kernels, call(): pl.pallas_call(body, out_shape=out, in_specs=list(specs), out_specs=tuple...  22.9 us
    ppermute x8, waiting for transfers between devices, swap_chip(): lax.ppermute(value, 'rt', [(i, i ^ 1 << orders[i & 1][stage]) for i in ra...  20.3 us
    ppermute x8, starting transfers between devices, swap_chip(): lax.ppermute(value, 'rt', [(i, i ^ 1 << orders[i & 1][stage]) for i in ra...  11.4 us
    ppermute x3, starting transfers between devices, shards(): lax.ppermute(piece, 'ct', [(i, i + shift) for i in range(bands - shift)])  10.5 us
    ppermute x4, waiting for transfers between devices, sweep(): fars.append(lax.ppermute(rest, 'ct', [(stage, stage - 2)]))  10.2 us
    ppermute x6, starting transfers between devices, sweep(): near = lax.ppermute(update, 'ct', [(stage, stage - 1)])  5.22 us
    ppermute x3, starting transfers between devices, shards(): lax.ppermute(pieces[mask], 'ct', [(i, i ^ mask) for i in range(bands)])  4.45 us
    ppermute x4, starting transfers between devices, sweep(): fars.append(lax.ppermute(rest, 'ct', [(stage, stage - 2)]))  3.91 us
  transfers between devices with their start and end apart: 31, of which 13 were waited for; matrix products, arithmetic and copies ran while one was open for 3% of the time, Pallas kernels for 18%

profile of v5, /device:TPU:0, one launch (start us, length us, event | category | flops | bytes accessed | tf_op | source)
XLA Modules:
  0.0 103.8 jit_solution(4630533679697940171)
XLA Ops:
  0.1 0.7 copy-done
  0.7 0.6 first_band.1
  1.4 0.5 collective-permute-start
  1.9 1.5 %collective-permute-done = f32[128,1024]{1,0:T(8,128)S(1)} collective-permute-done((f32[128,1024]{1,0:T(8,128)S(1)}, f32[128,1024]{1,0:T(8,128)S(1)}, u32[]{:S(2)}, u32[]{:S(2)}) %collective-permute-start) | collective-permute-done | bytes 524320 | tf_op jit(solution)/shard_map/ppermute | solution.py:60
  3.5 2.9 %collective-permute-start.2 = (f32[128,1024]{1,0:T(8,128)S(1)}, f32[128,1024]{1,0:T(8,128)S(1)}, u32[]{:S(2)}, u32[]{:S(2)}) collective-permute-start(f32[128,1024]{1,0:T(8,128)S(1)} %add.42), channel_id=1, source_target_pairs={{0,8},{4,20},{8,0},{12,28},{16,24},{20,4},{24,16},{28,12},{1,9},{5... | collective-permute-start | bytes 1572872 | tf_op jit(solution)/shard_map/ppermute | solution.py:65
  6.4 7.2 %front.1 = (f32[128,1024]{1,0:T(8,128)S(1)}, f32[128,1024]{1,0:T(8,128)S(1)}, f32[256,1024]{1,0:T(8,128)S(1)}, f32[256,1024]{1,0:T(8,128)S(1)}) custom-call(s32[2]{0:T(128)S(1)} %pad_add_fusion.where_ref, s32[48]{0:T(128)S(1)} %copy-done, f32[6,2,256,1024]{3,2,1,0:T(8,128)} %factor_ref.5, f32[6,256,256]{2,1,0:T(8,128)} %known_ref.1), custom_call_target="tpu_custom_call" | custom-call | tf_op jit(solution)/shard_map/front/pallas_call | solution.py:23
  13.6 0.8 collective-permute-start.1
  14.5 1.5 %collective-permute-done.1 = f32[128,1024]{1,0:T(8,128)S(1)} collective-permute-done((f32[128,1024]{1,0:T(8,128)S(1)}, f32[128,1024]{1,0:T(8,128)S(1)}, u32[]{:S(2)}, u32[]{:S(2)}) %collective-permute-start.1) | collective-permute-done | bytes 524320 | tf_op jit(solution)/shard_map/ppermute | solution.py:60
  16.0 0.4 collective-permute-start.11
  16.5 3.2 %collective-permute-start.3 = (f32[64,1024]{1,0:T(8,128)S(1)}, f32[64,1024]{1,0:T(8,128)S(1)}, u32[]{:S(2)}, u32[]{:S(2)}) collective-permute-start(f32[64,1024]{1,0:T(8,128)S(1)} %slice.41), channel_id=1, source_target_pairs={{0,8},{4,20},{8,0},{12,28},{16,24},{20,4},{24,16},{28,12},{1,9},{5... | collective-permute-start | bytes 786440 | tf_op jit(solution)/shard_map/ppermute | solution.py:65
  19.7 1.7 %top_band.1 = (f32[128,1024]{1,0:T(8,128)S(1)}, f32[128,1024]{1,0:T(8,128)}) custom-call(s32[2]{0:T(128)S(1)} %pad_add_fusion.where_ref, s32[48]{0:T(128)S(1)} %copy-done, f32[6,2,256,1024]{3,2,1,0:T(8,128)} %factor_ref.5), custom_call_target="tpu_custom_call" | custom-call | tf_op jit(solution)/shard_map/top_band/pallas_call | solution.py:23
  21.3 5.3 %collective-permute-done.3 = f32[64,1024]{1,0:T(8,128)S(1)} collective-permute-done((f32[64,1024]{1,0:T(8,128)S(1)}, f32[64,1024]{1,0:T(8,128)S(1)}, u32[]{:S(2)}, u32[]{:S(2)}) %collective-permute-start.3) | collective-permute-done | bytes 262176 | tf_op jit(solution)/shard_map/ppermute | solution.py:65
  26.7 1.2 %collective-permute-start.4 = (f32[32,1024]{1,0:T(8,128)S(1)}, f32[32,1024]{1,0:T(8,128)S(1)}, u32[]{:S(2)}, u32[]{:S(2)}) collective-permute-start(f32[32,1024]{1,0:T(8,128)S(1)} %slice.43), channel_id=1, source_target_pairs={{0,16},{4,12},{8,24},{12,4},{16,0},{20,28},{24,8},{28,20},{1,17},{... | collective-permute-start | bytes 393224 | tf_op jit(solution)/shard_map/ppermute | solution.py:65
  27.9 3.8 %collective-permute-done.4 = f32[32,1024]{1,0:T(8,128)S(1)} collective-permute-done((f32[32,1024]{1,0:T(8,128)S(1)}, f32[32,1024]{1,0:T(8,128)S(1)}, u32[]{:S(2)}, u32[]{:S(2)}) %collective-permute-start.4) | collective-permute-done | bytes 131104 | tf_op jit(solution)/shard_map/ppermute | solution.py:65
  31.7 0.2 pack_step.1
  31.9 2.2 %collective-permute-start.12 = (f32[192,1024]{1,0:T(8,128)S(1)}, f32[192,1024]{1,0:T(8,128)S(1)}, u32[]{:S(2)}, u32[]{:S(2)}) collective-permute-start(f32[192,1024]{1,0:T(8,128)S(1)} %get-tuple-element.75.refs_0_), channel_id=1, source_target_pairs={{0,8},{4,20},{8,0},{12,28},{16,24},{20,4},{24,16},{28,12},{1,9},{5... | collective-permute-start | bytes 2359304 | tf_op jit(solution)/shard_map/ppermute | solution.py:65
  34.1 0.1 add.51.mine_ref
  34.2 0.6 collective-permute-start.8
  34.8 0.6 constant_dynamic-slice_fusion.2
  35.4 4.1 %collective-permute-start.5 = (f32[32,256]{1,0:T(8,128)}, f32[32,256]{1,0:T(8,128)}, u32[]{:S(2)}, u32[]{:S(2)}) collective-permute-start(f32[32,256]{1,0:T(8,128)} %get-tuple-element.104), channel_id=1, source_target_pairs={{0,1},{1,2},{2,3},{4,5},{5,6},{6,7},{8,9},{9,10},{10,11},{12,13},{... | collective-permute-start | bytes 98312 | tf_op jit(solution)/shard_map/ppermute | solution.py:506
  39.5 4.5 %collective-permute-start.9 = (f32[32,256]{1,0:T(8,128)}, f32[32,256]{1,0:T(8,128)}, u32[]{:S(2)}, u32[]{:S(2)}) collective-permute-start(f32[32,256]{1,0:T(8,128)} %get-tuple-element.106), channel_id=1, source_target_pairs={{0,2},{1,3},{4,6},{5,7},{8,10},{9,11},{12,14},{13,15},{16,18},{17,... | collective-permute-start | bytes 98312 | tf_op jit(solution)/shard_map/ppermute | solution.py:506
  44.0 1.9 %collective-permute-start.10 = (f32[32,256]{1,0:T(8,128)}, f32[32,256]{1,0:T(8,128)}, u32[]{:S(2)}, u32[]{:S(2)}) collective-permute-start(f32[32,256]{1,0:T(8,128)} %get-tuple-element.105), channel_id=1, source_target_pairs={{0,3},{4,7},{8,11},{12,15},{16,19},{20,23},{24,27},{28,31}} | collective-permute-start | bytes 98312 | tf_op jit(solution)/shard_map/ppermute | solution.py:506
  45.9 1.2 %add.50.refs_3_ = f32[128,1024]{1,0:T(8,128)S(1)} add(f32[128,1024]{1,0:T(8,128)S(1)} %get-tuple-element.61, f32[128,1024]{1,0:T(8,128)} %collective-permute-done.6) | non-fusion elementwise | flops 131072 | bytes 1572864 | tf_op jit(solution)/shard_map/add | solution.py:512
  47.1 3.0 %join.2.tile_ref = f32[256,1024]{1,0:T(8,128)S(1)} custom-call(s32[2]{0:T(128)S(1)} %pad_add_fusion.where_ref, f32[128,1024]{1,0:T(8,128)S(1)} %add.51.mine_ref, f32[128,1024]{1,0:T(8,128)S(1)} %collective-permute-done.8.other_ref), custom_call_target="tpu_custom_call" | custom-call | tf_op jit(solution)/shard_map/join/pallas_call | solution.py:23
  50.1 0.8 fusion.6.base_ref
  51.0 0.6 stage.8
  51.7 1.0 collective-permute-start.17
  52.7 0.7 collective-permute-start.13
  53.4 0.6 rest.4
  53.9 0.7 collective-permute-start.15
  54.6 0.6 stage.9
  55.2 0.7 collective-permute-start.14
  55.9 10.5 %collective-permute-done.17.refs_4_ = f32[128,1024]{1,0:T(8,128)S(1)} collective-permute-done((f32[128,1024]{1,0:T(8,128)S(1)}, f32[128,1024]{1,0:T(8,128)S(1)}, u32[]{:S(2)}, u32[]{:S(2)}) %collective-permute-start.17) | collective-permute-done | bytes 524320 | tf_op jit(solution)/shard_map/ppermute | solution.py:65
  66.4 0.1 collective-permute-done.16.refs_2_
  66.5 0.7 stage.10
  67.1 0.7 collective-permute-start.20
  67.9 0.5 rest.5
  68.4 1.3 %collective-permute-start.19 = (f32[32,256]{1,0:T(8,128)S(1)}, f32[32,256]{1,0:T(8,128)S(1)}, u32[]{:S(2)}, u32[]{:S(2)}) collective-permute-start(f32[32,256]{1,0:T(8,128)S(1)} %rest.5), channel_id=1, source_target_pairs={{2,0},{6,4},{10,8},{14,12},{18,16},{22,20},{26,24},{30,28}} | collective-permute-start | bytes 98312 | tf_op jit(solution)/shard_map/ppermute | solution.py:397
  69.7 1.3 %collective-permute-start.18 = (f32[32,256]{1,0:T(8,128)S(1)}, f32[32,256]{1,0:T(8,128)S(1)}, u32[]{:S(2)}, u32[]{:S(2)}) collective-permute-start(f32[32,256]{1,0:T(8,128)S(1)} %get-tuple-element.85), channel_id=1, source_target_pairs={{1,0},{5,4},{9,8},{13,12},{17,16},{21,20},{25,24},{29,28}} | collective-permute-start | bytes 98312 | tf_op jit(solution)/shard_map/ppermute | solution.py:394
  71.0 4.2 %collective-permute-done.19.far_ref = f32[32,256]{1,0:T(8,128)S(1)} collective-permute-done((f32[32,256]{1,0:T(8,128)S(1)}, f32[32,256]{1,0:T(8,128)S(1)}, u32[]{:S(2)}, u32[]{:S(2)}) %collective-permute-start.19) | collective-permute-done | bytes 32800 | tf_op jit(solution)/shard_map/ppermute | solution.py:397
  75.3 0.5 collective-permute-done.18.near_ref
  75.8 0.6 collective-permute-done.20.refs_1_
  76.4 1.4 %stage.11 = (f32[32,256]{1,0:T(8,128)S(1)}, f32[32,256]{1,0:T(8,128)}, f32[128,1024]{1,0:T(8,128)S(1)}) custom-call(s32[2]{0:T(128)S(1)} %pad_add_fusion.where_ref, f32[32,256]{1,0:T(8,128)S(1)} %fusion.6.base_ref, f32[256,1024]{1,0:T(8,128)S(1)} %join.2.tile_ref, f32[32,1024]{1,0:T(8,128)S(1)} %slice_add_fusion.1.add_ref, ...), custom_call_target="tpu_custom_call" | custom-call | tf_op jit(solution)/shard_map/stage/pallas_call | solution.py:23
  77.8 1.2 %couple.1 = f32[4,32,256]{2,1,0:T(8,128)S(1)} custom-call(s32[2]{0:T(128)S(1)} %pad_add_fusion.where_ref, f32[32,1024]{1,0:T(8,128)S(1)} %get-tuple-element.84.sums_ref, f32[32,256]{1,0:T(8,128)S(1)} %get-tuple-element.88.solved_ref, f32[128,1024]{1,0:T(8,128)S(1)} %get-tuple-element.89.mine_ref, f32[128,1024]{1,0:T(8,128)S(1)} %collective-permute-done.21.other_ref), custom_call_target="tpu_custom_call" | custom-call | tf_op jit(solution)/shard_map/couple/pallas_call | solution.py:23
  79.0 0.6 collective-permute-start.22
  79.6 0.2 collective-permute-start.24
  79.8 3.7 %collective-permute-start.25 = (f32[32,256]{1,0:T(8,128)S(1)}, f32[32,256]{1,0:T(8,128)S(1)}, u32[]{:S(2)}, u32[]{:S(2)}) collective-permute-start(f32[32,256]{1,0:T(8,128)S(1)} %get-tuple-element.102), channel_id=1, source_target_pairs={{0,1},{1,0},{2,3},{3,2},{4,5},{5,4},{6,7},{7,6},{8,9},{9,8},{10,11... | collective-permute-start | bytes 98312 | tf_op jit(solution)/shard_map/ppermute | solution.py:527
  83.4 0.6 join.3.tile_ref
  84.1 1.0 collective-permute-done.22
  85.1 0.6 collective-permute-done.24
  85.7 0.6 stage.12
  86.3 0.7 collective-permute-start.26
  87.0 0.6 rest.6
  87.5 0.7 collective-permute-start.28
  88.2 0.6 stage.13
  88.8 0.7 collective-permute-start.27
  89.4 0.6 rest.7
  90.0 1.3 %collective-permute-start.30 = (f32[32,256]{1,0:T(8,128)S(1)}, f32[32,256]{1,0:T(8,128)S(1)}, u32[]{:S(2)}, u32[]{:S(2)}) collective-permute-start(f32[32,256]{1,0:T(8,128)S(1)} %rest.7), channel_id=1, source_target_pairs={{2,0},{6,4},{10,8},{14,12},{18,16},{22,20},{26,24},{30,28}} | collective-permute-start | bytes 98312 | tf_op jit(solution)/shard_map/ppermute | solution.py:397
  91.3 0.6 stage.14
  91.9 1.3 %collective-permute-start.29 = (f32[32,256]{1,0:T(8,128)S(1)}, f32[32,256]{1,0:T(8,128)S(1)}, u32[]{:S(2)}, u32[]{:S(2)}) collective-permute-start(f32[32,256]{1,0:T(8,128)S(1)} %get-tuple-element.98), channel_id=1, source_target_pairs={{1,0},{5,4},{9,8},{13,12},{17,16},{21,20},{25,24},{29,28}} | collective-permute-start | bytes 98312 | tf_op jit(solution)/shard_map/ppermute | solution.py:394
  93.2 6.0 %collective-permute-done.30.far_ref = f32[32,256]{1,0:T(8,128)S(1)} collective-permute-done((f32[32,256]{1,0:T(8,128)S(1)}, f32[32,256]{1,0:T(8,128)S(1)}, u32[]{:S(2)}, u32[]{:S(2)}) %collective-permute-start.30) | collective-permute-done | bytes 32800 | tf_op jit(solution)/shard_map/ppermute | solution.py:397
  99.2 2.6 %collective-permute-done.29.near_ref = f32[32,256]{1,0:T(8,128)S(1)} collective-permute-done((f32[32,256]{1,0:T(8,128)S(1)}, f32[32,256]{1,0:T(8,128)S(1)}, u32[]{:S(2)}, u32[]{:S(2)}) %collective-permute-start.29) | collective-permute-done | bytes 32800 | tf_op jit(solution)/shard_map/ppermute | solution.py:394
  101.8 1.4 %stage.15 = (f32[32,256]{1,0:T(8,128)S(1)}, f32[32,256]{1,0:T(8,128)}) custom-call(s32[2]{0:T(128)S(1)} %pad_add_fusion.where_ref, f32[32,256]{1,0:T(8,128)S(1)} %fusion.3.base_ref, f32[256,1024]{1,0:T(8,128)S(1)} %join.3.tile_ref, f32[32,1024]{1,0:T(8,128)S(1)} %broadcast_2_far_ref_add_ref.2.far_ref.add_ref, ...), custom_call_target="tpu_custom_call" | custom-call | tf_op jit(solution)/shard_map/stage/pallas_call | solution.py:23
  103.2 0.6 pad_maximum_fusion
  (38 shorter events, 0.5 us)
Async XLA Ops:
  0.1 0.7 copy-start
  1.4 2.1 %collective-permute-start = (f32[128,1024]{1,0:T(8,128)S(1)}, f32[128,1024]{1,0:T(8,128)S(1)}, u32[]{:S(2)}, u32[]{:S(2)}) collective-permute-start(f32[128,1024]{1,0:T(8,128)S(1)} %get-tuple-element.54), channel_id=1, source_target_pairs={{0,4},{4,0},{8,12},{12,8},{16,20},{20,16},{24,28},{28,24},{1,5},{5... | collective-permute-start | bytes 1572872 | tf_op jit(solution)/shard_map/ppermute | solution.py:60
  3.5 10.9 %collective-permute-start.2 = (f32[128,1024]{1,0:T(8,128)S(1)}, f32[128,1024]{1,0:T(8,128)S(1)}, u32[]{:S(2)}, u32[]{:S(2)}) collective-permute-start(f32[128,1024]{1,0:T(8,128)S(1)} %add.42), channel_id=1, source_target_pairs={{0,8},{4,20},{8,0},{12,28},{16,24},{20,4},{24,16},{28,12},{1,9},{5... | collective-permute-start | bytes 1572872 | tf_op jit(solution)/shard_map/ppermute | solution.py:65
  13.6 2.3 %collective-permute-start.1 = (f32[128,1024]{1,0:T(8,128)S(1)}, f32[128,1024]{1,0:T(8,128)S(1)}, u32[]{:S(2)}, u32[]{:S(2)}) collective-permute-start(f32[128,1024]{1,0:T(8,128)S(1)} %get-tuple-element.57), channel_id=1, source_target_pairs={{0,4},{4,0},{8,12},{12,8},{16,20},{20,16},{24,28},{28,24},{1,5},{5... | collective-permute-start | bytes 1572872 | tf_op jit(solution)/shard_map/ppermute | solution.py:60
  16.0 15.7 %collective-permute-start.11 = (f32[256,1024]{1,0:T(8,128)S(1)}, f32[256,1024]{1,0:T(8,128)S(1)}, u32[]{:S(2)}, u32[]{:S(2)}) collective-permute-start(f32[256,1024]{1,0:T(8,128)S(1)} %get-tuple-element.73), channel_id=1, source_target_pairs={{0,4},{4,0},{8,12},{12,8},{16,20},{20,16},{24,28},{28,24},{1,5},{5... | collective-permute-start | bytes 3145736 | tf_op jit(solution)/shard_map/ppermute | solution.py:60
  16.5 10.1 %collective-permute-start.3 = (f32[64,1024]{1,0:T(8,128)S(1)}, f32[64,1024]{1,0:T(8,128)S(1)}, u32[]{:S(2)}, u32[]{:S(2)}) collective-permute-start(f32[64,1024]{1,0:T(8,128)S(1)} %slice.41), channel_id=1, source_target_pairs={{0,8},{4,20},{8,0},{12,28},{16,24},{20,4},{24,16},{28,12},{1,9},{5... | collective-permute-start | bytes 786440 | tf_op jit(solution)/shard_map/ppermute | solution.py:65
  19.7 14.5 %collective-permute-start.7 = (f32[128,1024]{1,0:T(8,128)S(1)}, f32[128,1024]{1,0:T(8,128)S(1)}, u32[]{:S(2)}, u32[]{:S(2)}) collective-permute-start(f32[128,1024]{1,0:T(8,128)S(1)} %add.43), channel_id=1, source_target_pairs={{0,16},{4,12},{8,24},{12,4},{16,0},{20,28},{24,8},{28,20},{1,17},{... | collective-permute-start | bytes 1572872 | tf_op jit(solution)/shard_map/ppermute | solution.py:65
  26.7 5.0 %collective-permute-start.4 = (f32[32,1024]{1,0:T(8,128)S(1)}, f32[32,1024]{1,0:T(8,128)S(1)}, u32[]{:S(2)}, u32[]{:S(2)}) collective-permute-start(f32[32,1024]{1,0:T(8,128)S(1)} %slice.43), channel_id=1, source_target_pairs={{0,16},{4,12},{8,24},{12,4},{16,0},{20,28},{24,8},{28,20},{1,17},{... | collective-permute-start | bytes 393224 | tf_op jit(solution)/shard_map/ppermute | solution.py:65
  31.9 19.0 %collective-permute-start.12 = (f32[192,1024]{1,0:T(8,128)S(1)}, f32[192,1024]{1,0:T(8,128)S(1)}, u32[]{:S(2)}, u32[]{:S(2)}) collective-permute-start(f32[192,1024]{1,0:T(8,128)S(1)} %get-tuple-element.75.refs_0_), channel_id=1, source_target_pairs={{0,8},{4,20},{8,0},{12,28},{16,24},{20,4},{24,16},{28,12},{1,9},{5... | collective-permute-start | bytes 2359304 | tf_op jit(solution)/shard_map/ppermute | solution.py:65
  34.1 9.9 %collective-permute-start.6 = (f32[128,1024]{1,0:T(8,128)}, f32[128,1024]{1,0:T(8,128)}, u32[]{:S(2)}, u32[]{:S(2)}) collective-permute-start(f32[128,1024]{1,0:T(8,128)} %get-tuple-element.64), channel_id=1, source_target_pairs={{0,4},{4,0},{8,12},{12,8},{16,20},{20,16},{24,28},{28,24},{1,5},{5... | collective-permute-start | bytes 1572872 | tf_op jit(solution)/shard_map/ppermute | solution.py:60
  34.2 12.8 %collective-permute-start.8 = (f32[128,1024]{1,0:T(8,128)S(1)}, f32[128,1024]{1,0:T(8,128)S(1)}, u32[]{:S(2)}, u32[]{:S(2)}) collective-permute-start(f32[128,1024]{1,0:T(8,128)S(1)} %add.51.mine_ref), channel_id=1, source_target_pairs={{0,4},{4,0},{8,12},{12,8},{16,20},{20,16},{24,28},{28,24},{1,5},{5... | collective-permute-start | bytes 1572872 | tf_op jit(solution)/shard_map/ppermute | solution.py:60
  35.4 14.6 %collective-permute-start.5 = (f32[32,256]{1,0:T(8,128)}, f32[32,256]{1,0:T(8,128)}, u32[]{:S(2)}, u32[]{:S(2)}) collective-permute-start(f32[32,256]{1,0:T(8,128)} %get-tuple-element.104), channel_id=1, source_target_pairs={{0,1},{1,2},{2,3},{4,5},{5,6},{6,7},{8,9},{9,10},{10,11},{12,13},{... | collective-permute-start | bytes 98312 | tf_op jit(solution)/shard_map/ppermute | solution.py:506
  39.5 10.6 %collective-permute-start.9 = (f32[32,256]{1,0:T(8,128)}, f32[32,256]{1,0:T(8,128)}, u32[]{:S(2)}, u32[]{:S(2)}) collective-permute-start(f32[32,256]{1,0:T(8,128)} %get-tuple-element.106), channel_id=1, source_target_pairs={{0,2},{1,3},{4,6},{5,7},{8,10},{9,11},{12,14},{13,15},{16,18},{17,... | collective-permute-start | bytes 98312 | tf_op jit(solution)/shard_map/ppermute | solution.py:506
  44.0 6.1 %collective-permute-start.10 = (f32[32,256]{1,0:T(8,128)}, f32[32,256]{1,0:T(8,128)}, u32[]{:S(2)}, u32[]{:S(2)}) collective-permute-start(f32[32,256]{1,0:T(8,128)} %get-tuple-element.105), channel_id=1, source_target_pairs={{0,3},{4,7},{8,11},{12,15},{16,19},{20,23},{24,27},{28,31}} | collective-permute-start | bytes 98312 | tf_op jit(solution)/shard_map/ppermute | solution.py:506
  45.9 39.8 %copy-start.1 = (f32[2,256,32]{1,2,0:T(8,128)S(1)}, f32[2,256,32]{1,2,0:T(8,128)}, u32[]{:S(2)}) copy-start(f32[2,256,32]{1,2,0:T(8,128)} %param.7) | copy-start | bytes 196612
  51.6 14.8 %collective-permute-start.16 = (f32[160,1024]{1,0:T(8,128)S(1)}, f32[160,1024]{1,0:T(8,128)S(1)}, u32[]{:S(2)}, u32[]{:S(2)}) collective-permute-start(f32[160,1024]{1,0:T(8,128)S(1)} %get-tuple-element.81.refs_0_), channel_id=1, source_target_pairs={{0,16},{4,12},{8,24},{12,4},{16,0},{20,28},{24,8},{28,20},{1,17},{... | collective-permute-start | bytes 1966088 | tf_op jit(solution)/shard_map/ppermute | solution.py:65
  51.7 14.7 %collective-permute-start.17 = (f32[128,1024]{1,0:T(8,128)S(1)}, f32[128,1024]{1,0:T(8,128)S(1)}, u32[]{:S(2)}, u32[]{:S(2)}) collective-permute-start(f32[128,1024]{1,0:T(8,128)S(1)} %add.50.refs_3_), channel_id=1, source_target_pairs={{0,8},{4,20},{8,0},{12,28},{16,24},{20,4},{24,16},{28,12},{1,9},{5... | collective-permute-start | bytes 1572872 | tf_op jit(solution)/shard_map/ppermute | solution.py:65
  52.7 1.9 %collective-permute-start.13 = (f32[32,256]{1,0:T(8,128)S(1)}, f32[32,256]{1,0:T(8,128)S(1)}, u32[]{:S(2)}, u32[]{:S(2)}) collective-permute-start(f32[32,256]{1,0:T(8,128)S(1)} %get-tuple-element.77), channel_id=1, source_target_pairs={{3,2},{7,6},{11,10},{15,14},{19,18},{23,22},{27,26},{31,30}} | collective-permute-start | bytes 98312 | tf_op jit(solution)/shard_map/ppermute | solution.py:394
  53.9 1.9 %collective-permute-start.15 = (f32[32,512]{1,0:T(8,128)S(1)}, f32[32,512]{1,0:T(8,128)S(1)}, u32[]{:S(2)}, u32[]{:S(2)}) collective-permute-start(f32[32,512]{1,0:T(8,128)S(1)} %rest.4), channel_id=1, source_target_pairs={{3,1},{7,5},{11,9},{15,13},{19,17},{23,21},{27,25},{31,29}} | collective-permute-start | bytes 196616 | tf_op jit(solution)/shard_map/ppermute | solution.py:397
  55.2 0.7 collective-permute-start.14
  67.1 9.2 %collective-permute-start.20 = (f32[128,1024]{1,0:T(8,128)S(1)}, f32[128,1024]{1,0:T(8,128)S(1)}, u32[]{:S(2)}, u32[]{:S(2)}) collective-permute-start(f32[128,1024]{1,0:T(8,128)S(1)} %get-tuple-element.87.refs_0_), channel_id=1, source_target_pairs={{0,16},{4,12},{8,24},{12,4},{16,0},{20,28},{24,8},{28,20},{1,17},{... | collective-permute-start | bytes 1572872 | tf_op jit(solution)/shard_map/ppermute | solution.py:65
  67.9 9.9 %collective-permute-start.21 = (f32[128,1024]{1,0:T(8,128)S(1)}, f32[128,1024]{1,0:T(8,128)S(1)}, u32[]{:S(2)}, u32[]{:S(2)}) collective-permute-start(f32[128,1024]{1,0:T(8,128)S(1)} %get-tuple-element.89.mine_ref), channel_id=1, source_target_pairs={{0,4},{4,0},{8,12},{12,8},{16,20},{20,16},{24,28},{28,24},{1,5},{5... | collective-permute-start | bytes 1572872 | tf_op jit(solution)/shard_map/ppermute | solution.py:60
  68.4 6.8 %collective-permute-start.19 = (f32[32,256]{1,0:T(8,128)S(1)}, f32[32,256]{1,0:T(8,128)S(1)}, u32[]{:S(2)}, u32[]{:S(2)}) collective-permute-start(f32[32,256]{1,0:T(8,128)S(1)} %rest.5), channel_id=1, source_target_pairs={{2,0},{6,4},{10,8},{14,12},{18,16},{22,20},{26,24},{30,28}} | collective-permute-start | bytes 98312 | tf_op jit(solution)/shard_map/ppermute | solution.py:397
  69.7 6.0 %collective-permute-start.18 = (f32[32,256]{1,0:T(8,128)S(1)}, f32[32,256]{1,0:T(8,128)S(1)}, u32[]{:S(2)}, u32[]{:S(2)}) collective-permute-start(f32[32,256]{1,0:T(8,128)S(1)} %get-tuple-element.85), channel_id=1, source_target_pairs={{1,0},{5,4},{9,8},{13,12},{17,16},{21,20},{25,24},{29,28}} | collective-permute-start | bytes 98312 | tf_op jit(solution)/shard_map/ppermute | solution.py:394
  77.8 5.6 %collective-permute-start.23 = (f32[128,1024]{1,0:T(8,128)S(1)}, f32[128,1024]{1,0:T(8,128)S(1)}, u32[]{:S(2)}, u32[]{:S(2)}) collective-permute-start(f32[128,1024]{1,0:T(8,128)S(1)} %get-tuple-element.90.mine_ref), channel_id=1, source_target_pairs={{0,4},{4,0},{8,12},{12,8},{16,20},{20,16},{24,28},{28,24},{1,5},{5... | collective-permute-start | bytes 1572872 | tf_op jit(solution)/shard_map/ppermute | solution.py:60
  79.0 6.1 %collective-permute-start.22 = (f32[32,256]{1,0:T(8,128)S(1)}, f32[32,256]{1,0:T(8,128)S(1)}, u32[]{:S(2)}, u32[]{:S(2)}) collective-permute-start(f32[32,256]{1,0:T(8,128)S(1)} %get-tuple-element.101), channel_id=1, source_target_pairs={{0,3},{1,2},{2,1},{3,0},{4,7},{5,6},{6,5},{7,4},{8,11},{9,10},{10,... | collective-permute-start | bytes 98312 | tf_op jit(solution)/shard_map/ppermute | solution.py:527
  79.6 6.1 %collective-permute-start.24 = (f32[32,256]{1,0:T(8,128)S(1)}, f32[32,256]{1,0:T(8,128)S(1)}, u32[]{:S(2)}, u32[]{:S(2)}) collective-permute-start(f32[32,256]{1,0:T(8,128)S(1)} %get-tuple-element.103), channel_id=1, source_target_pairs={{0,2},{1,3},{2,0},{3,1},{4,6},{5,7},{6,4},{7,5},{8,10},{9,11},{10,... | collective-permute-start | bytes 98312 | tf_op jit(solution)/shard_map/ppermute | solution.py:527
  79.8 6.0 %collective-permute-start.25 = (f32[32,256]{1,0:T(8,128)S(1)}, f32[32,256]{1,0:T(8,128)S(1)}, u32[]{:S(2)}, u32[]{:S(2)}) collective-permute-start(f32[32,256]{1,0:T(8,128)S(1)} %get-tuple-element.102), channel_id=1, source_target_pairs={{0,1},{1,0},{2,3},{3,2},{4,5},{5,4},{6,7},{7,6},{8,9},{9,8},{10,11... | collective-permute-start | bytes 98312 | tf_op jit(solution)/shard_map/ppermute | solution.py:527
  86.3 1.9 %collective-permute-start.26 = (f32[32,256]{1,0:T(8,128)S(1)}, f32[32,256]{1,0:T(8,128)S(1)}, u32[]{:S(2)}, u32[]{:S(2)}) collective-permute-start(f32[32,256]{1,0:T(8,128)S(1)} %get-tuple-element.94), channel_id=1, source_target_pairs={{3,2},{7,6},{11,10},{15,14},{19,18},{23,22},{27,26},{31,30}} | collective-permute-start | bytes 98312 | tf_op jit(solution)/shard_map/ppermute | solution.py:394
  87.5 3.8 %collective-permute-start.28 = (f32[32,512]{1,0:T(8,128)S(1)}, f32[32,512]{1,0:T(8,128)S(1)}, u32[]{:S(2)}, u32[]{:S(2)}) collective-permute-start(f32[32,512]{1,0:T(8,128)S(1)} %rest.6), channel_id=1, source_target_pairs={{3,1},{7,5},{11,9},{15,13},{19,17},{23,21},{27,25},{31,29}} | collective-permute-start | bytes 196616 | tf_op jit(solution)/shard_map/ppermute | solution.py:397
  88.8 2.5 %collective-permute-start.27 = (f32[32,256]{1,0:T(8,128)S(1)}, f32[32,256]{1,0:T(8,128)S(1)}, u32[]{:S(2)}, u32[]{:S(2)}) collective-permute-start(f32[32,256]{1,0:T(8,128)S(1)} %get-tuple-element.96), channel_id=1, source_target_pairs={{2,1},{6,5},{10,9},{14,13},{18,17},{22,21},{26,25},{30,29}} | collective-permute-start | bytes 98312 | tf_op jit(solution)/shard_map/ppermute | solution.py:394
  90.0 9.2 %collective-permute-start.30 = (f32[32,256]{1,0:T(8,128)S(1)}, f32[32,256]{1,0:T(8,128)S(1)}, u32[]{:S(2)}, u32[]{:S(2)}) collective-permute-start(f32[32,256]{1,0:T(8,128)S(1)} %rest.7), channel_id=1, source_target_pairs={{2,0},{6,4},{10,8},{14,12},{18,16},{22,20},{26,24},{30,28}} | collective-permute-start | bytes 98312 | tf_op jit(solution)/shard_map/ppermute | solution.py:397
  91.9 9.9 %collective-permute-start.29 = (f32[32,256]{1,0:T(8,128)S(1)}, f32[32,256]{1,0:T(8,128)S(1)}, u32[]{:S(2)}, u32[]{:S(2)}) collective-permute-start(f32[32,256]{1,0:T(8,128)S(1)} %get-tuple-element.98), channel_id=1, source_target_pairs={{1,0},{5,4},{9,8},{13,12},{17,16},{21,20},{25,24},{29,28}} | collective-permute-start | bytes 98312 | tf_op jit(solution)/shard_map/ppermute | solution.py:394

commit v6 on v5

--- a/solution.py
+++ b/solution.py
@@ -83,43 +83,34 @@
     return tables
 
 
-def front_kernel(
-    where_ref, rows_ref, factor_ref, known_ref, keep_one, send_one, keep_ref, send_ref, factor_buf, known_buf, acc_ref, sems, low,
-    *, tables
-):
-    slots, _, band, _ = factor_buf.shape
+def accumulate(where_ref, rows_ref, factor_ref, known_ref, factor_buf, known_buf, acc_ref, sems, column):
+    slots = factor_buf.shape[0]
     me = where_ref[0]
 
     def live(slot):
         return rows_ref[me * slots + slot] >= 2
 
-    def copies(slot, column):
-        copy = pltpu.make_async_copy(factor_ref.at[slot, column], factor_buf.at[slot, column], sems.at[column, slot])
-        if column == 0:
-            return [copy]
-        return [pltpu.make_async_copy(known_ref.at[slot], known_buf.at[slot], sems.at[2, slot]), copy]
-
-    for column in (1, 0):
-        for slot in range(slots):
-
-            @pl.when(live(slot))
-            def _():
-                for copy in copies(slot, column):
-                    copy.start()
-
-    finish = put_band(where_ref, rows_ref, factor_ref, 1, 0, keep_ref, send_ref, 0, band // 2, low)
-    for column, keep, send, first in ((1, keep_one, send_one, 0), (0, keep_ref, send_ref, band // 2)):
-        acc_ref[...] = jnp.zeros_like(acc_ref)
-        for slot in range(slots):
-
-            @pl.when(live(slot))
-            def _():
-                for copy in copies(slot, column):
-                    copy.wait()
-                acc_ref[...] += dot_split(split(known_buf[slot]), split(factor_buf[slot, column]), ((0,), (0,)))
-
-        in_send_order(where_ref, acc_ref, keep, send, first, tables)
-    finish()
+    def copies(slot):
+        return (
+            pltpu.make_async_copy(known_ref.at[slot], known_buf.at[slot], sems.at[0, slot]),
+            pltpu.make_async_copy(factor_ref.at[slot, column], factor_buf.at[slot], sems.at[1, slot]),
+        )
+
+    for slot in range(slots):
+
+        @pl.when(live(slot))
+        def _():
+            for copy in copies(slot):
+                copy.start()
+
+    acc_ref[...] = jnp.zeros_like(acc_ref)
+    for slot in range(slots):
+
+        @pl.when(live(slot))
+        def _():
+            for copy in copies(slot):
+                copy.wait()
+            acc_ref[...] += dot_split(split(known_buf[slot]), split(factor_buf[slot]), ((0,), (0,)))
 
 
 def in_send_order(where_ref, acc_ref, keep_ref, send_ref, first, tables):
@@ -184,20 +175,44 @@
     return call(body, out, (SMEM, SMEM, HBM), (where, slot_row, factor_rows), "first_band", scratch)
 
 
-def front(where, slot_row, factor_rows, known, members):
+def partial_scratch(slots, band, width, total):
+    return [
+        pltpu.VMEM((slots, band, width), F32),
+        pltpu.VMEM((slots, band, total), F32),
+        pltpu.VMEM((total, width), F32),
+        pltpu.SemaphoreType.DMA((2, slots)),
+    ]
+
+
+def partial_one(where, slot_row, factor_rows, known, members):
     slots, _, band, width = factor_rows.shape
     total = known.shape[2]
-    one, rest = shape(total // 2, width), shape(band // 2 + total // 2, width)
-    scratch = [
-        pltpu.VMEM(factor_rows.shape, F32),
-        pltpu.VMEM(known.shape, F32),
-        pltpu.VMEM((total, width), F32),
-        pltpu.SemaphoreType.DMA((3, slots)),
-        pltpu.SemaphoreType.DMA((2,)),
-    ]
-    body = functools.partial(front_kernel, tables=send_tables(members))
+    tables = send_tables(members)
+
+    def body(where_ref, rows_ref, factor_ref, known_ref, keep_ref, send_ref, factor_buf, known_buf, acc_ref, sems):
+        accumulate(where_ref, rows_ref, factor_ref, known_ref, factor_buf, known_buf, acc_ref, sems, 1)
+        in_send_order(where_ref, acc_ref, keep_ref, send_ref, 0, tables)
+
+    out = (shape(total // 2, width), shape(total // 2, width))
     args = (where, slot_row, factor_rows, known)
-    return call(body, (one, one, rest, rest), (SMEM, SMEM, HBM, HBM), args, "front", scratch)
+    return call(body, out, (SMEM, SMEM, HBM, HBM), args, "partial_one", partial_scratch(slots, band, width, total))
+
+
+def pack_rest(where, slot_row, factor_rows, known, members):
+    slots, _, band, width = factor_rows.shape
+    half, total = band // 2, known.shape[2]
+    tables = send_tables(members)
+
+    def body(where_ref, rows_ref, factor_ref, known_ref, keep_ref, send_ref, factor_buf, known_buf, acc_ref, sems, low):
+        finish = put_band(where_ref, rows_ref, factor_ref, 1, 0, keep_ref, send_ref, 0, half, low)
+        accumulate(where_ref, rows_ref, factor_ref, known_ref, factor_buf, known_buf, acc_ref, sems, 0)
+        in_send_order(where_ref, acc_ref, keep_ref, send_ref, half, tables)
+        finish()
+
+    rows = half + total // 2
+    scratch = partial_scratch(slots, band, width, total) + [pltpu.SemaphoreType.DMA((2,))]
+    args = (where, slot_row, factor_rows, known)
+    return call(body, (shape(rows, width),) * 2, (SMEM, SMEM, HBM, HBM), args, "pack_rest", scratch)
 
 
 def top_band(where, slot_row, factor_rows):
@@ -401,11 +416,11 @@
 
 
 class Packs:
-    def __init__(self, pack, got, top, steps, bands, members):
-        self.pack, self.got, self.top, self.got_top = pack, got, top, None
+    def __init__(self, pack, got, top, got_top, steps, bands, members):
+        self.pack, self.got, self.top, self.got_top = pack, got, top, got_top
         self.steps, self.members = steps, members
         self.low_at = [bands - 2 - 2 * (steps - 1 - step) for step in range(steps)]
-        self.top_at = [bands - steps + step for step in range(steps)]
+        self.top_at = [0] + [bands - steps + step for step in range(steps)]
 
     def take(self, index):
         taken = ()
@@ -422,19 +437,11 @@
             tiles, sums, *outs = outs
             self.pack = (tiles, sums, self.pack[2])
             step = self.low_at.index(self.index) + 1
-            if step < self.steps:
-                self.got = swap_chip(tiles, self.members, step)
-            else:
-                self.got = swap_core(tiles, self.members)
-            if step == 1:
-                self.got_top = swap_chip(after(self.top, tiles), self.members, 0)
-        if self.index in self.top_at:
+            self.got = swap_chip(tiles, self.members, step) if step < self.steps else swap_core(tiles, self.members)
+        if outs:
             (self.top,) = outs
-            step = self.top_at.index(self.index) + 1
-            if step < self.steps:
-                self.got_top = swap_chip(self.top, self.members, step)
-            else:
-                self.got_top = swap_core(self.top, self.members)
+            step = self.top_at.index(self.index)
+            self.got_top = swap_chip(self.top, self.members, step) if step < self.steps else swap_core(self.top, self.members)
 
 
 def couple(where, sums, solved, mine, other, bands):
@@ -480,28 +487,31 @@
     keep, send = first_band(where, slot_row, factor_rows)
     tile_one = keep + swap_core(send, members)
     got_tile = swap_chip(tile_one, members, 0)
-    keep_one, send_one, keep, send = front(after(where, tile_one), slot_row, factor_rows, known, members)
+    keep_one, send_one = partial_one(after(where, tile_one), slot_row, factor_rows, known, members)
     got_sum = swap_core(send_one, members)
     tile_one = tile_one + after(got_tile, keep_one)
     got_tile = swap_chip(tile_one, members, 1)
     sum_one = keep_one + after(got_sum, tile_one)
-    got_pack = got_top = top = None
+    keep = send = top = send_top = got_pack = got_top = None
     for stage in range(stages):
         rows = sum_one.shape[0] // 2
         got_sum = swap_chip(sum_one[rows:], members, stage)
         if stage == 0:
-            got_pack = swap_core(after(send, sum_one), members)
+            keep, send = pack_rest(after(where, sum_one), slot_row, factor_rows, known, members)
+            got_sum = after(got_sum, keep)
+        if stage == 1:
             top, send_top = top_band(after(where, sum_one), slot_row, factor_rows)
             got_sum = after(got_sum, top)
         sum_one = sum_one[:rows] + got_sum
         if stage == 0:
-            got_top = swap_core(after(send_top, sum_one), members)
+            got_pack = swap_core(after(send, sum_one), members)
         if stage < stages - 1:
-            tile_one = tile_one + after(got_tile, sum_one)
+            tile_one = tile_one + (after(got_tile, sum_one) if stage < stages - 2 else got_tile)
             got_tile = swap_chip(tile_one, members, stage + 2) if stage < stages - 2 else None
+    got_top = swap_core(send_top, members)
 
     got_up = []
-    for shift in range(1, bands):
+    for shift in range(bands - 1, 0, -1):
         piece = own_band(sum_one, jnp.minimum(place + shift, bands - 1), band)
         got_up.append(lax.ppermute(piece, "ct", [(i, i + shift) for i in range(bands - shift)]))
 
@@ -509,14 +519,11 @@
 
     tiles, sums = pack_step(keep, keep, half, after(got_pack, sum_one), half, False)
     got_pack = swap_chip(tiles, members, 0)
-    top = top + after(got_top, sum_one)
-
-    tile_one = join_halves(after(where, sum_one, top), tile_one, other, 0, half, range(bands))
+    tile_one = join_halves(after(where, sum_one), tile_one, other, 0, half, range(bands))
+    packs = Packs((tiles, sums, half), got_pack, top, got_top, stages, bands, members)
     base = rhs[1].T - own_band(sum_one, place, band)
     for piece in got_up:
         base = base - after(piece, tile_one)
-
-    packs = Packs((tiles, sums, half), got_pack, top, stages, bands, members)
     solved_one = sweep(where, base, tile_one, sum_one, bands, packs)
 
     low, sums, _ = packs.pack

time: 104 us -> 106 us (1.019)
  Pallas kernels: 22.9 us -> 25.4 us
  other arithmetic: 3.03 us -> 1.86 us
    pallas_call x19 -> x20, Pallas kernels: 22.9 us -> 25.4 us  [call(): pl.pallas_call(body, out_shape=out, in_specs=list(specs), out_specs=tuple...]
    ppermute x4, waiting for transfers between devices: 10.2 us -> 12.2 us  [sweep(): fars.append(lax.ppermute(rest, 'ct', [(stage, stage - 2)]))]
    ppermute x7, waiting for transfers between devices: 3.02 us -> 1.55 us  [swap_core(): return lax.ppermute(value, 'rt', [(i, i ^ 1) for i in range(members)])]
    add x2 -> x1, other arithmetic: 1.25 us -> 0.08 us  [shards(): tile_one + (after(got_tile, sum_one) if stage < stages - 2 else got_tile)]
    ppermute x7, starting transfers between devices: 2.32 us -> 1.23 us  [swap_core(): return lax.ppermute(value, 'rt', [(i, i ^ 1) for i in range(members)])]
    ppermute x8, starting transfers between devices: 11.4 us -> 12.5 us  [swap_chip(): lax.ppermute(value, 'rt', [(i, i ^ 1 << orders[i & 1][stage]) for i in ra...]
  transfers between devices with their start and end apart: 31 -> 31, of which waited for: 13 -> 12; matrix products, arithmetic and copies ran while one was open for 3% -> 2% of each run, Pallas kernels for 18% -> 20%
where the time goes in v6:
time: 106 us; the launch traced here: 105 us
  waiting for transfers between devices  39 us (37%)
  starting transfers between devices  37.2 us (35%)
  Pallas kernels  25.4 us (24%)
  other arithmetic  1.86 us (2%)
  local copies, waits for them, and re-layouts  1.34 us (1%)
    pallas_call x20, Pallas kernels, call(): pl.pallas_call(body, out_shape=out, in_specs=list(specs), out_specs=tuple...  25.4 us
    ppermute x8, waiting for transfers between devices, swap_chip(): lax.ppermute(value, 'rt', [(i, i ^ 1 << orders[i & 1][stage]) for i in ra...  20.4 us
    ppermute x8, starting transfers between devices, swap_chip(): lax.ppermute(value, 'rt', [(i, i ^ 1 << orders[i & 1][stage]) for i in ra...  12.5 us
    ppermute x4, waiting for transfers between devices, sweep(): fars.append(lax.ppermute(rest, 'ct', [(stage, stage - 2)]))  12.2 us
    ppermute x3, starting transfers between devices, shards(): lax.ppermute(piece, 'ct', [(i, i + shift) for i in range(bands - shift)])  9.89 us
    ppermute x6, starting transfers between devices, sweep(): near = lax.ppermute(update, 'ct', [(stage, stage - 1)])  5.22 us
    ppermute x3, starting transfers between devices, shards(): lax.ppermute(pieces[mask], 'ct', [(i, i ^ mask) for i in range(bands)])  4.45 us
    ppermute x4, starting transfers between devices, sweep(): fars.append(lax.ppermute(rest, 'ct', [(stage, stage - 2)]))  3.91 us
  transfers between devices with their start and end apart: 31, of which 12 were waited for; matrix products, arithmetic and copies ran while one was open for 2% of the time, Pallas kernels for 20%

profile of v6, /device:TPU:0, one launch (start us, length us, event | category | flops | bytes accessed | tf_op | source)
XLA Modules:
  0.0 105.1 jit_solution(1851549880388361797)
XLA Ops:
  0.0 0.1 pad_add_fusion.where_ref
  0.1 0.7 copy-done
  0.7 0.6 first_band.1
  1.4 0.5 collective-permute-start
  1.9 1.5 %collective-permute-done = f32[128,1024]{1,0:T(8,128)S(1)} collective-permute-done((f32[128,1024]{1,0:T(8,128)S(1)}, f32[128,1024]{1,0:T(8,128)S(1)}, u32[]{:S(2)}, u32[]{:S(2)}) %collective-permute-start) | collective-permute-done | bytes 524320 | tf_op jit(solution)/shard_map/ppermute | solution.py:60
  3.5 4.1 %collective-permute-start.2 = (f32[128,1024]{1,0:T(8,128)S(1)}, f32[128,1024]{1,0:T(8,128)S(1)}, u32[]{:S(2)}, u32[]{:S(2)}) collective-permute-start(f32[128,1024]{1,0:T(8,128)S(1)} %add.39), channel_id=1, source_target_pairs={{0,8},{4,20},{8,0},{12,28},{16,24},{20,4},{24,16},{28,12},{1,9},{5... | collective-permute-start | bytes 1572872 | tf_op jit(solution)/shard_map/ppermute | solution.py:65
  7.6 4.5 %partial_one.1 = (f32[128,1024]{1,0:T(8,128)S(1)}, f32[128,1024]{1,0:T(8,128)S(1)}) custom-call(s32[2]{0:T(128)S(1)} %pad_add_fusion.where_ref, s32[48]{0:T(128)S(1)} %copy-done, f32[6,2,256,1024]{3,2,1,0:T(8,128)} %factor_ref.7, f32[6,256,256]{2,1,0:T(8,128)} %known_ref.3), custom_call_target="tpu_custom_call" | custom-call | tf_op jit(solution)/shard_map/partial_one/pallas_call | solution.py:23
  12.1 2.6 %collective-permute-done.2 = f32[128,1024]{1,0:T(8,128)S(1)} collective-permute-done((f32[128,1024]{1,0:T(8,128)S(1)}, f32[128,1024]{1,0:T(8,128)S(1)}, u32[]{:S(2)}, u32[]{:S(2)}) %collective-permute-start.2) | collective-permute-done | bytes 524320 | tf_op jit(solution)/shard_map/ppermute | solution.py:65
  14.9 2.1 %collective-permute-start.3 = (f32[64,1024]{1,0:T(8,128)S(1)}, f32[64,1024]{1,0:T(8,128)S(1)}, u32[]{:S(2)}, u32[]{:S(2)}) collective-permute-start(f32[64,1024]{1,0:T(8,128)S(1)} %slice.41), channel_id=1, source_target_pairs={{0,8},{4,20},{8,0},{12,28},{16,24},{20,4},{24,16},{28,12},{1,9},{5... | collective-permute-start | bytes 786440 | tf_op jit(solution)/shard_map/ppermute | solution.py:65
  17.0 4.6 %pack_rest.1 = (f32[256,1024]{1,0:T(8,128)S(1)}, f32[256,1024]{1,0:T(8,128)S(1)}) custom-call(s32[2]{0:T(128)S(1)} %pad_add_fusion.where_ref, s32[48]{0:T(128)S(1)} %copy-done, f32[6,2,256,1024]{3,2,1,0:T(8,128)} %factor_ref.7, f32[6,256,256]{2,1,0:T(8,128)} %known_ref.3), custom_call_target="tpu_custom_call" | custom-call | tf_op jit(solution)/shard_map/pack_rest/pallas_call | solution.py:23
  21.7 1.1 %collective-permute-start.6 = (f32[128,1024]{1,0:T(8,128)S(1)}, f32[128,1024]{1,0:T(8,128)S(1)}, u32[]{:S(2)}, u32[]{:S(2)}) collective-permute-start(f32[128,1024]{1,0:T(8,128)S(1)} %add.40), channel_id=1, source_target_pairs={{0,16},{4,12},{8,24},{12,4},{16,0},{20,28},{24,8},{28,20},{1,17},{... | collective-permute-start | bytes 1572872 | tf_op jit(solution)/shard_map/ppermute | solution.py:65
  22.8 1.1 %collective-permute-start.4 = (f32[32,1024]{1,0:T(8,128)S(1)}, f32[32,1024]{1,0:T(8,128)S(1)}, u32[]{:S(2)}, u32[]{:S(2)}) collective-permute-start(f32[32,1024]{1,0:T(8,128)S(1)} %slice.43), channel_id=1, source_target_pairs={{0,16},{4,12},{8,24},{12,4},{16,0},{20,28},{24,8},{28,20},{1,17},{... | collective-permute-start | bytes 393224 | tf_op jit(solution)/shard_map/ppermute | solution.py:65
  23.9 1.6 %top_band.1 = (f32[128,1024]{1,0:T(8,128)S(1)}, f32[128,1024]{1,0:T(8,128)}) custom-call(s32[2]{0:T(128)S(1)} %pad_add_fusion.where_ref, s32[48]{0:T(128)S(1)} %copy-done, f32[6,2,256,1024]{3,2,1,0:T(8,128)} %factor_ref.7), custom_call_target="tpu_custom_call" | custom-call | tf_op jit(solution)/shard_map/top_band/pallas_call | solution.py:23
  25.5 6.9 %collective-permute-done.4 = f32[32,1024]{1,0:T(8,128)S(1)} collective-permute-done((f32[32,1024]{1,0:T(8,128)S(1)}, f32[32,1024]{1,0:T(8,128)S(1)}, u32[]{:S(2)}, u32[]{:S(2)}) %collective-permute-start.4) | collective-permute-done | bytes 131104 | tf_op jit(solution)/shard_map/ppermute | solution.py:65
  32.4 0.1 pack_step.1
  32.5 1.8 %collective-permute-start.11 = (f32[192,1024]{1,0:T(8,128)S(1)}, f32[192,1024]{1,0:T(8,128)S(1)}, u32[]{:S(2)}, u32[]{:S(2)}) collective-permute-start(f32[192,1024]{1,0:T(8,128)S(1)} %get-tuple-element.72.refs_0_), channel_id=1, source_target_pairs={{0,8},{4,20},{8,0},{12,28},{16,24},{20,4},{24,16},{28,12},{1,9},{5... | collective-permute-start | bytes 2359304 | tf_op jit(solution)/shard_map/ppermute | solution.py:65
  34.3 0.1 add.47.mine_ref
  34.4 0.1 collective-permute-start.7
  34.5 0.5 collective-permute-start.12
  35.0 0.6 constant_dynamic-slice_fusion.2
  35.6 6.1 %collective-permute-start.5 = (f32[32,256]{1,0:T(8,128)}, f32[32,256]{1,0:T(8,128)}, u32[]{:S(2)}, u32[]{:S(2)}) collective-permute-start(f32[32,256]{1,0:T(8,128)} %get-tuple-element.102), channel_id=1, source_target_pairs={{0,3},{4,7},{8,11},{12,15},{16,19},{20,23},{24,27},{28,31}} | collective-permute-start | bytes 98312 | tf_op jit(solution)/shard_map/ppermute | solution.py:516
  41.7 1.9 %collective-permute-start.9 = (f32[32,256]{1,0:T(8,128)}, f32[32,256]{1,0:T(8,128)}, u32[]{:S(2)}, u32[]{:S(2)}) collective-permute-start(f32[32,256]{1,0:T(8,128)} %get-tuple-element.103), channel_id=1, source_target_pairs={{0,1},{1,2},{2,3},{4,5},{5,6},{6,7},{8,9},{9,10},{10,11},{12,13},{... | collective-permute-start | bytes 98312 | tf_op jit(solution)/shard_map/ppermute | solution.py:516
  43.6 1.9 %collective-permute-start.8 = (f32[32,256]{1,0:T(8,128)}, f32[32,256]{1,0:T(8,128)}, u32[]{:S(2)}, u32[]{:S(2)}) collective-permute-start(f32[32,256]{1,0:T(8,128)} %get-tuple-element.104), channel_id=1, source_target_pairs={{0,2},{1,3},{4,6},{5,7},{8,10},{9,11},{12,14},{13,15},{16,18},{17,... | collective-permute-start | bytes 98312 | tf_op jit(solution)/shard_map/ppermute | solution.py:516
  45.5 3.5 %join.2.tile_ref = f32[256,1024]{1,0:T(8,128)S(1)} custom-call(s32[2]{0:T(128)S(1)} %pad_add_fusion.where_ref, f32[128,1024]{1,0:T(8,128)S(1)} %add.47.mine_ref, f32[128,1024]{1,0:T(8,128)} %collective-permute-done.7.other_ref), custom_call_target="tpu_custom_call" | custom-call | tf_op jit(solution)/shard_map/join/pallas_call | solution.py:23
  49.1 0.8 fusion.6.base_ref
  50.0 0.7 stage.8
  50.7 0.5 collective-permute-start.16
  51.1 0.9 collective-permute-start.17
  52.0 0.7 collective-permute-start.13
  52.7 0.6 rest.4
  53.2 0.7 collective-permute-start.15
  53.9 0.6 stage.9
  54.5 0.7 collective-permute-start.14
  55.2 10.6 %collective-permute-done.17.refs_4_ = f32[128,1024]{1,0:T(8,128)S(1)} collective-permute-done((f32[128,1024]{1,0:T(8,128)S(1)}, f32[128,1024]{1,0:T(8,128)S(1)}, u32[]{:S(2)}, u32[]{:S(2)}) %collective-permute-start.17) | collective-permute-done | bytes 524320 | tf_op jit(solution)/shard_map/ppermute | solution.py:65
  65.7 0.1 collective-permute-done.16.refs_2_
  65.8 0.7 stage.10
  66.5 1.0 collective-permute-start.20
  67.5 0.5 rest.5
  68.0 1.3 %collective-permute-start.19 = (f32[32,256]{1,0:T(8,128)S(1)}, f32[32,256]{1,0:T(8,128)S(1)}, u32[]{:S(2)}, u32[]{:S(2)}) collective-permute-start(f32[32,256]{1,0:T(8,128)S(1)} %rest.5), channel_id=1, source_target_pairs={{2,0},{6,4},{10,8},{14,12},{18,16},{22,20},{26,24},{30,28}} | collective-permute-start | bytes 98312 | tf_op jit(solution)/shard_map/ppermute | solution.py:412
  69.3 1.3 %collective-permute-start.18 = (f32[32,256]{1,0:T(8,128)S(1)}, f32[32,256]{1,0:T(8,128)S(1)}, u32[]{:S(2)}, u32[]{:S(2)}) collective-permute-start(f32[32,256]{1,0:T(8,128)S(1)} %get-tuple-element.83), channel_id=1, source_target_pairs={{1,0},{5,4},{9,8},{13,12},{17,16},{21,20},{25,24},{29,28}} | collective-permute-start | bytes 98312 | tf_op jit(solution)/shard_map/ppermute | solution.py:409
  70.6 4.2 %collective-permute-done.19.far_ref = f32[32,256]{1,0:T(8,128)S(1)} collective-permute-done((f32[32,256]{1,0:T(8,128)S(1)}, f32[32,256]{1,0:T(8,128)S(1)}, u32[]{:S(2)}, u32[]{:S(2)}) %collective-permute-start.19) | collective-permute-done | bytes 32800 | tf_op jit(solution)/shard_map/ppermute | solution.py:412
  74.9 0.5 collective-permute-done.18.near_ref
  75.4 0.3 collective-permute-done.20.refs_1_
  75.7 1.4 %stage.11 = (f32[32,256]{1,0:T(8,128)S(1)}, f32[32,256]{1,0:T(8,128)}, f32[128,1024]{1,0:T(8,128)S(1)}) custom-call(s32[2]{0:T(128)S(1)} %pad_add_fusion.where_ref, f32[32,256]{1,0:T(8,128)S(1)} %fusion.6.base_ref, f32[256,1024]{1,0:T(8,128)S(1)} %join.2.tile_ref, f32[32,1024]{1,0:T(8,128)S(1)} %slice_add_fusion.1.add_ref, ...), custom_call_target="tpu_custom_call" | custom-call | tf_op jit(solution)/shard_map/stage/pallas_call | solution.py:23
  77.2 1.2 %couple.1 = f32[4,32,256]{2,1,0:T(8,128)S(1)} custom-call(s32[2]{0:T(128)S(1)} %pad_add_fusion.where_ref, f32[32,1024]{1,0:T(8,128)S(1)} %get-tuple-element.82.sums_ref, f32[32,256]{1,0:T(8,128)S(1)} %get-tuple-element.86.solved_ref, f32[128,1024]{1,0:T(8,128)S(1)} %get-tuple-element.87.mine_ref, f32[128,1024]{1,0:T(8,128)S(1)} %collective-permute-done.21.other_ref), custom_call_target="tpu_custom_call" | custom-call | tf_op jit(solution)/shard_map/couple/pallas_call | solution.py:23
  78.4 0.4 collective-permute-start.25
  78.9 3.9 %collective-permute-start.24 = (f32[32,256]{1,0:T(8,128)S(1)}, f32[32,256]{1,0:T(8,128)S(1)}, u32[]{:S(2)}, u32[]{:S(2)}) collective-permute-start(f32[32,256]{1,0:T(8,128)S(1)} %get-tuple-element.101), channel_id=1, source_target_pairs={{0,2},{1,3},{2,0},{3,1},{4,6},{5,7},{6,4},{7,5},{8,10},{9,11},{10,... | collective-permute-start | bytes 98312 | tf_op jit(solution)/shard_map/ppermute | solution.py:534
  82.8 0.6 join.3.tile_ref
  83.4 1.0 collective-permute-done.22
  84.4 0.7 collective-permute-done.24
  85.1 0.6 stage.12
  85.6 0.7 collective-permute-start.26
  86.3 0.6 rest.6
  86.9 0.7 collective-permute-start.28
  87.6 0.6 stage.13
  88.1 0.7 collective-permute-start.27
  88.8 0.6 rest.7
  89.4 1.3 %collective-permute-start.30 = (f32[32,256]{1,0:T(8,128)S(1)}, f32[32,256]{1,0:T(8,128)S(1)}, u32[]{:S(2)}, u32[]{:S(2)}) collective-permute-start(f32[32,256]{1,0:T(8,128)S(1)} %rest.7), channel_id=1, source_target_pairs={{2,0},{6,4},{10,8},{14,12},{18,16},{22,20},{26,24},{30,28}} | collective-permute-start | bytes 98312 | tf_op jit(solution)/shard_map/ppermute | solution.py:412
  90.7 0.6 stage.14
  91.2 1.3 %collective-permute-start.29 = (f32[32,256]{1,0:T(8,128)S(1)}, f32[32,256]{1,0:T(8,128)S(1)}, u32[]{:S(2)}, u32[]{:S(2)}) collective-permute-start(f32[32,256]{1,0:T(8,128)S(1)} %get-tuple-element.96), channel_id=1, source_target_pairs={{1,0},{5,4},{9,8},{13,12},{17,16},{21,20},{25,24},{29,28}} | collective-permute-start | bytes 98312 | tf_op jit(solution)/shard_map/ppermute | solution.py:409
  92.5 8.0 %collective-permute-done.30.far_ref = f32[32,256]{1,0:T(8,128)S(1)} collective-permute-done((f32[32,256]{1,0:T(8,128)S(1)}, f32[32,256]{1,0:T(8,128)S(1)}, u32[]{:S(2)}, u32[]{:S(2)}) %collective-permute-start.30) | collective-permute-done | bytes 32800 | tf_op jit(solution)/shard_map/ppermute | solution.py:412
  100.5 2.6 %collective-permute-done.29.near_ref = f32[32,256]{1,0:T(8,128)S(1)} collective-permute-done((f32[32,256]{1,0:T(8,128)S(1)}, f32[32,256]{1,0:T(8,128)S(1)}, u32[]{:S(2)}, u32[]{:S(2)}) %collective-permute-start.29) | collective-permute-done | bytes 32800 | tf_op jit(solution)/shard_map/ppermute | solution.py:409
  103.1 1.4 %stage.15 = (f32[32,256]{1,0:T(8,128)S(1)}, f32[32,256]{1,0:T(8,128)}) custom-call(s32[2]{0:T(128)S(1)} %pad_add_fusion.where_ref, f32[32,256]{1,0:T(8,128)S(1)} %fusion.3.base_ref, f32[256,1024]{1,0:T(8,128)S(1)} %join.3.tile_ref, f32[32,1024]{1,0:T(8,128)S(1)} %broadcast_2_far_ref_add_ref.2.far_ref.add_ref, ...), custom_call_target="tpu_custom_call" | custom-call | tf_op jit(solution)/shard_map/stage/pallas_call | solution.py:23
  104.5 0.6 pad_maximum_fusion
  (38 shorter events, 0.6 us)
Async XLA Ops:
  0.1 0.7 copy-start
  1.4 2.1 %collective-permute-start = (f32[128,1024]{1,0:T(8,128)S(1)}, f32[128,1024]{1,0:T(8,128)S(1)}, u32[]{:S(2)}, u32[]{:S(2)}) collective-permute-start(f32[128,1024]{1,0:T(8,128)S(1)} %get-tuple-element.53), channel_id=1, source_target_pairs={{0,4},{4,0},{8,12},{12,8},{16,20},{20,16},{24,28},{28,24},{1,5},{5... | collective-permute-start | bytes 1572872 | tf_op jit(solution)/shard_map/ppermute | solution.py:60
  3.5 11.2 %collective-permute-start.2 = (f32[128,1024]{1,0:T(8,128)S(1)}, f32[128,1024]{1,0:T(8,128)S(1)}, u32[]{:S(2)}, u32[]{:S(2)}) collective-permute-start(f32[128,1024]{1,0:T(8,128)S(1)} %add.39), channel_id=1, source_target_pairs={{0,8},{4,20},{8,0},{12,28},{16,24},{20,4},{24,16},{28,12},{1,9},{5... | collective-permute-start | bytes 1572872 | tf_op jit(solution)/shard_map/ppermute | solution.py:65
  12.1 2.7 %collective-permute-start.1 = (f32[128,1024]{1,0:T(8,128)S(1)}, f32[128,1024]{1,0:T(8,128)S(1)}, u32[]{:S(2)}, u32[]{:S(2)}) collective-permute-start(f32[128,1024]{1,0:T(8,128)S(1)} %get-tuple-element.56), channel_id=1, source_target_pairs={{0,4},{4,0},{8,12},{12,8},{16,20},{20,16},{24,28},{28,24},{1,5},{5... | collective-permute-start | bytes 1572872 | tf_op jit(solution)/shard_map/ppermute | solution.py:60
  14.9 6.7 %collective-permute-start.3 = (f32[64,1024]{1,0:T(8,128)S(1)}, f32[64,1024]{1,0:T(8,128)S(1)}, u32[]{:S(2)}, u32[]{:S(2)}) collective-permute-start(f32[64,1024]{1,0:T(8,128)S(1)} %slice.41), channel_id=1, source_target_pairs={{0,8},{4,20},{8,0},{12,28},{16,24},{20,4},{24,16},{28,12},{1,9},{5... | collective-permute-start | bytes 786440 | tf_op jit(solution)/shard_map/ppermute | solution.py:65
  21.6 10.8 %collective-permute-start.10 = (f32[256,1024]{1,0:T(8,128)S(1)}, f32[256,1024]{1,0:T(8,128)S(1)}, u32[]{:S(2)}, u32[]{:S(2)}) collective-permute-start(f32[256,1024]{1,0:T(8,128)S(1)} %get-tuple-element.70), channel_id=1, source_target_pairs={{0,4},{4,0},{8,12},{12,8},{16,20},{20,16},{24,28},{28,24},{1,5},{5... | collective-permute-start | bytes 3145736 | tf_op jit(solution)/shard_map/ppermute | solution.py:60
  21.7 12.6 %collective-permute-start.6 = (f32[128,1024]{1,0:T(8,128)S(1)}, f32[128,1024]{1,0:T(8,128)S(1)}, u32[]{:S(2)}, u32[]{:S(2)}) collective-permute-start(f32[128,1024]{1,0:T(8,128)S(1)} %add.40), channel_id=1, source_target_pairs={{0,16},{4,12},{8,24},{12,4},{16,0},{20,28},{24,8},{28,20},{1,17},{... | collective-permute-start | bytes 1572872 | tf_op jit(solution)/shard_map/ppermute | solution.py:65
  22.8 9.6 %collective-permute-start.4 = (f32[32,1024]{1,0:T(8,128)S(1)}, f32[32,1024]{1,0:T(8,128)S(1)}, u32[]{:S(2)}, u32[]{:S(2)}) collective-permute-start(f32[32,1024]{1,0:T(8,128)S(1)} %slice.43), channel_id=1, source_target_pairs={{0,16},{4,12},{8,24},{12,4},{16,0},{20,28},{24,8},{28,20},{1,17},{... | collective-permute-start | bytes 393224 | tf_op jit(solution)/shard_map/ppermute | solution.py:65
  32.5 17.4 %collective-permute-start.11 = (f32[192,1024]{1,0:T(8,128)S(1)}, f32[192,1024]{1,0:T(8,128)S(1)}, u32[]{:S(2)}, u32[]{:S(2)}) collective-permute-start(f32[192,1024]{1,0:T(8,128)S(1)} %get-tuple-element.72.refs_0_), channel_id=1, source_target_pairs={{0,8},{4,20},{8,0},{12,28},{16,24},{20,4},{24,16},{28,12},{1,9},{5... | collective-permute-start | bytes 2359304 | tf_op jit(solution)/shard_map/ppermute | solution.py:65
  34.4 9.2 %collective-permute-start.7 = (f32[128,1024]{1,0:T(8,128)S(1)}, f32[128,1024]{1,0:T(8,128)}, u32[]{:S(2)}, u32[]{:S(2)}) collective-permute-start(f32[128,1024]{1,0:T(8,128)S(1)} %add.47.mine_ref), channel_id=1, source_target_pairs={{0,4},{4,0},{8,12},{12,8},{16,20},{20,16},{24,28},{28,24},{1,5},{5... | collective-permute-start | bytes 1572872 | tf_op jit(solution)/shard_map/ppermute | solution.py:60
  34.5 15.4 %collective-permute-start.12 = (f32[128,1024]{1,0:T(8,128)}, f32[128,1024]{1,0:T(8,128)S(1)}, u32[]{:S(2)}, u32[]{:S(2)}) collective-permute-start(f32[128,1024]{1,0:T(8,128)} %get-tuple-element.74), channel_id=1, source_target_pairs={{0,4},{4,0},{8,12},{12,8},{16,20},{20,16},{24,28},{28,24},{1,5},{5... | collective-permute-start | bytes 1572872 | tf_op jit(solution)/shard_map/ppermute | solution.py:60
  35.6 13.4 %collective-permute-start.5 = (f32[32,256]{1,0:T(8,128)}, f32[32,256]{1,0:T(8,128)}, u32[]{:S(2)}, u32[]{:S(2)}) collective-permute-start(f32[32,256]{1,0:T(8,128)} %get-tuple-element.102), channel_id=1, source_target_pairs={{0,3},{4,7},{8,11},{12,15},{16,19},{20,23},{24,27},{28,31}} | collective-permute-start | bytes 98312 | tf_op jit(solution)/shard_map/ppermute | solution.py:516
  41.7 7.3 %collective-permute-start.9 = (f32[32,256]{1,0:T(8,128)}, f32[32,256]{1,0:T(8,128)}, u32[]{:S(2)}, u32[]{:S(2)}) collective-permute-start(f32[32,256]{1,0:T(8,128)} %get-tuple-element.103), channel_id=1, source_target_pairs={{0,1},{1,2},{2,3},{4,5},{5,6},{6,7},{8,9},{9,10},{10,11},{12,13},{... | collective-permute-start | bytes 98312 | tf_op jit(solution)/shard_map/ppermute | solution.py:516
  43.6 5.5 %collective-permute-start.8 = (f32[32,256]{1,0:T(8,128)}, f32[32,256]{1,0:T(8,128)}, u32[]{:S(2)}, u32[]{:S(2)}) collective-permute-start(f32[32,256]{1,0:T(8,128)} %get-tuple-element.104), channel_id=1, source_target_pairs={{0,2},{1,3},{4,6},{5,7},{8,10},{9,11},{12,14},{13,15},{16,18},{17,... | collective-permute-start | bytes 98312 | tf_op jit(solution)/shard_map/ppermute | solution.py:516
  45.5 39.6 %copy-start.1 = (f32[2,256,32]{1,2,0:T(8,128)S(1)}, f32[2,256,32]{1,2,0:T(8,128)}, u32[]{:S(2)}) copy-start(f32[2,256,32]{1,2,0:T(8,128)} %param.7) | copy-start | bytes 196612
  50.7 15.2 %collective-permute-start.16 = (f32[160,1024]{1,0:T(8,128)S(1)}, f32[160,1024]{1,0:T(8,128)S(1)}, u32[]{:S(2)}, u32[]{:S(2)}) collective-permute-start(f32[160,1024]{1,0:T(8,128)S(1)} %get-tuple-element.79.refs_0_), channel_id=1, source_target_pairs={{0,16},{4,12},{8,24},{12,4},{16,0},{20,28},{24,8},{28,20},{1,17},{... | collective-permute-start | bytes 1966088 | tf_op jit(solution)/shard_map/ppermute | solution.py:65
  51.1 14.6 %collective-permute-start.17 = (f32[128,1024]{1,0:T(8,128)S(1)}, f32[128,1024]{1,0:T(8,128)S(1)}, u32[]{:S(2)}, u32[]{:S(2)}) collective-permute-start(f32[128,1024]{1,0:T(8,128)S(1)} %get-tuple-element.81.refs_3_), channel_id=1, source_target_pairs={{0,8},{4,20},{8,0},{12,28},{16,24},{20,4},{24,16},{28,12},{1,9},{5... | collective-permute-start | bytes 1572872 | tf_op jit(solution)/shard_map/ppermute | solution.py:65
  52.0 1.9 %collective-permute-start.13 = (f32[32,256]{1,0:T(8,128)S(1)}, f32[32,256]{1,0:T(8,128)S(1)}, u32[]{:S(2)}, u32[]{:S(2)}) collective-permute-start(f32[32,256]{1,0:T(8,128)S(1)} %get-tuple-element.75), channel_id=1, source_target_pairs={{3,2},{7,6},{11,10},{15,14},{19,18},{23,22},{27,26},{31,30}} | collective-permute-start | bytes 98312 | tf_op jit(solution)/shard_map/ppermute | solution.py:409
  53.2 1.9 %collective-permute-start.15 = (f32[32,512]{1,0:T(8,128)S(1)}, f32[32,512]{1,0:T(8,128)S(1)}, u32[]{:S(2)}, u32[]{:S(2)}) collective-permute-start(f32[32,512]{1,0:T(8,128)S(1)} %rest.4), channel_id=1, source_target_pairs={{3,1},{7,5},{11,9},{15,13},{19,17},{23,21},{27,25},{31,29}} | collective-permute-start | bytes 196616 | tf_op jit(solution)/shard_map/ppermute | solution.py:412
  54.5 0.7 collective-permute-start.14
  66.5 9.2 %collective-permute-start.20 = (f32[128,1024]{1,0:T(8,128)S(1)}, f32[128,1024]{1,0:T(8,128)S(1)}, u32[]{:S(2)}, u32[]{:S(2)}) collective-permute-start(f32[128,1024]{1,0:T(8,128)S(1)} %get-tuple-element.85.refs_0_), channel_id=1, source_target_pairs={{0,16},{4,12},{8,24},{12,4},{16,0},{20,28},{24,8},{28,20},{1,17},{... | collective-permute-start | bytes 1572872 | tf_op jit(solution)/shard_map/ppermute | solution.py:65
  67.5 9.7 %collective-permute-start.21 = (f32[128,1024]{1,0:T(8,128)S(1)}, f32[128,1024]{1,0:T(8,128)S(1)}, u32[]{:S(2)}, u32[]{:S(2)}) collective-permute-start(f32[128,1024]{1,0:T(8,128)S(1)} %get-tuple-element.87.mine_ref), channel_id=1, source_target_pairs={{0,4},{4,0},{8,12},{12,8},{16,20},{20,16},{24,28},{28,24},{1,5},{5... | collective-permute-start | bytes 1572872 | tf_op jit(solution)/shard_map/ppermute | solution.py:60
  68.0 6.8 %collective-permute-start.19 = (f32[32,256]{1,0:T(8,128)S(1)}, f32[32,256]{1,0:T(8,128)S(1)}, u32[]{:S(2)}, u32[]{:S(2)}) collective-permute-start(f32[32,256]{1,0:T(8,128)S(1)} %rest.5), channel_id=1, source_target_pairs={{2,0},{6,4},{10,8},{14,12},{18,16},{22,20},{26,24},{30,28}} | collective-permute-start | bytes 98312 | tf_op jit(solution)/shard_map/ppermute | solution.py:412
  69.3 6.0 %collective-permute-start.18 = (f32[32,256]{1,0:T(8,128)S(1)}, f32[32,256]{1,0:T(8,128)S(1)}, u32[]{:S(2)}, u32[]{:S(2)}) collective-permute-start(f32[32,256]{1,0:T(8,128)S(1)} %get-tuple-element.83), channel_id=1, source_target_pairs={{1,0},{5,4},{9,8},{13,12},{17,16},{21,20},{25,24},{29,28}} | collective-permute-start | bytes 98312 | tf_op jit(solution)/shard_map/ppermute | solution.py:409
  77.1 5.6 %collective-permute-start.23 = (f32[128,1024]{1,0:T(8,128)S(1)}, f32[128,1024]{1,0:T(8,128)S(1)}, u32[]{:S(2)}, u32[]{:S(2)}) collective-permute-start(f32[128,1024]{1,0:T(8,128)S(1)} %get-tuple-element.88.mine_ref), channel_id=1, source_target_pairs={{0,4},{4,0},{8,12},{12,8},{16,20},{20,16},{24,28},{28,24},{1,5},{5... | collective-permute-start | bytes 1572872 | tf_op jit(solution)/shard_map/ppermute | solution.py:60
  78.3 6.1 %collective-permute-start.22 = (f32[32,256]{1,0:T(8,128)S(1)}, f32[32,256]{1,0:T(8,128)S(1)}, u32[]{:S(2)}, u32[]{:S(2)}) collective-permute-start(f32[32,256]{1,0:T(8,128)S(1)} %get-tuple-element.99), channel_id=1, source_target_pairs={{0,3},{1,2},{2,1},{3,0},{4,7},{5,6},{6,5},{7,4},{8,11},{9,10},{10,... | collective-permute-start | bytes 98312 | tf_op jit(solution)/shard_map/ppermute | solution.py:534
  78.4 6.0 %collective-permute-start.25 = (f32[32,256]{1,0:T(8,128)S(1)}, f32[32,256]{1,0:T(8,128)S(1)}, u32[]{:S(2)}, u32[]{:S(2)}) collective-permute-start(f32[32,256]{1,0:T(8,128)S(1)} %get-tuple-element.100), channel_id=1, source_target_pairs={{0,1},{1,0},{2,3},{3,2},{4,5},{5,4},{6,7},{7,6},{8,9},{9,8},{10,11... | collective-permute-start | bytes 98312 | tf_op jit(solution)/shard_map/ppermute | solution.py:534
  78.9 6.2 %collective-permute-start.24 = (f32[32,256]{1,0:T(8,128)S(1)}, f32[32,256]{1,0:T(8,128)S(1)}, u32[]{:S(2)}, u32[]{:S(2)}) collective-permute-start(f32[32,256]{1,0:T(8,128)S(1)} %get-tuple-element.101), channel_id=1, source_target_pairs={{0,2},{1,3},{2,0},{3,1},{4,6},{5,7},{6,4},{7,5},{8,10},{9,11},{10,... | collective-permute-start | bytes 98312 | tf_op jit(solution)/shard_map/ppermute | solution.py:534
  85.6 1.9 %collective-permute-start.26 = (f32[32,256]{1,0:T(8,128)S(1)}, f32[32,256]{1,0:T(8,128)S(1)}, u32[]{:S(2)}, u32[]{:S(2)}) collective-permute-start(f32[32,256]{1,0:T(8,128)S(1)} %get-tuple-element.92), channel_id=1, source_target_pairs={{3,2},{7,6},{11,10},{15,14},{19,18},{23,22},{27,26},{31,30}} | collective-permute-start | bytes 98312 | tf_op jit(solution)/shard_map/ppermute | solution.py:409
  86.9 3.8 %collective-permute-start.28 = (f32[32,512]{1,0:T(8,128)S(1)}, f32[32,512]{1,0:T(8,128)S(1)}, u32[]{:S(2)}, u32[]{:S(2)}) collective-permute-start(f32[32,512]{1,0:T(8,128)S(1)} %rest.6), channel_id=1, source_target_pairs={{3,1},{7,5},{11,9},{15,13},{19,17},{23,21},{27,25},{31,29}} | collective-permute-start | bytes 196616 | tf_op jit(solution)/shard_map/ppermute | solution.py:412
  88.1 2.5 %collective-permute-start.27 = (f32[32,256]{1,0:T(8,128)S(1)}, f32[32,256]{1,0:T(8,128)S(1)}, u32[]{:S(2)}, u32[]{:S(2)}) collective-permute-start(f32[32,256]{1,0:T(8,128)S(1)} %get-tuple-element.94), channel_id=1, source_target_pairs={{2,1},{6,5},{10,9},{14,13},{18,17},{22,21},{26,25},{30,29}} | collective-permute-start | bytes 98312 | tf_op jit(solution)/shard_map/ppermute | solution.py:409
  89.4 11.1 %collective-permute-start.30 = (f32[32,256]{1,0:T(8,128)S(1)}, f32[32,256]{1,0:T(8,128)S(1)}, u32[]{:S(2)}, u32[]{:S(2)}) collective-permute-start(f32[32,256]{1,0:T(8,128)S(1)} %rest.7), channel_id=1, source_target_pairs={{2,0},{6,4},{10,8},{14,12},{18,16},{22,20},{26,24},{30,28}} | collective-permute-start | bytes 98312 | tf_op jit(solution)/shard_map/ppermute | solution.py:412
  91.2 11.9 %collective-permute-start.29 = (f32[32,256]{1,0:T(8,128)S(1)}, f32[32,256]{1,0:T(8,128)S(1)}, u32[]{:S(2)}, u32[]{:S(2)}) collective-permute-start(f32[32,256]{1,0:T(8,128)S(1)} %get-tuple-element.96), channel_id=1, source_target_pairs={{1,0},{5,4},{9,8},{13,12},{17,16},{21,20},{25,24},{29,28}} | collective-permute-start | bytes 98312 | tf_op jit(solution)/shard_map/ppermute | solution.py:409

commit v7 on v6

--- a/solution.py
+++ b/solution.py
@@ -203,43 +203,18 @@
     half, total = band // 2, known.shape[2]
     tables = send_tables(members)
 
-    def body(where_ref, rows_ref, factor_ref, known_ref, keep_ref, send_ref, factor_buf, known_buf, acc_ref, sems, low):
-        finish = put_band(where_ref, rows_ref, factor_ref, 1, 0, keep_ref, send_ref, 0, half, low)
+    def body(where_ref, rows_ref, factor_ref, known_ref, keep_ref, send_ref, factor_buf, known_buf, acc_ref, sems, low, top):
         accumulate(where_ref, rows_ref, factor_ref, known_ref, factor_buf, known_buf, acc_ref, sems, 0)
-        in_send_order(where_ref, acc_ref, keep_ref, send_ref, half, tables)
-        finish()
-
-    rows = half + total // 2
-    scratch = partial_scratch(slots, band, width, total) + [pltpu.SemaphoreType.DMA((2,))]
+        finish_low = put_band(where_ref, rows_ref, factor_ref, 1, 0, keep_ref, send_ref, 0, half, low)
+        finish_top = put_band(where_ref, rows_ref, factor_ref, 0, 0, keep_ref, send_ref, half, half, top)
+        in_send_order(where_ref, acc_ref, keep_ref, send_ref, band, tables)
+        finish_low()
+        finish_top()
+
+    rows = band + total // 2
+    scratch = partial_scratch(slots, band, width, total) + [pltpu.SemaphoreType.DMA((2,))] * 2
     args = (where, slot_row, factor_rows, known)
     return call(body, (shape(rows, width),) * 2, (SMEM, SMEM, HBM, HBM), args, "pack_rest", scratch)
-
-
-def top_band(where, slot_row, factor_rows):
-    slots, _, band, width = factor_rows.shape
-    half = band // 2
-
-    def body(where_ref, rows_ref, factor_ref, keep_ref, send_ref, tile_ref, sem):
-        slot = owned_slot(where_ref, rows_ref, 0, slots)
-        core = where_ref[0] & 1
-
-        @pl.when(slot >= 0)
-        def _():
-            copy = pltpu.make_async_copy(factor_ref.at[slot, 0], tile_ref, sem)
-            copy.start()
-            copy.wait()
-            invert_diagonal(tile_ref, where_ref[1], range(width // band), band)
-            keep_ref[...] = tile_ref[pl.ds(pl.multiple_of(core * half, half), half), :]
-            send_ref[...] = tile_ref[pl.ds(pl.multiple_of((1 - core) * half, half), half), :]
-
-        @pl.when(slot < 0)
-        def _():
-            keep_ref[...] = jnp.zeros_like(keep_ref)
-            send_ref[...] = jnp.zeros_like(send_ref)
-
-    out = (shape(half, width), shape(half, width))
-    scratch = [pltpu.VMEM((band, width), F32), pltpu.SemaphoreType.DMA(())]
-    return call(body, out, (SMEM, SMEM, HBM), (where, slot_row, factor_rows), "top_band", scratch)
 
 
 def after(value, *others):
@@ -273,6 +248,21 @@
     add, out = pack_parts(*pack[1:])
     args = pack_inputs(*pack)
     return call(add, out, (VMEM,) * len(args), args, "pack_step")
+
+
+def unpack_first(keep, got, half):
+    rows, width = keep.shape
+    band = 2 * half
+    go = (rows - band) // 2
+
+    def body(keep_ref, got_ref, low_ref, sum_ref, top_ref):
+        low_ref[:half, :] = keep_ref[:half, :] + got_ref[:half, :]
+        top_ref[...] = keep_ref[half:band, :] + got_ref[half:band, :]
+        sum_ref[...] = keep_ref[band : band + go, :] + got_ref[band : band + go, :]
+        low_ref[half:, :] = keep_ref[band + go :, :] + got_ref[band + go :, :]
+
+    out = (shape(half + go, width), shape(go, width), shape(half, width))
+    return call(body, out, (VMEM, VMEM), (keep, got), "unpack_first")
 
 
 def inverse_of(block):
@@ -419,8 +409,8 @@
     def __init__(self, pack, got, top, got_top, steps, bands, members):
         self.pack, self.got, self.top, self.got_top = pack, got, top, got_top
         self.steps, self.members = steps, members
-        self.low_at = [bands - 2 - 2 * (steps - 1 - step) for step in range(steps)]
-        self.top_at = [0] + [bands - steps + step for step in range(steps)]
+        self.low_at = [bands - 1 - 2 * (steps - 1 - step) for step in range(steps)]
+        self.top_at = [bands - steps + step for step in range(steps - 1)]
 
     def take(self, index):
         taken = ()
@@ -440,8 +430,11 @@
             self.got = swap_chip(tiles, self.members, step) if step < self.steps else swap_core(tiles, self.members)
         if outs:
             (self.top,) = outs
-            step = self.top_at.index(self.index)
-            self.got_top = swap_chip(self.top, self.members, step) if step < self.steps else swap_core(self.top, self.members)
+            self.got_top = swap_chip(self.top, self.members, self.top_at.index(self.index) + 1)
+
+    def last_tile(self, where, ready, bands):
+        (tile,) = pack_step(self.top, None, 0, after(self.got_top, ready), self.top.shape[0], True)
+        return join_halves(where, tile, swap_core(tile, self.members), 0, tile.shape[0], range(bands))
 
 
 def couple(where, sums, solved, mine, other, bands):
@@ -490,46 +483,44 @@
     keep_one, send_one = partial_one(after(where, tile_one), slot_row, factor_rows, known, members)
     got_sum = swap_core(send_one, members)
     tile_one = tile_one + after(got_tile, keep_one)
-    got_tile = swap_chip(tile_one, members, 1)
     sum_one = keep_one + after(got_sum, tile_one)
-    keep = send = top = send_top = got_pack = got_top = None
+    keep = send = got_pack = got_tile = None
     for stage in range(stages):
         rows = sum_one.shape[0] // 2
         got_sum = swap_chip(sum_one[rows:], members, stage)
         if stage == 0:
             keep, send = pack_rest(after(where, sum_one), slot_row, factor_rows, known, members)
             got_sum = after(got_sum, keep)
-        if stage == 1:
-            top, send_top = top_band(after(where, sum_one), slot_row, factor_rows)
-            got_sum = after(got_sum, top)
         sum_one = sum_one[:rows] + got_sum
         if stage == 0:
             got_pack = swap_core(after(send, sum_one), members)
-        if stage < stages - 1:
-            tile_one = tile_one + (after(got_tile, sum_one) if stage < stages - 2 else got_tile)
-            got_tile = swap_chip(tile_one, members, stage + 2) if stage < stages - 2 else None
-    got_top = swap_core(send_top, members)
 
     got_up = []
     for shift in range(bands - 1, 0, -1):
         piece = own_band(sum_one, jnp.minimum(place + shift, bands - 1), band)
         got_up.append(lax.ppermute(piece, "ct", [(i, i + shift) for i in range(bands - shift)]))
 
+    for stage in range(1, stages):
+        got_tile = swap_chip(after(tile_one, sum_one), members, stage)
+        tile_one = tile_one + after(got_tile, *got_up)
     other = swap_core(tile_one, members)
 
-    tiles, sums = pack_step(keep, keep, half, after(got_pack, sum_one), half, False)
+    tiles, sums, top = unpack_first(keep, after(got_pack, sum_one), half)
+    tiles = after(tiles, tile_one)
     got_pack = swap_chip(tiles, members, 0)
+    got_top = swap_chip(after(top, tiles), members, 0)
+
     tile_one = join_halves(after(where, sum_one), tile_one, other, 0, half, range(bands))
     packs = Packs((tiles, sums, half), got_pack, top, got_top, stages, bands, members)
     base = rhs[1].T - own_band(sum_one, place, band)
     for piece in got_up:
-        base = base - after(piece, tile_one)
+        base = base - piece
     solved_one = sweep(where, base, tile_one, sum_one, bands, packs)
 
     low, sums, _ = packs.pack
     pieces = (couple if aligned else couple_plain)(where, sums, solved_one, low, packs.got, bands)
     base = rhs[0].T - pieces[0]
-    tile_zero = join_halves(where, packs.top, packs.got_top, 0, half, ())
+    tile_zero = packs.last_tile(where, pieces, bands)
     for mask in range(bands - 1, 0, -1):
         got = lax.ppermute(pieces[mask], "ct", [(i, i ^ mask) for i in range(bands)])
         base = base - after(got, tile_zero)

time: 106 us -> 110 us (1.038)
  Pallas kernels: 25.4 us -> 28.1 us
  waiting for transfers between devices: 39 us -> 41 us
    ppermute x4, waiting for transfers between devices: 12.2 us -> 5.19 us  [sweep(): fars.append(lax.ppermute(rest, 'ct', [(stage, stage - 2)]))]
    ppermute x6, waiting for transfers between devices: 3.19 us -> 7.5 us  [sweep(): near = lax.ppermute(update, 'ct', [(stage, stage - 1)])]
    ppermute x8, waiting for transfers between devices: 20.4 us -> 23.7 us  [swap_chip(): lax.ppermute(value, 'rt', [(i, i ^ 1 << orders[i & 1][stage]) for i in ra...]
    pallas_call x20, Pallas kernels: 25.4 us -> 28.1 us  [call(): pl.pallas_call(body, out_shape=out, in_specs=list(specs), out_specs=tuple...]
    ppermute x3, waiting for transfers between devices: 1.64 us -> 0.01 us  [shards(): lax.ppermute(pieces[mask], 'ct', [(i, i ^ mask) for i in range(bands)])]
    ppermute x7 -> x6, waiting for transfers between devices: 1.55 us -> 3.14 us  [swap_core(): return lax.ppermute(value, 'rt', [(i, i ^ 1) for i in range(members)])]
    ppermute x3, waiting for transfers between devices: 0.01 us -> 1.54 us  [shards(): lax.ppermute(piece, 'ct', [(i, i + shift) for i in range(bands - shift)])]
    unnamed x4 -> x14, local copies, waits for them, and re-layouts: 0.66 us -> 1.89 us
  transfers between devices with their start and end apart: 31 -> 30, of which waited for: 12 -> 12; matrix products, arithmetic and copies ran while one was open for 2% -> 1% of each run, Pallas kernels for 20% -> 19%
where the time goes in v7:
time: 110 us
  waiting for transfers between devices  41 us (37%)
  starting transfers between devices  36.5 us (33%)
  Pallas kernels  28.1 us (26%)
  local copies, waits for them, and re-layouts  1.95 us (2%)
  other arithmetic  1.84 us (2%)
    pallas_call x20, Pallas kernels, call(): pl.pallas_call(body, out_shape=out, in_specs=list(specs), out_specs=tuple...  28.1 us
    ppermute x8, waiting for transfers between devices, swap_chip(): lax.ppermute(value, 'rt', [(i, i ^ 1 << orders[i & 1][stage]) for i in ra...  23.7 us
    ppermute x8, starting transfers between devices, swap_chip(): lax.ppermute(value, 'rt', [(i, i ^ 1 << orders[i & 1][stage]) for i in ra...  12.9 us
    ppermute x3, starting transfers between devices, shards(): lax.ppermute(piece, 'ct', [(i, i + shift) for i in range(bands - shift)])  9.27 us
    ppermute x6, waiting for transfers between devices, sweep(): near = lax.ppermute(update, 'ct', [(stage, stage - 1)])  7.5 us
    ppermute x6, starting transfers between devices, sweep(): near = lax.ppermute(update, 'ct', [(stage, stage - 1)])  5.24 us
    ppermute x4, waiting for transfers between devices, sweep(): fars.append(lax.ppermute(rest, 'ct', [(stage, stage - 2)]))  5.19 us
    ppermute x3, starting transfers between devices, shards(): lax.ppermute(pieces[mask], 'ct', [(i, i ^ mask) for i in range(bands)])  4.45 us
  transfers between devices with their start and end apart: 30, of which 12 were waited for; matrix products, arithmetic and copies ran while one was open for 1% of the time, Pallas kernels for 19%

profile of v7, /device:TPU:0, one launch (start us, length us, event | category | flops | bytes accessed | tf_op | source)
XLA Modules:
  0.0 110.0 jit_solution(13454851270856961288)
XLA Ops:
  0.0 0.1 pad_add_fusion.where_ref
  0.1 0.7 copy-done.2
  0.7 1.8 %first_band.1 = (f32[128,1024]{1,0:T(8,128)S(1)}, f32[128,1024]{1,0:T(8,128)S(1)}) custom-call(s32[2]{0:T(128)S(1)} %pad_add_fusion.where_ref, s32[48]{0:T(128)S(1)} %copy-done.2, f32[6,2,256,1024]{3,2,1,0:T(8,128)} %factor_ref.5), custom_call_target="tpu_custom_call" | custom-call | tf_op jit(solution)/shard_map/first_band/pallas_call | solution.py:23
  2.5 0.1 collective-permute-start
  2.6 1.9 %collective-permute-done = f32[128,1024]{1,0:T(8,128)S(1)} collective-permute-done((f32[128,1024]{1,0:T(8,128)S(1)}, f32[128,1024]{1,0:T(8,128)S(1)}, u32[]{:S(2)}, u32[]{:S(2)}) %collective-permute-start) | collective-permute-done | bytes 524320 | tf_op jit(solution)/shard_map/ppermute | solution.py:60
  4.5 1.9 %collective-permute-start.2 = (f32[128,1024]{1,0:T(8,128)S(1)}, f32[128,1024]{1,0:T(8,128)S(1)}, u32[]{:S(2)}, u32[]{:S(2)}) collective-permute-start(f32[128,1024]{1,0:T(8,128)S(1)} %add.39), channel_id=1, source_target_pairs={{0,8},{4,20},{8,0},{12,28},{16,24},{20,4},{24,16},{28,12},{1,9},{5... | collective-permute-start | bytes 1572872 | tf_op jit(solution)/shard_map/ppermute | solution.py:65
  6.4 3.3 %partial_one.1 = (f32[128,1024]{1,0:T(8,128)S(1)}, f32[128,1024]{1,0:T(8,128)S(1)}) custom-call(s32[2]{0:T(128)S(1)} %pad_add_fusion.where_ref, s32[48]{0:T(128)S(1)} %copy-done.2, f32[6,2,256,1024]{3,2,1,0:T(8,128)} %factor_ref.5, f32[6,256,256]{2,1,0:T(8,128)} %known_ref.3), custom_call_target="tpu_custom_call" | custom-call | tf_op jit(solution)/shard_map/partial_one/pallas_call | solution.py:23
  9.7 0.6 collective-permute-start.1
  10.3 3.5 %collective-permute-done.2 = f32[128,1024]{1,0:T(8,128)S(1)} collective-permute-done((f32[128,1024]{1,0:T(8,128)S(1)}, f32[128,1024]{1,0:T(8,128)S(1)}, u32[]{:S(2)}, u32[]{:S(2)}) %collective-permute-start.2) | collective-permute-done | bytes 524320 | tf_op jit(solution)/shard_map/ppermute | solution.py:65
  14.0 1.9 %collective-permute-start.3 = (f32[64,1024]{1,0:T(8,128)S(1)}, f32[64,1024]{1,0:T(8,128)S(1)}, u32[]{:S(2)}, u32[]{:S(2)}) collective-permute-start(f32[64,1024]{1,0:T(8,128)S(1)} %slice.41), channel_id=1, source_target_pairs={{0,8},{4,20},{8,0},{12,28},{16,24},{20,4},{24,16},{28,12},{1,9},{5... | collective-permute-start | bytes 786440 | tf_op jit(solution)/shard_map/ppermute | solution.py:65
  15.8 5.7 %pack_rest.1 = (f32[384,1024]{1,0:T(8,128)S(1)}, f32[384,1024]{1,0:T(8,128)}) custom-call(s32[2]{0:T(128)S(1)} %pad_add_fusion.where_ref, s32[48]{0:T(128)S(1)} %copy-done.2, f32[6,2,256,1024]{3,2,1,0:T(8,128)} %factor_ref.5, f32[6,256,256]{2,1,0:T(8,128)} %known_ref.3), custom_call_target="tpu_custom_call" | custom-call | tf_op jit(solution)/shard_map/pack_rest/pallas_call | solution.py:23
  21.7 2.4 %collective-permute-start.4 = (f32[32,1024]{1,0:T(8,128)S(1)}, f32[32,1024]{1,0:T(8,128)S(1)}, u32[]{:S(2)}, u32[]{:S(2)}) collective-permute-start(f32[32,1024]{1,0:T(8,128)S(1)} %slice.43), channel_id=1, source_target_pairs={{0,16},{4,12},{8,24},{12,4},{16,0},{20,28},{24,8},{28,20},{1,17},{... | collective-permute-start | bytes 393224 | tf_op jit(solution)/shard_map/ppermute | solution.py:65
  24.1 2.9 %collective-permute-done.4 = f32[32,1024]{1,0:T(8,128)S(1)} collective-permute-done((f32[32,1024]{1,0:T(8,128)S(1)}, f32[32,1024]{1,0:T(8,128)S(1)}, u32[]{:S(2)}, u32[]{:S(2)}) %collective-permute-start.4) | collective-permute-done | bytes 131104 | tf_op jit(solution)/shard_map/ppermute | solution.py:65
  27.1 2.1 %collective-permute-start.8 = (f32[128,1024]{1,0:T(8,128)S(1)}, f32[128,1024]{1,0:T(8,128)S(1)}, u32[]{:S(2)}, u32[]{:S(2)}) collective-permute-start(f32[128,1024]{1,0:T(8,128)S(1)} %add.40), channel_id=1, source_target_pairs={{0,16},{4,12},{8,24},{12,4},{16,0},{20,28},{24,8},{28,20},{1,17},{... | collective-permute-start | bytes 1572872 | tf_op jit(solution)/shard_map/ppermute | solution.py:65
  29.2 5.5 %collective-permute-start.5 = (f32[32,256]{1,0:T(8,128)S(1)}, f32[32,256]{1,0:T(8,128)S(1)}, u32[]{:S(2)}, u32[]{:S(2)}) collective-permute-start(f32[32,256]{1,0:T(8,128)S(1)} %get-tuple-element.96), channel_id=1, source_target_pairs={{0,3},{4,7},{8,11},{12,15},{16,19},{20,23},{24,27},{28,31}} | collective-permute-start | bytes 98312 | tf_op jit(solution)/shard_map/ppermute | solution.py:501
  34.7 1.3 %collective-permute-start.6 = (f32[32,256]{1,0:T(8,128)S(1)}, f32[32,256]{1,0:T(8,128)S(1)}, u32[]{:S(2)}, u32[]{:S(2)}) collective-permute-start(f32[32,256]{1,0:T(8,128)S(1)} %get-tuple-element.98), channel_id=1, source_target_pairs={{0,2},{1,3},{4,6},{5,7},{8,10},{9,11},{12,14},{13,15},{16,18},{17,... | collective-permute-start | bytes 98312 | tf_op jit(solution)/shard_map/ppermute | solution.py:501
  36.0 2.5 %collective-permute-start.7 = (f32[32,256]{1,0:T(8,128)S(1)}, f32[32,256]{1,0:T(8,128)S(1)}, u32[]{:S(2)}, u32[]{:S(2)}) collective-permute-start(f32[32,256]{1,0:T(8,128)S(1)} %get-tuple-element.97), channel_id=1, source_target_pairs={{0,1},{1,2},{2,3},{4,5},{5,6},{6,7},{8,9},{9,10},{10,11},{12,13},{... | collective-permute-start | bytes 98312 | tf_op jit(solution)/shard_map/ppermute | solution.py:501
  38.5 1.5 %collective-permute-done.7 = f32[32,256]{1,0:T(8,128)S(1)} collective-permute-done((f32[32,256]{1,0:T(8,128)S(1)}, f32[32,256]{1,0:T(8,128)S(1)}, u32[]{:S(2)}, u32[]{:S(2)}) %collective-permute-start.7) | collective-permute-done | bytes 32800 | tf_op jit(solution)/shard_map/ppermute | solution.py:501
  40.1 0.5 copy-done.6
  40.6 1.6 %unpack_first.1 = (f32[192,1024]{1,0:T(8,128)S(1)}, f32[64,1024]{1,0:T(8,128)S(1)}, f32[128,1024]{1,0:T(8,128)S(1)}) custom-call(f32[384,1024]{1,0:T(8,128)S(1)} %get-tuple-element.57.keep_ref, f32[384,1024]{1,0:T(8,128)} %collective-permute-done.11.got_ref), custom_call_target="tpu_custom_call" | custom-call | tf_op jit(solution)/shard_map/unpack_first/pallas_call | solution.py:23
  42.2 0.7 copy-done
  42.9 1.1 %collective-permute-start.12 = (f32[192,1024]{1,0:T(8,128)S(1)}, f32[192,1024]{1,0:T(8,128)S(1)}, u32[]{:S(2)}, u32[]{:S(2)}) collective-permute-start(f32[192,1024]{1,0:T(8,128)S(1)} %get-tuple-element.68.refs_0_), channel_id=1, source_target_pairs={{0,8},{4,20},{8,0},{12,28},{16,24},{20,4},{24,16},{28,12},{1,9},{5... | collective-permute-start | bytes 2359304 | tf_op jit(solution)/shard_map/ppermute | solution.py:65
  44.1 0.8 fusion.6.base_ref
  44.9 1.1 collective-permute-done.9.other_ref
  46.0 3.2 %join.2.tile_ref = f32[256,1024]{1,0:T(8,128)S(1)} custom-call(s32[2]{0:T(128)S(1)} %pad_add_fusion.where_ref, f32[128,1024]{1,0:T(8,128)S(1)} %add.51.mine_ref, f32[128,1024]{1,0:T(8,128)S(1)} %collective-permute-done.9.other_ref), custom_call_target="tpu_custom_call" | custom-call | tf_op jit(solution)/shard_map/join/pallas_call | solution.py:23
  49.2 0.6 stage.8
  49.7 0.7 collective-permute-start.10
  50.4 4.5 %collective-permute-done.12.refs_2_ = f32[192,1024]{1,0:T(8,128)S(1)} collective-permute-done((f32[192,1024]{1,0:T(8,128)S(1)}, f32[192,1024]{1,0:T(8,128)S(1)}, u32[]{:S(2)}, u32[]{:S(2)}) %collective-permute-start.12) | collective-permute-done | bytes 786464 | tf_op jit(solution)/shard_map/ppermute | solution.py:65
  54.9 0.6 stage.9
  55.6 0.1 collective-permute-start.18
  55.7 1.6 %collective-permute-start.15 = (f32[128,1024]{1,0:T(8,128)S(1)}, f32[128,1024]{1,0:T(8,128)S(1)}, u32[]{:S(2)}, u32[]{:S(2)}) collective-permute-start(f32[128,1024]{1,0:T(8,128)S(1)} %get-tuple-element.73.refs_0_), channel_id=1, source_target_pairs={{0,8},{4,20},{8,0},{12,28},{16,24},{20,4},{24,16},{28,12},{1,9},{5... | collective-permute-start | bytes 1572872 | tf_op jit(solution)/shard_map/ppermute | solution.py:65
  57.2 0.5 rest.4
  57.8 0.7 collective-permute-start.14
  58.5 0.7 collective-permute-start.13
  59.1 0.6 rest.5
  59.7 1.3 %collective-permute-start.17 = (f32[32,256]{1,0:T(8,128)S(1)}, f32[32,256]{1,0:T(8,128)S(1)}, u32[]{:S(2)}, u32[]{:S(2)}) collective-permute-start(f32[32,256]{1,0:T(8,128)S(1)} %rest.5), channel_id=1, source_target_pairs={{2,0},{6,4},{10,8},{14,12},{18,16},{22,20},{26,24},{30,28}} | collective-permute-start | bytes 98312 | tf_op jit(solution)/shard_map/ppermute | solution.py:402
  61.0 6.6 %collective-permute-done.15.refs_1_ = f32[128,1024]{1,0:T(8,128)S(1)} collective-permute-done((f32[128,1024]{1,0:T(8,128)S(1)}, f32[128,1024]{1,0:T(8,128)S(1)}, u32[]{:S(2)}, u32[]{:S(2)}) %collective-permute-start.15) | collective-permute-done | bytes 524320 | tf_op jit(solution)/shard_map/ppermute | solution.py:65
  67.6 0.6 stage.10
  68.2 1.3 %collective-permute-start.16 = (f32[32,256]{1,0:T(8,128)S(1)}, f32[32,256]{1,0:T(8,128)S(1)}, u32[]{:S(2)}, u32[]{:S(2)}) collective-permute-start(f32[32,256]{1,0:T(8,128)S(1)} %get-tuple-element.74), channel_id=1, source_target_pairs={{1,0},{5,4},{9,8},{13,12},{17,16},{21,20},{25,24},{29,28}} | collective-permute-start | bytes 98312 | tf_op jit(solution)/shard_map/ppermute | solution.py:399
  69.6 4.5 %collective-permute-done.16.near_ref = f32[32,256]{1,0:T(8,128)S(1)} collective-permute-done((f32[32,256]{1,0:T(8,128)S(1)}, f32[32,256]{1,0:T(8,128)S(1)}, u32[]{:S(2)}, u32[]{:S(2)}) %collective-permute-start.16) | collective-permute-done | bytes 32800 | tf_op jit(solution)/shard_map/ppermute | solution.py:399
  74.1 1.4 %stage.11 = (f32[32,256]{1,0:T(8,128)S(1)}, f32[32,256]{1,0:T(8,128)}, f32[128,1024]{1,0:T(8,128)S(1)}, f32[32,1024]{1,0:T(8,128)S(1)}) custom-call(s32[2]{0:T(128)S(1)} %pad_add_fusion.where_ref, f32[32,256]{1,0:T(8,128)S(1)} %fusion.6.base_ref, f32[256,1024]{1,0:T(8,128)S(1)} %join.2.tile_ref, f32[32,1024]{1,0:T(8,128)S(1)} %slice_add_fusion.1.add_ref, ...), custom_call_target="tpu_custom_call" | custom-call | tf_op jit(solution)/shard_map/stage/pallas_call | solution.py:23
  75.5 1.7 %collective-permute-start.21 = (f32[128,1024]{1,0:T(8,128)S(1)}, f32[128,1024]{1,0:T(8,128)S(1)}, u32[]{:S(2)}, u32[]{:S(2)}) collective-permute-start(f32[128,1024]{1,0:T(8,128)S(1)} %get-tuple-element.81.tiles_ref), channel_id=1, source_target_pairs={{0,16},{4,12},{8,24},{12,4},{16,0},{20,28},{24,8},{28,20},{1,17},{... | collective-permute-start | bytes 1572872 | tf_op jit(solution)/shard_map/ppermute | solution.py:65
  77.3 0.2 collective-permute-done.19.other_ref
  77.4 1.2 %couple.1 = f32[4,32,256]{2,1,0:T(8,128)S(1)} custom-call(s32[2]{0:T(128)S(1)} %pad_add_fusion.where_ref, f32[32,1024]{1,0:T(8,128)S(1)} %get-tuple-element.78.sums_ref, f32[32,256]{1,0:T(8,128)S(1)} %get-tuple-element.79.solved_ref, f32[128,1024]{1,0:T(8,128)S(1)} %get-tuple-element.80.mine_ref, f32[128,1024]{1,0:T(8,128)S(1)} %collective-permute-done.19.other_ref), custom_call_target="tpu_custom_call" | custom-call | tf_op jit(solution)/shard_map/couple/pallas_call | solution.py:23
  78.6 6.1 %collective-permute-done.21.got_ref = f32[128,1024]{1,0:T(8,128)S(1)} collective-permute-done((f32[128,1024]{1,0:T(8,128)S(1)}, f32[128,1024]{1,0:T(8,128)S(1)}, u32[]{:S(2)}, u32[]{:S(2)}) %collective-permute-start.21) | collective-permute-done | bytes 524320 | tf_op jit(solution)/shard_map/ppermute | solution.py:65
  84.7 0.1 collective-permute-start.22
  84.8 0.1 collective-permute-start.20
  84.9 1.0 collective-permute-start.23
  85.9 3.4 %collective-permute-start.24 = (f32[32,256]{1,0:T(8,128)S(1)}, f32[32,256]{1,0:T(8,128)S(1)}, u32[]{:S(2)}, u32[]{:S(2)}) collective-permute-start(f32[32,256]{1,0:T(8,128)S(1)} %get-tuple-element.94), channel_id=1, source_target_pairs={{0,1},{1,0},{2,3},{3,2},{4,5},{5,4},{6,7},{7,6},{8,9},{9,8},{10,11... | collective-permute-start | bytes 98312 | tf_op jit(solution)/shard_map/ppermute | solution.py:525
  89.3 3.0 %join.3.tile_ref = f32[256,1024]{1,0:T(8,128)S(1)} custom-call(s32[2]{0:T(128)S(1)} %pad_add_fusion.where_ref, f32[128,1024]{1,0:T(8,128)S(1)} %pack_step.1.mine_ref, f32[128,1024]{1,0:T(8,128)S(1)} %collective-permute-done.22.other_ref), custom_call_target="tpu_custom_call" | custom-call | tf_op jit(solution)/shard_map/join/pallas_call | solution.py:23
  92.4 0.6 stage.12
  92.9 0.7 collective-permute-start.25
  93.6 0.6 rest.6
  94.2 0.7 collective-permute-start.27
  94.8 0.6 stage.13
  95.4 0.7 collective-permute-start.26
  96.1 0.6 rest.7
  96.6 1.3 %collective-permute-start.29 = (f32[32,256]{1,0:T(8,128)S(1)}, f32[32,256]{1,0:T(8,128)S(1)}, u32[]{:S(2)}, u32[]{:S(2)}) collective-permute-start(f32[32,256]{1,0:T(8,128)S(1)} %rest.7), channel_id=1, source_target_pairs={{2,0},{6,4},{10,8},{14,12},{18,16},{22,20},{26,24},{30,28}} | collective-permute-start | bytes 98312 | tf_op jit(solution)/shard_map/ppermute | solution.py:402
  98.0 0.6 stage.14
  98.5 1.3 %collective-permute-start.28 = (f32[32,256]{1,0:T(8,128)S(1)}, f32[32,256]{1,0:T(8,128)S(1)}, u32[]{:S(2)}, u32[]{:S(2)}) collective-permute-start(f32[32,256]{1,0:T(8,128)S(1)} %get-tuple-element.90), channel_id=1, source_target_pairs={{1,0},{5,4},{9,8},{13,12},{17,16},{21,20},{25,24},{29,28}} | collective-permute-start | bytes 98312 | tf_op jit(solution)/shard_map/ppermute | solution.py:399
  99.8 5.2 %collective-permute-done.29.far_ref = f32[32,256]{1,0:T(8,128)S(1)} collective-permute-done((f32[32,256]{1,0:T(8,128)S(1)}, f32[32,256]{1,0:T(8,128)S(1)}, u32[]{:S(2)}, u32[]{:S(2)}) %collective-permute-start.29) | collective-permute-done | bytes 32800 | tf_op jit(solution)/shard_map/ppermute | solution.py:402
  105.0 3.0 %collective-permute-done.28.near_ref = f32[32,256]{1,0:T(8,128)S(1)} collective-permute-done((f32[32,256]{1,0:T(8,128)S(1)}, f32[32,256]{1,0:T(8,128)S(1)}, u32[]{:S(2)}, u32[]{:S(2)}) %collective-permute-start.28) | collective-permute-done | bytes 32800 | tf_op jit(solution)/shard_map/ppermute | solution.py:399
  108.0 1.4 %stage.15 = (f32[32,256]{1,0:T(8,128)S(1)}, f32[32,256]{1,0:T(8,128)}) custom-call(s32[2]{0:T(128)S(1)} %pad_add_fusion.where_ref, f32[32,256]{1,0:T(8,128)S(1)} %fusion.3.base_ref, f32[256,1024]{1,0:T(8,128)S(1)} %join.3.tile_ref, f32[32,1024]{1,0:T(8,128)S(1)} %broadcast_2_far_ref_add_ref.2.far_ref.add_ref, ...), custom_call_target="tpu_custom_call" | custom-call | tf_op jit(solution)/shard_map/stage/pallas_call | solution.py:23
  109.3 0.6 pad_maximum_fusion
  (46 shorter events, 0.6 us)
Async XLA Ops:
  0.1 0.7 copy-start.2
  2.5 2.0 %collective-permute-start = (f32[128,1024]{1,0:T(8,128)S(1)}, f32[128,1024]{1,0:T(8,128)S(1)}, u32[]{:S(2)}, u32[]{:S(2)}) collective-permute-start(f32[128,1024]{1,0:T(8,128)S(1)} %get-tuple-element.50), channel_id=1, source_target_pairs={{0,4},{4,0},{8,12},{12,8},{16,20},{20,16},{24,28},{28,24},{1,5},{5... | collective-permute-start | bytes 1572872 | tf_op jit(solution)/shard_map/ppermute | solution.py:60
  4.5 9.2 %collective-permute-start.2 = (f32[128,1024]{1,0:T(8,128)S(1)}, f32[128,1024]{1,0:T(8,128)S(1)}, u32[]{:S(2)}, u32[]{:S(2)}) collective-permute-start(f32[128,1024]{1,0:T(8,128)S(1)} %add.39), channel_id=1, source_target_pairs={{0,8},{4,20},{8,0},{12,28},{16,24},{20,4},{24,16},{28,12},{1,9},{5... | collective-permute-start | bytes 1572872 | tf_op jit(solution)/shard_map/ppermute | solution.py:65
  9.7 4.1 %collective-permute-start.1 = (f32[128,1024]{1,0:T(8,128)S(1)}, f32[128,1024]{1,0:T(8,128)S(1)}, u32[]{:S(2)}, u32[]{:S(2)}) collective-permute-start(f32[128,1024]{1,0:T(8,128)S(1)} %get-tuple-element.53), channel_id=1, source_target_pairs={{0,4},{4,0},{8,12},{12,8},{16,20},{20,16},{24,28},{28,24},{1,5},{5... | collective-permute-start | bytes 1572872 | tf_op jit(solution)/shard_map/ppermute | solution.py:60
  14.0 7.5 %collective-permute-start.3 = (f32[64,1024]{1,0:T(8,128)S(1)}, f32[64,1024]{1,0:T(8,128)S(1)}, u32[]{:S(2)}, u32[]{:S(2)}) collective-permute-start(f32[64,1024]{1,0:T(8,128)S(1)} %slice.41), channel_id=1, source_target_pairs={{0,8},{4,20},{8,0},{12,28},{16,24},{20,4},{24,16},{28,12},{1,9},{5... | collective-permute-start | bytes 786440 | tf_op jit(solution)/shard_map/ppermute | solution.py:65
  21.6 19.1 %collective-permute-start.11 = (f32[384,1024]{1,0:T(8,128)}, f32[384,1024]{1,0:T(8,128)}, u32[]{:S(2)}, u32[]{:S(2)}) collective-permute-start(f32[384,1024]{1,0:T(8,128)} %get-tuple-element.65), channel_id=1, source_target_pairs={{0,4},{4,0},{8,12},{12,8},{16,20},{20,16},{24,28},{28,24},{1,5},{5... | collective-permute-start | bytes 4718600 | tf_op jit(solution)/shard_map/ppermute | solution.py:60
  21.7 5.4 %collective-permute-start.4 = (f32[32,1024]{1,0:T(8,128)S(1)}, f32[32,1024]{1,0:T(8,128)S(1)}, u32[]{:S(2)}, u32[]{:S(2)}) collective-permute-start(f32[32,1024]{1,0:T(8,128)S(1)} %slice.43), channel_id=1, source_target_pairs={{0,16},{4,12},{8,24},{12,4},{16,0},{20,28},{24,8},{28,20},{1,17},{... | collective-permute-start | bytes 393224 | tf_op jit(solution)/shard_map/ppermute | solution.py:65
  27.1 13.0 %collective-permute-start.8 = (f32[128,1024]{1,0:T(8,128)S(1)}, f32[128,1024]{1,0:T(8,128)S(1)}, u32[]{:S(2)}, u32[]{:S(2)}) collective-permute-start(f32[128,1024]{1,0:T(8,128)S(1)} %add.40), channel_id=1, source_target_pairs={{0,16},{4,12},{8,24},{12,4},{16,0},{20,28},{24,8},{28,20},{1,17},{... | collective-permute-start | bytes 1572872 | tf_op jit(solution)/shard_map/ppermute | solution.py:65
  29.2 9.3 %collective-permute-start.5 = (f32[32,256]{1,0:T(8,128)S(1)}, f32[32,256]{1,0:T(8,128)S(1)}, u32[]{:S(2)}, u32[]{:S(2)}) collective-permute-start(f32[32,256]{1,0:T(8,128)S(1)} %get-tuple-element.96), channel_id=1, source_target_pairs={{0,3},{4,7},{8,11},{12,15},{16,19},{20,23},{24,27},{28,31}} | collective-permute-start | bytes 98312 | tf_op jit(solution)/shard_map/ppermute | solution.py:501
  34.7 3.8 %collective-permute-start.6 = (f32[32,256]{1,0:T(8,128)S(1)}, f32[32,256]{1,0:T(8,128)S(1)}, u32[]{:S(2)}, u32[]{:S(2)}) collective-permute-start(f32[32,256]{1,0:T(8,128)S(1)} %get-tuple-element.98), channel_id=1, source_target_pairs={{0,2},{1,3},{4,6},{5,7},{8,10},{9,11},{12,14},{13,15},{16,18},{17,... | collective-permute-start | bytes 98312 | tf_op jit(solution)/shard_map/ppermute | solution.py:501
  36.0 4.1 %collective-permute-start.7 = (f32[32,256]{1,0:T(8,128)S(1)}, f32[32,256]{1,0:T(8,128)S(1)}, u32[]{:S(2)}, u32[]{:S(2)}) collective-permute-start(f32[32,256]{1,0:T(8,128)S(1)} %get-tuple-element.97), channel_id=1, source_target_pairs={{0,1},{1,2},{2,3},{4,5},{5,6},{6,7},{8,9},{9,10},{10,11},{12,13},{... | collective-permute-start | bytes 98312 | tf_op jit(solution)/shard_map/ppermute | solution.py:501
  38.5 1.6 %copy-start.4 = (f32[32,256]{1,0:T(8,128)}, f32[32,256]{1,0:T(8,128)S(1)}, u32[]{:S(2)}) copy-start(f32[32,256]{1,0:T(8,128)S(1)} %collective-permute-done.5) | copy-start | bytes 98308
  38.5 1.6 %copy-start.5 = (f32[32,256]{1,0:T(8,128)}, f32[32,256]{1,0:T(8,128)S(1)}, u32[]{:S(2)}) copy-start(f32[32,256]{1,0:T(8,128)S(1)} %collective-permute-done.6) | copy-start | bytes 98308
  40.0 0.6 copy-start.6
  42.2 0.7 copy-start
  42.9 12.0 %collective-permute-start.12 = (f32[192,1024]{1,0:T(8,128)S(1)}, f32[192,1024]{1,0:T(8,128)S(1)}, u32[]{:S(2)}, u32[]{:S(2)}) collective-permute-start(f32[192,1024]{1,0:T(8,128)S(1)} %get-tuple-element.68.refs_0_), channel_id=1, source_target_pairs={{0,8},{4,20},{8,0},{12,28},{16,24},{20,4},{24,16},{28,12},{1,9},{5... | collective-permute-start | bytes 2359304 | tf_op jit(solution)/shard_map/ppermute | solution.py:65
  44.1 1.9 %collective-permute-start.9 = (f32[128,1024]{1,0:T(8,128)S(1)}, f32[128,1024]{1,0:T(8,128)S(1)}, u32[]{:S(2)}, u32[]{:S(2)}) collective-permute-start(f32[128,1024]{1,0:T(8,128)S(1)} %add.51.mine_ref), channel_id=1, source_target_pairs={{0,4},{4,0},{8,12},{12,8},{16,20},{20,16},{24,28},{28,24},{1,5},{5... | collective-permute-start | bytes 1572872 | tf_op jit(solution)/shard_map/ppermute | solution.py:60
  44.9 10.0 %copy-start.1 = (f32[64,1024]{1,0:T(8,128)S(1)}, f32[64,1024]{1,0:T(8,128)}, u32[]{:S(2)}) copy-start(f32[64,1024]{1,0:T(8,128)} %copy-done) | copy-start | bytes 786436
  49.7 0.7 collective-permute-start.10
  55.6 18.5 %collective-permute-start.18 = (f32[160,1024]{1,0:T(8,128)S(1)}, f32[160,1024]{1,0:T(8,128)S(1)}, u32[]{:S(2)}, u32[]{:S(2)}) collective-permute-start(f32[160,1024]{1,0:T(8,128)S(1)} %get-tuple-element.76.refs_0_), channel_id=1, source_target_pairs={{0,16},{4,12},{8,24},{12,4},{16,0},{20,28},{24,8},{28,20},{1,17},{... | collective-permute-start | bytes 1966088 | tf_op jit(solution)/shard_map/ppermute | solution.py:65
  55.7 12.0 %collective-permute-start.15 = (f32[128,1024]{1,0:T(8,128)S(1)}, f32[128,1024]{1,0:T(8,128)S(1)}, u32[]{:S(2)}, u32[]{:S(2)}) collective-permute-start(f32[128,1024]{1,0:T(8,128)S(1)} %get-tuple-element.73.refs_0_), channel_id=1, source_target_pairs={{0,8},{4,20},{8,0},{12,28},{16,24},{20,4},{24,16},{28,12},{1,9},{5... | collective-permute-start | bytes 1572872 | tf_op jit(solution)/shard_map/ppermute | solution.py:65
  57.8 3.2 %collective-permute-start.14 = (f32[32,512]{1,0:T(8,128)S(1)}, f32[32,512]{1,0:T(8,128)S(1)}, u32[]{:S(2)}, u32[]{:S(2)}) collective-permute-start(f32[32,512]{1,0:T(8,128)S(1)} %rest.4), channel_id=1, source_target_pairs={{3,1},{7,5},{11,9},{15,13},{19,17},{23,21},{27,25},{31,29}} | collective-permute-start | bytes 196616 | tf_op jit(solution)/shard_map/ppermute | solution.py:402
  58.5 9.2 %collective-permute-start.13 = (f32[32,256]{1,0:T(8,128)S(1)}, f32[32,256]{1,0:T(8,128)S(1)}, u32[]{:S(2)}, u32[]{:S(2)}) collective-permute-start(f32[32,256]{1,0:T(8,128)S(1)} %get-tuple-element.70), channel_id=1, source_target_pairs={{2,1},{6,5},{10,9},{14,13},{18,17},{22,21},{26,25},{30,29}} | collective-permute-start | bytes 98312 | tf_op jit(solution)/shard_map/ppermute | solution.py:399
  59.7 9.8 %collective-permute-start.17 = (f32[32,256]{1,0:T(8,128)S(1)}, f32[32,256]{1,0:T(8,128)S(1)}, u32[]{:S(2)}, u32[]{:S(2)}) collective-permute-start(f32[32,256]{1,0:T(8,128)S(1)} %rest.5), channel_id=1, source_target_pairs={{2,0},{6,4},{10,8},{14,12},{18,16},{22,20},{26,24},{30,28}} | collective-permute-start | bytes 98312 | tf_op jit(solution)/shard_map/ppermute | solution.py:402
  68.2 5.8 %collective-permute-start.16 = (f32[32,256]{1,0:T(8,128)S(1)}, f32[32,256]{1,0:T(8,128)S(1)}, u32[]{:S(2)}, u32[]{:S(2)}) collective-permute-start(f32[32,256]{1,0:T(8,128)S(1)} %get-tuple-element.74), channel_id=1, source_target_pairs={{1,0},{5,4},{9,8},{13,12},{17,16},{21,20},{25,24},{29,28}} | collective-permute-start | bytes 98312 | tf_op jit(solution)/shard_map/ppermute | solution.py:399
  75.5 1.9 %collective-permute-start.19 = (f32[128,1024]{1,0:T(8,128)S(1)}, f32[128,1024]{1,0:T(8,128)S(1)}, u32[]{:S(2)}, u32[]{:S(2)}) collective-permute-start(f32[128,1024]{1,0:T(8,128)S(1)} %get-tuple-element.80.mine_ref), channel_id=1, source_target_pairs={{0,4},{4,0},{8,12},{12,8},{16,20},{20,16},{24,28},{28,24},{1,5},{5... | collective-permute-start | bytes 1572872 | tf_op jit(solution)/shard_map/ppermute | solution.py:60
  75.5 9.2 %collective-permute-start.21 = (f32[128,1024]{1,0:T(8,128)S(1)}, f32[128,1024]{1,0:T(8,128)S(1)}, u32[]{:S(2)}, u32[]{:S(2)}) collective-permute-start(f32[128,1024]{1,0:T(8,128)S(1)} %get-tuple-element.81.tiles_ref), channel_id=1, source_target_pairs={{0,16},{4,12},{8,24},{12,4},{16,0},{20,28},{24,8},{28,20},{1,17},{... | collective-permute-start | bytes 1572872 | tf_op jit(solution)/shard_map/ppermute | solution.py:65
  78.6 13.7 %copy-start.3 = (f32[2,256,32]{1,2,0:T(8,128)S(1)}, f32[2,256,32]{1,2,0:T(8,128)}, u32[]{:S(2)}) copy-start(f32[2,256,32]{1,2,0:T(8,128)} %param.7) | copy-start | bytes 196612
  84.7 4.6 %collective-permute-start.22 = (f32[128,1024]{1,0:T(8,128)S(1)}, f32[128,1024]{1,0:T(8,128)S(1)}, u32[]{:S(2)}, u32[]{:S(2)}) collective-permute-start(f32[128,1024]{1,0:T(8,128)S(1)} %pack_step.1.mine_ref), channel_id=1, source_target_pairs={{0,4},{4,0},{8,12},{12,8},{16,20},{20,16},{24,28},{28,24},{1,5},{5... | collective-permute-start | bytes 1572872 | tf_op jit(solution)/shard_map/ppermute | solution.py:60
  84.8 7.5 %collective-permute-start.20 = (f32[32,256]{1,0:T(8,128)S(1)}, f32[32,256]{1,0:T(8,128)S(1)}, u32[]{:S(2)}, u32[]{:S(2)}) collective-permute-start(f32[32,256]{1,0:T(8,128)S(1)} %get-tuple-element.93), channel_id=1, source_target_pairs={{0,3},{1,2},{2,1},{3,0},{4,7},{5,6},{6,5},{7,4},{8,11},{9,10},{10,... | collective-permute-start | bytes 98312 | tf_op jit(solution)/shard_map/ppermute | solution.py:525
  84.9 7.4 %collective-permute-start.23 = (f32[32,256]{1,0:T(8,128)S(1)}, f32[32,256]{1,0:T(8,128)S(1)}, u32[]{:S(2)}, u32[]{:S(2)}) collective-permute-start(f32[32,256]{1,0:T(8,128)S(1)} %get-tuple-element.95), channel_id=1, source_target_pairs={{0,2},{1,3},{2,0},{3,1},{4,6},{5,7},{6,4},{7,5},{8,10},{9,11},{10,... | collective-permute-start | bytes 98312 | tf_op jit(solution)/shard_map/ppermute | solution.py:525
  85.9 6.4 %collective-permute-start.24 = (f32[32,256]{1,0:T(8,128)S(1)}, f32[32,256]{1,0:T(8,128)S(1)}, u32[]{:S(2)}, u32[]{:S(2)}) collective-permute-start(f32[32,256]{1,0:T(8,128)S(1)} %get-tuple-element.94), channel_id=1, source_target_pairs={{0,1},{1,0},{2,3},{3,2},{4,5},{5,4},{6,7},{7,6},{8,9},{9,8},{10,11... | collective-permute-start | bytes 98312 | tf_op jit(solution)/shard_map/ppermute | solution.py:525
  92.9 1.9 %collective-permute-start.25 = (f32[32,256]{1,0:T(8,128)S(1)}, f32[32,256]{1,0:T(8,128)S(1)}, u32[]{:S(2)}, u32[]{:S(2)}) collective-permute-start(f32[32,256]{1,0:T(8,128)S(1)} %get-tuple-element.86), channel_id=1, source_target_pairs={{3,2},{7,6},{11,10},{15,14},{19,18},{23,22},{27,26},{31,30}} | collective-permute-start | bytes 98312 | tf_op jit(solution)/shard_map/ppermute | solution.py:399
  94.2 3.8 %collective-permute-start.27 = (f32[32,512]{1,0:T(8,128)S(1)}, f32[32,512]{1,0:T(8,128)S(1)}, u32[]{:S(2)}, u32[]{:S(2)}) collective-permute-start(f32[32,512]{1,0:T(8,128)S(1)} %rest.6), channel_id=1, source_target_pairs={{3,1},{7,5},{11,9},{15,13},{19,17},{23,21},{27,25},{31,29}} | collective-permute-start | bytes 196616 | tf_op jit(solution)/shard_map/ppermute | solution.py:402
  95.4 2.5 %collective-permute-start.26 = (f32[32,256]{1,0:T(8,128)S(1)}, f32[32,256]{1,0:T(8,128)S(1)}, u32[]{:S(2)}, u32[]{:S(2)}) collective-permute-start(f32[32,256]{1,0:T(8,128)S(1)} %get-tuple-element.88), channel_id=1, source_target_pairs={{2,1},{6,5},{10,9},{14,13},{18,17},{22,21},{26,25},{30,29}} | collective-permute-start | bytes 98312 | tf_op jit(solution)/shard_map/ppermute | solution.py:399
  96.6 8.4 %collective-permute-start.29 = (f32[32,256]{1,0:T(8,128)S(1)}, f32[32,256]{1,0:T(8,128)S(1)}, u32[]{:S(2)}, u32[]{:S(2)}) collective-permute-start(f32[32,256]{1,0:T(8,128)S(1)} %rest.7), channel_id=1, source_target_pairs={{2,0},{6,4},{10,8},{14,12},{18,16},{22,20},{26,24},{30,28}} | collective-permute-start | bytes 98312 | tf_op jit(solution)/shard_map/ppermute | solution.py:402
  98.5 9.5 %collective-permute-start.28 = (f32[32,256]{1,0:T(8,128)S(1)}, f32[32,256]{1,0:T(8,128)S(1)}, u32[]{:S(2)}, u32[]{:S(2)}) collective-permute-start(f32[32,256]{1,0:T(8,128)S(1)} %get-tuple-element.90), channel_id=1, source_target_pairs={{1,0},{5,4},{9,8},{13,12},{17,16},{21,20},{25,24},{29,28}} | collective-permute-start | bytes 98312 | tf_op jit(solution)/shard_map/ppermute | solution.py:399

commit v8 on v5

--- a/solution.py
+++ b/solution.py
@@ -401,11 +401,11 @@
 
 
 class Packs:
-    def __init__(self, pack, got, top, steps, bands, members):
-        self.pack, self.got, self.top, self.got_top = pack, got, top, None
+    def __init__(self, pack, got, top, got_top, steps, bands, members):
+        self.pack, self.got, self.top, self.got_top = pack, got, top, got_top
         self.steps, self.members = steps, members
         self.low_at = [bands - 2 - 2 * (steps - 1 - step) for step in range(steps)]
-        self.top_at = [bands - steps + step for step in range(steps)]
+        self.top_at = [bands - 1 - 2 * (steps - 1 - step) for step in range(steps)]
 
     def take(self, index):
         taken = ()
@@ -426,8 +426,6 @@
                 self.got = swap_chip(tiles, self.members, step)
             else:
                 self.got = swap_core(tiles, self.members)
-            if step == 1:
-                self.got_top = swap_chip(after(self.top, tiles), self.members, 0)
         if self.index in self.top_at:
             (self.top,) = outs
             step = self.top_at.index(self.index) + 1
@@ -509,14 +507,15 @@
 
     tiles, sums = pack_step(keep, keep, half, after(got_pack, sum_one), half, False)
     got_pack = swap_chip(tiles, members, 0)
-    top = top + after(got_top, sum_one)
+    (top,) = pack_step(top, None, 0, after(got_top, sum_one), half, True)
+    got_top = swap_chip(top, members, 0)
 
     tile_one = join_halves(after(where, sum_one, top), tile_one, other, 0, half, range(bands))
     base = rhs[1].T - own_band(sum_one, place, band)
     for piece in got_up:
         base = base - after(piece, tile_one)
 
-    packs = Packs((tiles, sums, half), got_pack, top, stages, bands, members)
+    packs = Packs((tiles, sums, half), got_pack, top, got_top, stages, bands, members)
     solved_one = sweep(where, base, tile_one, sum_one, bands, packs)
 
     low, sums, _ = packs.pack

time: 104 us -> 98.6 us (0.948)
  waiting for transfers between devices: 38.4 us -> 28.1 us
  starting transfers between devices: 37.8 us -> 42.7 us
  other arithmetic: 3.03 us -> 1.84 us
    ppermute x8, waiting for transfers between devices: 20.3 us -> 10.1 us  [swap_chip(): lax.ppermute(value, 'rt', [(i, i ^ 1 << orders[i & 1][stage]) for i in ra...]
    ppermute x8, starting transfers between devices: 11.4 us -> 14.7 us  [swap_chip(): lax.ppermute(value, 'rt', [(i, i ^ 1 << orders[i & 1][stage]) for i in ra...]
    ppermute x7, starting transfers between devices: 2.32 us -> 3.99 us  [swap_core(): return lax.ppermute(value, 'rt', [(i, i ^ 1) for i in range(members)])]
    add x1 -> x0, other arithmetic: 1.17 us -> none  [shards(): top = top + after(got_top, sum_one)]
    pallas_call x19 -> x20, Pallas kernels: 22.9 us -> 23.4 us  [call(): pl.pallas_call(body, out_shape=out, in_specs=list(specs), out_specs=tuple...]
  transfers between devices with their start and end apart: 31 -> 31, of which waited for: 13 -> 11; matrix products, arithmetic and copies ran while one was open for 3% -> 2% of each run, Pallas kernels for 18% -> 21%
where the time goes in v8:
time: 98.6 us; the launch traced here: 97.9 us
  starting transfers between devices  42.7 us (43%)
  waiting for transfers between devices  28.1 us (28%)
  Pallas kernels  23.4 us (24%)
  other arithmetic  1.84 us (2%)
  local copies, waits for them, and re-layouts  1.35 us (1%)
    pallas_call x20, Pallas kernels, call(): pl.pallas_call(body, out_shape=out, in_specs=list(specs), out_specs=tuple...  23.4 us
    ppermute x8, starting transfers between devices, swap_chip(): lax.ppermute(value, 'rt', [(i, i ^ 1 << orders[i & 1][stage]) for i in ra...  14.7 us
    ppermute x4, waiting for transfers between devices, sweep(): fars.append(lax.ppermute(rest, 'ct', [(stage, stage - 2)]))  10.5 us
    ppermute x3, starting transfers between devices, shards(): lax.ppermute(piece, 'ct', [(i, i + shift) for i in range(bands - shift)])  10.5 us
    ppermute x8, waiting for transfers between devices, swap_chip(): lax.ppermute(value, 'rt', [(i, i ^ 1 << orders[i & 1][stage]) for i in ra...  10.1 us
    ppermute x6, starting transfers between devices, sweep(): near = lax.ppermute(update, 'ct', [(stage, stage - 1)])  5.22 us
    ppermute x3, starting transfers between devices, shards(): lax.ppermute(pieces[mask], 'ct', [(i, i ^ mask) for i in range(bands)])  4.45 us
    ppermute x7, starting transfers between devices, swap_core(): return lax.ppermute(value, 'rt', [(i, i ^ 1) for i in range(members)])  3.99 us
  transfers between devices with their start and end apart: 31, of which 11 were waited for; matrix products, arithmetic and copies ran while one was open for 2% of the time, Pallas kernels for 21%

profile of v8, /device:TPU:0, one launch (start us, length us, event | category | flops | bytes accessed | tf_op | source)
XLA Modules:
  0.0 97.9 jit_solution(6955927100309822136)
XLA Ops:
  0.0 0.1 pad_add_fusion.where_ref
  0.1 0.7 copy-done
  0.7 0.6 first_band.1
  1.4 0.5 collective-permute-start
  1.9 1.5 %collective-permute-done = f32[128,1024]{1,0:T(8,128)S(1)} collective-permute-done((f32[128,1024]{1,0:T(8,128)S(1)}, f32[128,1024]{1,0:T(8,128)S(1)}, u32[]{:S(2)}, u32[]{:S(2)}) %collective-permute-start) | collective-permute-done | bytes 524320 | tf_op jit(solution)/shard_map/ppermute | solution.py:60
  3.5 2.9 %collective-permute-start.2 = (f32[128,1024]{1,0:T(8,128)S(1)}, f32[128,1024]{1,0:T(8,128)S(1)}, u32[]{:S(2)}, u32[]{:S(2)}) collective-permute-start(f32[128,1024]{1,0:T(8,128)S(1)} %add.39), channel_id=1, source_target_pairs={{0,8},{4,20},{8,0},{12,28},{16,24},{20,4},{24,16},{28,12},{1,9},{5... | collective-permute-start | bytes 1572872 | tf_op jit(solution)/shard_map/ppermute | solution.py:65
  6.4 7.2 %front.1 = (f32[128,1024]{1,0:T(8,128)S(1)}, f32[128,1024]{1,0:T(8,128)S(1)}, f32[256,1024]{1,0:T(8,128)S(1)}, f32[256,1024]{1,0:T(8,128)S(1)}) custom-call(s32[2]{0:T(128)S(1)} %pad_add_fusion.where_ref, s32[48]{0:T(128)S(1)} %copy-done, f32[6,2,256,1024]{3,2,1,0:T(8,128)} %factor_ref.5, f32[6,256,256]{2,1,0:T(8,128)} %known_ref.1), custom_call_target="tpu_custom_call" | custom-call | tf_op jit(solution)/shard_map/front/pallas_call | solution.py:23
  13.6 2.4 %collective-permute-start.1 = (f32[128,1024]{1,0:T(8,128)S(1)}, f32[128,1024]{1,0:T(8,128)S(1)}, u32[]{:S(2)}, u32[]{:S(2)}) collective-permute-start(f32[128,1024]{1,0:T(8,128)S(1)} %get-tuple-element.56), channel_id=1, source_target_pairs={{0,4},{4,0},{8,12},{12,8},{16,20},{20,16},{24,28},{28,24},{1,5},{5... | collective-permute-start | bytes 1572872 | tf_op jit(solution)/shard_map/ppermute | solution.py:60
  16.1 1.5 %collective-permute-done.1 = f32[128,1024]{1,0:T(8,128)S(1)} collective-permute-done((f32[128,1024]{1,0:T(8,128)S(1)}, f32[128,1024]{1,0:T(8,128)S(1)}, u32[]{:S(2)}, u32[]{:S(2)}) %collective-permute-start.1) | collective-permute-done | bytes 524320 | tf_op jit(solution)/shard_map/ppermute | solution.py:60
  17.6 0.4 collective-permute-start.11
  18.1 0.2 collective-permute-start.3
  18.3 1.6 %collective-permute-start.7 = (f32[128,1024]{1,0:T(8,128)S(1)}, f32[128,1024]{1,0:T(8,128)S(1)}, u32[]{:S(2)}, u32[]{:S(2)}) collective-permute-start(f32[128,1024]{1,0:T(8,128)S(1)} %add.40), channel_id=1, source_target_pairs={{0,16},{4,12},{8,24},{12,4},{16,0},{20,28},{24,8},{28,20},{1,17},{... | collective-permute-start | bytes 1572872 | tf_op jit(solution)/shard_map/ppermute | solution.py:65
  19.9 1.7 %top_band.1 = (f32[128,1024]{1,0:T(8,128)S(1)}, f32[128,1024]{1,0:T(8,128)}) custom-call(s32[2]{0:T(128)S(1)} %pad_add_fusion.where_ref, s32[48]{0:T(128)S(1)} %copy-done, f32[6,2,256,1024]{3,2,1,0:T(8,128)} %factor_ref.5), custom_call_target="tpu_custom_call" | custom-call | tf_op jit(solution)/shard_map/top_band/pallas_call | solution.py:23
  21.6 5.0 %collective-permute-done.3 = f32[64,1024]{1,0:T(8,128)S(1)} collective-permute-done((f32[64,1024]{1,0:T(8,128)S(1)}, f32[64,1024]{1,0:T(8,128)S(1)}, u32[]{:S(2)}, u32[]{:S(2)}) %collective-permute-start.3) | collective-permute-done | bytes 262176 | tf_op jit(solution)/shard_map/ppermute | solution.py:65
  26.6 2.5 %collective-permute-start.4 = (f32[32,1024]{1,0:T(8,128)S(1)}, f32[32,1024]{1,0:T(8,128)S(1)}, u32[]{:S(2)}, u32[]{:S(2)}) collective-permute-start(f32[32,1024]{1,0:T(8,128)S(1)} %slice.43), channel_id=1, source_target_pairs={{0,16},{4,12},{8,24},{12,4},{16,0},{20,28},{24,8},{28,20},{1,17},{... | collective-permute-start | bytes 393224 | tf_op jit(solution)/shard_map/ppermute | solution.py:65
  29.1 2.9 %collective-permute-done.4 = f32[32,1024]{1,0:T(8,128)S(1)} collective-permute-done((f32[32,1024]{1,0:T(8,128)S(1)}, f32[32,1024]{1,0:T(8,128)S(1)}, u32[]{:S(2)}, u32[]{:S(2)}) %collective-permute-start.4) | collective-permute-done | bytes 131104 | tf_op jit(solution)/shard_map/ppermute | solution.py:65
  32.0 0.1 pack_step.3
  32.2 0.1 collective-permute-start.12
  32.3 0.5 collective-permute-start.6
  32.8 0.1 collective-permute-start.8
  32.9 0.6 constant_dynamic-slice_fusion.2
  33.6 4.1 %collective-permute-start.5 = (f32[32,256]{1,0:T(8,128)}, f32[32,256]{1,0:T(8,128)}, u32[]{:S(2)}, u32[]{:S(2)}) collective-permute-start(f32[32,256]{1,0:T(8,128)} %get-tuple-element.102), channel_id=1, source_target_pairs={{0,1},{1,2},{2,3},{4,5},{5,6},{6,7},{8,9},{9,10},{10,11},{12,13},{... | collective-permute-start | bytes 98312 | tf_op jit(solution)/shard_map/ppermute | solution.py:504
  37.7 4.5 %collective-permute-start.9 = (f32[32,256]{1,0:T(8,128)}, f32[32,256]{1,0:T(8,128)}, u32[]{:S(2)}, u32[]{:S(2)}) collective-permute-start(f32[32,256]{1,0:T(8,128)} %get-tuple-element.104), channel_id=1, source_target_pairs={{0,2},{1,3},{4,6},{5,7},{8,10},{9,11},{12,14},{13,15},{16,18},{17,... | collective-permute-start | bytes 98312 | tf_op jit(solution)/shard_map/ppermute | solution.py:504
  42.2 1.9 %collective-permute-start.10 = (f32[32,256]{1,0:T(8,128)}, f32[32,256]{1,0:T(8,128)}, u32[]{:S(2)}, u32[]{:S(2)}) collective-permute-start(f32[32,256]{1,0:T(8,128)} %get-tuple-element.103), channel_id=1, source_target_pairs={{0,3},{4,7},{8,11},{12,15},{16,19},{20,23},{24,27},{28,31}} | collective-permute-start | bytes 98312 | tf_op jit(solution)/shard_map/ppermute | solution.py:504
  44.1 2.0 %collective-permute-start.14 = (f32[128,1024]{1,0:T(8,128)S(1)}, f32[128,1024]{1,0:T(8,128)S(1)}, u32[]{:S(2)}, u32[]{:S(2)}) collective-permute-start(f32[128,1024]{1,0:T(8,128)S(1)} %pack_step.2.refs_0_), channel_id=1, source_target_pairs={{0,8},{4,20},{8,0},{12,28},{16,24},{20,4},{24,16},{28,12},{1,9},{5... | collective-permute-start | bytes 1572872 | tf_op jit(solution)/shard_map/ppermute | solution.py:65
  46.1 3.5 %join.2.tile_ref = f32[256,1024]{1,0:T(8,128)S(1)} custom-call(s32[2]{0:T(128)S(1)} %pad_add_fusion.where_ref, f32[128,1024]{1,0:T(8,128)S(1)} %add.47.mine_ref, f32[128,1024]{1,0:T(8,128)} %collective-permute-done.8.other_ref), custom_call_target="tpu_custom_call" | custom-call | tf_op jit(solution)/shard_map/join/pallas_call | solution.py:23
  49.7 0.8 fusion.6.base_ref
  50.5 0.6 stage.8
  51.2 2.1 %collective-permute-start.17 = (f32[160,1024]{1,0:T(8,128)S(1)}, f32[160,1024]{1,0:T(8,128)S(1)}, u32[]{:S(2)}, u32[]{:S(2)}) collective-permute-start(f32[160,1024]{1,0:T(8,128)S(1)} %get-tuple-element.80.refs_0_), channel_id=1, source_target_pairs={{0,16},{4,12},{8,24},{12,4},{16,0},{20,28},{24,8},{28,20},{1,17},{... | collective-permute-start | bytes 1966088 | tf_op jit(solution)/shard_map/ppermute | solution.py:65
  53.3 0.7 collective-permute-start.13
  53.9 0.6 stage.9
  54.6 3.2 %collective-permute-start.20 = (f32[128,1024]{1,0:T(8,128)S(1)}, f32[128,1024]{1,0:T(8,128)S(1)}, u32[]{:S(2)}, u32[]{:S(2)}) collective-permute-start(f32[128,1024]{1,0:T(8,128)S(1)} %get-tuple-element.85.refs_0_), channel_id=1, source_target_pairs={{0,16},{4,12},{8,24},{12,4},{16,0},{20,28},{24,8},{28,20},{1,17},{... | collective-permute-start | bytes 1572872 | tf_op jit(solution)/shard_map/ppermute | solution.py:65
  57.8 0.5 rest.4
  58.3 0.7 collective-permute-start.16
  59.0 0.7 collective-permute-start.15
  59.7 2.1 %collective-permute-done.17.refs_2_ = f32[160,1024]{1,0:T(8,128)S(1)} collective-permute-done((f32[160,1024]{1,0:T(8,128)S(1)}, f32[160,1024]{1,0:T(8,128)S(1)}, u32[]{:S(2)}, u32[]{:S(2)}) %collective-permute-start.17) | collective-permute-done | bytes 655392 | tf_op jit(solution)/shard_map/ppermute | solution.py:65
  61.8 0.6 stage.10
  62.5 0.1 collective-permute-start.21
  62.5 0.6 rest.5
  63.1 1.3 %collective-permute-start.19 = (f32[32,256]{1,0:T(8,128)S(1)}, f32[32,256]{1,0:T(8,128)S(1)}, u32[]{:S(2)}, u32[]{:S(2)}) collective-permute-start(f32[32,256]{1,0:T(8,128)S(1)} %rest.5), channel_id=1, source_target_pairs={{2,0},{6,4},{10,8},{14,12},{18,16},{22,20},{26,24},{30,28}} | collective-permute-start | bytes 98312 | tf_op jit(solution)/shard_map/ppermute | solution.py:397
  64.4 1.3 %collective-permute-start.18 = (f32[32,256]{1,0:T(8,128)S(1)}, f32[32,256]{1,0:T(8,128)S(1)}, u32[]{:S(2)}, u32[]{:S(2)}) collective-permute-start(f32[32,256]{1,0:T(8,128)S(1)} %get-tuple-element.83), channel_id=1, source_target_pairs={{1,0},{5,4},{9,8},{13,12},{17,16},{21,20},{25,24},{29,28}} | collective-permute-start | bytes 98312 | tf_op jit(solution)/shard_map/ppermute | solution.py:394
  65.7 4.2 %collective-permute-done.19.far_ref = f32[32,256]{1,0:T(8,128)S(1)} collective-permute-done((f32[32,256]{1,0:T(8,128)S(1)}, f32[32,256]{1,0:T(8,128)S(1)}, u32[]{:S(2)}, u32[]{:S(2)}) %collective-permute-start.19) | collective-permute-done | bytes 32800 | tf_op jit(solution)/shard_map/ppermute | solution.py:397
  69.9 0.5 collective-permute-done.18.near_ref
  70.4 1.4 %stage.11 = (f32[32,256]{1,0:T(8,128)S(1)}, f32[32,256]{1,0:T(8,128)}, f32[128,1024]{1,0:T(8,128)S(1)}) custom-call(s32[2]{0:T(128)S(1)} %pad_add_fusion.where_ref, f32[32,256]{1,0:T(8,128)S(1)} %fusion.6.base_ref, f32[256,1024]{1,0:T(8,128)S(1)} %join.2.tile_ref, f32[32,1024]{1,0:T(8,128)S(1)} %slice_add_fusion.1.add_ref, ...), custom_call_target="tpu_custom_call" | custom-call | tf_op jit(solution)/shard_map/stage/pallas_call | solution.py:23
  71.8 1.2 %couple.1 = f32[4,32,256]{2,1,0:T(8,128)S(1)} custom-call(s32[2]{0:T(128)S(1)} %pad_add_fusion.where_ref, f32[32,1024]{1,0:T(8,128)S(1)} %get-tuple-element.82.sums_ref, f32[32,256]{1,0:T(8,128)S(1)} %get-tuple-element.86.solved_ref, f32[128,1024]{1,0:T(8,128)S(1)} %get-tuple-element.87.mine_ref, f32[128,1024]{1,0:T(8,128)S(1)} %collective-permute-done.21.other_ref), custom_call_target="tpu_custom_call" | custom-call | tf_op jit(solution)/shard_map/couple/pallas_call | solution.py:23
  73.1 0.8 collective-permute-start.24
  74.0 3.5 %collective-permute-start.25 = (f32[32,256]{1,0:T(8,128)S(1)}, f32[32,256]{1,0:T(8,128)S(1)}, u32[]{:S(2)}, u32[]{:S(2)}) collective-permute-start(f32[32,256]{1,0:T(8,128)S(1)} %get-tuple-element.100), channel_id=1, source_target_pairs={{0,1},{1,0},{2,3},{3,2},{4,5},{5,4},{6,7},{7,6},{8,9},{9,8},{10,11... | collective-permute-start | bytes 98312 | tf_op jit(solution)/shard_map/ppermute | solution.py:526
  77.5 0.6 join.3.tile_ref
  78.1 1.0 collective-permute-done.22
  79.1 0.3 collective-permute-done.25
  79.4 0.6 stage.12
  80.0 0.7 collective-permute-start.26
  80.7 0.6 rest.6
  81.2 0.7 collective-permute-start.28
  81.9 0.6 stage.13
  82.5 0.7 collective-permute-start.27
  83.1 0.6 rest.7
  83.7 1.3 %collective-permute-start.30 = (f32[32,256]{1,0:T(8,128)S(1)}, f32[32,256]{1,0:T(8,128)S(1)}, u32[]{:S(2)}, u32[]{:S(2)}) collective-permute-start(f32[32,256]{1,0:T(8,128)S(1)} %rest.7), channel_id=1, source_target_pairs={{2,0},{6,4},{10,8},{14,12},{18,16},{22,20},{26,24},{30,28}} | collective-permute-start | bytes 98312 | tf_op jit(solution)/shard_map/ppermute | solution.py:397
  85.0 0.6 stage.14
  85.6 1.3 %collective-permute-start.29 = (f32[32,256]{1,0:T(8,128)S(1)}, f32[32,256]{1,0:T(8,128)S(1)}, u32[]{:S(2)}, u32[]{:S(2)}) collective-permute-start(f32[32,256]{1,0:T(8,128)S(1)} %get-tuple-element.96), channel_id=1, source_target_pairs={{1,0},{5,4},{9,8},{13,12},{17,16},{21,20},{25,24},{29,28}} | collective-permute-start | bytes 98312 | tf_op jit(solution)/shard_map/ppermute | solution.py:394
  86.9 6.3 %collective-permute-done.30.far_ref = f32[32,256]{1,0:T(8,128)S(1)} collective-permute-done((f32[32,256]{1,0:T(8,128)S(1)}, f32[32,256]{1,0:T(8,128)S(1)}, u32[]{:S(2)}, u32[]{:S(2)}) %collective-permute-start.30) | collective-permute-done | bytes 32800 | tf_op jit(solution)/shard_map/ppermute | solution.py:397
  93.2 2.6 %collective-permute-done.29.near_ref = f32[32,256]{1,0:T(8,128)S(1)} collective-permute-done((f32[32,256]{1,0:T(8,128)S(1)}, f32[32,256]{1,0:T(8,128)S(1)}, u32[]{:S(2)}, u32[]{:S(2)}) %collective-permute-start.29) | collective-permute-done | bytes 32800 | tf_op jit(solution)/shard_map/ppermute | solution.py:394
  95.9 1.4 %stage.15 = (f32[32,256]{1,0:T(8,128)S(1)}, f32[32,256]{1,0:T(8,128)}) custom-call(s32[2]{0:T(128)S(1)} %pad_add_fusion.where_ref, f32[32,256]{1,0:T(8,128)S(1)} %fusion.3.base_ref, f32[256,1024]{1,0:T(8,128)S(1)} %join.3.tile_ref, f32[32,1024]{1,0:T(8,128)S(1)} %broadcast_2_far_ref_add_ref.2.far_ref.add_ref, ...), custom_call_target="tpu_custom_call" | custom-call | tf_op jit(solution)/shard_map/stage/pallas_call | solution.py:23
  97.2 0.6 pad_maximum_fusion
  (38 shorter events, 0.5 us)
Async XLA Ops:
  0.1 0.7 copy-start
  1.4 2.1 %collective-permute-start = (f32[128,1024]{1,0:T(8,128)S(1)}, f32[128,1024]{1,0:T(8,128)S(1)}, u32[]{:S(2)}, u32[]{:S(2)}) collective-permute-start(f32[128,1024]{1,0:T(8,128)S(1)} %get-tuple-element.53), channel_id=1, source_target_pairs={{0,4},{4,0},{8,12},{12,8},{16,20},{20,16},{24,28},{28,24},{1,5},{5... | collective-permute-start | bytes 1572872 | tf_op jit(solution)/shard_map/ppermute | solution.py:60
  3.5 12.5 %collective-permute-start.2 = (f32[128,1024]{1,0:T(8,128)S(1)}, f32[128,1024]{1,0:T(8,128)S(1)}, u32[]{:S(2)}, u32[]{:S(2)}) collective-permute-start(f32[128,1024]{1,0:T(8,128)S(1)} %add.39), channel_id=1, source_target_pairs={{0,8},{4,20},{8,0},{12,28},{16,24},{20,4},{24,16},{28,12},{1,9},{5... | collective-permute-start | bytes 1572872 | tf_op jit(solution)/shard_map/ppermute | solution.py:65
  13.6 3.9 %collective-permute-start.1 = (f32[128,1024]{1,0:T(8,128)S(1)}, f32[128,1024]{1,0:T(8,128)S(1)}, u32[]{:S(2)}, u32[]{:S(2)}) collective-permute-start(f32[128,1024]{1,0:T(8,128)S(1)} %get-tuple-element.56), channel_id=1, source_target_pairs={{0,4},{4,0},{8,12},{12,8},{16,20},{20,16},{24,28},{28,24},{1,5},{5... | collective-permute-start | bytes 1572872 | tf_op jit(solution)/shard_map/ppermute | solution.py:60
  17.6 14.4 %collective-permute-start.11 = (f32[256,1024]{1,0:T(8,128)S(1)}, f32[256,1024]{1,0:T(8,128)S(1)}, u32[]{:S(2)}, u32[]{:S(2)}) collective-permute-start(f32[256,1024]{1,0:T(8,128)S(1)} %get-tuple-element.72), channel_id=1, source_target_pairs={{0,4},{4,0},{8,12},{12,8},{16,20},{20,16},{24,28},{28,24},{1,5},{5... | collective-permute-start | bytes 3145736 | tf_op jit(solution)/shard_map/ppermute | solution.py:60
  18.1 8.5 %collective-permute-start.3 = (f32[64,1024]{1,0:T(8,128)S(1)}, f32[64,1024]{1,0:T(8,128)S(1)}, u32[]{:S(2)}, u32[]{:S(2)}) collective-permute-start(f32[64,1024]{1,0:T(8,128)S(1)} %slice.41), channel_id=1, source_target_pairs={{0,8},{4,20},{8,0},{12,28},{16,24},{20,4},{24,16},{28,12},{1,9},{5... | collective-permute-start | bytes 786440 | tf_op jit(solution)/shard_map/ppermute | solution.py:65
  18.3 14.4 %collective-permute-start.7 = (f32[128,1024]{1,0:T(8,128)S(1)}, f32[128,1024]{1,0:T(8,128)S(1)}, u32[]{:S(2)}, u32[]{:S(2)}) collective-permute-start(f32[128,1024]{1,0:T(8,128)S(1)} %add.40), channel_id=1, source_target_pairs={{0,16},{4,12},{8,24},{12,4},{16,0},{20,28},{24,8},{28,20},{1,17},{... | collective-permute-start | bytes 1572872 | tf_op jit(solution)/shard_map/ppermute | solution.py:65
  26.6 5.4 %collective-permute-start.4 = (f32[32,1024]{1,0:T(8,128)S(1)}, f32[32,1024]{1,0:T(8,128)S(1)}, u32[]{:S(2)}, u32[]{:S(2)}) collective-permute-start(f32[32,1024]{1,0:T(8,128)S(1)} %slice.43), channel_id=1, source_target_pairs={{0,16},{4,12},{8,24},{12,4},{16,0},{20,28},{24,8},{28,20},{1,17},{... | collective-permute-start | bytes 393224 | tf_op jit(solution)/shard_map/ppermute | solution.py:65
  32.2 18.3 %collective-permute-start.12 = (f32[192,1024]{1,0:T(8,128)S(1)}, f32[192,1024]{1,0:T(8,128)S(1)}, u32[]{:S(2)}, u32[]{:S(2)}) collective-permute-start(f32[192,1024]{1,0:T(8,128)S(1)} %get-tuple-element.74.refs_0_), channel_id=1, source_target_pairs={{0,8},{4,20},{8,0},{12,28},{16,24},{20,4},{24,16},{28,12},{1,9},{5... | collective-permute-start | bytes 2359304 | tf_op jit(solution)/shard_map/ppermute | solution.py:65
  32.3 9.9 %collective-permute-start.6 = (f32[128,1024]{1,0:T(8,128)}, f32[128,1024]{1,0:T(8,128)S(1)}, u32[]{:S(2)}, u32[]{:S(2)}) collective-permute-start(f32[128,1024]{1,0:T(8,128)} %get-tuple-element.63), channel_id=1, source_target_pairs={{0,4},{4,0},{8,12},{12,8},{16,20},{20,16},{24,28},{28,24},{1,5},{5... | collective-permute-start | bytes 1572872 | tf_op jit(solution)/shard_map/ppermute | solution.py:60
  32.8 11.3 %collective-permute-start.8 = (f32[128,1024]{1,0:T(8,128)S(1)}, f32[128,1024]{1,0:T(8,128)}, u32[]{:S(2)}, u32[]{:S(2)}) collective-permute-start(f32[128,1024]{1,0:T(8,128)S(1)} %add.47.mine_ref), channel_id=1, source_target_pairs={{0,4},{4,0},{8,12},{12,8},{16,20},{20,16},{24,28},{28,24},{1,5},{5... | collective-permute-start | bytes 1572872 | tf_op jit(solution)/shard_map/ppermute | solution.py:60
  33.6 16.1 %collective-permute-start.5 = (f32[32,256]{1,0:T(8,128)}, f32[32,256]{1,0:T(8,128)}, u32[]{:S(2)}, u32[]{:S(2)}) collective-permute-start(f32[32,256]{1,0:T(8,128)} %get-tuple-element.102), channel_id=1, source_target_pairs={{0,1},{1,2},{2,3},{4,5},{5,6},{6,7},{8,9},{9,10},{10,11},{12,13},{... | collective-permute-start | bytes 98312 | tf_op jit(solution)/shard_map/ppermute | solution.py:504
  37.7 12.0 %collective-permute-start.9 = (f32[32,256]{1,0:T(8,128)}, f32[32,256]{1,0:T(8,128)}, u32[]{:S(2)}, u32[]{:S(2)}) collective-permute-start(f32[32,256]{1,0:T(8,128)} %get-tuple-element.104), channel_id=1, source_target_pairs={{0,2},{1,3},{4,6},{5,7},{8,10},{9,11},{12,14},{13,15},{16,18},{17,... | collective-permute-start | bytes 98312 | tf_op jit(solution)/shard_map/ppermute | solution.py:504
  42.2 7.5 %collective-permute-start.10 = (f32[32,256]{1,0:T(8,128)}, f32[32,256]{1,0:T(8,128)}, u32[]{:S(2)}, u32[]{:S(2)}) collective-permute-start(f32[32,256]{1,0:T(8,128)} %get-tuple-element.103), channel_id=1, source_target_pairs={{0,3},{4,7},{8,11},{12,15},{16,19},{20,23},{24,27},{28,31}} | collective-permute-start | bytes 98312 | tf_op jit(solution)/shard_map/ppermute | solution.py:504
  44.0 35.4 %copy-start.1 = (f32[2,256,32]{1,2,0:T(8,128)S(1)}, f32[2,256,32]{1,2,0:T(8,128)}, u32[]{:S(2)}) copy-start(f32[2,256,32]{1,2,0:T(8,128)} %param.7) | copy-start | bytes 196612
  44.1 9.8 %collective-permute-start.14 = (f32[128,1024]{1,0:T(8,128)S(1)}, f32[128,1024]{1,0:T(8,128)S(1)}, u32[]{:S(2)}, u32[]{:S(2)}) collective-permute-start(f32[128,1024]{1,0:T(8,128)S(1)} %pack_step.2.refs_0_), channel_id=1, source_target_pairs={{0,8},{4,20},{8,0},{12,28},{16,24},{20,4},{24,16},{28,12},{1,9},{5... | collective-permute-start | bytes 1572872 | tf_op jit(solution)/shard_map/ppermute | solution.py:65
  51.2 10.7 %collective-permute-start.17 = (f32[160,1024]{1,0:T(8,128)S(1)}, f32[160,1024]{1,0:T(8,128)S(1)}, u32[]{:S(2)}, u32[]{:S(2)}) collective-permute-start(f32[160,1024]{1,0:T(8,128)S(1)} %get-tuple-element.80.refs_0_), channel_id=1, source_target_pairs={{0,16},{4,12},{8,24},{12,4},{16,0},{20,28},{24,8},{28,20},{1,17},{... | collective-permute-start | bytes 1966088 | tf_op jit(solution)/shard_map/ppermute | solution.py:65
  53.3 0.7 collective-permute-start.13
  54.6 15.4 %collective-permute-start.20 = (f32[128,1024]{1,0:T(8,128)S(1)}, f32[128,1024]{1,0:T(8,128)S(1)}, u32[]{:S(2)}, u32[]{:S(2)}) collective-permute-start(f32[128,1024]{1,0:T(8,128)S(1)} %get-tuple-element.85.refs_0_), channel_id=1, source_target_pairs={{0,16},{4,12},{8,24},{12,4},{16,0},{20,28},{24,8},{28,20},{1,17},{... | collective-permute-start | bytes 1572872 | tf_op jit(solution)/shard_map/ppermute | solution.py:65
  58.3 1.3 %collective-permute-start.16 = (f32[32,512]{1,0:T(8,128)S(1)}, f32[32,512]{1,0:T(8,128)S(1)}, u32[]{:S(2)}, u32[]{:S(2)}) collective-permute-start(f32[32,512]{1,0:T(8,128)S(1)} %rest.4), channel_id=1, source_target_pairs={{3,1},{7,5},{11,9},{15,13},{19,17},{23,21},{27,25},{31,29}} | collective-permute-start | bytes 196616 | tf_op jit(solution)/shard_map/ppermute | solution.py:397
  59.0 0.7 collective-permute-start.15
  62.5 9.4 %collective-permute-start.21 = (f32[128,1024]{1,0:T(8,128)S(1)}, f32[128,1024]{1,0:T(8,128)S(1)}, u32[]{:S(2)}, u32[]{:S(2)}) collective-permute-start(f32[128,1024]{1,0:T(8,128)S(1)} %get-tuple-element.87.mine_ref), channel_id=1, source_target_pairs={{0,4},{4,0},{8,12},{12,8},{16,20},{20,16},{24,28},{28,24},{1,5},{5... | collective-permute-start | bytes 1572872 | tf_op jit(solution)/shard_map/ppermute | solution.py:60
  63.1 6.8 %collective-permute-start.19 = (f32[32,256]{1,0:T(8,128)S(1)}, f32[32,256]{1,0:T(8,128)S(1)}, u32[]{:S(2)}, u32[]{:S(2)}) collective-permute-start(f32[32,256]{1,0:T(8,128)S(1)} %rest.5), channel_id=1, source_target_pairs={{2,0},{6,4},{10,8},{14,12},{18,16},{22,20},{26,24},{30,28}} | collective-permute-start | bytes 98312 | tf_op jit(solution)/shard_map/ppermute | solution.py:397
  64.4 6.0 %collective-permute-start.18 = (f32[32,256]{1,0:T(8,128)S(1)}, f32[32,256]{1,0:T(8,128)S(1)}, u32[]{:S(2)}, u32[]{:S(2)}) collective-permute-start(f32[32,256]{1,0:T(8,128)S(1)} %get-tuple-element.83), channel_id=1, source_target_pairs={{1,0},{5,4},{9,8},{13,12},{17,16},{21,20},{25,24},{29,28}} | collective-permute-start | bytes 98312 | tf_op jit(solution)/shard_map/ppermute | solution.py:394
  71.8 5.6 %collective-permute-start.23 = (f32[128,1024]{1,0:T(8,128)S(1)}, f32[128,1024]{1,0:T(8,128)S(1)}, u32[]{:S(2)}, u32[]{:S(2)}) collective-permute-start(f32[128,1024]{1,0:T(8,128)S(1)} %get-tuple-element.88.mine_ref), channel_id=1, source_target_pairs={{0,4},{4,0},{8,12},{12,8},{16,20},{20,16},{24,28},{28,24},{1,5},{5... | collective-permute-start | bytes 1572872 | tf_op jit(solution)/shard_map/ppermute | solution.py:60
  73.0 6.1 %collective-permute-start.22 = (f32[32,256]{1,0:T(8,128)S(1)}, f32[32,256]{1,0:T(8,128)S(1)}, u32[]{:S(2)}, u32[]{:S(2)}) collective-permute-start(f32[32,256]{1,0:T(8,128)S(1)} %get-tuple-element.99), channel_id=1, source_target_pairs={{0,3},{1,2},{2,1},{3,0},{4,7},{5,6},{6,5},{7,4},{8,11},{9,10},{10,... | collective-permute-start | bytes 98312 | tf_op jit(solution)/shard_map/ppermute | solution.py:526
  73.1 6.0 %collective-permute-start.24 = (f32[32,256]{1,0:T(8,128)S(1)}, f32[32,256]{1,0:T(8,128)S(1)}, u32[]{:S(2)}, u32[]{:S(2)}) collective-permute-start(f32[32,256]{1,0:T(8,128)S(1)} %get-tuple-element.101), channel_id=1, source_target_pairs={{0,2},{1,3},{2,0},{3,1},{4,6},{5,7},{6,4},{7,5},{8,10},{9,11},{10,... | collective-permute-start | bytes 98312 | tf_op jit(solution)/shard_map/ppermute | solution.py:526
  74.0 5.5 %collective-permute-start.25 = (f32[32,256]{1,0:T(8,128)S(1)}, f32[32,256]{1,0:T(8,128)S(1)}, u32[]{:S(2)}, u32[]{:S(2)}) collective-permute-start(f32[32,256]{1,0:T(8,128)S(1)} %get-tuple-element.100), channel_id=1, source_target_pairs={{0,1},{1,0},{2,3},{3,2},{4,5},{5,4},{6,7},{7,6},{8,9},{9,8},{10,11... | collective-permute-start | bytes 98312 | tf_op jit(solution)/shard_map/ppermute | solution.py:526
  80.0 1.9 %collective-permute-start.26 = (f32[32,256]{1,0:T(8,128)S(1)}, f32[32,256]{1,0:T(8,128)S(1)}, u32[]{:S(2)}, u32[]{:S(2)}) collective-permute-start(f32[32,256]{1,0:T(8,128)S(1)} %get-tuple-element.92), channel_id=1, source_target_pairs={{3,2},{7,6},{11,10},{15,14},{19,18},{23,22},{27,26},{31,30}} | collective-permute-start | bytes 98312 | tf_op jit(solution)/shard_map/ppermute | solution.py:394
  81.2 3.8 %collective-permute-start.28 = (f32[32,512]{1,0:T(8,128)S(1)}, f32[32,512]{1,0:T(8,128)S(1)}, u32[]{:S(2)}, u32[]{:S(2)}) collective-permute-start(f32[32,512]{1,0:T(8,128)S(1)} %rest.6), channel_id=1, source_target_pairs={{3,1},{7,5},{11,9},{15,13},{19,17},{23,21},{27,25},{31,29}} | collective-permute-start | bytes 196616 | tf_op jit(solution)/shard_map/ppermute | solution.py:397
  82.5 2.5 %collective-permute-start.27 = (f32[32,256]{1,0:T(8,128)S(1)}, f32[32,256]{1,0:T(8,128)S(1)}, u32[]{:S(2)}, u32[]{:S(2)}) collective-permute-start(f32[32,256]{1,0:T(8,128)S(1)} %get-tuple-element.94), channel_id=1, source_target_pairs={{2,1},{6,5},{10,9},{14,13},{18,17},{22,21},{26,25},{30,29}} | collective-permute-start | bytes 98312 | tf_op jit(solution)/shard_map/ppermute | solution.py:394
  83.7 9.5 %collective-permute-start.30 = (f32[32,256]{1,0:T(8,128)S(1)}, f32[32,256]{1,0:T(8,128)S(1)}, u32[]{:S(2)}, u32[]{:S(2)}) collective-permute-start(f32[32,256]{1,0:T(8,128)S(1)} %rest.7), channel_id=1, source_target_pairs={{2,0},{6,4},{10,8},{14,12},{18,16},{22,20},{26,24},{30,28}} | collective-permute-start | bytes 98312 | tf_op jit(solution)/shard_map/ppermute | solution.py:397
  85.6 10.3 %collective-permute-start.29 = (f32[32,256]{1,0:T(8,128)S(1)}, f32[32,256]{1,0:T(8,128)S(1)}, u32[]{:S(2)}, u32[]{:S(2)}) collective-permute-start(f32[32,256]{1,0:T(8,128)S(1)} %get-tuple-element.96), channel_id=1, source_target_pairs={{1,0},{5,4},{9,8},{13,12},{17,16},{21,20},{25,24},{29,28}} | collective-permute-start | bytes 98312 | tf_op jit(solution)/shard_map/ppermute | solution.py:394

commit v9 on v8

--- a/solution.py
+++ b/solution.py
@@ -321,22 +321,30 @@
 def run_stage(where, base, tile, add, near, far, held, stage, packs=()):
     columns, band = base.shape
     left = stage * band
-    last = max(left - band, 0)
+    wide = far is None
+    first = 0 if wide else max(left - band, 0)
+    width = max(left, band) - first
     inputs = [pack_inputs(*pack) for pack in packs]
     more = [pack_parts(*pack[1:]) for pack in packs]
     count = sum(len(args) for args in inputs)
-
-    def body(where_ref, base_ref, tile_ref, add_ref, near_ref, far_ref, held_ref, *refs):
+    come = (near,) if wide else (near, far)
+
+    def body(where_ref, base_ref, tile_ref, add_ref, held_ref, *refs):
+        come_refs, refs = refs[: len(come)], refs[len(come) :]
         ins, (solved_ref, update_ref), outs = refs[:count], refs[count : count + 2], refs[count + 2 :]
 
         @pl.when(where_ref[1] == stage)
         def _():
-            right = base_ref[...] - near_ref[...] - far_ref[:, left : left + band]
+            if wide:
+                right = base_ref[...] - come_refs[0][:, left:]
+            else:
+                right = base_ref[...] - come_refs[0][...] - come_refs[1][:, left : left + band]
             solved = dot3(right, tile_ref[:, left : left + band])
             solved_ref[...] = solved
             if stage > 0:
-                here = slice(last, left)
-                update_ref[...] = far_ref[:, here] + add_ref[:, here] + dot3(solved, tile_ref[:, here])
+                here = slice(first, left)
+                passed = come_refs[-1][:, here] + add_ref[:, here]
+                update_ref[...] = passed + dot3(solved, tile_ref[:, here])
 
         @pl.when(where_ref[1] != stage)
         def _():
@@ -346,8 +354,8 @@
             add_pack(*ins[: len(args)], *outs[: len(out)])
             ins, outs = ins[len(args) :], outs[len(out) :]
 
-    out = (shape(columns, band), shape(columns, band)) + sum((out for _, out in more), ())
-    args = (where, base, tile, add, near, far, held) + sum(inputs, ())
+    out = (shape(columns, band), shape(columns, width)) + sum((out for _, out in more), ())
+    args = (where, base, tile, add, held) + come + sum(inputs, ())
     return call(body, out, (SMEM,) + (VMEM,) * (len(args) - 1), args, "stage")
 
 
@@ -382,17 +390,18 @@
 def sweep(where, base, tile, add, bands, packs=None):
     columns, band = base.shape
     aligned = band % 128 == 0
+    wide = packs is not None and aligned
     stage_of, rest_of = (run_stage, run_rest) if aligned else (run_stage_plain, run_rest_plain)
-    near = jnp.zeros((columns, band), F32)
+    near = jnp.zeros((columns, bands * band if wide else band), F32)
     held = jnp.zeros((columns, band), F32)
-    fars = [jnp.zeros((columns, bands * band), F32)] * 2
+    fars = [None] * bands if wide else [jnp.zeros((columns, bands * band), F32)] * 2
     for stage in range(bands - 1, -1, -1):
         far = fars.pop(0)
         taken = packs.take(bands - 1 - stage) if packs else ()
         held, update, *more = stage_of(where, base, tile, add, near, far, held, stage, taken)
         if stage > 0:
             near = lax.ppermute(update, "ct", [(stage, stage - 1)])
-        if stage > 1:
+        if stage > 1 and not wide:
             rest = rest_of(where, tile, add, far, held, stage)
             fars.append(lax.ppermute(rest, "ct", [(stage, stage - 2)]))
         if more:
@@ -499,7 +508,7 @@
             got_tile = swap_chip(tile_one, members, stage + 2) if stage < stages - 2 else None
 
     got_up = []
-    for shift in range(1, bands):
+    for shift in range(bands - 1, 0, -1):
         piece = own_band(sum_one, jnp.minimum(place + shift, bands - 1), band)
         got_up.append(lax.ppermute(piece, "ct", [(i, i + shift) for i in range(bands - shift)]))
 

time: 98.6 us -> 96.3 us (0.977)
  starting transfers between devices: 42.7 us -> 31.8 us
  waiting for transfers between devices: 28.1 us -> 36.2 us
  Pallas kernels: 23.4 us -> 24.7 us
    ppermute x8, waiting for transfers between devices: 10.1 us -> 21.7 us  [swap_chip(): lax.ppermute(value, 'rt', [(i, i ^ 1 << orders[i & 1][stage]) for i in ra...]
    ppermute x8, starting transfers between devices: 14.7 us -> 8.2 us  [swap_chip(): lax.ppermute(value, 'rt', [(i, i ^ 1 << orders[i & 1][stage]) for i in ra...]
    ppermute x4 -> x2, waiting for transfers between devices: 10.5 us -> 6.32 us  [sweep(): fars.append(lax.ppermute(rest, 'ct', [(stage, stage - 2)]))]
    ppermute x7, starting transfers between devices: 3.99 us -> 1.49 us  [swap_core(): return lax.ppermute(value, 'rt', [(i, i ^ 1) for i in range(members)])]
    ppermute x4 -> x2, starting transfers between devices: 3.91 us -> 1.96 us  [sweep(): fars.append(lax.ppermute(rest, 'ct', [(stage, stage - 2)]))]
    pallas_call x20 -> x18, Pallas kernels: 23.4 us -> 24.7 us  [call(): pl.pallas_call(body, out_shape=out, in_specs=list(specs), out_specs=tuple...]
  transfers between devices with their start and end apart: 31 -> 29, of which waited for: 11 -> 12; matrix products, arithmetic and copies ran while one was open for 2% -> 2% of each run, Pallas kernels for 21% -> 23%
where the time goes in v9:
time: 96.3 us; the launch traced here: 96.4 us
  waiting for transfers between devices  36.2 us (38%)
  starting transfers between devices  31.8 us (33%)
  Pallas kernels  24.7 us (26%)
  other arithmetic  1.84 us (2%)
  local copies, waits for them, and re-layouts  1.34 us (1%)
    pallas_call x18, Pallas kernels, call(): pl.pallas_call(body, out_shape=out, in_specs=list(specs), out_specs=tuple...  24.7 us
    ppermute x8, waiting for transfers between devices, swap_chip(): lax.ppermute(value, 'rt', [(i, i ^ 1 << orders[i & 1][stage]) for i in ra...  21.7 us
    ppermute x3, starting transfers between devices, shards(): lax.ppermute(piece, 'ct', [(i, i + shift) for i in range(bands - shift)])  10.5 us
    ppermute x8, starting transfers between devices, swap_chip(): lax.ppermute(value, 'rt', [(i, i ^ 1 << orders[i & 1][stage]) for i in ra...  8.2 us
    ppermute x2, waiting for transfers between devices, sweep(): fars.append(lax.ppermute(rest, 'ct', [(stage, stage - 2)]))  6.32 us
    ppermute x6, starting transfers between devices, sweep(): near = lax.ppermute(update, 'ct', [(stage, stage - 1)])  5.23 us
    ppermute x3, starting transfers between devices, shards(): lax.ppermute(pieces[mask], 'ct', [(i, i ^ mask) for i in range(bands)])  4.45 us
    ppermute x6, waiting for transfers between devices, sweep(): near = lax.ppermute(update, 'ct', [(stage, stage - 1)])  3.55 us
  transfers between devices with their start and end apart: 29, of which 12 were waited for; matrix products, arithmetic and copies ran while one was open for 2% of the time, Pallas kernels for 23%

profile of v9, /device:TPU:0, one launch (start us, length us, event | category | flops | bytes accessed | tf_op | source)
XLA Modules:
  0.0 96.4 jit_solution(7876269883245926655)
XLA Ops:
  0.0 0.1 pad_add_fusion.where_ref
  0.1 0.7 copy-done
  0.7 0.6 first_band.1
  1.4 0.5 collective-permute-start
  1.9 1.5 %collective-permute-done = f32[128,1024]{1,0:T(8,128)S(1)} collective-permute-done((f32[128,1024]{1,0:T(8,128)S(1)}, f32[128,1024]{1,0:T(8,128)S(1)}, u32[]{:S(2)}, u32[]{:S(2)}) %collective-permute-start) | collective-permute-done | bytes 524320 | tf_op jit(solution)/shard_map/ppermute | solution.py:60
  3.4 0.1 add.39
  3.5 2.9 %collective-permute-start.2 = (f32[128,1024]{1,0:T(8,128)S(1)}, f32[128,1024]{1,0:T(8,128)S(1)}, u32[]{:S(2)}, u32[]{:S(2)}) collective-permute-start(f32[128,1024]{1,0:T(8,128)S(1)} %add.39), channel_id=1, source_target_pairs={{0,8},{4,20},{8,0},{12,28},{16,24},{20,4},{24,16},{28,12},{1,9},{5... | collective-permute-start | bytes 1572872 | tf_op jit(solution)/shard_map/ppermute | solution.py:65
  6.4 9.6 %front.1 = (f32[128,1024]{1,0:T(8,128)S(1)}, f32[128,1024]{1,0:T(8,128)S(1)}, f32[256,1024]{1,0:T(8,128)S(1)}, f32[256,1024]{1,0:T(8,128)S(1)}) custom-call(s32[2]{0:T(128)S(1)} %pad_add_fusion.where_ref, s32[48]{0:T(128)S(1)} %copy-done, f32[6,2,256,1024]{3,2,1,0:T(8,128)} %factor_ref.5, f32[6,256,256]{2,1,0:T(8,128)} %known_ref.1), custom_call_target="tpu_custom_call" | custom-call | tf_op jit(solution)/shard_map/front/pallas_call | solution.py:23
  16.1 0.1 collective-permute-start.1
  16.2 0.1 add.40
  16.2 1.8 %collective-permute-done.1 = f32[128,1024]{1,0:T(8,128)S(1)} collective-permute-done((f32[128,1024]{1,0:T(8,128)S(1)}, f32[128,1024]{1,0:T(8,128)S(1)}, u32[]{:S(2)}, u32[]{:S(2)}) %collective-permute-start.1) | collective-permute-done | bytes 524320 | tf_op jit(solution)/shard_map/ppermute | solution.py:60
  18.1 0.2 collective-permute-start.11
  18.3 0.1 collective-permute-start.3
  18.4 1.4 %collective-permute-start.7 = (f32[128,1024]{1,0:T(8,128)S(1)}, f32[128,1024]{1,0:T(8,128)S(1)}, u32[]{:S(2)}, u32[]{:S(2)}) collective-permute-start(f32[128,1024]{1,0:T(8,128)S(1)} %add.40), channel_id=1, source_target_pairs={{0,16},{4,12},{8,24},{12,4},{16,0},{20,28},{24,8},{28,20},{1,17},{... | collective-permute-start | bytes 1572872 | tf_op jit(solution)/shard_map/ppermute | solution.py:65
  19.8 1.6 %top_band.1 = (f32[128,1024]{1,0:T(8,128)S(1)}, f32[128,1024]{1,0:T(8,128)}) custom-call(s32[2]{0:T(128)S(1)} %pad_add_fusion.where_ref, s32[48]{0:T(128)S(1)} %copy-done, f32[6,2,256,1024]{3,2,1,0:T(8,128)} %factor_ref.5), custom_call_target="tpu_custom_call" | custom-call | tf_op jit(solution)/shard_map/top_band/pallas_call | solution.py:23
  21.5 6.0 %collective-permute-done.3 = f32[64,1024]{1,0:T(8,128)S(1)} collective-permute-done((f32[64,1024]{1,0:T(8,128)S(1)}, f32[64,1024]{1,0:T(8,128)S(1)}, u32[]{:S(2)}, u32[]{:S(2)}) %collective-permute-start.3) | collective-permute-done | bytes 262176 | tf_op jit(solution)/shard_map/ppermute | solution.py:65
  27.6 0.1 collective-permute-start.4
  27.6 5.0 %collective-permute-done.4 = f32[32,1024]{1,0:T(8,128)S(1)} collective-permute-done((f32[32,1024]{1,0:T(8,128)S(1)}, f32[32,1024]{1,0:T(8,128)S(1)}, u32[]{:S(2)}, u32[]{:S(2)}) %collective-permute-start.4) | collective-permute-done | bytes 131104 | tf_op jit(solution)/shard_map/ppermute | solution.py:65
  32.6 0.1 pack_step.3
  32.7 0.1 collective-permute-start.12
  32.8 0.1 collective-permute-start.6
  33.0 0.6 collective-permute-start.8
  33.5 0.6 constant_dynamic-slice_fusion.2
  34.2 6.1 %collective-permute-start.5 = (f32[32,256]{1,0:T(8,128)}, f32[32,256]{1,0:T(8,128)}, u32[]{:S(2)}, u32[]{:S(2)}) collective-permute-start(f32[32,256]{1,0:T(8,128)} %get-tuple-element.102), channel_id=1, source_target_pairs={{0,3},{4,7},{8,11},{12,15},{16,19},{20,23},{24,27},{28,31}} | collective-permute-start | bytes 98312 | tf_op jit(solution)/shard_map/ppermute | solution.py:513
  40.3 1.9 %collective-permute-start.9 = (f32[32,256]{1,0:T(8,128)}, f32[32,256]{1,0:T(8,128)}, u32[]{:S(2)}, u32[]{:S(2)}) collective-permute-start(f32[32,256]{1,0:T(8,128)} %get-tuple-element.104), channel_id=1, source_target_pairs={{0,2},{1,3},{4,6},{5,7},{8,10},{9,11},{12,14},{13,15},{16,18},{17,... | collective-permute-start | bytes 98312 | tf_op jit(solution)/shard_map/ppermute | solution.py:513
  42.2 2.5 %collective-permute-start.10 = (f32[32,256]{1,0:T(8,128)}, f32[32,256]{1,0:T(8,128)}, u32[]{:S(2)}, u32[]{:S(2)}) collective-permute-start(f32[32,256]{1,0:T(8,128)} %get-tuple-element.103), channel_id=1, source_target_pairs={{0,1},{1,2},{2,3},{4,5},{5,6},{6,7},{8,9},{9,10},{10,11},{12,13},{... | collective-permute-start | bytes 98312 | tf_op jit(solution)/shard_map/ppermute | solution.py:513
  44.7 2.0 %collective-permute-start.14 = (f32[128,1024]{1,0:T(8,128)S(1)}, f32[128,1024]{1,0:T(8,128)S(1)}, u32[]{:S(2)}, u32[]{:S(2)}) collective-permute-start(f32[128,1024]{1,0:T(8,128)S(1)} %pack_step.2.refs_1_), channel_id=1, source_target_pairs={{0,8},{4,20},{8,0},{12,28},{16,24},{20,4},{24,16},{28,12},{1,9},{5... | collective-permute-start | bytes 1572872 | tf_op jit(solution)/shard_map/ppermute | solution.py:65
  46.7 3.5 %join.2.tile_ref = f32[256,1024]{1,0:T(8,128)S(1)} custom-call(s32[2]{0:T(128)S(1)} %pad_add_fusion.where_ref, f32[128,1024]{1,0:T(8,128)S(1)} %add.47.mine_ref, f32[128,1024]{1,0:T(8,128)} %collective-permute-done.8.other_ref), custom_call_target="tpu_custom_call" | custom-call | tf_op jit(solution)/shard_map/join/pallas_call | solution.py:23
  50.3 0.8 fusion.6.base_ref
  51.1 0.6 stage.8
  51.8 0.1 collective-permute-start.16
  51.9 0.7 collective-permute-start.13
  52.5 2.8 %collective-permute-done.14.refs_2_ = f32[128,1024]{1,0:T(8,128)S(1)} collective-permute-done((f32[128,1024]{1,0:T(8,128)S(1)}, f32[128,1024]{1,0:T(8,128)S(1)}, u32[]{:S(2)}, u32[]{:S(2)}) %collective-permute-start.14) | collective-permute-done | bytes 524320 | tf_op jit(solution)/shard_map/ppermute | solution.py:65
  55.4 0.6 stage.9
  56.0 1.5 %collective-permute-start.18 = (f32[128,1024]{1,0:T(8,128)S(1)}, f32[128,1024]{1,0:T(8,128)S(1)}, u32[]{:S(2)}, u32[]{:S(2)}) collective-permute-start(f32[128,1024]{1,0:T(8,128)S(1)} %get-tuple-element.85.refs_1_), channel_id=1, source_target_pairs={{0,16},{4,12},{8,24},{12,4},{16,0},{20,28},{24,8},{28,20},{1,17},{... | collective-permute-start | bytes 1572872 | tf_op jit(solution)/shard_map/ppermute | solution.py:65
  57.5 0.7 collective-permute-start.15
  58.2 4.2 %collective-permute-done.16.refs_3_ = f32[160,1024]{1,0:T(8,128)S(1)} collective-permute-done((f32[160,1024]{1,0:T(8,128)S(1)}, f32[160,1024]{1,0:T(8,128)S(1)}, u32[]{:S(2)}, u32[]{:S(2)}) %collective-permute-start.16) | collective-permute-done | bytes 655392 | tf_op jit(solution)/shard_map/ppermute | solution.py:65
  62.4 0.6 stage.10
  63.1 0.1 collective-permute-start.19
  63.1 1.3 %collective-permute-start.17 = (f32[32,256]{1,0:T(8,128)S(1)}, f32[32,256]{1,0:T(8,128)S(1)}, u32[]{:S(2)}, u32[]{:S(2)}) collective-permute-start(f32[32,256]{1,0:T(8,128)S(1)} %get-tuple-element.84), channel_id=1, source_target_pairs={{1,0},{5,4},{9,8},{13,12},{17,16},{21,20},{25,24},{29,28}} | collective-permute-start | bytes 98312 | tf_op jit(solution)/shard_map/ppermute | solution.py:403
  64.4 3.6 %collective-permute-done.18.refs_2_ = f32[128,1024]{1,0:T(8,128)S(1)} collective-permute-done((f32[128,1024]{1,0:T(8,128)S(1)}, f32[128,1024]{1,0:T(8,128)S(1)}, u32[]{:S(2)}, u32[]{:S(2)}) %collective-permute-start.18) | collective-permute-done | bytes 524320 | tf_op jit(solution)/shard_map/ppermute | solution.py:65
  68.0 0.9 collective-permute-done.17.refs_0_
  69.0 1.4 %stage.11 = (f32[32,256]{1,0:T(8,128)S(1)}, f32[32,256]{1,0:T(8,128)}, f32[128,1024]{1,0:T(8,128)S(1)}) custom-call(s32[2]{0:T(128)S(1)} %pad_add_fusion.where_ref, f32[32,256]{1,0:T(8,128)S(1)} %fusion.6.base_ref, f32[256,1024]{1,0:T(8,128)S(1)} %join.2.tile_ref, f32[32,1024]{1,0:T(8,128)S(1)} %slice_add_fusion.1.add_ref, ...), custom_call_target="tpu_custom_call" | custom-call | tf_op jit(solution)/shard_map/stage/pallas_call | solution.py:23
  70.4 1.2 %couple.1 = f32[4,32,256]{2,1,0:T(8,128)S(1)} custom-call(s32[2]{0:T(128)S(1)} %pad_add_fusion.where_ref, f32[32,1024]{1,0:T(8,128)S(1)} %get-tuple-element.82.sums_ref, f32[32,256]{1,0:T(8,128)S(1)} %get-tuple-element.86.solved_ref, f32[128,1024]{1,0:T(8,128)S(1)} %get-tuple-element.87.mine_ref, f32[128,1024]{1,0:T(8,128)S(1)} %collective-permute-done.19.other_ref), custom_call_target="tpu_custom_call" | custom-call | tf_op jit(solution)/shard_map/couple/pallas_call | solution.py:23
  71.6 0.1 collective-permute-start.20
  71.6 1.0 %collective-permute-start.22 = (f32[32,256]{1,0:T(8,128)S(1)}, f32[32,256]{1,0:T(8,128)S(1)}, u32[]{:S(2)}, u32[]{:S(2)}) collective-permute-start(f32[32,256]{1,0:T(8,128)S(1)} %get-tuple-element.101), channel_id=1, source_target_pairs={{0,2},{1,3},{2,0},{3,1},{4,6},{5,7},{6,4},{7,5},{8,10},{9,11},{10,... | collective-permute-start | bytes 98312 | tf_op jit(solution)/shard_map/ppermute | solution.py:535
  72.6 3.4 %collective-permute-start.23 = (f32[32,256]{1,0:T(8,128)S(1)}, f32[32,256]{1,0:T(8,128)S(1)}, u32[]{:S(2)}, u32[]{:S(2)}) collective-permute-start(f32[32,256]{1,0:T(8,128)S(1)} %get-tuple-element.100), channel_id=1, source_target_pairs={{0,1},{1,0},{2,3},{3,2},{4,5},{5,4},{6,7},{7,6},{8,9},{9,8},{10,11... | collective-permute-start | bytes 98312 | tf_op jit(solution)/shard_map/ppermute | solution.py:535
  76.0 0.6 join.3.tile_ref
  76.6 1.0 %collective-permute-done.20 = f32[32,256]{1,0:T(8,128)S(1)} collective-permute-done((f32[32,256]{1,0:T(8,128)S(1)}, f32[32,256]{1,0:T(8,128)S(1)}, u32[]{:S(2)}, u32[]{:S(2)}) %collective-permute-start.20) | collective-permute-done | bytes 32800 | tf_op jit(solution)/shard_map/ppermute | solution.py:535
  77.6 0.3 collective-permute-done.23
  77.9 0.6 stage.12
  78.5 0.7 collective-permute-start.24
  79.2 0.6 rest.2
  79.7 0.7 collective-permute-start.26
  80.4 0.6 stage.13
  81.0 0.7 collective-permute-start.25
  81.7 0.6 rest.3
  82.2 1.3 %collective-permute-start.28 = (f32[32,256]{1,0:T(8,128)S(1)}, f32[32,256]{1,0:T(8,128)S(1)}, u32[]{:S(2)}, u32[]{:S(2)}) collective-permute-start(f32[32,256]{1,0:T(8,128)S(1)} %rest.3), channel_id=1, source_target_pairs={{2,0},{6,4},{10,8},{14,12},{18,16},{22,20},{26,24},{30,28}} | collective-permute-start | bytes 98312 | tf_op jit(solution)/shard_map/ppermute | solution.py:406
  83.5 0.6 stage.14
  84.1 1.3 %collective-permute-start.27 = (f32[32,256]{1,0:T(8,128)S(1)}, f32[32,256]{1,0:T(8,128)S(1)}, u32[]{:S(2)}, u32[]{:S(2)}) collective-permute-start(f32[32,256]{1,0:T(8,128)S(1)} %get-tuple-element.97), channel_id=1, source_target_pairs={{1,0},{5,4},{9,8},{13,12},{17,16},{21,20},{25,24},{29,28}} | collective-permute-start | bytes 98312 | tf_op jit(solution)/shard_map/ppermute | solution.py:403
  85.4 6.3 %collective-permute-done.28.refs_1_ = f32[32,256]{1,0:T(8,128)S(1)} collective-permute-done((f32[32,256]{1,0:T(8,128)S(1)}, f32[32,256]{1,0:T(8,128)S(1)}, u32[]{:S(2)}, u32[]{:S(2)}) %collective-permute-start.28) | collective-permute-done | bytes 32800 | tf_op jit(solution)/shard_map/ppermute | solution.py:406
  91.7 2.6 %collective-permute-done.27.refs_0_ = f32[32,256]{1,0:T(8,128)S(1)} collective-permute-done((f32[32,256]{1,0:T(8,128)S(1)}, f32[32,256]{1,0:T(8,128)S(1)}, u32[]{:S(2)}, u32[]{:S(2)}) %collective-permute-start.27) | collective-permute-done | bytes 32800 | tf_op jit(solution)/shard_map/ppermute | solution.py:403
  94.4 1.4 %stage.15 = (f32[32,256]{1,0:T(8,128)S(1)}, f32[32,256]{1,0:T(8,128)}) custom-call(s32[2]{0:T(128)S(1)} %pad_add_fusion.where_ref, f32[32,256]{1,0:T(8,128)S(1)} %fusion.3.base_ref, f32[256,1024]{1,0:T(8,128)S(1)} %join.3.tile_ref, f32[32,1024]{1,0:T(8,128)S(1)} %broadcast_3_refs_0__add_ref_refs_1__far_ref.2.refs_0_.add_ref.refs_1_.far_ref, ...), custom_call_target="tpu_custom_call" | custom-call | tf_op jit(solution)/shard_map/stage/pallas_call | solution.py:23
  95.7 0.6 pad_maximum_fusion
  (32 shorter events, 0.3 us)
Async XLA Ops:
  0.1 0.7 copy-start
  1.4 2.1 %collective-permute-start = (f32[128,1024]{1,0:T(8,128)S(1)}, f32[128,1024]{1,0:T(8,128)S(1)}, u32[]{:S(2)}, u32[]{:S(2)}) collective-permute-start(f32[128,1024]{1,0:T(8,128)S(1)} %get-tuple-element.53), channel_id=1, source_target_pairs={{0,4},{4,0},{8,12},{12,8},{16,20},{20,16},{24,28},{28,24},{1,5},{5... | collective-permute-start | bytes 1572872 | tf_op jit(solution)/shard_map/ppermute | solution.py:60
  3.5 12.6 %collective-permute-start.2 = (f32[128,1024]{1,0:T(8,128)S(1)}, f32[128,1024]{1,0:T(8,128)S(1)}, u32[]{:S(2)}, u32[]{:S(2)}) collective-permute-start(f32[128,1024]{1,0:T(8,128)S(1)} %add.39), channel_id=1, source_target_pairs={{0,8},{4,20},{8,0},{12,28},{16,24},{20,4},{24,16},{28,12},{1,9},{5... | collective-permute-start | bytes 1572872 | tf_op jit(solution)/shard_map/ppermute | solution.py:65
  16.1 2.0 %collective-permute-start.1 = (f32[128,1024]{1,0:T(8,128)S(1)}, f32[128,1024]{1,0:T(8,128)S(1)}, u32[]{:S(2)}, u32[]{:S(2)}) collective-permute-start(f32[128,1024]{1,0:T(8,128)S(1)} %get-tuple-element.56), channel_id=1, source_target_pairs={{0,4},{4,0},{8,12},{12,8},{16,20},{20,16},{24,28},{28,24},{1,5},{5... | collective-permute-start | bytes 1572872 | tf_op jit(solution)/shard_map/ppermute | solution.py:60
  18.1 14.5 %collective-permute-start.11 = (f32[256,1024]{1,0:T(8,128)S(1)}, f32[256,1024]{1,0:T(8,128)S(1)}, u32[]{:S(2)}, u32[]{:S(2)}) collective-permute-start(f32[256,1024]{1,0:T(8,128)S(1)} %get-tuple-element.72), channel_id=1, source_target_pairs={{0,4},{4,0},{8,12},{12,8},{16,20},{20,16},{24,28},{28,24},{1,5},{5... | collective-permute-start | bytes 3145736 | tf_op jit(solution)/shard_map/ppermute | solution.py:60
  18.3 9.2 %collective-permute-start.3 = (f32[64,1024]{1,0:T(8,128)S(1)}, f32[64,1024]{1,0:T(8,128)S(1)}, u32[]{:S(2)}, u32[]{:S(2)}) collective-permute-start(f32[64,1024]{1,0:T(8,128)S(1)} %slice.41), channel_id=1, source_target_pairs={{0,8},{4,20},{8,0},{12,28},{16,24},{20,4},{24,16},{28,12},{1,9},{5... | collective-permute-start | bytes 786440 | tf_op jit(solution)/shard_map/ppermute | solution.py:65
  18.4 14.5 %collective-permute-start.7 = (f32[128,1024]{1,0:T(8,128)S(1)}, f32[128,1024]{1,0:T(8,128)S(1)}, u32[]{:S(2)}, u32[]{:S(2)}) collective-permute-start(f32[128,1024]{1,0:T(8,128)S(1)} %add.40), channel_id=1, source_target_pairs={{0,16},{4,12},{8,24},{12,4},{16,0},{20,28},{24,8},{28,20},{1,17},{... | collective-permute-start | bytes 1572872 | tf_op jit(solution)/shard_map/ppermute | solution.py:65
  27.6 5.0 %collective-permute-start.4 = (f32[32,1024]{1,0:T(8,128)S(1)}, f32[32,1024]{1,0:T(8,128)S(1)}, u32[]{:S(2)}, u32[]{:S(2)}) collective-permute-start(f32[32,1024]{1,0:T(8,128)S(1)} %slice.43), channel_id=1, source_target_pairs={{0,16},{4,12},{8,24},{12,4},{16,0},{20,28},{24,8},{28,20},{1,17},{... | collective-permute-start | bytes 393224 | tf_op jit(solution)/shard_map/ppermute | solution.py:65
  32.7 18.4 %collective-permute-start.12 = (f32[192,1024]{1,0:T(8,128)S(1)}, f32[192,1024]{1,0:T(8,128)S(1)}, u32[]{:S(2)}, u32[]{:S(2)}) collective-permute-start(f32[192,1024]{1,0:T(8,128)S(1)} %get-tuple-element.74.refs_1_), channel_id=1, source_target_pairs={{0,8},{4,20},{8,0},{12,28},{16,24},{20,4},{24,16},{28,12},{1,9},{5... | collective-permute-start | bytes 2359304 | tf_op jit(solution)/shard_map/ppermute | solution.py:65
  32.8 9.3 %collective-permute-start.6 = (f32[128,1024]{1,0:T(8,128)}, f32[128,1024]{1,0:T(8,128)S(1)}, u32[]{:S(2)}, u32[]{:S(2)}) collective-permute-start(f32[128,1024]{1,0:T(8,128)} %get-tuple-element.63), channel_id=1, source_target_pairs={{0,4},{4,0},{8,12},{12,8},{16,20},{20,16},{24,28},{28,24},{1,5},{5... | collective-permute-start | bytes 1572872 | tf_op jit(solution)/shard_map/ppermute | solution.py:60
  33.0 11.7 %collective-permute-start.8 = (f32[128,1024]{1,0:T(8,128)S(1)}, f32[128,1024]{1,0:T(8,128)}, u32[]{:S(2)}, u32[]{:S(2)}) collective-permute-start(f32[128,1024]{1,0:T(8,128)S(1)} %add.47.mine_ref), channel_id=1, source_target_pairs={{0,4},{4,0},{8,12},{12,8},{16,20},{20,16},{24,28},{28,24},{1,5},{5... | collective-permute-start | bytes 1572872 | tf_op jit(solution)/shard_map/ppermute | solution.py:60
  34.2 16.1 %collective-permute-start.5 = (f32[32,256]{1,0:T(8,128)}, f32[32,256]{1,0:T(8,128)}, u32[]{:S(2)}, u32[]{:S(2)}) collective-permute-start(f32[32,256]{1,0:T(8,128)} %get-tuple-element.102), channel_id=1, source_target_pairs={{0,3},{4,7},{8,11},{12,15},{16,19},{20,23},{24,27},{28,31}} | collective-permute-start | bytes 98312 | tf_op jit(solution)/shard_map/ppermute | solution.py:513
  40.3 10.0 %collective-permute-start.9 = (f32[32,256]{1,0:T(8,128)}, f32[32,256]{1,0:T(8,128)}, u32[]{:S(2)}, u32[]{:S(2)}) collective-permute-start(f32[32,256]{1,0:T(8,128)} %get-tuple-element.104), channel_id=1, source_target_pairs={{0,2},{1,3},{4,6},{5,7},{8,10},{9,11},{12,14},{13,15},{16,18},{17,... | collective-permute-start | bytes 98312 | tf_op jit(solution)/shard_map/ppermute | solution.py:513
  42.2 8.1 %collective-permute-start.10 = (f32[32,256]{1,0:T(8,128)}, f32[32,256]{1,0:T(8,128)}, u32[]{:S(2)}, u32[]{:S(2)}) collective-permute-start(f32[32,256]{1,0:T(8,128)} %get-tuple-element.103), channel_id=1, source_target_pairs={{0,1},{1,2},{2,3},{4,5},{5,6},{6,7},{8,9},{9,10},{10,11},{12,13},{... | collective-permute-start | bytes 98312 | tf_op jit(solution)/shard_map/ppermute | solution.py:513
  44.6 33.3 %copy-start.1 = (f32[2,256,32]{1,2,0:T(8,128)S(1)}, f32[2,256,32]{1,2,0:T(8,128)}, u32[]{:S(2)}) copy-start(f32[2,256,32]{1,2,0:T(8,128)} %param.7) | copy-start | bytes 196612
  44.7 10.6 %collective-permute-start.14 = (f32[128,1024]{1,0:T(8,128)S(1)}, f32[128,1024]{1,0:T(8,128)S(1)}, u32[]{:S(2)}, u32[]{:S(2)}) collective-permute-start(f32[128,1024]{1,0:T(8,128)S(1)} %pack_step.2.refs_1_), channel_id=1, source_target_pairs={{0,8},{4,20},{8,0},{12,28},{16,24},{20,4},{24,16},{28,12},{1,9},{5... | collective-permute-start | bytes 1572872 | tf_op jit(solution)/shard_map/ppermute | solution.py:65
  51.8 10.7 %collective-permute-start.16 = (f32[160,1024]{1,0:T(8,128)S(1)}, f32[160,1024]{1,0:T(8,128)S(1)}, u32[]{:S(2)}, u32[]{:S(2)}) collective-permute-start(f32[160,1024]{1,0:T(8,128)S(1)} %get-tuple-element.80.refs_1_), channel_id=1, source_target_pairs={{0,16},{4,12},{8,24},{12,4},{16,0},{20,28},{24,8},{28,20},{1,17},{... | collective-permute-start | bytes 1966088 | tf_op jit(solution)/shard_map/ppermute | solution.py:65
  51.9 3.5 %collective-permute-start.13 = (f32[32,768]{1,0:T(8,128)S(1)}, f32[32,768]{1,0:T(8,128)S(1)}, u32[]{:S(2)}, u32[]{:S(2)}) collective-permute-start(f32[32,768]{1,0:T(8,128)S(1)} %get-tuple-element.77), channel_id=1, source_target_pairs={{3,2},{7,6},{11,10},{15,14},{19,18},{23,22},{27,26},{31,30}} | collective-permute-start | bytes 294920 | tf_op jit(solution)/shard_map/ppermute | solution.py:403
  56.0 12.1 %collective-permute-start.18 = (f32[128,1024]{1,0:T(8,128)S(1)}, f32[128,1024]{1,0:T(8,128)S(1)}, u32[]{:S(2)}, u32[]{:S(2)}) collective-permute-start(f32[128,1024]{1,0:T(8,128)S(1)} %get-tuple-element.85.refs_1_), channel_id=1, source_target_pairs={{0,16},{4,12},{8,24},{12,4},{16,0},{20,28},{24,8},{28,20},{1,17},{... | collective-permute-start | bytes 1572872 | tf_op jit(solution)/shard_map/ppermute | solution.py:65
  57.5 0.7 collective-permute-start.15
  63.1 7.3 %collective-permute-start.19 = (f32[128,1024]{1,0:T(8,128)S(1)}, f32[128,1024]{1,0:T(8,128)S(1)}, u32[]{:S(2)}, u32[]{:S(2)}) collective-permute-start(f32[128,1024]{1,0:T(8,128)S(1)} %get-tuple-element.87.mine_ref), channel_id=1, source_target_pairs={{0,4},{4,0},{8,12},{12,8},{16,20},{20,16},{24,28},{28,24},{1,5},{5... | collective-permute-start | bytes 1572872 | tf_op jit(solution)/shard_map/ppermute | solution.py:60
  63.1 5.8 %collective-permute-start.17 = (f32[32,256]{1,0:T(8,128)S(1)}, f32[32,256]{1,0:T(8,128)S(1)}, u32[]{:S(2)}, u32[]{:S(2)}) collective-permute-start(f32[32,256]{1,0:T(8,128)S(1)} %get-tuple-element.84), channel_id=1, source_target_pairs={{1,0},{5,4},{9,8},{13,12},{17,16},{21,20},{25,24},{29,28}} | collective-permute-start | bytes 98312 | tf_op jit(solution)/shard_map/ppermute | solution.py:403
  70.4 5.6 %collective-permute-start.21 = (f32[128,1024]{1,0:T(8,128)S(1)}, f32[128,1024]{1,0:T(8,128)S(1)}, u32[]{:S(2)}, u32[]{:S(2)}) collective-permute-start(f32[128,1024]{1,0:T(8,128)S(1)} %get-tuple-element.88.mine_ref), channel_id=1, source_target_pairs={{0,4},{4,0},{8,12},{12,8},{16,20},{20,16},{24,28},{28,24},{1,5},{5... | collective-permute-start | bytes 1572872 | tf_op jit(solution)/shard_map/ppermute | solution.py:60
  71.6 6.1 %collective-permute-start.20 = (f32[32,256]{1,0:T(8,128)S(1)}, f32[32,256]{1,0:T(8,128)S(1)}, u32[]{:S(2)}, u32[]{:S(2)}) collective-permute-start(f32[32,256]{1,0:T(8,128)S(1)} %get-tuple-element.99), channel_id=1, source_target_pairs={{0,3},{1,2},{2,1},{3,0},{4,7},{5,6},{6,5},{7,4},{8,11},{9,10},{10,... | collective-permute-start | bytes 98312 | tf_op jit(solution)/shard_map/ppermute | solution.py:535
  71.6 6.0 %collective-permute-start.22 = (f32[32,256]{1,0:T(8,128)S(1)}, f32[32,256]{1,0:T(8,128)S(1)}, u32[]{:S(2)}, u32[]{:S(2)}) collective-permute-start(f32[32,256]{1,0:T(8,128)S(1)} %get-tuple-element.101), channel_id=1, source_target_pairs={{0,2},{1,3},{2,0},{3,1},{4,6},{5,7},{6,4},{7,5},{8,10},{9,11},{10,... | collective-permute-start | bytes 98312 | tf_op jit(solution)/shard_map/ppermute | solution.py:535
  72.6 5.3 %collective-permute-start.23 = (f32[32,256]{1,0:T(8,128)S(1)}, f32[32,256]{1,0:T(8,128)S(1)}, u32[]{:S(2)}, u32[]{:S(2)}) collective-permute-start(f32[32,256]{1,0:T(8,128)S(1)} %get-tuple-element.100), channel_id=1, source_target_pairs={{0,1},{1,0},{2,3},{3,2},{4,5},{5,4},{6,7},{7,6},{8,9},{9,8},{10,11... | collective-permute-start | bytes 98312 | tf_op jit(solution)/shard_map/ppermute | solution.py:535
  78.5 1.9 %collective-permute-start.24 = (f32[32,256]{1,0:T(8,128)S(1)}, f32[32,256]{1,0:T(8,128)S(1)}, u32[]{:S(2)}, u32[]{:S(2)}) collective-permute-start(f32[32,256]{1,0:T(8,128)S(1)} %get-tuple-element.93), channel_id=1, source_target_pairs={{3,2},{7,6},{11,10},{15,14},{19,18},{23,22},{27,26},{31,30}} | collective-permute-start | bytes 98312 | tf_op jit(solution)/shard_map/ppermute | solution.py:403
  79.7 3.8 %collective-permute-start.26 = (f32[32,512]{1,0:T(8,128)S(1)}, f32[32,512]{1,0:T(8,128)S(1)}, u32[]{:S(2)}, u32[]{:S(2)}) collective-permute-start(f32[32,512]{1,0:T(8,128)S(1)} %rest.2), channel_id=1, source_target_pairs={{3,1},{7,5},{11,9},{15,13},{19,17},{23,21},{27,25},{31,29}} | collective-permute-start | bytes 196616 | tf_op jit(solution)/shard_map/ppermute | solution.py:406
  81.0 2.5 %collective-permute-start.25 = (f32[32,256]{1,0:T(8,128)S(1)}, f32[32,256]{1,0:T(8,128)S(1)}, u32[]{:S(2)}, u32[]{:S(2)}) collective-permute-start(f32[32,256]{1,0:T(8,128)S(1)} %get-tuple-element.95), channel_id=1, source_target_pairs={{2,1},{6,5},{10,9},{14,13},{18,17},{22,21},{26,25},{30,29}} | collective-permute-start | bytes 98312 | tf_op jit(solution)/shard_map/ppermute | solution.py:403
  82.2 9.5 %collective-permute-start.28 = (f32[32,256]{1,0:T(8,128)S(1)}, f32[32,256]{1,0:T(8,128)S(1)}, u32[]{:S(2)}, u32[]{:S(2)}) collective-permute-start(f32[32,256]{1,0:T(8,128)S(1)} %rest.3), channel_id=1, source_target_pairs={{2,0},{6,4},{10,8},{14,12},{18,16},{22,20},{26,24},{30,28}} | collective-permute-start | bytes 98312 | tf_op jit(solution)/shard_map/ppermute | solution.py:406
  84.1 10.3 %collective-permute-start.27 = (f32[32,256]{1,0:T(8,128)S(1)}, f32[32,256]{1,0:T(8,128)S(1)}, u32[]{:S(2)}, u32[]{:S(2)}) collective-permute-start(f32[32,256]{1,0:T(8,128)S(1)} %get-tuple-element.97), channel_id=1, source_target_pairs={{1,0},{5,4},{9,8},{13,12},{17,16},{21,20},{25,24},{29,28}} | collective-permute-start | bytes 98312 | tf_op jit(solution)/shard_map/ppermute | solution.py:403

commit v10 on v9

--- a/solution.py
+++ b/solution.py
@@ -225,6 +225,34 @@
     out = (shape(half, width), shape(half, width))
     scratch = [pltpu.VMEM((band, width), F32), pltpu.SemaphoreType.DMA(())]
     return call(body, out, (SMEM, SMEM, HBM), (where, slot_row, factor_rows), "top_band", scratch)
+
+
+def finish_sum(where, value, got, rhs, bands):
+    columns, width = got.shape
+    band = width // bands
+
+    def body(where_ref, value_ref, got_ref, rhs_ref, total_ref, base_ref, *piece_refs):
+        total_ref[...] = value_ref[:columns, :] + got_ref[...]
+        place = where_ref[1]
+
+        def own(spot):
+            return total_ref[:, pl.ds(pl.multiple_of(spot * band, band), band)]
+
+        base_ref[...] = rhs_ref[1] - own(place)
+        for shift, piece_ref in enumerate(piece_refs, 1):
+            piece_ref[...] = own(jnp.minimum(place + shift, bands - 1))
+
+    out = (shape(columns, width),) + (shape(columns, band),) * bands
+    total, base, *pieces = call(body, out, (SMEM,) + (VMEM,) * 3, (where, value, got, rhs), "finish_sum")
+    return total, base, pieces
+
+
+def finish_plain(where, value, got, rhs, bands):
+    total = value[: got.shape[0]] + got
+    band = total.shape[1] // bands
+    spots = [jnp.minimum(where[1] + shift, bands - 1) for shift in range(bands)]
+    base, *pieces = [own_band(total, spot, band) for spot in spots]
+    return total, rhs[1] - base, pieces
 
 
 def after(value, *others):
@@ -318,7 +346,7 @@
     return call(body, shape(2 * half, width), (SMEM, VMEM, VMEM), (where, mine, other), "join")
 
 
-def run_stage(where, base, tile, add, near, far, held, stage, packs=()):
+def run_stage(where, base, tile, add, near, far, held, stage, packs=(), ups=(), other=None):
     columns, band = base.shape
     left = stage * band
     wide = far is None
@@ -328,10 +356,16 @@
     more = [pack_parts(*pack[1:]) for pack in packs]
     count = sum(len(args) for args in inputs)
     come = (near,) if wide else (near, far)
+    stacked = other is not None
+    extra = ups + ((other,) if stacked else ())
 
     def body(where_ref, base_ref, tile_ref, add_ref, held_ref, *refs):
         come_refs, refs = refs[: len(come)], refs[len(come) :]
+        extra_refs, refs = refs[: len(extra)], refs[len(extra) :]
         ins, (solved_ref, update_ref), outs = refs[:count], refs[count : count + 2], refs[count + 2 :]
+        if stacked:
+            solved_ref[1] = extra_refs[-1][...]
+            solved_ref = solved_ref.at[0]
 
         @pl.when(where_ref[1] == stage)
         def _():
@@ -339,6 +373,8 @@
                 right = base_ref[...] - come_refs[0][:, left:]
             else:
                 right = base_ref[...] - come_refs[0][...] - come_refs[1][:, left : left + band]
+            for up_ref in extra_refs[: len(ups)]:
+                right = right - up_ref[...]
             solved = dot3(right, tile_ref[:, left : left + band])
             solved_ref[...] = solved
             if stage > 0:
@@ -354,8 +390,9 @@
             add_pack(*ins[: len(args)], *outs[: len(out)])
             ins, outs = ins[len(args) :], outs[len(out) :]
 
-    out = (shape(columns, band), shape(columns, width)) + sum((out for _, out in more), ())
-    args = (where, base, tile, add, held) + come + sum(inputs, ())
+    answer = shape(2, columns, band) if stacked else shape(columns, band)
+    out = (answer, shape(columns, width)) + sum((out for _, out in more), ())
+    args = (where, base, tile, add, held) + come + extra + sum(inputs, ())
     return call(body, out, (SMEM,) + (VMEM,) * (len(args) - 1), args, "stage")
 
 
@@ -371,15 +408,16 @@
     return call(body, shape(columns, last), (SMEM,) + (VMEM,) * 4, (where, tile, add, far, solved), "rest")
 
 
-def run_stage_plain(where, base, tile, add, near, far, held, stage, packs=()):
+def run_stage_plain(where, base, tile, add, near, far, held, stage, packs=(), ups=(), other=None):
     high = lax.Precision.HIGHEST
     band = base.shape[1]
     left = stage * band
     here = slice(max(left - band, 0), max(left, band))
-    solved = jnp.dot(base - near - far[:, left : left + band], tile[:, left : left + band], precision=high)
+    solved = jnp.dot(base - near - far[:, left : left + band] - sum(ups), tile[:, left : left + band], precision=high)
     update = jnp.dot(solved, tile[:, here], precision=high) + add[:, here] + far[:, here]
     more = sum((tuple(pack_step(*pack)) for pack in packs), ())
-    return (jnp.where(where[1] == stage, solved, held), update) + more
+    solved = jnp.where(where[1] == stage, solved, held)
+    return (solved if other is None else jnp.stack([solved, other]), update) + more
 
 
 def run_rest_plain(where, tile, add, far, solved, stage):
@@ -387,7 +425,7 @@
     return far[:, :last] + add[:, :last] + jnp.dot(solved, tile[:, :last], precision=lax.Precision.HIGHEST)
 
 
-def sweep(where, base, tile, add, bands, packs=None):
+def sweep(where, base, tile, add, bands, packs=None, ups=(), other=None):
     columns, band = base.shape
     aligned = band % 128 == 0
     wide = packs is not None and aligned
@@ -398,7 +436,8 @@
     for stage in range(bands - 1, -1, -1):
         far = fars.pop(0)
         taken = packs.take(bands - 1 - stage) if packs else ()
-        held, update, *more = stage_of(where, base, tile, add, near, far, held, stage, taken)
+        last = other if stage == 0 else None
+        held, update, *more = stage_of(where, base, tile, add, near, far, held, stage, taken, ups, last)
         if stage > 0:
             near = lax.ppermute(update, "ct", [(stage, stage - 1)])
         if stage > 1 and not wide:
@@ -444,29 +483,32 @@
                 self.got_top = swap_core(self.top, self.members)
 
 
-def couple(where, sums, solved, mine, other, bands):
+def couple(where, sums, solved, mine, other, rhs, bands):
     columns, band = solved.shape
     half, width = mine.shape
 
-    def body(where_ref, sums_ref, solved_ref, mine_ref, other_ref, out_ref, tile_ref, whole_ref):
+    def body(where_ref, sums_ref, solved_ref, mine_ref, other_ref, rhs_ref, *refs):
+        outs, (tile_ref, whole_ref) = refs[:bands], refs[bands:]
         core = where_ref[0] & 1
         tile_ref[pl.ds(pl.multiple_of(core * half, half), half), :] = mine_ref[...]
         tile_ref[pl.ds(pl.multiple_of((1 - core) * half, half), half), :] = other_ref[...]
         whole_ref[...] = sums_ref[...] + dot3(solved_ref[...], tile_ref[...])
-        for mask in range(bands):
+        for mask, out_ref in enumerate(outs):
             start = pl.multiple_of((where_ref[1] ^ mask) * band, band)
-            out_ref[mask] = whole_ref[:, pl.ds(start, band)]
+            piece = whole_ref[:, pl.ds(start, band)]
+            out_ref[...] = piece if mask else rhs_ref[0] - piece
 
     scratch = [pltpu.VMEM((band, width), F32), pltpu.VMEM((columns, width), F32)]
-    args = (where, sums, solved, mine, other)
-    return call(body, shape(bands, columns, band), (SMEM,) + (VMEM,) * 4, args, "couple", scratch)
-
-
-def couple_plain(where, sums, solved, mine, other, bands):
+    args = (where, sums, solved, mine, other, rhs)
+    return call(body, (shape(columns, band),) * bands, (SMEM,) + (VMEM,) * 5, args, "couple", scratch)
+
+
+def couple_plain(where, sums, solved, mine, other, rhs, bands):
     band = solved.shape[1]
     tile = join_halves(where, mine, other, 0, band // 2, ())
     whole = sums + jnp.dot(solved, tile, precision=lax.Precision.HIGHEST)
-    return jnp.stack([own_band(whole, where[1] ^ mask, band) for mask in range(bands)])
+    pieces = [own_band(whole, where[1] ^ mask, band) for mask in range(bands)]
+    return [rhs[0] - pieces[0]] + pieces[1:]
 
 
 def own_band(value, spot, band):
@@ -483,6 +525,7 @@
     where = jnp.stack([lax.axis_index("rt"), place]).astype(jnp.int32)
     factor_rows = pltpu.with_memory_space_constraint(factor_rows, pltpu.HBM)
     known = pltpu.with_memory_space_constraint(known, pltpu.HBM)
+    rhs = jnp.swapaxes(rhs, 1, 2)
 
     keep, send = first_band(where, slot_row, factor_rows)
     tile_one = keep + swap_core(send, members)
@@ -500,7 +543,11 @@
             got_pack = swap_core(after(send, sum_one), members)
             top, send_top = top_band(after(where, sum_one), slot_row, factor_rows)
             got_sum = after(got_sum, top)
-        sum_one = sum_one[:rows] + got_sum
+        if stage < stages - 1:
+            sum_one = sum_one[:rows] + got_sum
+        else:
+            finish = finish_sum if aligned else finish_plain
+            sum_one, base, pieces = finish(where, sum_one, got_sum, rhs, bands)
         if stage == 0:
             got_top = swap_core(after(send_top, sum_one), members)
         if stage < stages - 1:
@@ -509,8 +556,7 @@
 
     got_up = []
     for shift in range(bands - 1, 0, -1):
-        piece = own_band(sum_one, jnp.minimum(place + shift, bands - 1), band)
-        got_up.append(lax.ppermute(piece, "ct", [(i, i + shift) for i in range(bands - shift)]))
+        got_up.append(lax.ppermute(pieces[shift - 1], "ct", [(i, i + shift) for i in range(bands - shift)]))
 
     other = swap_core(tile_one, members)
 
@@ -520,24 +566,21 @@
     got_top = swap_chip(top, members, 0)
 
     tile_one = join_halves(after(where, sum_one, top), tile_one, other, 0, half, range(bands))
-    base = rhs[1].T - own_band(sum_one, place, band)
-    for piece in got_up:
-        base = base - after(piece, tile_one)
-
     packs = Packs((tiles, sums, half), got_pack, top, got_top, stages, bands, members)
-    solved_one = sweep(where, base, tile_one, sum_one, bands, packs)
+    ups = tuple(after(piece, tile_one) for piece in got_up)
+    solved_one = sweep(where, base, tile_one, sum_one, bands, packs, ups)
 
     low, sums, _ = packs.pack
-    pieces = (couple if aligned else couple_plain)(where, sums, solved_one, low, packs.got, bands)
-    base = rhs[0].T - pieces[0]
+    base, *pieces = (couple if aligned else couple_plain)(where, sums, solved_one, low, packs.got, rhs, bands)
     tile_zero = join_halves(where, packs.top, packs.got_top, 0, half, ())
+    ups = ()
     for mask in range(bands - 1, 0, -1):
-        got = lax.ppermute(pieces[mask], "ct", [(i, i ^ mask) for i in range(bands)])
-        base = base - after(got, tile_zero)
+        got = lax.ppermute(pieces[mask - 1], "ct", [(i, i ^ mask) for i in range(bands)])
+        ups += (after(got, tile_zero),)
 
     nothing = jnp.zeros((columns, width), F32)
-    solved_zero = sweep(where, base, tile_zero, nothing, bands)
-    return jnp.stack([solved_zero.T, solved_one.T])
+    answer = sweep(where, base, tile_zero, nothing, bands, None, ups, solved_one)
+    return jnp.swapaxes(answer, 1, 2)
 
 
 def solution(mesh):

time: 96.3 us -> 96.6 us (level)
  starting transfers between devices: 31.8 us -> 37.5 us
  waiting for transfers between devices: 36.2 us -> 34.3 us
  other arithmetic: 1.84 us -> 0.4 us
    ppermute x8, starting transfers between devices: 8.2 us -> 15.2 us  [swap_chip(): lax.ppermute(value, 'rt', [(i, i ^ 1 << orders[i & 1][stage]) for i in ra...]
    ppermute x8, waiting for transfers between devices: 21.7 us -> 15.2 us  [swap_chip(): lax.ppermute(value, 'rt', [(i, i ^ 1 << orders[i & 1][stage]) for i in ra...]
    ppermute x6, waiting for transfers between devices: 3.55 us -> 7.09 us  [sweep(): near = lax.ppermute(update, 'ct', [(stage, stage - 1)])]
    ppermute x6, starting transfers between devices: 14.9 us -> 13.7 us  [the longest x3 9.26 us: shards(): lax.ppermute(pieces[shift - 1], 'ct', [(i, i + shift) for i in range(band...]
    pallas_call x18 -> x19, Pallas kernels: 24.7 us -> 24.1 us  [call(): pl.pallas_call(body, out_shape=out, in_specs=list(specs), out_specs=tuple...]
  transfers between devices with their start and end apart: 29 -> 29, of which waited for: 12 -> 11; matrix products, arithmetic and copies ran while one was open for 2% -> 0% of each run, Pallas kernels for 23% -> 22%
where the time goes in v10:
time: 96.6 us; the launch traced here: 97.3 us
  starting transfers between devices  37.5 us (39%)
  waiting for transfers between devices  34.3 us (36%)
  Pallas kernels  24.1 us (25%)
    pallas_call x19, Pallas kernels, call(): pl.pallas_call(body, out_shape=out, in_specs=list(specs), out_specs=tuple...  24.1 us
    ppermute x8, starting transfers between devices, swap_chip(): lax.ppermute(value, 'rt', [(i, i ^ 1 << orders[i & 1][stage]) for i in ra...  15.2 us
    ppermute x8, waiting for transfers between devices, swap_chip(): lax.ppermute(value, 'rt', [(i, i ^ 1 << orders[i & 1][stage]) for i in ra...  15.2 us
    ppermute x3, starting transfers between devices, shards(): lax.ppermute(pieces[shift - 1], 'ct', [(i, i + shift) for i in range(band...  9.26 us
    ppermute x6, waiting for transfers between devices, sweep(): near = lax.ppermute(update, 'ct', [(stage, stage - 1)])  7.09 us
    ppermute x2, waiting for transfers between devices, sweep(): fars.append(lax.ppermute(rest, 'ct', [(stage, stage - 2)]))  6.97 us
    ppermute x6, starting transfers between devices, sweep(): near = lax.ppermute(update, 'ct', [(stage, stage - 1)])  5.22 us
    ppermute x3, starting transfers between devices, shards(): lax.ppermute(pieces[mask - 1], 'ct', [(i, i ^ mask) for i in range(bands)])  4.44 us
  transfers between devices with their start and end apart: 29, of which 11 were waited for; matrix products, arithmetic and copies ran while one was open for 0% of the time, Pallas kernels for 22%

profile of v10, /device:TPU:0, one launch (start us, length us, event | category | flops | bytes accessed | tf_op | source)
XLA Modules:
  0.0 97.3 jit_solution(5743578419149416889)
XLA Ops:
  0.0 0.1 pad_add_fusion.where_ref
  0.1 0.7 copy-done.1
  0.7 0.6 first_band.1
  1.4 0.5 collective-permute-start
  1.9 1.5 %collective-permute-done = f32[128,1024]{1,0:T(8,128)S(1)} collective-permute-done((f32[128,1024]{1,0:T(8,128)S(1)}, f32[128,1024]{1,0:T(8,128)S(1)}, u32[]{:S(2)}, u32[]{:S(2)}) %collective-permute-start) | collective-permute-done | bytes 524320 | tf_op jit(solution)/shard_map/ppermute | solution.py:60
  3.4 0.1 add.15
  3.5 0.0 copy-start
  3.5 2.9 %collective-permute-start.2 = (f32[128,1024]{1,0:T(8,128)S(1)}, f32[128,1024]{1,0:T(8,128)S(1)}, u32[]{:S(2)}, u32[]{:S(2)}) collective-permute-start(f32[128,1024]{1,0:T(8,128)S(1)} %add.15), channel_id=1, source_target_pairs={{0,8},{4,20},{8,0},{12,28},{16,24},{20,4},{24,16},{28,12},{1,9},{5... | collective-permute-start | bytes 1572872 | tf_op jit(solution)/shard_map/ppermute | solution.py:65
  6.4 9.6 %front.1 = (f32[128,1024]{1,0:T(8,128)S(1)}, f32[128,1024]{1,0:T(8,128)S(1)}, f32[256,1024]{1,0:T(8,128)S(1)}, f32[256,1024]{1,0:T(8,128)S(1)}) custom-call(s32[2]{0:T(128)S(1)} %pad_add_fusion.where_ref, s32[48]{0:T(128)S(1)} %copy-done.1, f32[6,2,256,1024]{3,2,1,0:T(8,128)} %factor_ref.5, f32[6,256,256]{2,1,0:T(8,128)} %known_ref.1), custom_call_target="tpu_custom_call" | custom-call | tf_op jit(solution)/shard_map/front/pallas_call | solution.py:23
  16.1 0.1 collective-permute-start.1
  16.2 0.1 add.16
  16.3 1.8 %collective-permute-done.1 = f32[128,1024]{1,0:T(8,128)S(1)} collective-permute-done((f32[128,1024]{1,0:T(8,128)S(1)}, f32[128,1024]{1,0:T(8,128)S(1)}, u32[]{:S(2)}, u32[]{:S(2)}) %collective-permute-start.1) | collective-permute-done | bytes 524320 | tf_op jit(solution)/shard_map/ppermute | solution.py:60
  18.1 0.1 add.17
  18.1 0.2 collective-permute-start.11
  18.4 0.1 collective-permute-start.3
  18.4 2.2 %collective-permute-start.6 = (f32[128,1024]{1,0:T(8,128)S(1)}, f32[128,1024]{1,0:T(8,128)S(1)}, u32[]{:S(2)}, u32[]{:S(2)}) collective-permute-start(f32[128,1024]{1,0:T(8,128)S(1)} %add.16), channel_id=1, source_target_pairs={{0,16},{4,12},{8,24},{12,4},{16,0},{20,28},{24,8},{28,20},{1,17},{... | collective-permute-start | bytes 1572872 | tf_op jit(solution)/shard_map/ppermute | solution.py:65
  20.6 0.8 top_band.1
  21.4 4.9 %collective-permute-done.3 = f32[64,1024]{1,0:T(8,128)S(1)} collective-permute-done((f32[64,1024]{1,0:T(8,128)S(1)}, f32[64,1024]{1,0:T(8,128)S(1)}, u32[]{:S(2)}, u32[]{:S(2)}) %collective-permute-start.3) | collective-permute-done | bytes 262176 | tf_op jit(solution)/shard_map/ppermute | solution.py:65
  26.4 3.4 %collective-permute-start.4 = (f32[32,1024]{1,0:T(8,128)S(1)}, f32[32,1024]{1,0:T(8,128)S(1)}, u32[]{:S(2)}, u32[]{:S(2)}) collective-permute-start(f32[32,1024]{1,0:T(8,128)S(1)} %slice.14), channel_id=1, source_target_pairs={{0,16},{4,12},{8,24},{12,4},{16,0},{20,28},{24,8},{28,20},{1,17},{... | collective-permute-start | bytes 393224 | tf_op jit(solution)/shard_map/ppermute | solution.py:65
  29.8 2.9 %collective-permute-done.4.got_ref = f32[32,1024]{1,0:T(8,128)S(1)} collective-permute-done((f32[32,1024]{1,0:T(8,128)S(1)}, f32[32,1024]{1,0:T(8,128)S(1)}, u32[]{:S(2)}, u32[]{:S(2)}) %collective-permute-start.4) | collective-permute-done | bytes 131104 | tf_op jit(solution)/shard_map/ppermute | solution.py:65
  32.7 0.6 finish_sum.1
  33.3 0.1 pack_step.3
  33.4 0.1 collective-permute-start.12
  33.6 0.1 add.19.mine_ref
  33.6 0.5 collective-permute-start.7
  34.2 0.1 pack_step.2.refs_4_
  34.2 1.6 %collective-permute-start.14 = (f32[128,1024]{1,0:T(8,128)S(1)}, f32[128,1024]{1,0:T(8,128)S(1)}, u32[]{:S(2)}, u32[]{:S(2)}) collective-permute-start(f32[128,1024]{1,0:T(8,128)S(1)} %pack_step.2.refs_4_), channel_id=1, source_target_pairs={{0,8},{4,20},{8,0},{12,28},{16,24},{20,4},{24,16},{28,12},{1,9},{5... | collective-permute-start | bytes 1572872 | tf_op jit(solution)/shard_map/ppermute | solution.py:65
  35.8 3.5 %collective-permute-start.10 = (f32[32,256]{1,0:T(8,128)S(1)}, f32[32,256]{1,0:T(8,128)S(1)}, u32[]{:S(2)}, u32[]{:S(2)}) collective-permute-start(f32[32,256]{1,0:T(8,128)S(1)} %get-tuple-element.82), channel_id=1, source_target_pairs={{0,1},{1,2},{2,3},{4,5},{5,6},{6,7},{8,9},{9,10},{10,11},{12,13},{... | collective-permute-start | bytes 98312 | tf_op jit(solution)/shard_map/ppermute | solution.py:559
  39.3 4.5 %collective-permute-start.9 = (f32[32,256]{1,0:T(8,128)S(1)}, f32[32,256]{1,0:T(8,128)S(1)}, u32[]{:S(2)}, u32[]{:S(2)}) collective-permute-start(f32[32,256]{1,0:T(8,128)S(1)} %get-tuple-element.80), channel_id=1, source_target_pairs={{0,2},{1,3},{4,6},{5,7},{8,10},{9,11},{12,14},{13,15},{16,18},{17,... | collective-permute-start | bytes 98312 | tf_op jit(solution)/shard_map/ppermute | solution.py:559
  43.8 1.3 %collective-permute-start.8 = (f32[32,256]{1,0:T(8,128)S(1)}, f32[32,256]{1,0:T(8,128)S(1)}, u32[]{:S(2)}, u32[]{:S(2)}) collective-permute-start(f32[32,256]{1,0:T(8,128)S(1)} %get-tuple-element.78), channel_id=1, source_target_pairs={{0,3},{4,7},{8,11},{12,15},{16,19},{20,23},{24,27},{28,31}} | collective-permute-start | bytes 98312 | tf_op jit(solution)/shard_map/ppermute | solution.py:559
  45.1 3.0 %join.2.tile_ref = f32[256,1024]{1,0:T(8,128)S(1)} custom-call(s32[2]{0:T(128)S(1)} %pad_add_fusion.where_ref, f32[128,1024]{1,0:T(8,128)S(1)} %add.19.mine_ref, f32[128,1024]{1,0:T(8,128)S(1)} %collective-permute-done.7.other_ref), custom_call_target="tpu_custom_call" | custom-call | tf_op jit(solution)/shard_map/join/pallas_call | solution.py:23
  48.2 0.7 stage.8
  48.8 2.1 %collective-permute-start.16 = (f32[160,1024]{1,0:T(8,128)S(1)}, f32[160,1024]{1,0:T(8,128)S(1)}, u32[]{:S(2)}, u32[]{:S(2)}) collective-permute-start(f32[160,1024]{1,0:T(8,128)S(1)} %get-tuple-element.94.refs_4_), channel_id=1, source_target_pairs={{0,16},{4,12},{8,24},{12,4},{16,0},{20,28},{24,8},{28,20},{1,17},{... | collective-permute-start | bytes 1966088 | tf_op jit(solution)/shard_map/ppermute | solution.py:65
  50.9 0.7 collective-permute-start.13
  51.6 0.6 stage.9
  52.2 2.9 %collective-permute-start.18 = (f32[128,1024]{1,0:T(8,128)S(1)}, f32[128,1024]{1,0:T(8,128)S(1)}, u32[]{:S(2)}, u32[]{:S(2)}) collective-permute-start(f32[128,1024]{1,0:T(8,128)S(1)} %get-tuple-element.99.refs_4_), channel_id=1, source_target_pairs={{0,16},{4,12},{8,24},{12,4},{16,0},{20,28},{24,8},{28,20},{1,17},{... | collective-permute-start | bytes 1572872 | tf_op jit(solution)/shard_map/ppermute | solution.py:65
  55.1 0.7 collective-permute-start.15
  55.8 3.7 %collective-permute-done.16.refs_6_ = f32[160,1024]{1,0:T(8,128)S(1)} collective-permute-done((f32[160,1024]{1,0:T(8,128)S(1)}, f32[160,1024]{1,0:T(8,128)S(1)}, u32[]{:S(2)}, u32[]{:S(2)}) %collective-permute-start.16) | collective-permute-done | bytes 655392 | tf_op jit(solution)/shard_map/ppermute | solution.py:65
  59.5 0.6 stage.10
  60.1 1.3 %collective-permute-start.17 = (f32[32,256]{1,0:T(8,128)S(1)}, f32[32,256]{1,0:T(8,128)S(1)}, u32[]{:S(2)}, u32[]{:S(2)}) collective-permute-start(f32[32,256]{1,0:T(8,128)S(1)} %get-tuple-element.98), channel_id=1, source_target_pairs={{1,0},{5,4},{9,8},{13,12},{17,16},{21,20},{25,24},{29,28}} | collective-permute-start | bytes 98312 | tf_op jit(solution)/shard_map/ppermute | solution.py:442
  61.4 0.1 collective-permute-start.19
  61.5 3.6 %collective-permute-done.18.refs_5_ = f32[128,1024]{1,0:T(8,128)S(1)} collective-permute-done((f32[128,1024]{1,0:T(8,128)S(1)}, f32[128,1024]{1,0:T(8,128)S(1)}, u32[]{:S(2)}, u32[]{:S(2)}) %collective-permute-start.18) | collective-permute-done | bytes 524320 | tf_op jit(solution)/shard_map/ppermute | solution.py:65
  65.1 4.5 %collective-permute-done.17.refs_0_ = f32[32,256]{1,0:T(8,128)S(1)} collective-permute-done((f32[32,256]{1,0:T(8,128)S(1)}, f32[32,256]{1,0:T(8,128)S(1)}, u32[]{:S(2)}, u32[]{:S(2)}) %collective-permute-start.17) | collective-permute-done | bytes 32800 | tf_op jit(solution)/shard_map/ppermute | solution.py:442
  69.6 1.4 %stage.11 = (f32[32,256]{1,0:T(8,128)S(1)}, f32[32,256]{1,0:T(8,128)}, f32[128,1024]{1,0:T(8,128)S(1)}) custom-call(s32[2]{0:T(128)S(1)} %pad_add_fusion.where_ref, f32[32,256]{1,0:T(8,128)S(1)} %get-tuple-element.71.base_ref, f32[256,1024]{1,0:T(8,128)S(1)} %join.2.tile_ref, f32[32,1024]{1,0:T(8,128)S(1)} %get-tuple-element.72.add_ref, ...), custom_call_target="tpu_custom_call" | custom-call | tf_op jit(solution)/shard_map/stage/pallas_call | solution.py:23
  71.0 1.2 %couple.1 = (f32[32,256]{1,0:T(8,128)S(1)}, f32[32,256]{1,0:T(8,128)S(1)}, f32[32,256]{1,0:T(8,128)S(1)}, f32[32,256]{1,0:T(8,128)S(1)}) custom-call(s32[2]{0:T(128)S(1)} %pad_add_fusion.where_ref, f32[32,1024]{1,0:T(8,128)S(1)} %get-tuple-element.96.sums_ref, f32[32,256]{1,0:T(8,128)S(1)} %get-tuple-element.100.solved_ref.refs_5_, ...), custom_call_target="tpu_custom_call" | custom-call | tf_op jit(solution)/shard_map/couple/pallas_call | solution.py:23
  72.2 0.1 collective-permute-start.23
  72.3 0.1 collective-permute-start.22
  72.3 4.3 %collective-permute-start.21 = (f32[32,256]{1,0:T(8,128)S(1)}, f32[32,256]{1,0:T(8,128)S(1)}, u32[]{:S(2)}, u32[]{:S(2)}) collective-permute-start(f32[32,256]{1,0:T(8,128)S(1)} %get-tuple-element.104), channel_id=1, source_target_pairs={{0,3},{1,2},{2,1},{3,0},{4,7},{5,6},{6,5},{7,4},{8,11},{9,10},{10,... | collective-permute-start | bytes 98312 | tf_op jit(solution)/shard_map/ppermute | solution.py:578
  76.6 0.6 join.3.tile_ref
  77.3 0.1 collective-permute-done.22.refs_3_
  77.4 1.6 %collective-permute-done.21.refs_2_ = f32[32,256]{1,0:T(8,128)S(1)} collective-permute-done((f32[32,256]{1,0:T(8,128)S(1)}, f32[32,256]{1,0:T(8,128)S(1)}, u32[]{:S(2)}, u32[]{:S(2)}) %collective-permute-start.21) | collective-permute-done | bytes 32800 | tf_op jit(solution)/shard_map/ppermute | solution.py:578
  78.9 0.6 stage.12
  79.5 0.7 collective-permute-start.24
  80.2 0.6 rest.2
  80.7 0.7 collective-permute-start.26
  81.4 0.6 stage.13
  82.0 0.7 collective-permute-start.25
  82.7 0.6 rest.3
  83.2 1.3 %collective-permute-start.28 = (f32[32,256]{1,0:T(8,128)S(1)}, f32[32,256]{1,0:T(8,128)S(1)}, u32[]{:S(2)}, u32[]{:S(2)}) collective-permute-start(f32[32,256]{1,0:T(8,128)S(1)} %rest.3), channel_id=1, source_target_pairs={{2,0},{6,4},{10,8},{14,12},{18,16},{22,20},{26,24},{30,28}} | collective-permute-start | bytes 98312 | tf_op jit(solution)/shard_map/ppermute | solution.py:445
  84.5 0.6 stage.14
  85.1 1.3 %collective-permute-start.27 = (f32[32,256]{1,0:T(8,128)S(1)}, f32[32,256]{1,0:T(8,128)S(1)}, u32[]{:S(2)}, u32[]{:S(2)}) collective-permute-start(f32[32,256]{1,0:T(8,128)S(1)} %get-tuple-element.115), channel_id=1, source_target_pairs={{1,0},{5,4},{9,8},{13,12},{17,16},{21,20},{25,24},{29,28}} | collective-permute-start | bytes 98312 | tf_op jit(solution)/shard_map/ppermute | solution.py:442
  86.4 7.0 %collective-permute-done.28.refs_1_ = f32[32,256]{1,0:T(8,128)S(1)} collective-permute-done((f32[32,256]{1,0:T(8,128)S(1)}, f32[32,256]{1,0:T(8,128)S(1)}, u32[]{:S(2)}, u32[]{:S(2)}) %collective-permute-start.28) | collective-permute-done | bytes 32800 | tf_op jit(solution)/shard_map/ppermute | solution.py:445
  93.4 2.6 %collective-permute-done.27.refs_0_ = f32[32,256]{1,0:T(8,128)S(1)} collective-permute-done((f32[32,256]{1,0:T(8,128)S(1)}, f32[32,256]{1,0:T(8,128)S(1)}, u32[]{:S(2)}, u32[]{:S(2)}) %collective-permute-start.27) | collective-permute-done | bytes 32800 | tf_op jit(solution)/shard_map/ppermute | solution.py:442
  96.0 1.4 %stage.15 = (f32[2,32,256]{2,1,0:T(8,128)}, f32[32,256]{1,0:T(8,128)}) custom-call(s32[2]{0:T(128)S(1)} %pad_add_fusion.where_ref, f32[32,256]{1,0:T(8,128)S(1)} %get-tuple-element.102.base_ref, f32[256,1024]{1,0:T(8,128)S(1)} %join.3.tile_ref, f32[32,1024]{1,0:T(8,128)S(1)} %broadcast_3_refs_0__add_ref_refs_1__far_ref.2.refs_0_.add_ref.refs_1_.far_ref, ...), custom_call_target="tpu_custom_call" | custom-call | tf_op jit(solution)/shard_map/stage/pallas_call | solution.py:23
  (27 shorter events, 0.1 us)
Async XLA Ops:
  0.1 0.7 copy-start.1
  1.4 2.1 %collective-permute-start = (f32[128,1024]{1,0:T(8,128)S(1)}, f32[128,1024]{1,0:T(8,128)S(1)}, u32[]{:S(2)}, u32[]{:S(2)}) collective-permute-start(f32[128,1024]{1,0:T(8,128)S(1)} %get-tuple-element.62), channel_id=1, source_target_pairs={{0,4},{4,0},{8,12},{12,8},{16,20},{20,16},{24,28},{28,24},{1,5},{5... | collective-permute-start | bytes 1572872 | tf_op jit(solution)/shard_map/ppermute | solution.py:60
  3.5 29.2 %copy-start = (f32[2,256,32]{1,2,0:T(8,128)S(1)}, f32[2,256,32]{1,2,0:T(8,128)}, u32[]{:S(2)}) copy-start(f32[2,256,32]{1,2,0:T(8,128)} %param.7) | copy-start | bytes 196612
  3.5 12.6 %collective-permute-start.2 = (f32[128,1024]{1,0:T(8,128)S(1)}, f32[128,1024]{1,0:T(8,128)S(1)}, u32[]{:S(2)}, u32[]{:S(2)}) collective-permute-start(f32[128,1024]{1,0:T(8,128)S(1)} %add.15), channel_id=1, source_target_pairs={{0,8},{4,20},{8,0},{12,28},{16,24},{20,4},{24,16},{28,12},{1,9},{5... | collective-permute-start | bytes 1572872 | tf_op jit(solution)/shard_map/ppermute | solution.py:65
  16.1 2.0 %collective-permute-start.1 = (f32[128,1024]{1,0:T(8,128)S(1)}, f32[128,1024]{1,0:T(8,128)S(1)}, u32[]{:S(2)}, u32[]{:S(2)}) collective-permute-start(f32[128,1024]{1,0:T(8,128)S(1)} %get-tuple-element.65), channel_id=1, source_target_pairs={{0,4},{4,0},{8,12},{12,8},{16,20},{20,16},{24,28},{28,24},{1,5},{5... | collective-permute-start | bytes 1572872 | tf_op jit(solution)/shard_map/ppermute | solution.py:60
  18.1 15.2 %collective-permute-start.11 = (f32[256,1024]{1,0:T(8,128)S(1)}, f32[256,1024]{1,0:T(8,128)S(1)}, u32[]{:S(2)}, u32[]{:S(2)}) collective-permute-start(f32[256,1024]{1,0:T(8,128)S(1)} %get-tuple-element.86), channel_id=1, source_target_pairs={{0,4},{4,0},{8,12},{12,8},{16,20},{20,16},{24,28},{28,24},{1,5},{5... | collective-permute-start | bytes 3145736 | tf_op jit(solution)/shard_map/ppermute | solution.py:60
  18.4 8.0 %collective-permute-start.3 = (f32[64,1024]{1,0:T(8,128)S(1)}, f32[64,1024]{1,0:T(8,128)S(1)}, u32[]{:S(2)}, u32[]{:S(2)}) collective-permute-start(f32[64,1024]{1,0:T(8,128)S(1)} %slice.13), channel_id=1, source_target_pairs={{0,8},{4,20},{8,0},{12,28},{16,24},{20,4},{24,16},{28,12},{1,9},{5... | collective-permute-start | bytes 786440 | tf_op jit(solution)/shard_map/ppermute | solution.py:65
  18.4 15.1 %collective-permute-start.6 = (f32[128,1024]{1,0:T(8,128)S(1)}, f32[128,1024]{1,0:T(8,128)S(1)}, u32[]{:S(2)}, u32[]{:S(2)}) collective-permute-start(f32[128,1024]{1,0:T(8,128)S(1)} %add.16), channel_id=1, source_target_pairs={{0,16},{4,12},{8,24},{12,4},{16,0},{20,28},{24,8},{28,20},{1,17},{... | collective-permute-start | bytes 1572872 | tf_op jit(solution)/shard_map/ppermute | solution.py:65
  26.4 6.3 %collective-permute-start.4 = (f32[32,1024]{1,0:T(8,128)S(1)}, f32[32,1024]{1,0:T(8,128)S(1)}, u32[]{:S(2)}, u32[]{:S(2)}) collective-permute-start(f32[32,1024]{1,0:T(8,128)S(1)} %slice.14), channel_id=1, source_target_pairs={{0,16},{4,12},{8,24},{12,4},{16,0},{20,28},{24,8},{28,20},{1,17},{... | collective-permute-start | bytes 393224 | tf_op jit(solution)/shard_map/ppermute | solution.py:65
  29.8 4.4 %collective-permute-start.5 = (f32[128,1024]{1,0:T(8,128)S(1)}, f32[128,1024]{1,0:T(8,128)S(1)}, u32[]{:S(2)}, u32[]{:S(2)}) collective-permute-start(f32[128,1024]{1,0:T(8,128)S(1)} %get-tuple-element.74), channel_id=1, source_target_pairs={{0,4},{4,0},{8,12},{12,8},{16,20},{20,16},{24,28},{28,24},{1,5},{5... | collective-permute-start | bytes 1572872 | tf_op jit(solution)/shard_map/ppermute | solution.py:60
  33.4 14.7 %collective-permute-start.12 = (f32[192,1024]{1,0:T(8,128)S(1)}, f32[192,1024]{1,0:T(8,128)S(1)}, u32[]{:S(2)}, u32[]{:S(2)}) collective-permute-start(f32[192,1024]{1,0:T(8,128)S(1)} %get-tuple-element.88.refs_4_), channel_id=1, source_target_pairs={{0,8},{4,20},{8,0},{12,28},{16,24},{20,4},{24,16},{28,12},{1,9},{5... | collective-permute-start | bytes 2359304 | tf_op jit(solution)/shard_map/ppermute | solution.py:65
  33.6 10.2 %collective-permute-start.7 = (f32[128,1024]{1,0:T(8,128)S(1)}, f32[128,1024]{1,0:T(8,128)S(1)}, u32[]{:S(2)}, u32[]{:S(2)}) collective-permute-start(f32[128,1024]{1,0:T(8,128)S(1)} %add.19.mine_ref), channel_id=1, source_target_pairs={{0,4},{4,0},{8,12},{12,8},{16,20},{20,16},{24,28},{28,24},{1,5},{5... | collective-permute-start | bytes 1572872 | tf_op jit(solution)/shard_map/ppermute | solution.py:60
  34.2 17.3 %collective-permute-start.14 = (f32[128,1024]{1,0:T(8,128)S(1)}, f32[128,1024]{1,0:T(8,128)S(1)}, u32[]{:S(2)}, u32[]{:S(2)}) collective-permute-start(f32[128,1024]{1,0:T(8,128)S(1)} %pack_step.2.refs_4_), channel_id=1, source_target_pairs={{0,8},{4,20},{8,0},{12,28},{16,24},{20,4},{24,16},{28,12},{1,9},{5... | collective-permute-start | bytes 1572872 | tf_op jit(solution)/shard_map/ppermute | solution.py:65
  35.8 12.3 %collective-permute-start.10 = (f32[32,256]{1,0:T(8,128)S(1)}, f32[32,256]{1,0:T(8,128)S(1)}, u32[]{:S(2)}, u32[]{:S(2)}) collective-permute-start(f32[32,256]{1,0:T(8,128)S(1)} %get-tuple-element.82), channel_id=1, source_target_pairs={{0,1},{1,2},{2,3},{4,5},{5,6},{6,7},{8,9},{9,10},{10,11},{12,13},{... | collective-permute-start | bytes 98312 | tf_op jit(solution)/shard_map/ppermute | solution.py:559
  39.3 8.8 %collective-permute-start.9 = (f32[32,256]{1,0:T(8,128)S(1)}, f32[32,256]{1,0:T(8,128)S(1)}, u32[]{:S(2)}, u32[]{:S(2)}) collective-permute-start(f32[32,256]{1,0:T(8,128)S(1)} %get-tuple-element.80), channel_id=1, source_target_pairs={{0,2},{1,3},{4,6},{5,7},{8,10},{9,11},{12,14},{13,15},{16,18},{17,... | collective-permute-start | bytes 98312 | tf_op jit(solution)/shard_map/ppermute | solution.py:559
  43.8 4.3 %collective-permute-start.8 = (f32[32,256]{1,0:T(8,128)S(1)}, f32[32,256]{1,0:T(8,128)S(1)}, u32[]{:S(2)}, u32[]{:S(2)}) collective-permute-start(f32[32,256]{1,0:T(8,128)S(1)} %get-tuple-element.78), channel_id=1, source_target_pairs={{0,3},{4,7},{8,11},{12,15},{16,19},{20,23},{24,27},{28,31}} | collective-permute-start | bytes 98312 | tf_op jit(solution)/shard_map/ppermute | solution.py:559
  48.8 10.7 %collective-permute-start.16 = (f32[160,1024]{1,0:T(8,128)S(1)}, f32[160,1024]{1,0:T(8,128)S(1)}, u32[]{:S(2)}, u32[]{:S(2)}) collective-permute-start(f32[160,1024]{1,0:T(8,128)S(1)} %get-tuple-element.94.refs_4_), channel_id=1, source_target_pairs={{0,16},{4,12},{8,24},{12,4},{16,0},{20,28},{24,8},{28,20},{1,17},{... | collective-permute-start | bytes 1966088 | tf_op jit(solution)/shard_map/ppermute | solution.py:65
  50.9 0.7 collective-permute-start.13
  52.2 12.9 %collective-permute-start.18 = (f32[128,1024]{1,0:T(8,128)S(1)}, f32[128,1024]{1,0:T(8,128)S(1)}, u32[]{:S(2)}, u32[]{:S(2)}) collective-permute-start(f32[128,1024]{1,0:T(8,128)S(1)} %get-tuple-element.99.refs_4_), channel_id=1, source_target_pairs={{0,16},{4,12},{8,24},{12,4},{16,0},{20,28},{24,8},{28,20},{1,17},{... | collective-permute-start | bytes 1572872 | tf_op jit(solution)/shard_map/ppermute | solution.py:65
  55.1 0.7 collective-permute-start.15
  60.1 9.5 %collective-permute-start.17 = (f32[32,256]{1,0:T(8,128)S(1)}, f32[32,256]{1,0:T(8,128)S(1)}, u32[]{:S(2)}, u32[]{:S(2)}) collective-permute-start(f32[32,256]{1,0:T(8,128)S(1)} %get-tuple-element.98), channel_id=1, source_target_pairs={{1,0},{5,4},{9,8},{13,12},{17,16},{21,20},{25,24},{29,28}} | collective-permute-start | bytes 98312 | tf_op jit(solution)/shard_map/ppermute | solution.py:442
  61.4 9.6 %collective-permute-start.19 = (f32[128,1024]{1,0:T(8,128)S(1)}, f32[128,1024]{1,0:T(8,128)S(1)}, u32[]{:S(2)}, u32[]{:S(2)}) collective-permute-start(f32[128,1024]{1,0:T(8,128)S(1)} %get-tuple-element.101.mine_ref), channel_id=1, source_target_pairs={{0,4},{4,0},{8,12},{12,8},{16,20},{20,16},{24,28},{28,24},{1,5},{5... | collective-permute-start | bytes 1572872 | tf_op jit(solution)/shard_map/ppermute | solution.py:60
  71.0 5.6 %collective-permute-start.20 = (f32[128,1024]{1,0:T(8,128)S(1)}, f32[128,1024]{1,0:T(8,128)S(1)}, u32[]{:S(2)}, u32[]{:S(2)}) collective-permute-start(f32[128,1024]{1,0:T(8,128)S(1)} %get-tuple-element.103.mine_ref), channel_id=1, source_target_pairs={{0,4},{4,0},{8,12},{12,8},{16,20},{20,16},{24,28},{28,24},{1,5},{5... | collective-permute-start | bytes 1572872 | tf_op jit(solution)/shard_map/ppermute | solution.py:60
  72.2 5.1 %collective-permute-start.23 = (f32[32,256]{1,0:T(8,128)S(1)}, f32[32,256]{1,0:T(8,128)S(1)}, u32[]{:S(2)}, u32[]{:S(2)}) collective-permute-start(f32[32,256]{1,0:T(8,128)S(1)} %get-tuple-element.108), channel_id=1, source_target_pairs={{0,1},{1,0},{2,3},{3,2},{4,5},{5,4},{6,7},{7,6},{8,9},{9,8},{10,11... | collective-permute-start | bytes 98312 | tf_op jit(solution)/shard_map/ppermute | solution.py:578
  72.3 5.1 %collective-permute-start.22 = (f32[32,256]{1,0:T(8,128)S(1)}, f32[32,256]{1,0:T(8,128)S(1)}, u32[]{:S(2)}, u32[]{:S(2)}) collective-permute-start(f32[32,256]{1,0:T(8,128)S(1)} %get-tuple-element.106), channel_id=1, source_target_pairs={{0,2},{1,3},{2,0},{3,1},{4,6},{5,7},{6,4},{7,5},{8,10},{9,11},{10,... | collective-permute-start | bytes 98312 | tf_op jit(solution)/shard_map/ppermute | solution.py:578
  72.3 6.6 %collective-permute-start.21 = (f32[32,256]{1,0:T(8,128)S(1)}, f32[32,256]{1,0:T(8,128)S(1)}, u32[]{:S(2)}, u32[]{:S(2)}) collective-permute-start(f32[32,256]{1,0:T(8,128)S(1)} %get-tuple-element.104), channel_id=1, source_target_pairs={{0,3},{1,2},{2,1},{3,0},{4,7},{5,6},{6,5},{7,4},{8,11},{9,10},{10,... | collective-permute-start | bytes 98312 | tf_op jit(solution)/shard_map/ppermute | solution.py:578
  79.5 1.9 %collective-permute-start.24 = (f32[32,256]{1,0:T(8,128)S(1)}, f32[32,256]{1,0:T(8,128)S(1)}, u32[]{:S(2)}, u32[]{:S(2)}) collective-permute-start(f32[32,256]{1,0:T(8,128)S(1)} %get-tuple-element.111), channel_id=1, source_target_pairs={{3,2},{7,6},{11,10},{15,14},{19,18},{23,22},{27,26},{31,30}} | collective-permute-start | bytes 98312 | tf_op jit(solution)/shard_map/ppermute | solution.py:442
  80.7 3.8 %collective-permute-start.26 = (f32[32,512]{1,0:T(8,128)S(1)}, f32[32,512]{1,0:T(8,128)S(1)}, u32[]{:S(2)}, u32[]{:S(2)}) collective-permute-start(f32[32,512]{1,0:T(8,128)S(1)} %rest.2), channel_id=1, source_target_pairs={{3,1},{7,5},{11,9},{15,13},{19,17},{23,21},{27,25},{31,29}} | collective-permute-start | bytes 196616 | tf_op jit(solution)/shard_map/ppermute | solution.py:445
  82.0 2.5 %collective-permute-start.25 = (f32[32,256]{1,0:T(8,128)S(1)}, f32[32,256]{1,0:T(8,128)S(1)}, u32[]{:S(2)}, u32[]{:S(2)}) collective-permute-start(f32[32,256]{1,0:T(8,128)S(1)} %get-tuple-element.113), channel_id=1, source_target_pairs={{2,1},{6,5},{10,9},{14,13},{18,17},{22,21},{26,25},{30,29}} | collective-permute-start | bytes 98312 | tf_op jit(solution)/shard_map/ppermute | solution.py:442
  83.2 10.2 %collective-permute-start.28 = (f32[32,256]{1,0:T(8,128)S(1)}, f32[32,256]{1,0:T(8,128)S(1)}, u32[]{:S(2)}, u32[]{:S(2)}) collective-permute-start(f32[32,256]{1,0:T(8,128)S(1)} %rest.3), channel_id=1, source_target_pairs={{2,0},{6,4},{10,8},{14,12},{18,16},{22,20},{26,24},{30,28}} | collective-permute-start | bytes 98312 | tf_op jit(solution)/shard_map/ppermute | solution.py:445
  85.1 10.9 %collective-permute-start.27 = (f32[32,256]{1,0:T(8,128)S(1)}, f32[32,256]{1,0:T(8,128)S(1)}, u32[]{:S(2)}, u32[]{:S(2)}) collective-permute-start(f32[32,256]{1,0:T(8,128)S(1)} %get-tuple-element.115), channel_id=1, source_target_pairs={{1,0},{5,4},{9,8},{13,12},{17,16},{21,20},{25,24},{29,28}} | collective-permute-start | bytes 98312 | tf_op jit(solution)/shard_map/ppermute | solution.py:442

commit v11 on v10

--- a/solution.py
+++ b/solution.py
@@ -445,6 +445,8 @@
             fars.append(lax.ppermute(rest, "ct", [(stage, stage - 2)]))
         if more:
             packs.put(*more)
+        if packs:
+            near = packs.loose(held, near)
     return held
 
 
@@ -452,18 +454,28 @@
     def __init__(self, pack, got, top, got_top, steps, bands, members):
         self.pack, self.got, self.top, self.got_top = pack, got, top, got_top
         self.steps, self.members = steps, members
-        self.low_at = [bands - 2 - 2 * (steps - 1 - step) for step in range(steps)]
+        self.low_at = [bands - 2 - 2 * (steps - 1 - step) for step in range(steps - 1)]
+        self.loose_at = bands - 2
         self.top_at = [bands - 1 - 2 * (steps - 1 - step) for step in range(steps)]
 
     def take(self, index):
         taken = ()
         if index in self.low_at:
             tiles, sums, rows = self.pack
-            taken += ((tiles, sums, 0, self.got, rows, index == self.low_at[-1]),)
+            taken += ((tiles, sums, 0, self.got, rows, False),)
         if index in self.top_at:
             taken += ((self.top, None, 0, self.got_top, self.top.shape[0], True),)
         self.index = index
         return taken
+
+    def loose(self, held, near):
+        if self.index != self.loose_at:
+            return near
+        tiles, sums, rows = self.pack
+        tiles, sums = pack_step(tiles, sums, 0, after(self.got, held), rows, True)
+        self.pack = (tiles, sums, rows)
+        self.got = swap_core(tiles, self.members)
+        return after(near, tiles)
 
     def put(self, *outs):
         if self.index in self.low_at:
@@ -562,7 +574,7 @@
 
     tiles, sums = pack_step(keep, keep, half, after(got_pack, sum_one), half, False)
     got_pack = swap_chip(tiles, members, 0)
-    (top,) = pack_step(top, None, 0, after(got_top, sum_one), half, True)
+    (top,) = pack_step(top, None, 0, after(got_top, other), half, True)
     got_top = swap_chip(top, members, 0)
 
     tile_one = join_halves(after(where, sum_one, top), tile_one, other, 0, half, range(bands))

time: 96.6 us -> 96.8 us (level)
  starting transfers between devices: 37.5 us -> 44.5 us
  Pallas kernels: 24.1 us -> 20.4 us
  waiting for transfers between devices: 34.3 us -> 30.7 us
    ppermute x8, waiting for transfers between devices: 15.2 us -> 6.33 us  [swap_chip(): lax.ppermute(value, 'rt', [(i, i ^ 1 << orders[i & 1][stage]) for i in ra...]
    ppermute x8, starting transfers between devices: 15.2 us -> 21.7 us  [swap_chip(): lax.ppermute(value, 'rt', [(i, i ^ 1 << orders[i & 1][stage]) for i in ra...]
    ppermute x6, waiting for transfers between devices: 7.09 us -> 13.1 us  [sweep(): near = lax.ppermute(update, 'ct', [(stage, stage - 1)])]
    pallas_call x19 -> x20, Pallas kernels: 24.1 us -> 20.4 us  [call(): pl.pallas_call(body, out_shape=out, in_specs=list(specs), out_specs=tuple...]
  transfers between devices with their start and end apart: 29 -> 29, of which waited for: 11 -> 13; matrix products, arithmetic and copies ran while one was open for 0% -> 0% of each run, Pallas kernels for 22% -> 18%
where the time goes in v11:
time: 96.8 us; the launch traced here: 97.1 us
  starting transfers between devices  44.5 us (46%)
  waiting for transfers between devices  30.7 us (32%)
  Pallas kernels  20.4 us (21%)
    ppermute x8, starting transfers between devices, swap_chip(): lax.ppermute(value, 'rt', [(i, i ^ 1 << orders[i & 1][stage]) for i in ra...  21.7 us
    pallas_call x20, Pallas kernels, call(): pl.pallas_call(body, out_shape=out, in_specs=list(specs), out_specs=tuple...  20.4 us
    ppermute x6, waiting for transfers between devices, sweep(): near = lax.ppermute(update, 'ct', [(stage, stage - 1)])  13.1 us
    ppermute x3, starting transfers between devices, shards(): lax.ppermute(pieces[shift - 1], 'ct', [(i, i + shift) for i in range(band...  9.25 us
    ppermute x2, waiting for transfers between devices, sweep(): fars.append(lax.ppermute(rest, 'ct', [(stage, stage - 2)]))  6.97 us
    ppermute x8, waiting for transfers between devices, swap_chip(): lax.ppermute(value, 'rt', [(i, i ^ 1 << orders[i & 1][stage]) for i in ra...  6.33 us
    ppermute x6, starting transfers between devices, sweep(): near = lax.ppermute(update, 'ct', [(stage, stage - 1)])  5.22 us
    ppermute x3, starting transfers between devices, shards(): lax.ppermute(pieces[mask - 1], 'ct', [(i, i ^ mask) for i in range(bands)])  4.44 us
  transfers between devices with their start and end apart: 29, of which 13 were waited for; matrix products, arithmetic and copies ran while one was open for 0% of the time, Pallas kernels for 18%

profile of v11, /device:TPU:0, one launch (start us, length us, event | category | flops | bytes accessed | tf_op | source)
XLA Modules:
  0.0 97.1 jit_solution(1537056751828317508)
XLA Ops:
  0.0 0.1 pad_add_fusion.where_ref
  0.1 0.7 copy-done.1
  0.7 0.6 first_band.1
  1.4 0.5 collective-permute-start
  1.9 1.5 %collective-permute-done = f32[128,1024]{1,0:T(8,128)S(1)} collective-permute-done((f32[128,1024]{1,0:T(8,128)S(1)}, f32[128,1024]{1,0:T(8,128)S(1)}, u32[]{:S(2)}, u32[]{:S(2)}) %collective-permute-start) | collective-permute-done | bytes 524320 | tf_op jit(solution)/shard_map/ppermute | solution.py:60
  3.4 0.1 add.15
  3.5 2.9 %collective-permute-start.2 = (f32[128,1024]{1,0:T(8,128)S(1)}, f32[128,1024]{1,0:T(8,128)S(1)}, u32[]{:S(2)}, u32[]{:S(2)}) collective-permute-start(f32[128,1024]{1,0:T(8,128)S(1)} %add.15), channel_id=1, source_target_pairs={{0,8},{4,20},{8,0},{12,28},{16,24},{20,4},{24,16},{28,12},{1,9},{5... | collective-permute-start | bytes 1572872 | tf_op jit(solution)/shard_map/ppermute | solution.py:65
  6.4 6.0 %front.1 = (f32[128,1024]{1,0:T(8,128)S(1)}, f32[128,1024]{1,0:T(8,128)S(1)}, f32[256,1024]{1,0:T(8,128)S(1)}, f32[256,1024]{1,0:T(8,128)S(1)}) custom-call(s32[2]{0:T(128)S(1)} %pad_add_fusion.where_ref, s32[48]{0:T(128)S(1)} %copy-done.1, f32[6,2,256,1024]{3,2,1,0:T(8,128)} %factor_ref.5, f32[6,256,256]{2,1,0:T(8,128)} %known_ref.1), custom_call_target="tpu_custom_call" | custom-call | tf_op jit(solution)/shard_map/front/pallas_call | solution.py:23
  12.4 0.8 collective-permute-start.1
  13.2 0.4 collective-permute-done.2
  13.6 0.1 add.16
  13.7 1.1 %collective-permute-done.1 = f32[128,1024]{1,0:T(8,128)S(1)} collective-permute-done((f32[128,1024]{1,0:T(8,128)S(1)}, f32[128,1024]{1,0:T(8,128)S(1)}, u32[]{:S(2)}, u32[]{:S(2)}) %collective-permute-start.1) | collective-permute-done | bytes 524320 | tf_op jit(solution)/shard_map/ppermute | solution.py:60
  14.7 0.1 add.17
  14.8 0.4 collective-permute-start.11
  15.3 0.7 collective-permute-start.3
  16.0 4.0 %collective-permute-start.6 = (f32[128,1024]{1,0:T(8,128)S(1)}, f32[128,1024]{1,0:T(8,128)S(1)}, u32[]{:S(2)}, u32[]{:S(2)}) collective-permute-start(f32[128,1024]{1,0:T(8,128)S(1)} %add.16), channel_id=1, source_target_pairs={{0,16},{4,12},{8,24},{12,4},{16,0},{20,28},{24,8},{28,20},{1,17},{... | collective-permute-start | bytes 1572872 | tf_op jit(solution)/shard_map/ppermute | solution.py:65
  20.0 0.8 top_band.1
  20.8 0.9 collective-permute-done.3
  21.8 7.4 %collective-permute-start.4 = (f32[32,1024]{1,0:T(8,128)S(1)}, f32[32,1024]{1,0:T(8,128)S(1)}, u32[]{:S(2)}, u32[]{:S(2)}) collective-permute-start(f32[32,1024]{1,0:T(8,128)S(1)} %slice.14), channel_id=1, source_target_pairs={{0,16},{4,12},{8,24},{12,4},{16,0},{20,28},{24,8},{28,20},{1,17},{... | collective-permute-start | bytes 393224 | tf_op jit(solution)/shard_map/ppermute | solution.py:65
  29.2 0.4 collective-permute-done.6
  29.7 0.2 collective-permute-start.7
  29.8 2.3 %collective-permute-done.4.got_ref = f32[32,1024]{1,0:T(8,128)S(1)} collective-permute-done((f32[32,1024]{1,0:T(8,128)S(1)}, f32[32,1024]{1,0:T(8,128)S(1)}, u32[]{:S(2)}, u32[]{:S(2)}) %collective-permute-start.4) | collective-permute-done | bytes 131104 | tf_op jit(solution)/shard_map/ppermute | solution.py:65
  32.1 0.6 finish_sum.1
  32.7 0.1 pack_step.4
  32.8 0.1 collective-permute-start.12
  33.0 2.0 %collective-permute-start.15 = (f32[128,1024]{1,0:T(8,128)S(1)}, f32[128,1024]{1,0:T(8,128)S(1)}, u32[]{:S(2)}, u32[]{:S(2)}) collective-permute-start(f32[128,1024]{1,0:T(8,128)S(1)} %pack_step.3.refs_4_), channel_id=1, source_target_pairs={{0,8},{4,20},{8,0},{12,28},{16,24},{20,4},{24,16},{28,12},{1,9},{5... | collective-permute-start | bytes 1572872 | tf_op jit(solution)/shard_map/ppermute | solution.py:65
  35.0 3.5 %collective-permute-start.10 = (f32[32,256]{1,0:T(8,128)S(1)}, f32[32,256]{1,0:T(8,128)S(1)}, u32[]{:S(2)}, u32[]{:S(2)}) collective-permute-start(f32[32,256]{1,0:T(8,128)S(1)} %get-tuple-element.84), channel_id=1, source_target_pairs={{0,1},{1,2},{2,3},{4,5},{5,6},{6,7},{8,9},{9,10},{10,11},{12,13},{... | collective-permute-start | bytes 98312 | tf_op jit(solution)/shard_map/ppermute | solution.py:571
  38.5 4.5 %collective-permute-start.9 = (f32[32,256]{1,0:T(8,128)S(1)}, f32[32,256]{1,0:T(8,128)S(1)}, u32[]{:S(2)}, u32[]{:S(2)}) collective-permute-start(f32[32,256]{1,0:T(8,128)S(1)} %get-tuple-element.82), channel_id=1, source_target_pairs={{0,2},{1,3},{4,6},{5,7},{8,10},{9,11},{12,14},{13,15},{16,18},{17,... | collective-permute-start | bytes 98312 | tf_op jit(solution)/shard_map/ppermute | solution.py:571
  43.0 1.3 %collective-permute-start.8 = (f32[32,256]{1,0:T(8,128)S(1)}, f32[32,256]{1,0:T(8,128)S(1)}, u32[]{:S(2)}, u32[]{:S(2)}) collective-permute-start(f32[32,256]{1,0:T(8,128)S(1)} %get-tuple-element.80), channel_id=1, source_target_pairs={{0,3},{4,7},{8,11},{12,15},{16,19},{20,23},{24,27},{28,31}} | collective-permute-start | bytes 98312 | tf_op jit(solution)/shard_map/ppermute | solution.py:571
  44.3 3.0 %join.2.tile_ref = f32[256,1024]{1,0:T(8,128)S(1)} custom-call(s32[2]{0:T(128)S(1)} %pad_add_fusion.where_ref, f32[128,1024]{1,0:T(8,128)S(1)} %add.19.mine_ref, f32[128,1024]{1,0:T(8,128)S(1)} %collective-permute-done.7.other_ref), custom_call_target="tpu_custom_call" | custom-call | tf_op jit(solution)/shard_map/join/pallas_call | solution.py:23
  47.4 0.6 stage.8
  48.0 2.1 %collective-permute-start.13 = (f32[160,1024]{1,0:T(8,128)S(1)}, f32[160,1024]{1,0:T(8,128)S(1)}, u32[]{:S(2)}, u32[]{:S(2)}) collective-permute-start(f32[160,1024]{1,0:T(8,128)S(1)} %get-tuple-element.92.tiles_ref), channel_id=1, source_target_pairs={{0,16},{4,12},{8,24},{12,4},{16,0},{20,28},{24,8},{28,20},{1,17},{... | collective-permute-start | bytes 1966088 | tf_op jit(solution)/shard_map/ppermute | solution.py:65
  50.1 0.7 collective-permute-start.14
  50.8 1.5 %collective-permute-done.15.refs_5_ = f32[128,1024]{1,0:T(8,128)S(1)} collective-permute-done((f32[128,1024]{1,0:T(8,128)S(1)}, f32[128,1024]{1,0:T(8,128)S(1)}, u32[]{:S(2)}, u32[]{:S(2)}) %collective-permute-start.15) | collective-permute-done | bytes 524320 | tf_op jit(solution)/shard_map/ppermute | solution.py:65
  52.3 0.6 stage.9
  52.9 2.4 %collective-permute-start.18 = (f32[128,1024]{1,0:T(8,128)S(1)}, f32[128,1024]{1,0:T(8,128)S(1)}, u32[]{:S(2)}, u32[]{:S(2)}) collective-permute-start(f32[128,1024]{1,0:T(8,128)S(1)} %get-tuple-element.104.refs_4_), channel_id=1, source_target_pairs={{0,16},{4,12},{8,24},{12,4},{16,0},{20,28},{24,8},{28,20},{1,17},{... | collective-permute-start | bytes 1572872 | tf_op jit(solution)/shard_map/ppermute | solution.py:65
  55.3 0.7 collective-permute-start.16
  55.9 0.6 stage.10
  56.5 1.3 %collective-permute-start.17 = (f32[32,256]{1,0:T(8,128)S(1)}, f32[32,256]{1,0:T(8,128)S(1)}, u32[]{:S(2)}, u32[]{:S(2)}) collective-permute-start(f32[32,256]{1,0:T(8,128)S(1)} %get-tuple-element.101), channel_id=1, source_target_pairs={{1,0},{5,4},{9,8},{13,12},{17,16},{21,20},{25,24},{29,28}} | collective-permute-start | bytes 98312 | tf_op jit(solution)/shard_map/ppermute | solution.py:442
  57.8 0.9 collective-permute-done.13.got_ref
  58.7 0.1 pack_step.5
  58.8 0.1 collective-permute-start.19
  58.8 10.5 %collective-permute-done.17.refs_0_ = f32[32,256]{1,0:T(8,128)S(1)} collective-permute-done((f32[32,256]{1,0:T(8,128)S(1)}, f32[32,256]{1,0:T(8,128)S(1)}, u32[]{:S(2)}, u32[]{:S(2)}) %collective-permute-start.17) | collective-permute-done | bytes 32800 | tf_op jit(solution)/shard_map/ppermute | solution.py:442
  69.3 1.4 %stage.11 = (f32[32,256]{1,0:T(8,128)S(1)}, f32[32,256]{1,0:T(8,128)}, f32[128,1024]{1,0:T(8,128)S(1)}) custom-call(s32[2]{0:T(128)S(1)} %pad_add_fusion.where_ref, f32[32,256]{1,0:T(8,128)S(1)} %get-tuple-element.73.base_ref, f32[256,1024]{1,0:T(8,128)S(1)} %join.2.tile_ref, f32[32,1024]{1,0:T(8,128)S(1)} %get-tuple-element.74.add_ref, ...), custom_call_target="tpu_custom_call" | custom-call | tf_op jit(solution)/shard_map/stage/pallas_call | solution.py:23
  70.8 1.2 %couple.1 = (f32[32,256]{1,0:T(8,128)S(1)}, f32[32,256]{1,0:T(8,128)S(1)}, f32[32,256]{1,0:T(8,128)S(1)}, f32[32,256]{1,0:T(8,128)S(1)}) custom-call(s32[2]{0:T(128)S(1)} %pad_add_fusion.where_ref, f32[32,1024]{1,0:T(8,128)S(1)} %get-tuple-element.100.sums_ref, f32[32,256]{1,0:T(8,128)S(1)} %get-tuple-element.105.solved_ref.refs_5_, ...), custom_call_target="tpu_custom_call" | custom-call | tf_op jit(solution)/shard_map/couple/pallas_call | solution.py:23
  71.9 0.1 collective-permute-start.23
  72.0 0.1 collective-permute-start.22
  72.1 4.3 %collective-permute-start.21 = (f32[32,256]{1,0:T(8,128)S(1)}, f32[32,256]{1,0:T(8,128)S(1)}, u32[]{:S(2)}, u32[]{:S(2)}) collective-permute-start(f32[32,256]{1,0:T(8,128)S(1)} %get-tuple-element.108), channel_id=1, source_target_pairs={{0,3},{1,2},{2,1},{3,0},{4,7},{5,6},{6,5},{7,4},{8,11},{9,10},{10,... | collective-permute-start | bytes 98312 | tf_op jit(solution)/shard_map/ppermute | solution.py:590
  76.4 0.6 join.3.tile_ref
  77.0 0.1 collective-permute-done.22.refs_3_
  77.1 1.6 %collective-permute-done.21.refs_2_ = f32[32,256]{1,0:T(8,128)S(1)} collective-permute-done((f32[32,256]{1,0:T(8,128)S(1)}, f32[32,256]{1,0:T(8,128)S(1)}, u32[]{:S(2)}, u32[]{:S(2)}) %collective-permute-start.21) | collective-permute-done | bytes 32800 | tf_op jit(solution)/shard_map/ppermute | solution.py:590
  78.7 0.6 stage.12
  79.3 0.7 collective-permute-start.24
  79.9 0.6 rest.2
  80.5 0.7 collective-permute-start.26
  81.2 0.6 stage.13
  81.7 0.7 collective-permute-start.25
  82.4 0.6 rest.3
  83.0 1.3 %collective-permute-start.28 = (f32[32,256]{1,0:T(8,128)S(1)}, f32[32,256]{1,0:T(8,128)S(1)}, u32[]{:S(2)}, u32[]{:S(2)}) collective-permute-start(f32[32,256]{1,0:T(8,128)S(1)} %rest.3), channel_id=1, source_target_pairs={{2,0},{6,4},{10,8},{14,12},{18,16},{22,20},{26,24},{30,28}} | collective-permute-start | bytes 98312 | tf_op jit(solution)/shard_map/ppermute | solution.py:445
  84.3 0.6 stage.14
  84.8 1.3 %collective-permute-start.27 = (f32[32,256]{1,0:T(8,128)S(1)}, f32[32,256]{1,0:T(8,128)S(1)}, u32[]{:S(2)}, u32[]{:S(2)}) collective-permute-start(f32[32,256]{1,0:T(8,128)S(1)} %get-tuple-element.119), channel_id=1, source_target_pairs={{1,0},{5,4},{9,8},{13,12},{17,16},{21,20},{25,24},{29,28}} | collective-permute-start | bytes 98312 | tf_op jit(solution)/shard_map/ppermute | solution.py:442
  86.1 7.0 %collective-permute-done.28.refs_1_ = f32[32,256]{1,0:T(8,128)S(1)} collective-permute-done((f32[32,256]{1,0:T(8,128)S(1)}, f32[32,256]{1,0:T(8,128)S(1)}, u32[]{:S(2)}, u32[]{:S(2)}) %collective-permute-start.28) | collective-permute-done | bytes 32800 | tf_op jit(solution)/shard_map/ppermute | solution.py:445
  93.1 2.6 %collective-permute-done.27.refs_0_ = f32[32,256]{1,0:T(8,128)S(1)} collective-permute-done((f32[32,256]{1,0:T(8,128)S(1)}, f32[32,256]{1,0:T(8,128)S(1)}, u32[]{:S(2)}, u32[]{:S(2)}) %collective-permute-start.27) | collective-permute-done | bytes 32800 | tf_op jit(solution)/shard_map/ppermute | solution.py:442
  95.7 1.4 %stage.15 = (f32[2,32,256]{2,1,0:T(8,128)}, f32[32,256]{1,0:T(8,128)}) custom-call(s32[2]{0:T(128)S(1)} %pad_add_fusion.where_ref, f32[32,256]{1,0:T(8,128)S(1)} %get-tuple-element.106.base_ref, f32[256,1024]{1,0:T(8,128)S(1)} %join.3.tile_ref, f32[32,1024]{1,0:T(8,128)S(1)} %broadcast_3_refs_0__add_ref_refs_1__far_ref.2.refs_0_.add_ref.refs_1_.far_ref, ...), custom_call_target="tpu_custom_call" | custom-call | tf_op jit(solution)/shard_map/stage/pallas_call | solution.py:23
  (28 shorter events, 0.2 us)
Async XLA Ops:
  0.1 0.7 copy-start.1
  1.4 2.1 %collective-permute-start = (f32[128,1024]{1,0:T(8,128)S(1)}, f32[128,1024]{1,0:T(8,128)S(1)}, u32[]{:S(2)}, u32[]{:S(2)}) collective-permute-start(f32[128,1024]{1,0:T(8,128)S(1)} %get-tuple-element.64), channel_id=1, source_target_pairs={{0,4},{4,0},{8,12},{12,8},{16,20},{20,16},{24,28},{28,24},{1,5},{5... | collective-permute-start | bytes 1572872 | tf_op jit(solution)/shard_map/ppermute | solution.py:60
  3.5 10.1 %collective-permute-start.2 = (f32[128,1024]{1,0:T(8,128)S(1)}, f32[128,1024]{1,0:T(8,128)S(1)}, u32[]{:S(2)}, u32[]{:S(2)}) collective-permute-start(f32[128,1024]{1,0:T(8,128)S(1)} %add.15), channel_id=1, source_target_pairs={{0,8},{4,20},{8,0},{12,28},{16,24},{20,4},{24,16},{28,12},{1,9},{5... | collective-permute-start | bytes 1572872 | tf_op jit(solution)/shard_map/ppermute | solution.py:65
  12.4 19.7 %copy-start = (f32[2,256,32]{1,2,0:T(8,128)S(1)}, f32[2,256,32]{1,2,0:T(8,128)}, u32[]{:S(2)}) copy-start(f32[2,256,32]{1,2,0:T(8,128)} %param.7) | copy-start | bytes 196612
  12.4 2.3 %collective-permute-start.1 = (f32[128,1024]{1,0:T(8,128)S(1)}, f32[128,1024]{1,0:T(8,128)S(1)}, u32[]{:S(2)}, u32[]{:S(2)}) collective-permute-start(f32[128,1024]{1,0:T(8,128)S(1)} %get-tuple-element.67), channel_id=1, source_target_pairs={{0,4},{4,0},{8,12},{12,8},{16,20},{20,16},{24,28},{28,24},{1,5},{5... | collective-permute-start | bytes 1572872 | tf_op jit(solution)/shard_map/ppermute | solution.py:60
  14.8 17.9 %collective-permute-start.11 = (f32[256,1024]{1,0:T(8,128)S(1)}, f32[256,1024]{1,0:T(8,128)S(1)}, u32[]{:S(2)}, u32[]{:S(2)}) collective-permute-start(f32[256,1024]{1,0:T(8,128)S(1)} %get-tuple-element.88), channel_id=1, source_target_pairs={{0,4},{4,0},{8,12},{12,8},{16,20},{20,16},{24,28},{28,24},{1,5},{5... | collective-permute-start | bytes 3145736 | tf_op jit(solution)/shard_map/ppermute | solution.py:60
  15.3 6.4 %collective-permute-start.3 = (f32[64,1024]{1,0:T(8,128)S(1)}, f32[64,1024]{1,0:T(8,128)S(1)}, u32[]{:S(2)}, u32[]{:S(2)}) collective-permute-start(f32[64,1024]{1,0:T(8,128)S(1)} %slice.13), channel_id=1, source_target_pairs={{0,8},{4,20},{8,0},{12,28},{16,24},{20,4},{24,16},{28,12},{1,9},{5... | collective-permute-start | bytes 786440 | tf_op jit(solution)/shard_map/ppermute | solution.py:65
  16.0 13.6 %collective-permute-start.6 = (f32[128,1024]{1,0:T(8,128)S(1)}, f32[128,1024]{1,0:T(8,128)S(1)}, u32[]{:S(2)}, u32[]{:S(2)}) collective-permute-start(f32[128,1024]{1,0:T(8,128)S(1)} %add.16), channel_id=1, source_target_pairs={{0,16},{4,12},{8,24},{12,4},{16,0},{20,28},{24,8},{28,20},{1,17},{... | collective-permute-start | bytes 1572872 | tf_op jit(solution)/shard_map/ppermute | solution.py:65
  21.8 10.4 %collective-permute-start.4 = (f32[32,1024]{1,0:T(8,128)S(1)}, f32[32,1024]{1,0:T(8,128)S(1)}, u32[]{:S(2)}, u32[]{:S(2)}) collective-permute-start(f32[32,1024]{1,0:T(8,128)S(1)} %slice.14), channel_id=1, source_target_pairs={{0,16},{4,12},{8,24},{12,4},{16,0},{20,28},{24,8},{28,20},{1,17},{... | collective-permute-start | bytes 393224 | tf_op jit(solution)/shard_map/ppermute | solution.py:65
  29.2 3.8 %collective-permute-start.5 = (f32[128,1024]{1,0:T(8,128)S(1)}, f32[128,1024]{1,0:T(8,128)S(1)}, u32[]{:S(2)}, u32[]{:S(2)}) collective-permute-start(f32[128,1024]{1,0:T(8,128)S(1)} %get-tuple-element.76), channel_id=1, source_target_pairs={{0,4},{4,0},{8,12},{12,8},{16,20},{20,16},{24,28},{28,24},{1,5},{5... | collective-permute-start | bytes 1572872 | tf_op jit(solution)/shard_map/ppermute | solution.py:60
  29.7 3.3 %collective-permute-start.7 = (f32[128,1024]{1,0:T(8,128)S(1)}, f32[128,1024]{1,0:T(8,128)S(1)}, u32[]{:S(2)}, u32[]{:S(2)}) collective-permute-start(f32[128,1024]{1,0:T(8,128)S(1)} %add.19.mine_ref), channel_id=1, source_target_pairs={{0,4},{4,0},{8,12},{12,8},{16,20},{20,16},{24,28},{28,24},{1,5},{5... | collective-permute-start | bytes 1572872 | tf_op jit(solution)/shard_map/ppermute | solution.py:60
  32.8 14.5 %collective-permute-start.12 = (f32[192,1024]{1,0:T(8,128)S(1)}, f32[192,1024]{1,0:T(8,128)S(1)}, u32[]{:S(2)}, u32[]{:S(2)}) collective-permute-start(f32[192,1024]{1,0:T(8,128)S(1)} %get-tuple-element.90.refs_4_), channel_id=1, source_target_pairs={{0,8},{4,20},{8,0},{12,28},{16,24},{20,4},{24,16},{28,12},{1,9},{5... | collective-permute-start | bytes 2359304 | tf_op jit(solution)/shard_map/ppermute | solution.py:65
  33.0 19.2 %collective-permute-start.15 = (f32[128,1024]{1,0:T(8,128)S(1)}, f32[128,1024]{1,0:T(8,128)S(1)}, u32[]{:S(2)}, u32[]{:S(2)}) collective-permute-start(f32[128,1024]{1,0:T(8,128)S(1)} %pack_step.3.refs_4_), channel_id=1, source_target_pairs={{0,8},{4,20},{8,0},{12,28},{16,24},{20,4},{24,16},{28,12},{1,9},{5... | collective-permute-start | bytes 1572872 | tf_op jit(solution)/shard_map/ppermute | solution.py:65
  35.0 12.3 %collective-permute-start.10 = (f32[32,256]{1,0:T(8,128)S(1)}, f32[32,256]{1,0:T(8,128)S(1)}, u32[]{:S(2)}, u32[]{:S(2)}) collective-permute-start(f32[32,256]{1,0:T(8,128)S(1)} %get-tuple-element.84), channel_id=1, source_target_pairs={{0,1},{1,2},{2,3},{4,5},{5,6},{6,7},{8,9},{9,10},{10,11},{12,13},{... | collective-permute-start | bytes 98312 | tf_op jit(solution)/shard_map/ppermute | solution.py:571
  38.5 8.8 %collective-permute-start.9 = (f32[32,256]{1,0:T(8,128)S(1)}, f32[32,256]{1,0:T(8,128)S(1)}, u32[]{:S(2)}, u32[]{:S(2)}) collective-permute-start(f32[32,256]{1,0:T(8,128)S(1)} %get-tuple-element.82), channel_id=1, source_target_pairs={{0,2},{1,3},{4,6},{5,7},{8,10},{9,11},{12,14},{13,15},{16,18},{17,... | collective-permute-start | bytes 98312 | tf_op jit(solution)/shard_map/ppermute | solution.py:571
  43.0 4.3 %collective-permute-start.8 = (f32[32,256]{1,0:T(8,128)S(1)}, f32[32,256]{1,0:T(8,128)S(1)}, u32[]{:S(2)}, u32[]{:S(2)}) collective-permute-start(f32[32,256]{1,0:T(8,128)S(1)} %get-tuple-element.80), channel_id=1, source_target_pairs={{0,3},{4,7},{8,11},{12,15},{16,19},{20,23},{24,27},{28,31}} | collective-permute-start | bytes 98312 | tf_op jit(solution)/shard_map/ppermute | solution.py:571
  48.0 10.7 %collective-permute-start.13 = (f32[160,1024]{1,0:T(8,128)S(1)}, f32[160,1024]{1,0:T(8,128)S(1)}, u32[]{:S(2)}, u32[]{:S(2)}) collective-permute-start(f32[160,1024]{1,0:T(8,128)S(1)} %get-tuple-element.92.tiles_ref), channel_id=1, source_target_pairs={{0,16},{4,12},{8,24},{12,4},{16,0},{20,28},{24,8},{28,20},{1,17},{... | collective-permute-start | bytes 1966088 | tf_op jit(solution)/shard_map/ppermute | solution.py:65
  50.1 2.1 %collective-permute-start.14 = (f32[32,768]{1,0:T(8,128)S(1)}, f32[32,768]{1,0:T(8,128)S(1)}, u32[]{:S(2)}, u32[]{:S(2)}) collective-permute-start(f32[32,768]{1,0:T(8,128)S(1)} %get-tuple-element.95), channel_id=1, source_target_pairs={{3,2},{7,6},{11,10},{15,14},{19,18},{23,22},{27,26},{31,30}} | collective-permute-start | bytes 294920 | tf_op jit(solution)/shard_map/ppermute | solution.py:442
  52.9 16.4 %collective-permute-start.18 = (f32[128,1024]{1,0:T(8,128)S(1)}, f32[128,1024]{1,0:T(8,128)S(1)}, u32[]{:S(2)}, u32[]{:S(2)}) collective-permute-start(f32[128,1024]{1,0:T(8,128)S(1)} %get-tuple-element.104.refs_4_), channel_id=1, source_target_pairs={{0,16},{4,12},{8,24},{12,4},{16,0},{20,28},{24,8},{28,20},{1,17},{... | collective-permute-start | bytes 1572872 | tf_op jit(solution)/shard_map/ppermute | solution.py:65
  55.3 0.7 collective-permute-start.16
  56.5 12.8 %collective-permute-start.17 = (f32[32,256]{1,0:T(8,128)S(1)}, f32[32,256]{1,0:T(8,128)S(1)}, u32[]{:S(2)}, u32[]{:S(2)}) collective-permute-start(f32[32,256]{1,0:T(8,128)S(1)} %get-tuple-element.101), channel_id=1, source_target_pairs={{1,0},{5,4},{9,8},{13,12},{17,16},{21,20},{25,24},{29,28}} | collective-permute-start | bytes 98312 | tf_op jit(solution)/shard_map/ppermute | solution.py:442
  58.8 12.0 %collective-permute-start.19 = (f32[128,1024]{1,0:T(8,128)S(1)}, f32[128,1024]{1,0:T(8,128)S(1)}, u32[]{:S(2)}, u32[]{:S(2)}) collective-permute-start(f32[128,1024]{1,0:T(8,128)S(1)} %get-tuple-element.102.mine_ref), channel_id=1, source_target_pairs={{0,4},{4,0},{8,12},{12,8},{16,20},{20,16},{24,28},{28,24},{1,5},{5... | collective-permute-start | bytes 1572872 | tf_op jit(solution)/shard_map/ppermute | solution.py:60
  70.8 5.6 %collective-permute-start.20 = (f32[128,1024]{1,0:T(8,128)S(1)}, f32[128,1024]{1,0:T(8,128)S(1)}, u32[]{:S(2)}, u32[]{:S(2)}) collective-permute-start(f32[128,1024]{1,0:T(8,128)S(1)} %get-tuple-element.107.mine_ref), channel_id=1, source_target_pairs={{0,4},{4,0},{8,12},{12,8},{16,20},{20,16},{24,28},{28,24},{1,5},{5... | collective-permute-start | bytes 1572872 | tf_op jit(solution)/shard_map/ppermute | solution.py:60
  71.9 5.1 %collective-permute-start.23 = (f32[32,256]{1,0:T(8,128)S(1)}, f32[32,256]{1,0:T(8,128)S(1)}, u32[]{:S(2)}, u32[]{:S(2)}) collective-permute-start(f32[32,256]{1,0:T(8,128)S(1)} %get-tuple-element.112), channel_id=1, source_target_pairs={{0,1},{1,0},{2,3},{3,2},{4,5},{5,4},{6,7},{7,6},{8,9},{9,8},{10,11... | collective-permute-start | bytes 98312 | tf_op jit(solution)/shard_map/ppermute | solution.py:590
  72.0 5.1 %collective-permute-start.22 = (f32[32,256]{1,0:T(8,128)S(1)}, f32[32,256]{1,0:T(8,128)S(1)}, u32[]{:S(2)}, u32[]{:S(2)}) collective-permute-start(f32[32,256]{1,0:T(8,128)S(1)} %get-tuple-element.110), channel_id=1, source_target_pairs={{0,2},{1,3},{2,0},{3,1},{4,6},{5,7},{6,4},{7,5},{8,10},{9,11},{10,... | collective-permute-start | bytes 98312 | tf_op jit(solution)/shard_map/ppermute | solution.py:590
  72.1 6.6 %collective-permute-start.21 = (f32[32,256]{1,0:T(8,128)S(1)}, f32[32,256]{1,0:T(8,128)S(1)}, u32[]{:S(2)}, u32[]{:S(2)}) collective-permute-start(f32[32,256]{1,0:T(8,128)S(1)} %get-tuple-element.108), channel_id=1, source_target_pairs={{0,3},{1,2},{2,1},{3,0},{4,7},{5,6},{6,5},{7,4},{8,11},{9,10},{10,... | collective-permute-start | bytes 98312 | tf_op jit(solution)/shard_map/ppermute | solution.py:590
  79.3 1.9 %collective-permute-start.24 = (f32[32,256]{1,0:T(8,128)S(1)}, f32[32,256]{1,0:T(8,128)S(1)}, u32[]{:S(2)}, u32[]{:S(2)}) collective-permute-start(f32[32,256]{1,0:T(8,128)S(1)} %get-tuple-element.115), channel_id=1, source_target_pairs={{3,2},{7,6},{11,10},{15,14},{19,18},{23,22},{27,26},{31,30}} | collective-permute-start | bytes 98312 | tf_op jit(solution)/shard_map/ppermute | solution.py:442
  80.5 3.8 %collective-permute-start.26 = (f32[32,512]{1,0:T(8,128)S(1)}, f32[32,512]{1,0:T(8,128)S(1)}, u32[]{:S(2)}, u32[]{:S(2)}) collective-permute-start(f32[32,512]{1,0:T(8,128)S(1)} %rest.2), channel_id=1, source_target_pairs={{3,1},{7,5},{11,9},{15,13},{19,17},{23,21},{27,25},{31,29}} | collective-permute-start | bytes 196616 | tf_op jit(solution)/shard_map/ppermute | solution.py:445
  81.7 2.5 %collective-permute-start.25 = (f32[32,256]{1,0:T(8,128)S(1)}, f32[32,256]{1,0:T(8,128)S(1)}, u32[]{:S(2)}, u32[]{:S(2)}) collective-permute-start(f32[32,256]{1,0:T(8,128)S(1)} %get-tuple-element.117), channel_id=1, source_target_pairs={{2,1},{6,5},{10,9},{14,13},{18,17},{22,21},{26,25},{30,29}} | collective-permute-start | bytes 98312 | tf_op jit(solution)/shard_map/ppermute | solution.py:442
  83.0 10.2 %collective-permute-start.28 = (f32[32,256]{1,0:T(8,128)S(1)}, f32[32,256]{1,0:T(8,128)S(1)}, u32[]{:S(2)}, u32[]{:S(2)}) collective-permute-start(f32[32,256]{1,0:T(8,128)S(1)} %rest.3), channel_id=1, source_target_pairs={{2,0},{6,4},{10,8},{14,12},{18,16},{22,20},{26,24},{30,28}} | collective-permute-start | bytes 98312 | tf_op jit(solution)/shard_map/ppermute | solution.py:445
  84.8 10.9 %collective-permute-start.27 = (f32[32,256]{1,0:T(8,128)S(1)}, f32[32,256]{1,0:T(8,128)S(1)}, u32[]{:S(2)}, u32[]{:S(2)}) collective-permute-start(f32[32,256]{1,0:T(8,128)S(1)} %get-tuple-element.119), channel_id=1, source_target_pairs={{1,0},{5,4},{9,8},{13,12},{17,16},{21,20},{25,24},{29,28}} | collective-permute-start | bytes 98312 | tf_op jit(solution)/shard_map/ppermute | solution.py:442

commit v12 on v11

--- a/solution.py
+++ b/solution.py
@@ -456,7 +456,7 @@
         self.steps, self.members = steps, members
         self.low_at = [bands - 2 - 2 * (steps - 1 - step) for step in range(steps - 1)]
         self.loose_at = bands - 2
-        self.top_at = [bands - 1 - 2 * (steps - 1 - step) for step in range(steps)]
+        self.top_at = [bands - steps + step for step in range(steps)]
 
     def take(self, index):
         taken = ()

time: 96.8 us -> 95.7 us (0.989)
  starting transfers between devices: 44.5 us -> 34.3 us
  waiting for transfers between devices: 30.7 us -> 38.1 us
  Pallas kernels: 20.4 us -> 21.6 us
    ppermute x8, starting transfers between devices: 21.7 us -> 8.24 us  [swap_chip(): lax.ppermute(value, 'rt', [(i, i ^ 1 << orders[i & 1][stage]) for i in ra...]
    ppermute x8, waiting for transfers between devices: 6.33 us -> 17.7 us  [swap_chip(): lax.ppermute(value, 'rt', [(i, i ^ 1 << orders[i & 1][stage]) for i in ra...]
    ppermute x6, waiting for transfers between devices: 13.1 us -> 8.06 us  [sweep(): near = lax.ppermute(update, 'ct', [(stage, stage - 1)])]
    ppermute x3, starting transfers between devices: 4.44 us -> 8.31 us  [shards(): lax.ppermute(pieces[mask - 1], 'ct', [(i, i ^ mask) for i in range(bands)])]
    pallas_call x20, Pallas kernels: 20.4 us -> 21.6 us  [call(): pl.pallas_call(body, out_shape=out, in_specs=list(specs), out_specs=tuple...]
    ppermute x3, waiting for transfers between devices: 1.67 us -> 2.79 us  [shards(): lax.ppermute(pieces[mask - 1], 'ct', [(i, i ^ mask) for i in range(bands)])]
  transfers between devices with their start and end apart: 29 -> 29, of which waited for: 13 -> 11; matrix products, arithmetic and copies ran while one was open for 0% -> 0% of each run, Pallas kernels for 18% -> 20%
where the time goes in v12:
time: 95.7 us; the launch traced here: 95.4 us
  waiting for transfers between devices  38.1 us (40%)
  starting transfers between devices  34.3 us (36%)
  Pallas kernels  21.6 us (23%)
    pallas_call x20, Pallas kernels, call(): pl.pallas_call(body, out_shape=out, in_specs=list(specs), out_specs=tuple...  21.6 us
    ppermute x8, waiting for transfers between devices, swap_chip(): lax.ppermute(value, 'rt', [(i, i ^ 1 << orders[i & 1][stage]) for i in ra...  17.7 us
    ppermute x3, starting transfers between devices, shards(): lax.ppermute(pieces[shift - 1], 'ct', [(i, i + shift) for i in range(band...  9.26 us
    ppermute x3, starting transfers between devices, shards(): lax.ppermute(pieces[mask - 1], 'ct', [(i, i ^ mask) for i in range(bands)])  8.31 us
    ppermute x8, starting transfers between devices, swap_chip(): lax.ppermute(value, 'rt', [(i, i ^ 1 << orders[i & 1][stage]) for i in ra...  8.24 us
    ppermute x6, waiting for transfers between devices, sweep(): near = lax.ppermute(update, 'ct', [(stage, stage - 1)])  8.06 us
    ppermute x2, waiting for transfers between devices, sweep(): fars.append(lax.ppermute(rest, 'ct', [(stage, stage - 2)]))  6.17 us
    ppermute x6, starting transfers between devices, sweep(): near = lax.ppermute(update, 'ct', [(stage, stage - 1)])  5.23 us
  transfers between devices with their start and end apart: 29, of which 11 were waited for; matrix products, arithmetic and copies ran while one was open for 0% of the time, Pallas kernels for 20%

profile of v12, /device:TPU:0, one launch (start us, length us, event | category | flops | bytes accessed | tf_op | source)
XLA Modules:
  0.0 95.4 jit_solution(11932270790755982231)
XLA Ops:
  0.0 0.1 pad_add_fusion.where_ref
  0.1 0.7 copy-done.1
  0.7 0.6 first_band.1
  1.4 0.5 collective-permute-start
  1.9 1.5 %collective-permute-done = f32[128,1024]{1,0:T(8,128)S(1)} collective-permute-done((f32[128,1024]{1,0:T(8,128)S(1)}, f32[128,1024]{1,0:T(8,128)S(1)}, u32[]{:S(2)}, u32[]{:S(2)}) %collective-permute-start) | collective-permute-done | bytes 524320 | tf_op jit(solution)/shard_map/ppermute | solution.py:60
  3.4 0.1 add.15
  3.5 2.9 %collective-permute-start.2 = (f32[128,1024]{1,0:T(8,128)S(1)}, f32[128,1024]{1,0:T(8,128)S(1)}, u32[]{:S(2)}, u32[]{:S(2)}) collective-permute-start(f32[128,1024]{1,0:T(8,128)S(1)} %add.15), channel_id=1, source_target_pairs={{0,8},{4,20},{8,0},{12,28},{16,24},{20,4},{24,16},{28,12},{1,9},{5... | collective-permute-start | bytes 1572872 | tf_op jit(solution)/shard_map/ppermute | solution.py:65
  6.4 7.2 %front.1 = (f32[128,1024]{1,0:T(8,128)S(1)}, f32[128,1024]{1,0:T(8,128)S(1)}, f32[256,1024]{1,0:T(8,128)S(1)}, f32[256,1024]{1,0:T(8,128)S(1)}) custom-call(s32[2]{0:T(128)S(1)} %pad_add_fusion.where_ref, s32[48]{0:T(128)S(1)} %copy-done.1, f32[6,2,256,1024]{3,2,1,0:T(8,128)} %factor_ref.5, f32[6,256,256]{2,1,0:T(8,128)} %known_ref.1), custom_call_target="tpu_custom_call" | custom-call | tf_op jit(solution)/shard_map/front/pallas_call | solution.py:23
  13.6 0.1 collective-permute-start.1
  13.7 0.1 add.16
  13.8 1.8 %collective-permute-done.1 = f32[128,1024]{1,0:T(8,128)S(1)} collective-permute-done((f32[128,1024]{1,0:T(8,128)S(1)}, f32[128,1024]{1,0:T(8,128)S(1)}, u32[]{:S(2)}, u32[]{:S(2)}) %collective-permute-start.1) | collective-permute-done | bytes 524320 | tf_op jit(solution)/shard_map/ppermute | solution.py:60
  15.6 0.1 add.17
  15.7 0.2 collective-permute-start.11
  15.9 2.5 %collective-permute-start.3 = (f32[64,1024]{1,0:T(8,128)S(1)}, f32[64,1024]{1,0:T(8,128)S(1)}, u32[]{:S(2)}, u32[]{:S(2)}) collective-permute-start(f32[64,1024]{1,0:T(8,128)S(1)} %slice.13), channel_id=1, source_target_pairs={{0,8},{4,20},{8,0},{12,28},{16,24},{20,4},{24,16},{28,12},{1,9},{5... | collective-permute-start | bytes 786440 | tf_op jit(solution)/shard_map/ppermute | solution.py:65
  18.4 0.2 collective-permute-start.6
  18.6 0.8 top_band.1
  19.4 6.1 %collective-permute-done.3 = f32[64,1024]{1,0:T(8,128)S(1)} collective-permute-done((f32[64,1024]{1,0:T(8,128)S(1)}, f32[64,1024]{1,0:T(8,128)S(1)}, u32[]{:S(2)}, u32[]{:S(2)}) %collective-permute-start.3) | collective-permute-done | bytes 262176 | tf_op jit(solution)/shard_map/ppermute | solution.py:65
  25.6 0.1 collective-permute-start.4
  25.7 0.2 collective-permute-start.5
  25.8 1.8 %collective-permute-done.6 = f32[128,1024]{1,0:T(8,128)S(1)} collective-permute-done((f32[128,1024]{1,0:T(8,128)S(1)}, f32[128,1024]{1,0:T(8,128)S(1)}, u32[]{:S(2)}, u32[]{:S(2)}) %collective-permute-start.6) | collective-permute-done | bytes 524320 | tf_op jit(solution)/shard_map/ppermute | solution.py:65
  27.6 0.1 add.19.mine_ref
  27.7 0.3 collective-permute-start.7
  27.9 2.7 %collective-permute-done.4.got_ref = f32[32,1024]{1,0:T(8,128)S(1)} collective-permute-done((f32[32,1024]{1,0:T(8,128)S(1)}, f32[32,1024]{1,0:T(8,128)S(1)}, u32[]{:S(2)}, u32[]{:S(2)}) %collective-permute-start.4) | collective-permute-done | bytes 131104 | tf_op jit(solution)/shard_map/ppermute | solution.py:65
  30.6 0.6 finish_sum.1
  31.2 0.1 pack_step.4
  31.3 2.1 %collective-permute-start.12 = (f32[192,1024]{1,0:T(8,128)S(1)}, f32[192,1024]{1,0:T(8,128)S(1)}, u32[]{:S(2)}, u32[]{:S(2)}) collective-permute-start(f32[192,1024]{1,0:T(8,128)S(1)} %get-tuple-element.90.refs_4_), channel_id=1, source_target_pairs={{0,8},{4,20},{8,0},{12,28},{16,24},{20,4},{24,16},{28,12},{1,9},{5... | collective-permute-start | bytes 2359304 | tf_op jit(solution)/shard_map/ppermute | solution.py:65
  33.4 0.1 pack_step.3.refs_4_
  33.5 0.1 collective-permute-start.16
  33.6 3.5 %collective-permute-start.10 = (f32[32,256]{1,0:T(8,128)S(1)}, f32[32,256]{1,0:T(8,128)S(1)}, u32[]{:S(2)}, u32[]{:S(2)}) collective-permute-start(f32[32,256]{1,0:T(8,128)S(1)} %get-tuple-element.84), channel_id=1, source_target_pairs={{0,1},{1,2},{2,3},{4,5},{5,6},{6,7},{8,9},{9,10},{10,11},{12,13},{... | collective-permute-start | bytes 98312 | tf_op jit(solution)/shard_map/ppermute | solution.py:571
  37.1 4.5 %collective-permute-start.9 = (f32[32,256]{1,0:T(8,128)S(1)}, f32[32,256]{1,0:T(8,128)S(1)}, u32[]{:S(2)}, u32[]{:S(2)}) collective-permute-start(f32[32,256]{1,0:T(8,128)S(1)} %get-tuple-element.82), channel_id=1, source_target_pairs={{0,2},{1,3},{4,6},{5,7},{8,10},{9,11},{12,14},{13,15},{16,18},{17,... | collective-permute-start | bytes 98312 | tf_op jit(solution)/shard_map/ppermute | solution.py:571
  41.6 1.3 %collective-permute-start.8 = (f32[32,256]{1,0:T(8,128)S(1)}, f32[32,256]{1,0:T(8,128)S(1)}, u32[]{:S(2)}, u32[]{:S(2)}) collective-permute-start(f32[32,256]{1,0:T(8,128)S(1)} %get-tuple-element.80), channel_id=1, source_target_pairs={{0,3},{4,7},{8,11},{12,15},{16,19},{20,23},{24,27},{28,31}} | collective-permute-start | bytes 98312 | tf_op jit(solution)/shard_map/ppermute | solution.py:571
  42.9 3.0 %join.2.tile_ref = f32[256,1024]{1,0:T(8,128)S(1)} custom-call(s32[2]{0:T(128)S(1)} %pad_add_fusion.where_ref, f32[128,1024]{1,0:T(8,128)S(1)} %add.19.mine_ref, f32[128,1024]{1,0:T(8,128)S(1)} %collective-permute-done.7.other_ref), custom_call_target="tpu_custom_call" | custom-call | tf_op jit(solution)/shard_map/join/pallas_call | solution.py:23
  45.9 0.6 stage.8
  46.6 0.7 collective-permute-start.14
  47.3 0.1 collective-permute-start.13
  47.4 0.6 stage.9
  47.9 0.7 collective-permute-start.15
  48.6 1.8 %collective-permute-done.16.refs_5_ = f32[128,1024]{1,0:T(8,128)S(1)} collective-permute-done((f32[128,1024]{1,0:T(8,128)S(1)}, f32[128,1024]{1,0:T(8,128)S(1)}, u32[]{:S(2)}, u32[]{:S(2)}) %collective-permute-start.16) | collective-permute-done | bytes 524320 | tf_op jit(solution)/shard_map/ppermute | solution.py:65
  50.4 0.6 stage.10
  51.1 0.2 collective-permute-start.18
  51.3 1.3 %collective-permute-start.17 = (f32[32,256]{1,0:T(8,128)S(1)}, f32[32,256]{1,0:T(8,128)S(1)}, u32[]{:S(2)}, u32[]{:S(2)}) collective-permute-start(f32[32,256]{1,0:T(8,128)S(1)} %get-tuple-element.101), channel_id=1, source_target_pairs={{1,0},{5,4},{9,8},{13,12},{17,16},{21,20},{25,24},{29,28}} | collective-permute-start | bytes 98312 | tf_op jit(solution)/shard_map/ppermute | solution.py:442
  52.6 5.3 %collective-permute-done.13.got_ref = f32[160,1024]{1,0:T(8,128)S(1)} collective-permute-done((f32[160,1024]{1,0:T(8,128)S(1)}, f32[160,1024]{1,0:T(8,128)S(1)}, u32[]{:S(2)}, u32[]{:S(2)}) %collective-permute-start.13) | collective-permute-done | bytes 655392 | tf_op jit(solution)/shard_map/ppermute | solution.py:65
  57.9 0.1 pack_step.5
  58.0 0.1 collective-permute-start.19
  58.1 5.5 %collective-permute-done.17.refs_0_ = f32[32,256]{1,0:T(8,128)S(1)} collective-permute-done((f32[32,256]{1,0:T(8,128)S(1)}, f32[32,256]{1,0:T(8,128)S(1)}, u32[]{:S(2)}, u32[]{:S(2)}) %collective-permute-start.17) | collective-permute-done | bytes 32800 | tf_op jit(solution)/shard_map/ppermute | solution.py:442
  63.6 1.4 %stage.11 = (f32[32,256]{1,0:T(8,128)S(1)}, f32[32,256]{1,0:T(8,128)}, f32[128,1024]{1,0:T(8,128)S(1)}) custom-call(s32[2]{0:T(128)S(1)} %pad_add_fusion.where_ref, f32[32,256]{1,0:T(8,128)S(1)} %get-tuple-element.73.base_ref, f32[256,1024]{1,0:T(8,128)S(1)} %join.2.tile_ref, f32[32,1024]{1,0:T(8,128)S(1)} %get-tuple-element.74.add_ref, ...), custom_call_target="tpu_custom_call" | custom-call | tf_op jit(solution)/shard_map/stage/pallas_call | solution.py:23
  65.0 1.2 %couple.1 = (f32[32,256]{1,0:T(8,128)S(1)}, f32[32,256]{1,0:T(8,128)S(1)}, f32[32,256]{1,0:T(8,128)S(1)}, f32[32,256]{1,0:T(8,128)S(1)}) custom-call(s32[2]{0:T(128)S(1)} %pad_add_fusion.where_ref, f32[32,1024]{1,0:T(8,128)S(1)} %get-tuple-element.100.sums_ref, f32[32,256]{1,0:T(8,128)S(1)} %get-tuple-element.105.solved_ref.refs_5_, ...), custom_call_target="tpu_custom_call" | custom-call | tf_op jit(solution)/shard_map/couple/pallas_call | solution.py:23
  66.2 5.9 %collective-permute-start.23 = (f32[32,256]{1,0:T(8,128)S(1)}, f32[32,256]{1,0:T(8,128)S(1)}, u32[]{:S(2)}, u32[]{:S(2)}) collective-permute-start(f32[32,256]{1,0:T(8,128)S(1)} %get-tuple-element.112), channel_id=1, source_target_pairs={{0,1},{1,0},{2,3},{3,2},{4,5},{5,4},{6,7},{7,6},{8,9},{9,8},{10,11... | collective-permute-start | bytes 98312 | tf_op jit(solution)/shard_map/ppermute | solution.py:590
  72.0 2.4 %collective-permute-start.21 = (f32[32,256]{1,0:T(8,128)S(1)}, f32[32,256]{1,0:T(8,128)S(1)}, u32[]{:S(2)}, u32[]{:S(2)}) collective-permute-start(f32[32,256]{1,0:T(8,128)S(1)} %get-tuple-element.108), channel_id=1, source_target_pairs={{0,3},{1,2},{2,1},{3,0},{4,7},{5,6},{6,5},{7,4},{8,11},{9,10},{10,... | collective-permute-start | bytes 98312 | tf_op jit(solution)/shard_map/ppermute | solution.py:590
  74.5 0.6 join.3.tile_ref
  75.1 2.8 %collective-permute-done.22.refs_3_ = f32[32,256]{1,0:T(8,128)S(1)} collective-permute-done((f32[32,256]{1,0:T(8,128)S(1)}, f32[32,256]{1,0:T(8,128)S(1)}, u32[]{:S(2)}, u32[]{:S(2)}) %collective-permute-start.22) | collective-permute-done | bytes 32800 | tf_op jit(solution)/shard_map/ppermute | solution.py:590
  77.9 0.6 stage.12
  78.5 0.7 collective-permute-start.24
  79.1 0.6 rest.2
  79.7 0.7 collective-permute-start.26
  80.4 0.6 stage.13
  81.0 0.7 collective-permute-start.25
  81.6 0.6 rest.3
  82.2 1.3 %collective-permute-start.28 = (f32[32,256]{1,0:T(8,128)S(1)}, f32[32,256]{1,0:T(8,128)S(1)}, u32[]{:S(2)}, u32[]{:S(2)}) collective-permute-start(f32[32,256]{1,0:T(8,128)S(1)} %rest.3), channel_id=1, source_target_pairs={{2,0},{6,4},{10,8},{14,12},{18,16},{22,20},{26,24},{30,28}} | collective-permute-start | bytes 98312 | tf_op jit(solution)/shard_map/ppermute | solution.py:445
  83.5 0.6 stage.14
  84.1 1.3 %collective-permute-start.27 = (f32[32,256]{1,0:T(8,128)S(1)}, f32[32,256]{1,0:T(8,128)S(1)}, u32[]{:S(2)}, u32[]{:S(2)}) collective-permute-start(f32[32,256]{1,0:T(8,128)S(1)} %get-tuple-element.119), channel_id=1, source_target_pairs={{1,0},{5,4},{9,8},{13,12},{17,16},{21,20},{25,24},{29,28}} | collective-permute-start | bytes 98312 | tf_op jit(solution)/shard_map/ppermute | solution.py:442
  85.4 6.2 %collective-permute-done.28.refs_1_ = f32[32,256]{1,0:T(8,128)S(1)} collective-permute-done((f32[32,256]{1,0:T(8,128)S(1)}, f32[32,256]{1,0:T(8,128)S(1)}, u32[]{:S(2)}, u32[]{:S(2)}) %collective-permute-start.28) | collective-permute-done | bytes 32800 | tf_op jit(solution)/shard_map/ppermute | solution.py:445
  91.5 2.5 %collective-permute-done.27.refs_0_ = f32[32,256]{1,0:T(8,128)S(1)} collective-permute-done((f32[32,256]{1,0:T(8,128)S(1)}, f32[32,256]{1,0:T(8,128)S(1)}, u32[]{:S(2)}, u32[]{:S(2)}) %collective-permute-start.27) | collective-permute-done | bytes 32800 | tf_op jit(solution)/shard_map/ppermute | solution.py:442
  94.1 1.4 %stage.15 = (f32[2,32,256]{2,1,0:T(8,128)}, f32[32,256]{1,0:T(8,128)}) custom-call(s32[2]{0:T(128)S(1)} %pad_add_fusion.where_ref, f32[32,256]{1,0:T(8,128)S(1)} %get-tuple-element.106.base_ref, f32[256,1024]{1,0:T(8,128)S(1)} %join.3.tile_ref, f32[32,1024]{1,0:T(8,128)S(1)} %broadcast_3_refs_0__add_ref_refs_1__far_ref.2.refs_0_.add_ref.refs_1_.far_ref, ...), custom_call_target="tpu_custom_call" | custom-call | tf_op jit(solution)/shard_map/stage/pallas_call | solution.py:23
  (28 shorter events, 0.1 us)
Async XLA Ops:
  0.1 0.7 copy-start.1
  1.4 2.1 %collective-permute-start = (f32[128,1024]{1,0:T(8,128)S(1)}, f32[128,1024]{1,0:T(8,128)S(1)}, u32[]{:S(2)}, u32[]{:S(2)}) collective-permute-start(f32[128,1024]{1,0:T(8,128)S(1)} %get-tuple-element.64), channel_id=1, source_target_pairs={{0,4},{4,0},{8,12},{12,8},{16,20},{20,16},{24,28},{28,24},{1,5},{5... | collective-permute-start | bytes 1572872 | tf_op jit(solution)/shard_map/ppermute | solution.py:60
  3.5 10.2 %collective-permute-start.2 = (f32[128,1024]{1,0:T(8,128)S(1)}, f32[128,1024]{1,0:T(8,128)S(1)}, u32[]{:S(2)}, u32[]{:S(2)}) collective-permute-start(f32[128,1024]{1,0:T(8,128)S(1)} %add.15), channel_id=1, source_target_pairs={{0,8},{4,20},{8,0},{12,28},{16,24},{20,4},{24,16},{28,12},{1,9},{5... | collective-permute-start | bytes 1572872 | tf_op jit(solution)/shard_map/ppermute | solution.py:65
  13.6 17.0 %copy-start = (f32[2,256,32]{1,2,0:T(8,128)S(1)}, f32[2,256,32]{1,2,0:T(8,128)}, u32[]{:S(2)}) copy-start(f32[2,256,32]{1,2,0:T(8,128)} %param.7) | copy-start | bytes 196612
  13.6 2.0 %collective-permute-start.1 = (f32[128,1024]{1,0:T(8,128)S(1)}, f32[128,1024]{1,0:T(8,128)S(1)}, u32[]{:S(2)}, u32[]{:S(2)}) collective-permute-start(f32[128,1024]{1,0:T(8,128)S(1)} %get-tuple-element.67), channel_id=1, source_target_pairs={{0,4},{4,0},{8,12},{12,8},{16,20},{20,16},{24,28},{28,24},{1,5},{5... | collective-permute-start | bytes 1572872 | tf_op jit(solution)/shard_map/ppermute | solution.py:60
  15.7 15.5 %collective-permute-start.11 = (f32[256,1024]{1,0:T(8,128)S(1)}, f32[256,1024]{1,0:T(8,128)S(1)}, u32[]{:S(2)}, u32[]{:S(2)}) collective-permute-start(f32[256,1024]{1,0:T(8,128)S(1)} %get-tuple-element.88), channel_id=1, source_target_pairs={{0,4},{4,0},{8,12},{12,8},{16,20},{20,16},{24,28},{28,24},{1,5},{5... | collective-permute-start | bytes 3145736 | tf_op jit(solution)/shard_map/ppermute | solution.py:60
  15.9 9.6 %collective-permute-start.3 = (f32[64,1024]{1,0:T(8,128)S(1)}, f32[64,1024]{1,0:T(8,128)S(1)}, u32[]{:S(2)}, u32[]{:S(2)}) collective-permute-start(f32[64,1024]{1,0:T(8,128)S(1)} %slice.13), channel_id=1, source_target_pairs={{0,8},{4,20},{8,0},{12,28},{16,24},{20,4},{24,16},{28,12},{1,9},{5... | collective-permute-start | bytes 786440 | tf_op jit(solution)/shard_map/ppermute | solution.py:65
  18.4 9.2 %collective-permute-start.6 = (f32[128,1024]{1,0:T(8,128)S(1)}, f32[128,1024]{1,0:T(8,128)S(1)}, u32[]{:S(2)}, u32[]{:S(2)}) collective-permute-start(f32[128,1024]{1,0:T(8,128)S(1)} %add.16), channel_id=1, source_target_pairs={{0,16},{4,12},{8,24},{12,4},{16,0},{20,28},{24,8},{28,20},{1,17},{... | collective-permute-start | bytes 1572872 | tf_op jit(solution)/shard_map/ppermute | solution.py:65
  25.6 5.0 %collective-permute-start.4 = (f32[32,1024]{1,0:T(8,128)S(1)}, f32[32,1024]{1,0:T(8,128)S(1)}, u32[]{:S(2)}, u32[]{:S(2)}) collective-permute-start(f32[32,1024]{1,0:T(8,128)S(1)} %slice.14), channel_id=1, source_target_pairs={{0,16},{4,12},{8,24},{12,4},{16,0},{20,28},{24,8},{28,20},{1,17},{... | collective-permute-start | bytes 393224 | tf_op jit(solution)/shard_map/ppermute | solution.py:65
  25.7 7.8 %collective-permute-start.5 = (f32[128,1024]{1,0:T(8,128)S(1)}, f32[128,1024]{1,0:T(8,128)S(1)}, u32[]{:S(2)}, u32[]{:S(2)}) collective-permute-start(f32[128,1024]{1,0:T(8,128)S(1)} %get-tuple-element.76), channel_id=1, source_target_pairs={{0,4},{4,0},{8,12},{12,8},{16,20},{20,16},{24,28},{28,24},{1,5},{5... | collective-permute-start | bytes 1572872 | tf_op jit(solution)/shard_map/ppermute | solution.py:60
  27.7 5.8 %collective-permute-start.7 = (f32[128,1024]{1,0:T(8,128)S(1)}, f32[128,1024]{1,0:T(8,128)S(1)}, u32[]{:S(2)}, u32[]{:S(2)}) collective-permute-start(f32[128,1024]{1,0:T(8,128)S(1)} %add.19.mine_ref), channel_id=1, source_target_pairs={{0,4},{4,0},{8,12},{12,8},{16,20},{20,16},{24,28},{28,24},{1,5},{5... | collective-permute-start | bytes 1572872 | tf_op jit(solution)/shard_map/ppermute | solution.py:60
  31.3 14.6 %collective-permute-start.12 = (f32[192,1024]{1,0:T(8,128)S(1)}, f32[192,1024]{1,0:T(8,128)S(1)}, u32[]{:S(2)}, u32[]{:S(2)}) collective-permute-start(f32[192,1024]{1,0:T(8,128)S(1)} %get-tuple-element.90.refs_4_), channel_id=1, source_target_pairs={{0,8},{4,20},{8,0},{12,28},{16,24},{20,4},{24,16},{28,12},{1,9},{5... | collective-permute-start | bytes 2359304 | tf_op jit(solution)/shard_map/ppermute | solution.py:65
  33.5 16.9 %collective-permute-start.16 = (f32[128,1024]{1,0:T(8,128)S(1)}, f32[128,1024]{1,0:T(8,128)S(1)}, u32[]{:S(2)}, u32[]{:S(2)}) collective-permute-start(f32[128,1024]{1,0:T(8,128)S(1)} %pack_step.3.refs_4_), channel_id=1, source_target_pairs={{0,8},{4,20},{8,0},{12,28},{16,24},{20,4},{24,16},{28,12},{1,9},{5... | collective-permute-start | bytes 1572872 | tf_op jit(solution)/shard_map/ppermute | solution.py:65
  33.6 12.3 %collective-permute-start.10 = (f32[32,256]{1,0:T(8,128)S(1)}, f32[32,256]{1,0:T(8,128)S(1)}, u32[]{:S(2)}, u32[]{:S(2)}) collective-permute-start(f32[32,256]{1,0:T(8,128)S(1)} %get-tuple-element.84), channel_id=1, source_target_pairs={{0,1},{1,2},{2,3},{4,5},{5,6},{6,7},{8,9},{9,10},{10,11},{12,13},{... | collective-permute-start | bytes 98312 | tf_op jit(solution)/shard_map/ppermute | solution.py:571
  37.1 8.8 %collective-permute-start.9 = (f32[32,256]{1,0:T(8,128)S(1)}, f32[32,256]{1,0:T(8,128)S(1)}, u32[]{:S(2)}, u32[]{:S(2)}) collective-permute-start(f32[32,256]{1,0:T(8,128)S(1)} %get-tuple-element.82), channel_id=1, source_target_pairs={{0,2},{1,3},{4,6},{5,7},{8,10},{9,11},{12,14},{13,15},{16,18},{17,... | collective-permute-start | bytes 98312 | tf_op jit(solution)/shard_map/ppermute | solution.py:571
  41.6 4.3 %collective-permute-start.8 = (f32[32,256]{1,0:T(8,128)S(1)}, f32[32,256]{1,0:T(8,128)S(1)}, u32[]{:S(2)}, u32[]{:S(2)}) collective-permute-start(f32[32,256]{1,0:T(8,128)S(1)} %get-tuple-element.80), channel_id=1, source_target_pairs={{0,3},{4,7},{8,11},{12,15},{16,19},{20,23},{24,27},{28,31}} | collective-permute-start | bytes 98312 | tf_op jit(solution)/shard_map/ppermute | solution.py:571
  46.6 0.8 collective-permute-start.14
  47.3 10.7 %collective-permute-start.13 = (f32[160,1024]{1,0:T(8,128)S(1)}, f32[160,1024]{1,0:T(8,128)S(1)}, u32[]{:S(2)}, u32[]{:S(2)}) collective-permute-start(f32[160,1024]{1,0:T(8,128)S(1)} %get-tuple-element.92.tiles_ref), channel_id=1, source_target_pairs={{0,16},{4,12},{8,24},{12,4},{16,0},{20,28},{24,8},{28,20},{1,17},{... | collective-permute-start | bytes 1966088 | tf_op jit(solution)/shard_map/ppermute | solution.py:65
  47.9 2.5 %collective-permute-start.15 = (f32[32,512]{1,0:T(8,128)S(1)}, f32[32,512]{1,0:T(8,128)S(1)}, u32[]{:S(2)}, u32[]{:S(2)}) collective-permute-start(f32[32,512]{1,0:T(8,128)S(1)} %get-tuple-element.97), channel_id=1, source_target_pairs={{2,1},{6,5},{10,9},{14,13},{18,17},{22,21},{26,25},{30,29}} | collective-permute-start | bytes 196616 | tf_op jit(solution)/shard_map/ppermute | solution.py:442
  51.1 12.5 %collective-permute-start.18 = (f32[128,1024]{1,0:T(8,128)S(1)}, f32[128,1024]{1,0:T(8,128)S(1)}, u32[]{:S(2)}, u32[]{:S(2)}) collective-permute-start(f32[128,1024]{1,0:T(8,128)S(1)} %get-tuple-element.104.refs_4_), channel_id=1, source_target_pairs={{0,16},{4,12},{8,24},{12,4},{16,0},{20,28},{24,8},{28,20},{1,17},{... | collective-permute-start | bytes 1572872 | tf_op jit(solution)/shard_map/ppermute | solution.py:65
  51.3 12.3 %collective-permute-start.17 = (f32[32,256]{1,0:T(8,128)S(1)}, f32[32,256]{1,0:T(8,128)S(1)}, u32[]{:S(2)}, u32[]{:S(2)}) collective-permute-start(f32[32,256]{1,0:T(8,128)S(1)} %get-tuple-element.101), channel_id=1, source_target_pairs={{1,0},{5,4},{9,8},{13,12},{17,16},{21,20},{25,24},{29,28}} | collective-permute-start | bytes 98312 | tf_op jit(solution)/shard_map/ppermute | solution.py:442
  58.0 7.0 %collective-permute-start.19 = (f32[128,1024]{1,0:T(8,128)S(1)}, f32[128,1024]{1,0:T(8,128)S(1)}, u32[]{:S(2)}, u32[]{:S(2)}) collective-permute-start(f32[128,1024]{1,0:T(8,128)S(1)} %get-tuple-element.102.mine_ref), channel_id=1, source_target_pairs={{0,4},{4,0},{8,12},{12,8},{16,20},{20,16},{24,28},{28,24},{1,5},{5... | collective-permute-start | bytes 1572872 | tf_op jit(solution)/shard_map/ppermute | solution.py:60
  65.0 9.5 %collective-permute-start.20 = (f32[128,1024]{1,0:T(8,128)S(1)}, f32[128,1024]{1,0:T(8,128)S(1)}, u32[]{:S(2)}, u32[]{:S(2)}) collective-permute-start(f32[128,1024]{1,0:T(8,128)S(1)} %get-tuple-element.107.mine_ref), channel_id=1, source_target_pairs={{0,4},{4,0},{8,12},{12,8},{16,20},{20,16},{24,28},{28,24},{1,5},{5... | collective-permute-start | bytes 1572872 | tf_op jit(solution)/shard_map/ppermute | solution.py:60
  66.2 8.9 %collective-permute-start.23 = (f32[32,256]{1,0:T(8,128)S(1)}, f32[32,256]{1,0:T(8,128)S(1)}, u32[]{:S(2)}, u32[]{:S(2)}) collective-permute-start(f32[32,256]{1,0:T(8,128)S(1)} %get-tuple-element.112), channel_id=1, source_target_pairs={{0,1},{1,0},{2,3},{3,2},{4,5},{5,4},{6,7},{7,6},{8,9},{9,8},{10,11... | collective-permute-start | bytes 98312 | tf_op jit(solution)/shard_map/ppermute | solution.py:590
  72.0 5.9 %collective-permute-start.22 = (f32[32,256]{1,0:T(8,128)S(1)}, f32[32,256]{1,0:T(8,128)S(1)}, u32[]{:S(2)}, u32[]{:S(2)}) collective-permute-start(f32[32,256]{1,0:T(8,128)S(1)} %get-tuple-element.110), channel_id=1, source_target_pairs={{0,2},{1,3},{2,0},{3,1},{4,6},{5,7},{6,4},{7,5},{8,10},{9,11},{10,... | collective-permute-start | bytes 98312 | tf_op jit(solution)/shard_map/ppermute | solution.py:590
  72.0 5.9 %collective-permute-start.21 = (f32[32,256]{1,0:T(8,128)S(1)}, f32[32,256]{1,0:T(8,128)S(1)}, u32[]{:S(2)}, u32[]{:S(2)}) collective-permute-start(f32[32,256]{1,0:T(8,128)S(1)} %get-tuple-element.108), channel_id=1, source_target_pairs={{0,3},{1,2},{2,1},{3,0},{4,7},{5,6},{6,5},{7,4},{8,11},{9,10},{10,... | collective-permute-start | bytes 98312 | tf_op jit(solution)/shard_map/ppermute | solution.py:590
  78.5 1.9 %collective-permute-start.24 = (f32[32,256]{1,0:T(8,128)S(1)}, f32[32,256]{1,0:T(8,128)S(1)}, u32[]{:S(2)}, u32[]{:S(2)}) collective-permute-start(f32[32,256]{1,0:T(8,128)S(1)} %get-tuple-element.115), channel_id=1, source_target_pairs={{3,2},{7,6},{11,10},{15,14},{19,18},{23,22},{27,26},{31,30}} | collective-permute-start | bytes 98312 | tf_op jit(solution)/shard_map/ppermute | solution.py:442
  79.7 3.8 %collective-permute-start.26 = (f32[32,512]{1,0:T(8,128)S(1)}, f32[32,512]{1,0:T(8,128)S(1)}, u32[]{:S(2)}, u32[]{:S(2)}) collective-permute-start(f32[32,512]{1,0:T(8,128)S(1)} %rest.2), channel_id=1, source_target_pairs={{3,1},{7,5},{11,9},{15,13},{19,17},{23,21},{27,25},{31,29}} | collective-permute-start | bytes 196616 | tf_op jit(solution)/shard_map/ppermute | solution.py:445
  81.0 2.5 %collective-permute-start.25 = (f32[32,256]{1,0:T(8,128)S(1)}, f32[32,256]{1,0:T(8,128)S(1)}, u32[]{:S(2)}, u32[]{:S(2)}) collective-permute-start(f32[32,256]{1,0:T(8,128)S(1)} %get-tuple-element.117), channel_id=1, source_target_pairs={{2,1},{6,5},{10,9},{14,13},{18,17},{22,21},{26,25},{30,29}} | collective-permute-start | bytes 98312 | tf_op jit(solution)/shard_map/ppermute | solution.py:442
  82.2 9.4 %collective-permute-start.28 = (f32[32,256]{1,0:T(8,128)S(1)}, f32[32,256]{1,0:T(8,128)S(1)}, u32[]{:S(2)}, u32[]{:S(2)}) collective-permute-start(f32[32,256]{1,0:T(8,128)S(1)} %rest.3), channel_id=1, source_target_pairs={{2,0},{6,4},{10,8},{14,12},{18,16},{22,20},{26,24},{30,28}} | collective-permute-start | bytes 98312 | tf_op jit(solution)/shard_map/ppermute | solution.py:445
  84.1 10.0 %collective-permute-start.27 = (f32[32,256]{1,0:T(8,128)S(1)}, f32[32,256]{1,0:T(8,128)S(1)}, u32[]{:S(2)}, u32[]{:S(2)}) collective-permute-start(f32[32,256]{1,0:T(8,128)S(1)} %get-tuple-element.119), channel_id=1, source_target_pairs={{1,0},{5,4},{9,8},{13,12},{17,16},{21,20},{25,24},{29,28}} | collective-permute-start | bytes 98312 | tf_op jit(solution)/shard_map/ppermute | solution.py:442
